TPU v7x, 128 devices: a whole 4x4x4 slice. The times are simulated.
128 devices in a mesh: bond: 8 (over x, core), op: 16 (over y, z).
Axes of the slice: x: 4, y: 4, z: 4, core: 2. Of those that a mesh axis runs over, the one named last changes fastest.
Arguments:
- wave_slab: bfloat16 [8192, 8192], P('op', 'bond'), may hold values from -6 to 6
- left_blocks: bfloat16 [32, 16, 2, 128, 128], P('op'), may hold values from -0.375 to 0.375
- right_blocks: bfloat16 [32, 64, 2, 128, 128], P('op'), may hold values from -0.0625 to 0.0625
- sector_size: int32 [64], replicated, may hold values from 1 to 128
- left_pairs: int32 [32, 16, 2], P('op'), may hold values from 0 to 63
- right_pairs: int32 [32, 64, 2], P('op'), may hold values from 0 to 63
Outputs:
- applied: float32 [2048, 8192], P('bond', 'op')
All inputs are finite; a program needn't handle non-finite values.
Results may differ from a plain program's by a relative error of at most 0.0029.
Values may be sent and summed in bfloat16 or wider, within the bound.
No kernel may reach another device: no remote copies, remote signals or barrier semaphores. Data moves between devices by JAX's collectives and lax.ppermute only.
A program may use at most 128 MiB of HBM per device.

v0:
```python
import functools

import jax
import jax.numpy as jnp
from jax import lax
from jax.experimental import pallas as pl
from jax.experimental.pallas import tpu as pltpu
from jax.sharding import PartitionSpec as P


TILE = 128
SIDE = 4
GROUP = SIDE * SIDE
BF16 = jnp.bfloat16
F32 = jnp.float32
CHUNKS = (256, 256, 256, 256)
NEAR_GROUPS = ((0, 1), (2, 3))


def move(value, step_y, step_z):
    pairs = [
        (y * SIDE + z, (y + step_y) % SIDE * SIDE + (z + step_z) % SIDE)
        for y in range(SIDE)
        for z in range(SIDE)
    ]
    return lax.ppermute(value, "op", pairs)


def left_kernel(first_sector, layout, place, pairs, size, *refs):
    pieces = refs[: len(layout)]
    left_hbm, out, whole, left, sems, left_sem = refs[len(layout) :]
    y, z, bond = place[0], place[1], place[2]
    width = whole.shape[2]
    copies = [pltpu.make_async_copy(left_hbm, left, left_sem)]
    for piece, (upper, far, first) in zip(pieces, layout):
        for slot in range(piece.shape[0]):
            near = first + slot
            step_y, step_z = (far, near) if upper else (near, far)
            owner = (y + SIDE - step_y) % SIDE * SIDE + (z + SIDE - step_z) % SIDE
            start = owner * 4 + (0 if upper else 2)
            copies.append(
                pltpu.make_async_copy(
                    piece.at[slot], whole.at[pl.ds(start, 2)], sems.at[len(copies) - 1]
                )
            )
    for copy in copies:
        copy.start()
    for copy in copies:
        copy.wait()
    lane = lax.broadcasted_iota(jnp.int32, (TILE, TILE), 1)
    strip_sectors = 8
    col_live = jnp.concatenate(
        [
            (lane[:1] < size[bond * strip_sectors + first_sector + s]).astype(F32)
            for s in range(width // TILE)
        ],
        axis=1,
    )
    terms, rows = left.shape[0], left.shape[1]
    zero = jnp.zeros((TILE, TILE), BF16)
    unroll = 4

    @pl.loop(0, terms * rows // unroll)
    def _(trip):
        for u in range(unroll):
            step = trip * unroll + u
            term, row = step // rows, step % rows
            low, high = pairs[step * 2], pairs[step * 2 + 1]
            lhs = jnp.concatenate(
                [
                    jnp.where(lane < size[low], left[term, row, 0], zero),
                    jnp.where(lane < size[high], left[term, row, 1], zero),
                ],
                axis=1,
            )
            rhs = jnp.concatenate([whole[low], whole[high]], axis=0)
            middle = (jnp.dot(lhs, rhs, preferred_element_type=F32) * col_live).astype(BF16)
            for s in range(width // TILE):
                out[row // 2, s, term, pl.ds(row % 2 * TILE, TILE), :] = middle[
                    :, s * TILE : (s + 1) * TILE
                ]


def left_stage(pieces, layout, left_blocks, place, pairs, size, first_sector):
    width = pieces[0].shape[-1]
    terms = left_blocks.shape[0]
    sector_count = width // TILE
    return pl.pallas_call(
        functools.partial(left_kernel, first_sector, layout),
        out_shape=jax.ShapeDtypeStruct((8, sector_count, terms, 2 * TILE, TILE), BF16),
        grid_spec=pltpu.PrefetchScalarGridSpec(
            num_scalar_prefetch=3,
            grid=(1,),
            in_specs=[pl.BlockSpec(memory_space=pl.ANY)] * (len(pieces) + 1),
            out_specs=pl.BlockSpec(
                (8, sector_count, terms, 2 * TILE, TILE), lambda i, *_: (0, 0, 0, 0, 0)
            ),
            scratch_shapes=[
                pltpu.VMEM((64, TILE, width), BF16),
                pltpu.VMEM(left_blocks.shape, BF16),
                pltpu.SemaphoreType.DMA((32,)),
                pltpu.SemaphoreType.DMA(()),
            ],
        ),
        compiler_params=pltpu.CompilerParams(vmem_limit_bytes=60 << 20),
        cost_estimate=pl.CostEstimate(
            flops=2 * terms * 2048 * 256 * width,
            bytes_accessed=8192 * width * 2 + (2 << 20) + terms * 2048 * width * 2,
            transcendentals=0,
        ),
    )(place, pairs, size, *pieces, left_blocks)


def right_kernel(counts, place, pairs, size, *refs):
    arrived = refs[: len(counts)]
    right_hbm = refs[len(counts)]
    outs_a = refs[len(counts) + 1 : len(counts) + 5]
    outs_b = refs[len(counts) + 5 : len(counts) + 9]
    middle, right, sum_a, sum_b, sems, right_sems, out_sems = refs[len(counts) + 9 :]
    bond = place[2]
    copies = []
    first = 0
    for chunk, count in zip(arrived, counts):
        for source in range(8):
            copies.append(
                pltpu.make_async_copy(
                    chunk.at[source],
                    middle.at[pl.ds(source * 8 + first, count)],
                    sems.at[len(copies)],
                )
            )
        first += count
    for copy in copies:
        copy.start()

    def owner_of(step_z, step_y):
        return (place[0] + step_y) % SIDE * SIDE + (place[1] + step_z) % SIDE

    def right_copy(step_z, step_y):
        return pltpu.make_async_copy(
            right_hbm.at[:, pl.ds(owner_of(step_z, step_y) * 4, 4)],
            right.at[step_z * SIDE + step_y],
            right_sems.at[step_z * SIDE + step_y],
        )

    for step_z in range(SIDE):
        for step_y in range(SIDE):
            right_copy(step_z, step_y).start()
    rows = middle.shape[2]
    terms = middle.shape[1]
    line = lax.broadcasted_iota(jnp.int32, (TILE, TILE), 0)
    lane = lax.broadcasted_iota(jnp.int32, (TILE, TILE), 1)
    row_live = jnp.concatenate([line < size[bond * 2 + h] for h in range(rows // TILE)], axis=0)
    lanes = jnp.concatenate([lane] * (rows // TILE), axis=0)
    for copy in copies:
        copy.wait()
    sent = []
    for step_z in range(SIDE):

        @pl.loop(0, SIDE)
        def _(step_y):
            right_copy(step_z, step_y).wait()
            owner = owner_of(step_z, step_y)
            blocks = right.at[step_z * SIDE + step_y]
            for q in range(4):
                col = owner * 4 + q
                lhs = jnp.concatenate(
                    [
                        middle[pairs[(term * 64 + col) * 2 + p], term]
                        for term in range(terms)
                        for p in range(2)
                    ],
                    axis=1,
                )
                rhs = jnp.concatenate(
                    [blocks[term, q, p] for term in range(terms) for p in range(2)], axis=0
                )
                product = jnp.dot(lhs, rhs, preferred_element_type=F32)
                keep = row_live & (lanes < size[col])
                value = jnp.where(keep, product, 0.0).astype(BF16)
                if q < 2:
                    sum_a[step_z, step_y, :, q * TILE : (q + 1) * TILE] = value
                else:
                    sum_b[step_y, step_z, :, (q - 2) * TILE : (q - 1) * TILE] = value

        sent.append(
            pltpu.make_async_copy(sum_a.at[step_z], outs_a[step_z], out_sems.at[len(sent)])
        )
        sent[-1].start()
        for k in range(SIDE):
            sent.append(
                pltpu.make_async_copy(
                    sum_b.at[k, step_z], outs_b[k].at[step_z], out_sems.at[len(sent)]
                )
            )
            sent[-1].start()
    for copy in sent:
        copy.wait()


def right_stage(arrived, right_blocks, place, pairs, size):
    counts = tuple(a.shape[1] for a in arrived)
    terms, rows = arrived[0].shape[2], arrived[0].shape[3]
    shape = jax.ShapeDtypeStruct((SIDE, rows, 2 * TILE), BF16)
    anywhere = pl.BlockSpec(memory_space=pl.ANY)
    return pl.pallas_call(
        functools.partial(right_kernel, counts),
        name="right",
        out_shape=[shape] * 8,
        grid_spec=pltpu.PrefetchScalarGridSpec(
            num_scalar_prefetch=3,
            grid=(1,),
            in_specs=[anywhere] * (len(counts) + 1),
            out_specs=[anywhere] * 8,
            scratch_shapes=[
                pltpu.VMEM((64, terms, rows, TILE), BF16),
                pltpu.VMEM((GROUP, terms, 4, 2, TILE, TILE), BF16),
                pltpu.VMEM((SIDE, SIDE, rows, 2 * TILE), BF16),
                pltpu.VMEM((SIDE, SIDE, rows, 2 * TILE), BF16),
                pltpu.SemaphoreType.DMA((8 * len(counts),)),
                pltpu.SemaphoreType.DMA((GROUP,)),
                pltpu.SemaphoreType.DMA((SIDE * (SIDE + 1),)),
            ],
        ),
        compiler_params=pltpu.CompilerParams(vmem_limit_bytes=60 << 20),
        cost_estimate=pl.CostEstimate(
            flops=2 * terms * rows * 256 * 8192,
            bytes_accessed=(20 << 20),
            transcendentals=0,
        ),
    )(place, pairs, size, *arrived, right_blocks)


def sum_kernel(*refs):
    inputs, outputs = refs[:8], refs[8:]
    for half in range(2):
        mine = inputs[half * 4 : half * 4 + 4]
        total = mine[0][...].astype(F32)
        for other in mine[1:]:
            total = total + other[...].astype(F32)
        kept = outputs[half * 4 : half * 4 + 4]
        kept[0][...] = total[0]
        for k in range(1, SIDE):
            kept[k][...] = total[k].astype(BF16)


def sum_stage(pieces):
    rows, width = pieces[0].shape[1:]
    whole = pl.BlockSpec(memory_space=pltpu.VMEM)
    kinds = [F32, BF16, BF16, BF16]
    return pl.pallas_call(
        sum_kernel,
        name="near_sum",
        out_shape=[jax.ShapeDtypeStruct((rows, width), kind) for kind in kinds * 2],
        in_specs=[whole] * 8,
        out_specs=[whole] * 8,
        compiler_params=pltpu.CompilerParams(vmem_limit_bytes=16 << 20),
    )(*pieces)


def last_kernel(*refs):
    out = refs[8]
    width = refs[0].shape[1]
    for half in range(2):
        mine = refs[half * 4 : half * 4 + 4]
        total = mine[0][...]
        for other in mine[1:]:
            total = total + other[...].astype(F32)
        out[:, half * width : (half + 1) * width] = total


def last_stage(pieces):
    rows, width = pieces[0].shape
    whole = pl.BlockSpec(memory_space=pltpu.VMEM)
    return pl.pallas_call(
        last_kernel,
        name="far_sum",
        out_shape=jax.ShapeDtypeStruct((rows, 2 * width), F32),
        in_specs=[whole] * 8,
        out_specs=whole,
        compiler_params=pltpu.CompilerParams(vmem_limit_bytes=16 << 20),
    )(*pieces)


def near_row(value, upper):
    steps = [(0, d) if upper else (d, 0) for d in range(1, SIDE)]
    return [value] + [move(value, *step) for step in steps]


def far_pieces(row, upper, forward):
    def turn(value, d):
        return move(value, d, 0) if upper else move(value, 0, d)

    before, after = turn(row, 1), turn(row, SIDE - 1)
    if not forward:
        opposite = turn(row, 2)
        return [(row, 0, 0), (before, 1, 0), (after, 3, 0), (opposite, 2, 0)]
    half = SIDE // 2
    return [
        (row, 0, 0),
        (before, 1, 0),
        (after, 3, 0),
        (turn(before[:half], 1), 2, 0),
        (turn(after[half:], SIDE - 1), 2, half),
    ]


def apply_slab(wave_slab, left_blocks, right_blocks, sector_size, left_pairs, right_pairs):
    group = lax.axis_index("op")
    place = jnp.stack([group // SIDE, group % SIDE, lax.axis_index("bond")]).astype(jnp.int32)
    lefts, rights = left_pairs.reshape(-1), right_pairs.reshape(-1)
    sectors = wave_slab.reshape(4, TILE, wave_slab.shape[1])
    starts = [sum(CHUNKS[:chunk]) for chunk in range(len(CHUNKS) + 1)]
    rows = {}
    for members in NEAR_GROUPS:
        low, high = starts[members[0]], starts[members[-1] + 1]
        both = [near_row(sectors[:2, :, low:high], True), near_row(sectors[2:, :, low:high], False)]
        for chunk in members:
            part = slice(starts[chunk] - low, starts[chunk + 1] - low)
            rows[chunk] = [jnp.stack([v[:, :, part] for v in side]) for side in both]
    arrived = []
    for chunk in range(len(CHUNKS)):
        pieces, layout = [], []
        for row, upper in zip(rows[chunk], (True, False)):
            for value, far, first in far_pieces(row, upper, chunk > 0):
                pieces.append(value)
                layout.append((upper, far, first))
        middle = left_stage(
            pieces, tuple(layout), left_blocks, place, lefts, sector_size, starts[chunk] // TILE
        )
        arrived.append(
            lax.all_to_all(middle, "bond", split_axis=0, concat_axis=0, tiled=True)
        )
    parts = right_stage(arrived, right_blocks, place, rights, sector_size)
    near = [parts[0]] + [move(parts[d], 0, d) for d in range(1, SIDE)]
    near += [parts[4]] + [move(parts[4 + d], d, 0) for d in range(1, SIDE)]
    sums = sum_stage(near)
    far = [sums[0]] + [move(sums[d], d, 0) for d in range(1, SIDE)]
    far += [sums[4]] + [move(sums[4 + d], 0, d) for d in range(1, SIDE)]
    return last_stage(far)


def solution(mesh):
    placed = (
        P("op", "bond"),
        P("op", None, None, None, None),
        P("op", None, None, None, None),
        P(),
        P("op", None, None),
        P("op", None, None),
    )
    return jax.shard_map(
        apply_slab, mesh=mesh, in_specs=placed, out_specs=P("bond", "op"), check_vma=False
    )
```

profile of v0, /device:TPU:0, one launch (start us, length us, event | category | flops | bytes accessed | tf_op | source)
XLA Modules:
  0.0 301.1 jit_solution(13066046062575199063)
XLA Ops:
  5.8 3.6 %collective-permute-start.21 = (bf16[2,128,512]{2,1,0:T(8,128)(2,1)}, bf16[2,128,512]{2,1,0:T(8,128)(2,1)}, u32[]{:S(2)}, u32[]{:S(2)}) collective-permute-start(bf16[2,128,512]{2,1,0:T(8,128)(2,1)} %get-tuple-element.46), channel_id=1, source_target_pairs={{0,2},{1,3},{2,0},{3,1},{4,6},{5,7},{6,4},{7,5},{8,10},{9,11},{10,... | collective-permute-start | bytes 786440 | tf_op jit(solution)/shard_map/ppermute | solution.py:26
  9.4 2.9 collective-permute-start.7
  15.1 3.3 %collective-permute-done.7 = bf16[2,128,512]{2,1,0:T(8,128)(2,1)S(1)} collective-permute-done((bf16[2,128,512]{2,1,0:T(8,128)(2,1)S(1)}, bf16[2,128,512]{2,1,0:T(8,128)(2,1)S(1)}, u32[]{:S(2)}, u32[]{:S(2)}) %collective-permute-start.7) | collective-permute-done | bytes 262176 | tf_op jit(solution)/shard_map/ppermute | solution.py:26
  18.4 3.9 %collective-permute-start.1 = (bf16[2,128,512]{2,1,0:T(8,128)(2,1)S(1)}, bf16[2,128,512]{2,1,0:T(8,128)(2,1)S(1)}, u32[]{:S(2)}, u32[]{:S(2)}) collective-permute-start(bf16[2,128,512]{2,1,0:T(8,128)(2,1)S(1)} %get-tuple-element.48), channel_id=1, source_target_pairs={{0,2},{1,3},{2,0},{3,1},{4,6},{5,7},{6,4},{7,5},{8,10},{9,11},{10,... | collective-permute-start | bytes 786440 | tf_op jit(solution)/shard_map/ppermute | solution.py:26
  24.5 3.3 %collective-permute-done = bf16[2,128,512]{2,1,0:T(8,128)(2,1)S(1)} collective-permute-done((bf16[2,128,512]{2,1,0:T(8,128)(2,1)S(1)}, bf16[2,128,512]{2,1,0:T(8,128)(2,1)S(1)}, u32[]{:S(2)}, u32[]{:S(2)}) %collective-permute-start) | collective-permute-done | bytes 262176 | tf_op jit(solution)/shard_map/ppermute | solution.py:26
  29.3 3.0 collective-permute-done.1
  37.7 2.4 collective-permute-start.4
  40.2 7.2 %collective-permute-done.10.refs_6_ = bf16[4,2,128,256]{3,2,1,0:T(8,128)(2,1)S(1)} collective-permute-done((bf16[4,2,128,256]{3,2,1,0:T(8,128)(2,1)S(1)}, bf16[4,2,128,256]{3,2,1,0:T(8,128)(2,1)S(1)}, u32[]{:S(2)}, u32[]{:S(2)}) %collective-permute-start.10) | collective-permute-done | bytes 524320 | tf_op jit(solution)/shard_map/ppermute | solution.py:26
  52.2 7.2 %collective-permute-start.22 = (bf16[2,128,512]{2,1,0:T(8,128)(2,1)}, bf16[2,128,512]{2,1,0:T(8,128)(2,1)}, u32[]{:S(2)}, u32[]{:S(2)}) collective-permute-start(bf16[2,128,512]{2,1,0:T(8,128)(2,1)} %get-tuple-element.46), channel_id=1, source_target_pairs={{0,3},{1,0},{2,1},{3,2},{4,7},{5,4},{6,5},{7,6},{8,11},{9,8},{10,9... | collective-permute-start | bytes 786440 | tf_op jit(solution)/shard_map/ppermute | solution.py:26
  63.4 2.5 collective-permute-start.29
  66.0 7.5 %shard_map.64 = bf16[8,2,2,256,128]{4,3,2,1,0:T(8,128)(2,1)} custom-call(s32[3]{0:T(128)} %pad_add_fusion.place, s32[64]{0:T(128)} %reshape.10.pairs, s32[64]{0:T(128)} %size.9, bf16[4,2,128,256]{3,2,1,0:T(8,128)(2,1)} %copy-done.8, bf16[4,2,128,256]{3,2,1,0:T(8,128)(2,1)} %copy-done.28, bf16[4,2,128,256]{3,2,1,0:T(8,128)(2,1)} %collective-permute-done.4.refs_2_, ...), custom_call_target="tpu_custom_call" | custom-call | flops 536870912 | bytes 8388608 | tf_op jit(solution)/shard_map/pallas_call | solution.py:88
  73.5 4.4 %all-to-all-start = ((bf16[8,2,2,256,128]{4,3,2,1,0:T(8,128)(2,1)}), bf16[8,2,2,256,128]{4,3,2,1,0:T(8,128)(2,1)S(1)}, u32[]{:S(2)}, u32[]{:S(2)}) async-start(bf16[8,2,2,256,128]{4,3,2,1,0:T(8,128)(2,1)} %shard_map.64), calls=%async_computation | async-start | bytes 4194304 | tf_op jit(solution)/shard_map/all_to_all | solution.py:332
  79.8 3.2 %collective-permute-start.35 = (bf16[4,2,128,256]{3,2,1,0:T(8,128)(2,1)S(1)}, bf16[4,2,128,256]{3,2,1,0:T(8,128)(2,1)S(1)}, u32[]{:S(2)}, u32[]{:S(2)}) collective-permute-start(bf16[4,2,128,256]{3,2,1,0:T(8,128)(2,1)S(1)} %pad_maximum_fusion.6.refs_0_), channel_id=1, source_target_pairs={{0,12},{1,13},{2,14},{3,15},{4,0},{5,1},{6,2},{7,3},{8,4},{9,5},{1... | collective-permute-start | bytes 1572872 | tf_op jit(solution)/shard_map/ppermute | solution.py:26
  89.7 2.7 collective-permute-start.39
  92.4 2.9 collective-permute-done.34.refs_1_
  95.5 3.3 %collective-permute-start.37 = (bf16[2,2,128,256]{3,2,1,0:T(8,128)(2,1)S(1)}, bf16[2,2,128,256]{3,2,1,0:T(8,128)(2,1)S(1)}, u32[]{:S(2)}, u32[]{:S(2)}) collective-permute-start(bf16[2,2,128,256]{3,2,1,0:T(8,128)(2,1)S(1)} %slice.241), channel_id=1, source_target_pairs={{0,12},{1,13},{2,14},{3,15},{4,0},{5,1},{6,2},{7,3},{8,4},{9,5},{1... | collective-permute-start | bytes 786440 | tf_op jit(solution)/shard_map/ppermute | solution.py:26
  98.8 5.6 %collective-permute-done.38.refs_6_ = bf16[4,2,128,256]{3,2,1,0:T(8,128)(2,1)S(1)} collective-permute-done((bf16[4,2,128,256]{3,2,1,0:T(8,128)(2,1)S(1)}, bf16[4,2,128,256]{3,2,1,0:T(8,128)(2,1)S(1)}, u32[]{:S(2)}, u32[]{:S(2)}) %collective-permute-start.38) | collective-permute-done | bytes 524320 | tf_op jit(solution)/shard_map/ppermute | solution.py:26
  105.4 2.4 collective-permute-start.41
  109.3 4.0 %collective-permute-done.40.refs_8_ = bf16[2,2,128,256]{3,2,1,0:T(8,128)(2,1)S(1)} collective-permute-done((bf16[2,2,128,256]{3,2,1,0:T(8,128)(2,1)S(1)}, bf16[2,2,128,256]{3,2,1,0:T(8,128)(2,1)S(1)}, u32[]{:S(2)}, u32[]{:S(2)}) %collective-permute-start.40) | collective-permute-done | bytes 262176 | tf_op jit(solution)/shard_map/ppermute | solution.py:26
  114.7 7.4 %shard_map.67 = bf16[8,2,2,256,128]{4,3,2,1,0:T(8,128)(2,1)} custom-call(s32[3]{0:T(128)} %pad_add_fusion.place, s32[64]{0:T(128)} %reshape.10.pairs, s32[64]{0:T(128)} %size.9, bf16[4,2,128,256]{3,2,1,0:T(8,128)(2,1)} %copy-done.6, bf16[4,2,128,256]{3,2,1,0:T(8,128)(2,1)} %copy-done.13, bf16[4,2,128,256]{3,2,1,0:T(8,128)(2,1)} %copy-done.14, ...), custom_call_target="tpu_custom_call" | custom-call | flops 536870912 | bytes 8388608 | tf_op jit(solution)/shard_map/pallas_call | solution.py:88
  123.5 4.4 %all-to-all-start.3 = ((bf16[8,2,2,256,128]{4,3,2,1,0:T(8,128)(2,1)}), bf16[8,2,2,256,128]{4,3,2,1,0:T(8,128)(2,1)}, u32[]{:S(2)}, u32[]{:S(2)}) async-start(bf16[8,2,2,256,128]{4,3,2,1,0:T(8,128)(2,1)} %shard_map.67), calls=%async_computation.3 | async-start | bytes 4194304 | tf_op jit(solution)/shard_map/all_to_all | solution.py:332
  128.3 3.2 %collective-permute-start.24 = (bf16[4,2,128,256]{3,2,1,0:T(8,128)(2,1)S(1)}, bf16[4,2,128,256]{3,2,1,0:T(8,128)(2,1)S(1)}, u32[]{:S(2)}, u32[]{:S(2)}) collective-permute-start(bf16[4,2,128,256]{3,2,1,0:T(8,128)(2,1)S(1)} %pad_maximum_fusion.4.refs_0_), channel_id=1, source_target_pairs={{0,12},{1,13},{2,14},{3,15},{4,0},{5,1},{6,2},{7,3},{8,4},{9,5},{1... | collective-permute-start | bytes 1572872 | tf_op jit(solution)/shard_map/ppermute | solution.py:26
  132.3 2.6 collective-permute-start.31
  134.9 8.8 %collective-permute-done.23.refs_1_ = bf16[4,2,128,256]{3,2,1,0:T(8,128)(2,1)S(1)} collective-permute-done((bf16[4,2,128,256]{3,2,1,0:T(8,128)(2,1)S(1)}, bf16[4,2,128,256]{3,2,1,0:T(8,128)(2,1)S(1)}, u32[]{:S(2)}, u32[]{:S(2)}) %collective-permute-start.23) | collective-permute-done | bytes 524320 | tf_op jit(solution)/shard_map/ppermute | solution.py:26
  143.9 3.3 %collective-permute-start.26 = (bf16[2,2,128,256]{3,2,1,0:T(8,128)(2,1)S(1)}, bf16[2,2,128,256]{3,2,1,0:T(8,128)(2,1)S(1)}, u32[]{:S(2)}, u32[]{:S(2)}) collective-permute-start(bf16[2,2,128,256]{3,2,1,0:T(8,128)(2,1)S(1)} %slice.228), channel_id=1, source_target_pairs={{0,12},{1,13},{2,14},{3,15},{4,0},{5,1},{6,2},{7,3},{8,4},{9,5},{1... | collective-permute-start | bytes 786440 | tf_op jit(solution)/shard_map/ppermute | solution.py:26
  147.9 2.7 collective-permute-start.33
  150.6 2.3 collective-permute-done.25.refs_3_
  152.8 3.0 collective-permute-done.32.refs_8_
  155.9 7.5 %shard_map.66 = bf16[8,2,2,256,128]{4,3,2,1,0:T(8,128)(2,1)} custom-call(s32[3]{0:T(128)} %pad_add_fusion.place, s32[64]{0:T(128)} %reshape.10.pairs, s32[64]{0:T(128)} %size.9, bf16[4,2,128,256]{3,2,1,0:T(8,128)(2,1)} %copy-done.9, bf16[4,2,128,256]{3,2,1,0:T(8,128)(2,1)} %copy-done.16, bf16[4,2,128,256]{3,2,1,0:T(8,128)(2,1)} %copy-done.18, ...), custom_call_target="tpu_custom_call" | custom-call | flops 536870912 | bytes 8388608 | tf_op jit(solution)/shard_map/pallas_call | solution.py:88
  163.4 4.2 %all-to-all-start.2 = ((bf16[8,2,2,256,128]{4,3,2,1,0:T(8,128)(2,1)}), bf16[8,2,2,256,128]{4,3,2,1,0:T(8,128)(2,1)S(1)}, u32[]{:S(2)}, u32[]{:S(2)}) async-start(bf16[8,2,2,256,128]{4,3,2,1,0:T(8,128)(2,1)} %shard_map.66), calls=%async_computation.2 | async-start | bytes 4194304 | tf_op jit(solution)/shard_map/all_to_all | solution.py:332
  167.9 3.2 %collective-permute-start.13 = (bf16[4,2,128,256]{3,2,1,0:T(8,128)(2,1)S(1)}, bf16[4,2,128,256]{3,2,1,0:T(8,128)(2,1)S(1)}, u32[]{:S(2)}, u32[]{:S(2)}) collective-permute-start(bf16[4,2,128,256]{3,2,1,0:T(8,128)(2,1)S(1)} %pad_maximum_fusion.2.refs_0_), channel_id=1, source_target_pairs={{0,12},{1,13},{2,14},{3,15},{4,0},{5,1},{6,2},{7,3},{8,4},{9,5},{1... | collective-permute-start | bytes 1572872 | tf_op jit(solution)/shard_map/ppermute | solution.py:26
  172.8 2.6 collective-permute-start.17
  175.4 7.9 %collective-permute-done.12.refs_1_ = bf16[4,2,128,256]{3,2,1,0:T(8,128)(2,1)S(1)} collective-permute-done((bf16[4,2,128,256]{3,2,1,0:T(8,128)(2,1)S(1)}, bf16[4,2,128,256]{3,2,1,0:T(8,128)(2,1)S(1)}, u32[]{:S(2)}, u32[]{:S(2)}) %collective-permute-start.12) | collective-permute-done | bytes 524320 | tf_op jit(solution)/shard_map/ppermute | solution.py:26
  183.5 3.3 %collective-permute-start.15 = (bf16[2,2,128,256]{3,2,1,0:T(8,128)(2,1)S(1)}, bf16[2,2,128,256]{3,2,1,0:T(8,128)(2,1)}, u32[]{:S(2)}, u32[]{:S(2)}) collective-permute-start(bf16[2,2,128,256]{3,2,1,0:T(8,128)(2,1)S(1)} %slice.215), channel_id=1, source_target_pairs={{0,12},{1,13},{2,14},{3,15},{4,0},{5,1},{6,2},{7,3},{8,4},{9,5},{1... | collective-permute-start | bytes 786440 | tf_op jit(solution)/shard_map/ppermute | solution.py:26
  188.1 2.6 collective-permute-start.19
  192.5 3.5 %collective-permute-done.18.refs_8_ = bf16[2,2,128,256]{3,2,1,0:T(8,128)(2,1)} collective-permute-done((bf16[2,2,128,256]{3,2,1,0:T(8,128)(2,1)S(1)}, bf16[2,2,128,256]{3,2,1,0:T(8,128)(2,1)}, u32[]{:S(2)}, u32[]{:S(2)}) %collective-permute-start.18) | collective-permute-done | bytes 262176 | tf_op jit(solution)/shard_map/ppermute | solution.py:26
  196.1 7.5 %shard_map.65 = bf16[8,2,2,256,128]{4,3,2,1,0:T(8,128)(2,1)} custom-call(s32[3]{0:T(128)} %pad_add_fusion.place, s32[64]{0:T(128)} %reshape.10.pairs, s32[64]{0:T(128)} %size.9, bf16[4,2,128,256]{3,2,1,0:T(8,128)(2,1)} %copy-done.7, bf16[4,2,128,256]{3,2,1,0:T(8,128)(2,1)} %copy-done.15, bf16[4,2,128,256]{3,2,1,0:T(8,128)(2,1)} %copy-done.17, ...), custom_call_target="tpu_custom_call" | custom-call | flops 536870912 | bytes 8388608 | tf_op jit(solution)/shard_map/pallas_call | solution.py:88
  204.9 4.4 %all-to-all-start.1 = ((bf16[8,2,2,256,128]{4,3,2,1,0:T(8,128)(2,1)}), bf16[8,2,2,256,128]{4,3,2,1,0:T(8,128)(2,1)}, u32[]{:S(2)}, u32[]{:S(2)}) async-start(bf16[8,2,2,256,128]{4,3,2,1,0:T(8,128)(2,1)} %shard_map.65), calls=%async_computation.1 | async-start | bytes 4194304 | tf_op jit(solution)/shard_map/all_to_all | solution.py:332
  210.1 26.3 %all-to-all-done.1.refs_1_ = bf16[8,2,2,256,128]{4,3,2,1,0:T(8,128)(2,1)} async-done(((bf16[8,2,2,256,128]{4,3,2,1,0:T(8,128)(2,1)}), bf16[8,2,2,256,128]{4,3,2,1,0:T(8,128)(2,1)}, u32[]{:S(2)}, u32[]{:S(2)}) %all-to-all-start.1) | async-done | bytes 2097184 | tf_op jit(solution)/shard_map/all_to_all | solution.py:332
  236.4 14.6 %right.1 = (bf16[4,256,256]{2,1,0:T(8,128)(2,1)}, bf16[4,256,256]{2,1,0:T(8,128)(2,1)}, bf16[4,256,256]{2,1,0:T(8,128)(2,1)}, bf16[4,256,256]{2,1,0:T(8,128)(2,1...) custom-call(s32[3]{0:T(128)} %pad_add_fusion.place, ...), custom_call_target="tpu_custom_call" | custom-call | flops 2147483648 | bytes 20971520 | tf_op jit(solution)/shard_map/right/pallas_call | solution.py:206
  251.9 3.9 %collective-permute-start.43 = (bf16[4,256,256]{2,1,0:T(8,128)(2,1)}, bf16[4,256,256]{2,1,0:T(8,128)(2,1)S(1)}, u32[]{:S(2)}, u32[]{:S(2)}) collective-permute-start(bf16[4,256,256]{2,1,0:T(8,128)(2,1)} %get-tuple-element.23), channel_id=1, source_target_pairs={{0,2},{1,3},{2,0},{3,1},{4,6},{5,7},{6,4},{7,5},{8,10},{9,11},{10,... | collective-permute-start | bytes 1572872 | tf_op jit(solution)/shard_map/ppermute | solution.py:26
  258.1 8.3 %collective-permute-done.42.refs_1_ = bf16[4,256,256]{2,1,0:T(8,128)(2,1)S(1)} collective-permute-done((bf16[4,256,256]{2,1,0:T(8,128)(2,1)}, bf16[4,256,256]{2,1,0:T(8,128)(2,1)S(1)}, u32[]{:S(2)}, u32[]{:S(2)}) %collective-permute-start.42) | collective-permute-done | bytes 524320 | tf_op jit(solution)/shard_map/ppermute | solution.py:26
  266.8 11.7 %collective-permute-done.43.refs_2_ = bf16[4,256,256]{2,1,0:T(8,128)(2,1)S(1)} collective-permute-done((bf16[4,256,256]{2,1,0:T(8,128)(2,1)}, bf16[4,256,256]{2,1,0:T(8,128)(2,1)S(1)}, u32[]{:S(2)}, u32[]{:S(2)}) %collective-permute-start.43) | collective-permute-done | bytes 524320 | tf_op jit(solution)/shard_map/ppermute | solution.py:26
  278.5 2.9 collective-permute-done.45.refs_5_
  285.0 3.9 %collective-permute-start.49 = (bf16[256,256]{1,0:T(8,128)(2,1)S(1)}, bf16[256,256]{1,0:T(8,128)(2,1)S(1)}, u32[]{:S(2)}, u32[]{:S(2)}) collective-permute-start(bf16[256,256]{1,0:T(8,128)(2,1)S(1)} %get-tuple-element.31), channel_id=1, source_target_pairs={{0,8},{1,9},{2,10},{3,11},{4,12},{5,13},{6,14},{7,15},{8,0},{9,1},... | collective-permute-start | bytes 393224 | tf_op jit(solution)/shard_map/ppermute | solution.py:26
  288.8 2.5 collective-permute-start.51
  291.4 3.7 %collective-permute-start.52 = (bf16[256,256]{1,0:T(8,128)(2,1)S(1)}, bf16[256,256]{1,0:T(8,128)(2,1)S(1)}, u32[]{:S(2)}, u32[]{:S(2)}) collective-permute-start(bf16[256,256]{1,0:T(8,128)(2,1)S(1)} %get-tuple-element.35), channel_id=1, source_target_pairs={{0,2},{1,3},{2,0},{3,1},{4,6},{5,7},{6,4},{7,5},{8,10},{9,11},{10,... | collective-permute-start | bytes 393224 | tf_op jit(solution)/shard_map/ppermute | solution.py:26
  295.1 2.6 collective-permute-start.53
  (218 shorter events, 60.1 us)
Async XLA Ops:
  2.2 12.3 %collective-permute-start.6 = (bf16[2,128,512]{2,1,0:T(8,128)(2,1)S(1)}, bf16[2,128,512]{2,1,0:T(8,128)(2,1)S(1)}, u32[]{:S(2)}, u32[]{:S(2)}) collective-permute-start(bf16[2,128,512]{2,1,0:T(8,128)(2,1)S(1)} %get-tuple-element.47), channel_id=1, source_target_pairs={{0,4},{1,5},{2,6},{3,7},{4,8},{5,9},{6,10},{7,11},{8,12},{9,13},{1... | collective-permute-start | bytes 786440 | tf_op jit(solution)/shard_map/ppermute | solution.py:26
  3.9 33.0 %collective-permute-start.20 = (bf16[2,128,512]{2,1,0:T(8,128)(2,1)}, bf16[2,128,512]{2,1,0:T(8,128)(2,1)}, u32[]{:S(2)}, u32[]{:S(2)}) collective-permute-start(bf16[2,128,512]{2,1,0:T(8,128)(2,1)} %get-tuple-element.46), channel_id=1, source_target_pairs={{0,1},{1,2},{2,3},{3,0},{4,5},{5,6},{6,7},{7,4},{8,9},{9,10},{10,1... | collective-permute-start | bytes 786440 | tf_op jit(solution)/shard_map/ppermute | solution.py:26
  5.8 31.9 %collective-permute-start.21 = (bf16[2,128,512]{2,1,0:T(8,128)(2,1)}, bf16[2,128,512]{2,1,0:T(8,128)(2,1)}, u32[]{:S(2)}, u32[]{:S(2)}) collective-permute-start(bf16[2,128,512]{2,1,0:T(8,128)(2,1)} %get-tuple-element.46), channel_id=1, source_target_pairs={{0,2},{1,3},{2,0},{3,1},{4,6},{5,7},{6,4},{7,5},{8,10},{9,11},{10,... | collective-permute-start | bytes 786440 | tf_op jit(solution)/shard_map/ppermute | solution.py:26
  9.4 9.0 %collective-permute-start.7 = (bf16[2,128,512]{2,1,0:T(8,128)(2,1)S(1)}, bf16[2,128,512]{2,1,0:T(8,128)(2,1)S(1)}, u32[]{:S(2)}, u32[]{:S(2)}) collective-permute-start(bf16[2,128,512]{2,1,0:T(8,128)(2,1)S(1)} %get-tuple-element.47), channel_id=1, source_target_pairs={{0,8},{1,9},{2,10},{3,11},{4,12},{5,13},{6,14},{7,15},{8,0},{9,1},... | collective-permute-start | bytes 786440 | tf_op jit(solution)/shard_map/ppermute | solution.py:26
  12.3 10.7 %collective-permute-start.8 = (bf16[2,128,512]{2,1,0:T(8,128)(2,1)S(1)}, bf16[2,128,512]{2,1,0:T(8,128)(2,1)S(1)}, u32[]{:S(2)}, u32[]{:S(2)}) collective-permute-start(bf16[2,128,512]{2,1,0:T(8,128)(2,1)S(1)} %get-tuple-element.47), channel_id=1, source_target_pairs={{0,12},{1,13},{2,14},{3,15},{4,0},{5,1},{6,2},{7,3},{8,4},{9,5},{1... | collective-permute-start | bytes 786440 | tf_op jit(solution)/shard_map/ppermute | solution.py:26
  14.5 13.4 %collective-permute-start = (bf16[2,128,512]{2,1,0:T(8,128)(2,1)S(1)}, bf16[2,128,512]{2,1,0:T(8,128)(2,1)S(1)}, u32[]{:S(2)}, u32[]{:S(2)}) collective-permute-start(bf16[2,128,512]{2,1,0:T(8,128)(2,1)S(1)} %get-tuple-element.48), channel_id=1, source_target_pairs={{0,1},{1,2},{2,3},{3,0},{4,5},{5,6},{6,7},{7,4},{8,9},{9,10},{10,1... | collective-permute-start | bytes 786440 | tf_op jit(solution)/shard_map/ppermute | solution.py:26
  18.4 13.8 %collective-permute-start.1 = (bf16[2,128,512]{2,1,0:T(8,128)(2,1)S(1)}, bf16[2,128,512]{2,1,0:T(8,128)(2,1)S(1)}, u32[]{:S(2)}, u32[]{:S(2)}) collective-permute-start(bf16[2,128,512]{2,1,0:T(8,128)(2,1)S(1)} %get-tuple-element.48), channel_id=1, source_target_pairs={{0,2},{1,3},{2,0},{3,1},{4,6},{5,7},{6,4},{7,5},{8,10},{9,11},{10,... | collective-permute-start | bytes 786440 | tf_op jit(solution)/shard_map/ppermute | solution.py:26
  23.0 13.2 %collective-permute-start.2 = (bf16[2,128,512]{2,1,0:T(8,128)(2,1)S(1)}, bf16[2,128,512]{2,1,0:T(8,128)(2,1)S(1)}, u32[]{:S(2)}, u32[]{:S(2)}) collective-permute-start(bf16[2,128,512]{2,1,0:T(8,128)(2,1)S(1)} %get-tuple-element.48), channel_id=1, source_target_pairs={{0,3},{1,0},{2,1},{3,2},{4,7},{5,4},{6,5},{7,6},{8,11},{9,8},{10,9... | collective-permute-start | bytes 786440 | tf_op jit(solution)/shard_map/ppermute | solution.py:26
  27.9 19.5 %collective-permute-start.10 = (bf16[4,2,128,256]{3,2,1,0:T(8,128)(2,1)S(1)}, bf16[4,2,128,256]{3,2,1,0:T(8,128)(2,1)S(1)}, u32[]{:S(2)}, u32[]{:S(2)}) collective-permute-start(bf16[4,2,128,256]{3,2,1,0:T(8,128)(2,1)S(1)} %pad_maximum_fusion.1.refs_4_), channel_id=1, source_target_pairs={{0,3},{1,0},{2,1},{3,2},{4,7},{5,4},{6,5},{7,6},{8,11},{9,8},{10,9... | collective-permute-start | bytes 1572872 | tf_op jit(solution)/shard_map/ppermute | solution.py:26
  32.2 20.0 %collective-permute-start.11 = (bf16[4,2,128,256]{3,2,1,0:T(8,128)(2,1)S(1)}, bf16[4,2,128,256]{3,2,1,0:T(8,128)(2,1)S(1)}, u32[]{:S(2)}, u32[]{:S(2)}) collective-permute-start(bf16[4,2,128,256]{3,2,1,0:T(8,128)(2,1)S(1)} %pad_maximum_fusion.1.refs_4_), channel_id=1, source_target_pairs={{0,2},{1,3},{2,0},{3,1},{4,6},{5,7},{6,4},{7,5},{8,10},{9,11},{10,... | collective-permute-start | bytes 1572872 | tf_op jit(solution)/shard_map/ppermute | solution.py:26
  36.1 25.0 %collective-permute-start.9 = (bf16[4,2,128,256]{3,2,1,0:T(8,128)(2,1)S(1)}, bf16[4,2,128,256]{3,2,1,0:T(8,128)(2,1)S(1)}, u32[]{:S(2)}, u32[]{:S(2)}) collective-permute-start(bf16[4,2,128,256]{3,2,1,0:T(8,128)(2,1)S(1)} %pad_maximum_fusion.1.refs_4_), channel_id=1, source_target_pairs={{0,1},{1,2},{2,3},{3,0},{4,5},{5,6},{6,7},{7,4},{8,9},{9,10},{10,1... | collective-permute-start | bytes 1572872 | tf_op jit(solution)/shard_map/ppermute | solution.py:26
  36.9 24.4 %collective-permute-start.3 = (bf16[4,2,128,256]{3,2,1,0:T(8,128)(2,1)S(1)}, bf16[4,2,128,256]{3,2,1,0:T(8,128)(2,1)S(1)}, u32[]{:S(2)}, u32[]{:S(2)}) collective-permute-start(bf16[4,2,128,256]{3,2,1,0:T(8,128)(2,1)S(1)} %pad_maximum_fusion.refs_0_), channel_id=1, source_target_pairs={{0,4},{1,5},{2,6},{3,7},{4,8},{5,9},{6,10},{7,11},{8,12},{9,13},{1... | collective-permute-start | bytes 1572872 | tf_op jit(solution)/shard_map/ppermute | solution.py:26
  37.7 25.7 %collective-permute-start.4 = (bf16[4,2,128,256]{3,2,1,0:T(8,128)(2,1)S(1)}, bf16[4,2,128,256]{3,2,1,0:T(8,128)(2,1)}, u32[]{:S(2)}, u32[]{:S(2)}) collective-permute-start(bf16[4,2,128,256]{3,2,1,0:T(8,128)(2,1)S(1)} %pad_maximum_fusion.refs_0_), channel_id=1, source_target_pairs={{0,12},{1,13},{2,14},{3,15},{4,0},{5,1},{6,2},{7,3},{8,4},{9,5},{1... | collective-permute-start | bytes 1572872 | tf_op jit(solution)/shard_map/ppermute | solution.py:26
  47.4 18.6 %collective-permute-start.5 = (bf16[4,2,128,256]{3,2,1,0:T(8,128)(2,1)S(1)}, bf16[4,2,128,256]{3,2,1,0:T(8,128)(2,1)}, u32[]{:S(2)}, u32[]{:S(2)}) collective-permute-start(bf16[4,2,128,256]{3,2,1,0:T(8,128)(2,1)S(1)} %pad_maximum_fusion.refs_0_), channel_id=1, source_target_pairs={{0,8},{1,9},{2,10},{3,11},{4,12},{5,13},{6,14},{7,15},{8,0},{9,1},... | collective-permute-start | bytes 1572872 | tf_op jit(solution)/shard_map/ppermute | solution.py:26
  52.2 25.7 %collective-permute-start.22 = (bf16[2,128,512]{2,1,0:T(8,128)(2,1)}, bf16[2,128,512]{2,1,0:T(8,128)(2,1)}, u32[]{:S(2)}, u32[]{:S(2)}) collective-permute-start(bf16[2,128,512]{2,1,0:T(8,128)(2,1)} %get-tuple-element.46), channel_id=1, source_target_pairs={{0,3},{1,0},{2,1},{3,2},{4,7},{5,4},{6,5},{7,6},{8,11},{9,8},{10,9... | collective-permute-start | bytes 786440 | tf_op jit(solution)/shard_map/ppermute | solution.py:26
  61.1 21.9 %collective-permute-start.27 = (bf16[2,128,512]{2,1,0:T(8,128)(2,1)}, bf16[2,128,512]{2,1,0:T(8,128)(2,1)}, u32[]{:S(2)}, u32[]{:S(2)}) collective-permute-start(bf16[2,128,512]{2,1,0:T(8,128)(2,1)} %get-tuple-element.45), channel_id=1, source_target_pairs={{0,4},{1,5},{2,6},{3,7},{4,8},{5,9},{6,10},{7,11},{8,12},{9,13},{1... | collective-permute-start | bytes 786440 | tf_op jit(solution)/shard_map/ppermute | solution.py:26
  61.3 23.4 %collective-permute-start.28 = (bf16[2,128,512]{2,1,0:T(8,128)(2,1)}, bf16[2,128,512]{2,1,0:T(8,128)(2,1)}, u32[]{:S(2)}, u32[]{:S(2)}) collective-permute-start(bf16[2,128,512]{2,1,0:T(8,128)(2,1)} %get-tuple-element.45), channel_id=1, source_target_pairs={{0,8},{1,9},{2,10},{3,11},{4,12},{5,13},{6,14},{7,15},{8,0},{9,1},... | collective-permute-start | bytes 786440 | tf_op jit(solution)/shard_map/ppermute | solution.py:26
  63.4 22.9 %collective-permute-start.29 = (bf16[2,128,512]{2,1,0:T(8,128)(2,1)}, bf16[2,128,512]{2,1,0:T(8,128)(2,1)}, u32[]{:S(2)}, u32[]{:S(2)}) collective-permute-start(bf16[2,128,512]{2,1,0:T(8,128)(2,1)} %get-tuple-element.45), channel_id=1, source_target_pairs={{0,12},{1,13},{2,14},{3,15},{4,0},{5,1},{6,2},{7,3},{8,4},{9,5},{1... | collective-permute-start | bytes 786440 | tf_op jit(solution)/shard_map/ppermute | solution.py:26
  73.5 48.7 %all-to-all-start = ((bf16[8,2,2,256,128]{4,3,2,1,0:T(8,128)(2,1)}), bf16[8,2,2,256,128]{4,3,2,1,0:T(8,128)(2,1)S(1)}, u32[]{:S(2)}, u32[]{:S(2)}) async-start(bf16[8,2,2,256,128]{4,3,2,1,0:T(8,128)(2,1)} %shard_map.64), calls=%async_computation | async-start | bytes 4194304 | tf_op jit(solution)/shard_map/all_to_all | solution.py:332
  79.7 15.6 %collective-permute-start.34 = (bf16[4,2,128,256]{3,2,1,0:T(8,128)(2,1)S(1)}, bf16[4,2,128,256]{3,2,1,0:T(8,128)(2,1)S(1)}, u32[]{:S(2)}, u32[]{:S(2)}) collective-permute-start(bf16[4,2,128,256]{3,2,1,0:T(8,128)(2,1)S(1)} %pad_maximum_fusion.6.refs_0_), channel_id=1, source_target_pairs={{0,4},{1,5},{2,6},{3,7},{4,8},{5,9},{6,10},{7,11},{8,12},{9,13},{1... | collective-permute-start | bytes 1572872 | tf_op jit(solution)/shard_map/ppermute | solution.py:26
  79.8 15.6 %collective-permute-start.35 = (bf16[4,2,128,256]{3,2,1,0:T(8,128)(2,1)S(1)}, bf16[4,2,128,256]{3,2,1,0:T(8,128)(2,1)S(1)}, u32[]{:S(2)}, u32[]{:S(2)}) collective-permute-start(bf16[4,2,128,256]{3,2,1,0:T(8,128)(2,1)S(1)} %pad_maximum_fusion.6.refs_0_), channel_id=1, source_target_pairs={{0,12},{1,13},{2,14},{3,15},{4,0},{5,1},{6,2},{7,3},{8,4},{9,5},{1... | collective-permute-start | bytes 1572872 | tf_op jit(solution)/shard_map/ppermute | solution.py:26
  88.1 16.3 %collective-permute-start.38 = (bf16[4,2,128,256]{3,2,1,0:T(8,128)(2,1)S(1)}, bf16[4,2,128,256]{3,2,1,0:T(8,128)(2,1)S(1)}, u32[]{:S(2)}, u32[]{:S(2)}) collective-permute-start(bf16[4,2,128,256]{3,2,1,0:T(8,128)(2,1)S(1)} %pad_maximum_fusion.7.refs_5_), channel_id=1, source_target_pairs={{0,1},{1,2},{2,3},{3,0},{4,5},{5,6},{6,7},{7,4},{8,9},{9,10},{10,1... | collective-permute-start | bytes 1572872 | tf_op jit(solution)/shard_map/ppermute | solution.py:26
  89.7 15.6 %collective-permute-start.39 = (bf16[4,2,128,256]{3,2,1,0:T(8,128)(2,1)S(1)}, bf16[4,2,128,256]{3,2,1,0:T(8,128)(2,1)S(1)}, u32[]{:S(2)}, u32[]{:S(2)}) collective-permute-start(bf16[4,2,128,256]{3,2,1,0:T(8,128)(2,1)S(1)} %pad_maximum_fusion.7.refs_5_), channel_id=1, source_target_pairs={{0,3},{1,0},{2,1},{3,2},{4,7},{5,4},{6,5},{7,6},{8,11},{9,8},{10,9... | collective-permute-start | bytes 1572872 | tf_op jit(solution)/shard_map/ppermute | solution.py:26
  95.4 12.4 %collective-permute-start.36 = (bf16[2,2,128,256]{3,2,1,0:T(8,128)(2,1)S(1)}, bf16[2,2,128,256]{3,2,1,0:T(8,128)(2,1)S(1)}, u32[]{:S(2)}, u32[]{:S(2)}) collective-permute-start(bf16[2,2,128,256]{3,2,1,0:T(8,128)(2,1)S(1)} %slice.240), channel_id=1, source_target_pairs={{0,4},{1,5},{2,6},{3,7},{4,8},{5,9},{6,10},{7,11},{8,12},{9,13},{1... | collective-permute-start | bytes 786440 | tf_op jit(solution)/shard_map/ppermute | solution.py:26
  95.5 13.0 %collective-permute-start.37 = (bf16[2,2,128,256]{3,2,1,0:T(8,128)(2,1)S(1)}, bf16[2,2,128,256]{3,2,1,0:T(8,128)(2,1)S(1)}, u32[]{:S(2)}, u32[]{:S(2)}) collective-permute-start(bf16[2,2,128,256]{3,2,1,0:T(8,128)(2,1)S(1)} %slice.241), channel_id=1, source_target_pairs={{0,12},{1,13},{2,14},{3,15},{4,0},{5,1},{6,2},{7,3},{8,4},{9,5},{1... | collective-permute-start | bytes 786440 | tf_op jit(solution)/shard_map/ppermute | solution.py:26
  123.5 39.9 %all-to-all-start.3 = ((bf16[8,2,2,256,128]{4,3,2,1,0:T(8,128)(2,1)}), bf16[8,2,2,256,128]{4,3,2,1,0:T(8,128)(2,1)}, u32[]{:S(2)}, u32[]{:S(2)}) async-start(bf16[8,2,2,256,128]{4,3,2,1,0:T(8,128)(2,1)} %shard_map.67), calls=%async_computation.3 | async-start | bytes 4194304 | tf_op jit(solution)/shard_map/all_to_all | solution.py:332
  128.0 15.7 %collective-permute-start.23 = (bf16[4,2,128,256]{3,2,1,0:T(8,128)(2,1)S(1)}, bf16[4,2,128,256]{3,2,1,0:T(8,128)(2,1)S(1)}, u32[]{:S(2)}, u32[]{:S(2)}) collective-permute-start(bf16[4,2,128,256]{3,2,1,0:T(8,128)(2,1)S(1)} %pad_maximum_fusion.4.refs_0_), channel_id=1, source_target_pairs={{0,4},{1,5},{2,6},{3,7},{4,8},{5,9},{6,10},{7,11},{8,12},{9,13},{1... | collective-permute-start | bytes 1572872 | tf_op jit(solution)/shard_map/ppermute | solution.py:26
  128.3 15.5 %collective-permute-start.24 = (bf16[4,2,128,256]{3,2,1,0:T(8,128)(2,1)S(1)}, bf16[4,2,128,256]{3,2,1,0:T(8,128)(2,1)S(1)}, u32[]{:S(2)}, u32[]{:S(2)}) collective-permute-start(bf16[4,2,128,256]{3,2,1,0:T(8,128)(2,1)S(1)} %pad_maximum_fusion.4.refs_0_), channel_id=1, source_target_pairs={{0,12},{1,13},{2,14},{3,15},{4,0},{5,1},{6,2},{7,3},{8,4},{9,5},{1... | collective-permute-start | bytes 1572872 | tf_op jit(solution)/shard_map/ppermute | solution.py:26
  131.6 15.5 %collective-permute-start.30 = (bf16[4,2,128,256]{3,2,1,0:T(8,128)(2,1)S(1)}, bf16[4,2,128,256]{3,2,1,0:T(8,128)(2,1)S(1)}, u32[]{:S(2)}, u32[]{:S(2)}) collective-permute-start(bf16[4,2,128,256]{3,2,1,0:T(8,128)(2,1)S(1)} %pad_maximum_fusion.5.refs_5_), channel_id=1, source_target_pairs={{0,1},{1,2},{2,3},{3,0},{4,5},{5,6},{6,7},{7,4},{8,9},{9,10},{10,1... | collective-permute-start | bytes 1572872 | tf_op jit(solution)/shard_map/ppermute | solution.py:26
  132.3 15.5 %collective-permute-start.31 = (bf16[4,2,128,256]{3,2,1,0:T(8,128)(2,1)S(1)}, bf16[4,2,128,256]{3,2,1,0:T(8,128)(2,1)S(1)}, u32[]{:S(2)}, u32[]{:S(2)}) collective-permute-start(bf16[4,2,128,256]{3,2,1,0:T(8,128)(2,1)S(1)} %pad_maximum_fusion.5.refs_5_), channel_id=1, source_target_pairs={{0,3},{1,0},{2,1},{3,2},{4,7},{5,4},{6,5},{7,6},{8,11},{9,8},{10,9... | collective-permute-start | bytes 1572872 | tf_op jit(solution)/shard_map/ppermute | solution.py:26
  143.7 9.1 %collective-permute-start.25 = (bf16[2,2,128,256]{3,2,1,0:T(8,128)(2,1)S(1)}, bf16[2,2,128,256]{3,2,1,0:T(8,128)(2,1)S(1)}, u32[]{:S(2)}, u32[]{:S(2)}) collective-permute-start(bf16[2,2,128,256]{3,2,1,0:T(8,128)(2,1)S(1)} %slice.227), channel_id=1, source_target_pairs={{0,4},{1,5},{2,6},{3,7},{4,8},{5,9},{6,10},{7,11},{8,12},{9,13},{1... | collective-permute-start | bytes 786440 | tf_op jit(solution)/shard_map/ppermute | solution.py:26
  143.9 9.0 %collective-permute-start.26 = (bf16[2,2,128,256]{3,2,1,0:T(8,128)(2,1)S(1)}, bf16[2,2,128,256]{3,2,1,0:T(8,128)(2,1)S(1)}, u32[]{:S(2)}, u32[]{:S(2)}) collective-permute-start(bf16[2,2,128,256]{3,2,1,0:T(8,128)(2,1)S(1)} %slice.228), channel_id=1, source_target_pairs={{0,12},{1,13},{2,14},{3,15},{4,0},{5,1},{6,2},{7,3},{8,4},{9,5},{1... | collective-permute-start | bytes 786440 | tf_op jit(solution)/shard_map/ppermute | solution.py:26
  163.4 40.1 %all-to-all-start.2 = ((bf16[8,2,2,256,128]{4,3,2,1,0:T(8,128)(2,1)}), bf16[8,2,2,256,128]{4,3,2,1,0:T(8,128)(2,1)S(1)}, u32[]{:S(2)}, u32[]{:S(2)}) async-start(bf16[8,2,2,256,128]{4,3,2,1,0:T(8,128)(2,1)} %shard_map.66), calls=%async_computation.2 | async-start | bytes 4194304 | tf_op jit(solution)/shard_map/all_to_all | solution.py:332
  167.8 15.6 %collective-permute-start.12 = (bf16[4,2,128,256]{3,2,1,0:T(8,128)(2,1)S(1)}, bf16[4,2,128,256]{3,2,1,0:T(8,128)(2,1)S(1)}, u32[]{:S(2)}, u32[]{:S(2)}) collective-permute-start(bf16[4,2,128,256]{3,2,1,0:T(8,128)(2,1)S(1)} %pad_maximum_fusion.2.refs_0_), channel_id=1, source_target_pairs={{0,4},{1,5},{2,6},{3,7},{4,8},{5,9},{6,10},{7,11},{8,12},{9,13},{1... | collective-permute-start | bytes 1572872 | tf_op jit(solution)/shard_map/ppermute | solution.py:26
  167.9 15.6 %collective-permute-start.13 = (bf16[4,2,128,256]{3,2,1,0:T(8,128)(2,1)S(1)}, bf16[4,2,128,256]{3,2,1,0:T(8,128)(2,1)S(1)}, u32[]{:S(2)}, u32[]{:S(2)}) collective-permute-start(bf16[4,2,128,256]{3,2,1,0:T(8,128)(2,1)S(1)} %pad_maximum_fusion.2.refs_0_), channel_id=1, source_target_pairs={{0,12},{1,13},{2,14},{3,15},{4,0},{5,1},{6,2},{7,3},{8,4},{9,5},{1... | collective-permute-start | bytes 1572872 | tf_op jit(solution)/shard_map/ppermute | solution.py:26
  172.1 15.1 %collective-permute-start.16 = (bf16[4,2,128,256]{3,2,1,0:T(8,128)(2,1)S(1)}, bf16[4,2,128,256]{3,2,1,0:T(8,128)(2,1)S(1)}, u32[]{:S(2)}, u32[]{:S(2)}) collective-permute-start(bf16[4,2,128,256]{3,2,1,0:T(8,128)(2,1)S(1)} %pad_maximum_fusion.3.refs_5_), channel_id=1, source_target_pairs={{0,1},{1,2},{2,3},{3,0},{4,5},{5,6},{6,7},{7,4},{8,9},{9,10},{10,1... | collective-permute-start | bytes 1572872 | tf_op jit(solution)/shard_map/ppermute | solution.py:26
  172.8 14.7 %collective-permute-start.17 = (bf16[4,2,128,256]{3,2,1,0:T(8,128)(2,1)S(1)}, bf16[4,2,128,256]{3,2,1,0:T(8,128)(2,1)S(1)}, u32[]{:S(2)}, u32[]{:S(2)}) collective-permute-start(bf16[4,2,128,256]{3,2,1,0:T(8,128)(2,1)S(1)} %pad_maximum_fusion.3.refs_5_), channel_id=1, source_target_pairs={{0,3},{1,0},{2,1},{3,2},{4,7},{5,4},{6,5},{7,6},{8,11},{9,8},{10,9... | collective-permute-start | bytes 1572872 | tf_op jit(solution)/shard_map/ppermute | solution.py:26
  183.4 9.1 %collective-permute-start.14 = (bf16[2,2,128,256]{3,2,1,0:T(8,128)(2,1)S(1)}, bf16[2,2,128,256]{3,2,1,0:T(8,128)(2,1)S(1)}, u32[]{:S(2)}, u32[]{:S(2)}) collective-permute-start(bf16[2,2,128,256]{3,2,1,0:T(8,128)(2,1)S(1)} %slice.214), channel_id=1, source_target_pairs={{0,4},{1,5},{2,6},{3,7},{4,8},{5,9},{6,10},{7,11},{8,12},{9,13},{1... | collective-permute-start | bytes 786440 | tf_op jit(solution)/shard_map/ppermute | solution.py:26
  183.5 9.0 %collective-permute-start.15 = (bf16[2,2,128,256]{3,2,1,0:T(8,128)(2,1)S(1)}, bf16[2,2,128,256]{3,2,1,0:T(8,128)(2,1)}, u32[]{:S(2)}, u32[]{:S(2)}) collective-permute-start(bf16[2,2,128,256]{3,2,1,0:T(8,128)(2,1)S(1)} %slice.215), channel_id=1, source_target_pairs={{0,12},{1,13},{2,14},{3,15},{4,0},{5,1},{6,2},{7,3},{8,4},{9,5},{1... | collective-permute-start | bytes 786440 | tf_op jit(solution)/shard_map/ppermute | solution.py:26
  204.9 31.5 %all-to-all-start.1 = ((bf16[8,2,2,256,128]{4,3,2,1,0:T(8,128)(2,1)}), bf16[8,2,2,256,128]{4,3,2,1,0:T(8,128)(2,1)}, u32[]{:S(2)}, u32[]{:S(2)}) async-start(bf16[8,2,2,256,128]{4,3,2,1,0:T(8,128)(2,1)} %shard_map.65), calls=%async_computation.1 | async-start | bytes 4194304 | tf_op jit(solution)/shard_map/all_to_all | solution.py:332
  251.0 15.3 %collective-permute-start.42 = (bf16[4,256,256]{2,1,0:T(8,128)(2,1)}, bf16[4,256,256]{2,1,0:T(8,128)(2,1)S(1)}, u32[]{:S(2)}, u32[]{:S(2)}) collective-permute-start(bf16[4,256,256]{2,1,0:T(8,128)(2,1)} %get-tuple-element.22), channel_id=1, source_target_pairs={{0,1},{1,2},{2,3},{3,0},{4,5},{5,6},{6,7},{7,4},{8,9},{9,10},{10,1... | collective-permute-start | bytes 1572872 | tf_op jit(solution)/shard_map/ppermute | solution.py:26
  251.9 26.7 %collective-permute-start.43 = (bf16[4,256,256]{2,1,0:T(8,128)(2,1)}, bf16[4,256,256]{2,1,0:T(8,128)(2,1)S(1)}, u32[]{:S(2)}, u32[]{:S(2)}) collective-permute-start(bf16[4,256,256]{2,1,0:T(8,128)(2,1)} %get-tuple-element.23), channel_id=1, source_target_pairs={{0,2},{1,3},{2,0},{3,1},{4,6},{5,7},{6,4},{7,5},{8,10},{9,11},{10,... | collective-permute-start | bytes 1572872 | tf_op jit(solution)/shard_map/ppermute | solution.py:26
  255.7 22.8 %collective-permute-start.44 = (bf16[4,256,256]{2,1,0:T(8,128)(2,1)}, bf16[4,256,256]{2,1,0:T(8,128)(2,1)S(1)}, u32[]{:S(2)}, u32[]{:S(2)}) collective-permute-start(bf16[4,256,256]{2,1,0:T(8,128)(2,1)} %get-tuple-element.24), channel_id=1, source_target_pairs={{0,3},{1,0},{2,1},{3,2},{4,7},{5,4},{6,5},{7,6},{8,11},{9,8},{10,9... | collective-permute-start | bytes 1572872 | tf_op jit(solution)/shard_map/ppermute | solution.py:26
  256.3 25.2 %collective-permute-start.45 = (bf16[4,256,256]{2,1,0:T(8,128)(2,1)}, bf16[4,256,256]{2,1,0:T(8,128)(2,1)S(1)}, u32[]{:S(2)}, u32[]{:S(2)}) collective-permute-start(bf16[4,256,256]{2,1,0:T(8,128)(2,1)} %get-tuple-element.26), channel_id=1, source_target_pairs={{0,4},{1,5},{2,6},{3,7},{4,8},{5,9},{6,10},{7,11},{8,12},{9,13},{1... | collective-permute-start | bytes 1572872 | tf_op jit(solution)/shard_map/ppermute | solution.py:26
  256.3 25.2 %collective-permute-start.46 = (bf16[4,256,256]{2,1,0:T(8,128)(2,1)}, bf16[4,256,256]{2,1,0:T(8,128)(2,1)S(1)}, u32[]{:S(2)}, u32[]{:S(2)}) collective-permute-start(bf16[4,256,256]{2,1,0:T(8,128)(2,1)} %get-tuple-element.27), channel_id=1, source_target_pairs={{0,8},{1,9},{2,10},{3,11},{4,12},{5,13},{6,14},{7,15},{8,0},{9,1},... | collective-permute-start | bytes 1572872 | tf_op jit(solution)/shard_map/ppermute | solution.py:26
  266.4 15.7 %collective-permute-start.47 = (bf16[4,256,256]{2,1,0:T(8,128)(2,1)}, bf16[4,256,256]{2,1,0:T(8,128)(2,1)S(1)}, u32[]{:S(2)}, u32[]{:S(2)}) collective-permute-start(bf16[4,256,256]{2,1,0:T(8,128)(2,1)} %get-tuple-element.28), channel_id=1, source_target_pairs={{0,12},{1,13},{2,14},{3,15},{4,0},{5,1},{6,2},{7,3},{8,4},{9,5},{1... | collective-permute-start | bytes 1572872 | tf_op jit(solution)/shard_map/ppermute | solution.py:26
  284.6 10.4 %collective-permute-start.48 = (bf16[256,256]{1,0:T(8,128)(2,1)S(1)}, bf16[256,256]{1,0:T(8,128)(2,1)S(1)}, u32[]{:S(2)}, u32[]{:S(2)}) collective-permute-start(bf16[256,256]{1,0:T(8,128)(2,1)S(1)} %get-tuple-element.30), channel_id=1, source_target_pairs={{0,4},{1,5},{2,6},{3,7},{4,8},{5,9},{6,10},{7,11},{8,12},{9,13},{1... | collective-permute-start | bytes 393224 | tf_op jit(solution)/shard_map/ppermute | solution.py:26
  285.0 12.7 %collective-permute-start.49 = (bf16[256,256]{1,0:T(8,128)(2,1)S(1)}, bf16[256,256]{1,0:T(8,128)(2,1)S(1)}, u32[]{:S(2)}, u32[]{:S(2)}) collective-permute-start(bf16[256,256]{1,0:T(8,128)(2,1)S(1)} %get-tuple-element.31), channel_id=1, source_target_pairs={{0,8},{1,9},{2,10},{3,11},{4,12},{5,13},{6,14},{7,15},{8,0},{9,1},... | collective-permute-start | bytes 393224 | tf_op jit(solution)/shard_map/ppermute | solution.py:26
  (62 other events, 579.2 us)
where the time goes:
time: 302 us; the launch traced here: 301 us
  starting transfers between devices  112 us (37%)
  waiting for transfers between devices  112 us (37%)
  Pallas kernels  45.8 us (15%)
  local copies, waits for them, and re-layouts  27.7 us (9%)
    ppermute x54, starting transfers between devices, move(): return lax.ppermute(value, 'op', pairs)  95 us
    ppermute x54, waiting for transfers between devices, move(): return lax.ppermute(value, 'op', pairs)  85.9 us
    pallas_call x4, Pallas kernels, left_stage(): pl.pallas_call(functools.partial(left_kernel, first_sector, layout), out_...  29.9 us
    all_to_all x4, waiting for transfers between devices, apply_slab(): lax.all_to_all(middle, 'bond', split_axis=0, concat_axis=0, tiled=True)  26.3 us
    all_to_all x4, starting transfers between devices, apply_slab(): lax.all_to_all(middle, 'bond', split_axis=0, concat_axis=0, tiled=True)  17.4 us
    another operation x13, local copies, waits for them, and re-layouts, apply_slab(): rows[chunk] = [jnp.stack([v[:, :, part] for v in side]) for side in both]  14.8 us
    pallas_call x1, Pallas kernels, right_stage(): pl.pallas_call(functools.partial(right_kernel, counts), name='right', out...  14.6 us
    unnamed x106, local copies, waits for them, and re-layouts  9.08 us
  transfers between devices with their start and end apart: 58, of which 24 were waited for; matrix products, arithmetic and copies ran while one was open for 6% of the time, Pallas kernels for 10%

commit v1 on v0

v1 whole, which is shorter than its diff:
```python
import functools

import jax
import jax.numpy as jnp
from jax import lax
from jax.experimental import pallas as pl
from jax.experimental.pallas import tpu as pltpu
from jax.sharding import PartitionSpec as P


TILE = 128
SIDE = 4
GROUP = SIDE * SIDE
BF16 = jnp.bfloat16
F32 = jnp.float32
CHUNKS = (2, 2, 2, 2)


def move(value, step_y, step_z):
    pairs = [
        (y * SIDE + z, (y + step_y) % SIDE * SIDE + (z + step_z) % SIDE)
        for y in range(SIDE)
        for z in range(SIDE)
    ]
    return lax.ppermute(value, "op", pairs)


def pack_kernel(plans, wave, *refs):
    outs, sems = refs[-len(plans) - 1 : -1], refs[-1]
    gots = refs[: -len(plans) - 1]
    copies = []
    for out, plan in zip(outs, plans):
        for slot, (source, side, unit) in enumerate(plan):
            if source is None:
                block = wave.at[2 * side : 2 * side + 2, :, unit * TILE : (unit + 1) * TILE]
            else:
                block = gots[source].at[unit]
            copies.append(pltpu.make_async_copy(block, out.at[slot], sems.at[len(copies)]))
    for copy in copies:
        copy.start()
    for copy in copies:
        copy.wait()


def pack_stage(wave, gots, plans):
    shapes = [(len(plan), 2, TILE, TILE) for plan in plans]
    return pl.pallas_call(
        functools.partial(pack_kernel, plans),
        out_shape=[jax.ShapeDtypeStruct(shape, BF16) for shape in shapes],
        grid_spec=pltpu.PrefetchScalarGridSpec(
            num_scalar_prefetch=0,
            grid=(1,),
            in_specs=[pl.BlockSpec(memory_space=pl.ANY)] * (1 + len(gots)),
            out_specs=[pl.BlockSpec(shape, lambda i: (0, 0, 0, 0)) for shape in shapes],
            scratch_shapes=[pltpu.SemaphoreType.DMA((sum(len(plan) for plan in plans),))],
        ),
        compiler_params=pltpu.CompilerParams(vmem_limit_bytes=8 << 20),
        cost_estimate=pl.CostEstimate(flops=0, bytes_accessed=3 << 20, transcendentals=0),
    )(wave, *gots)


def left_kernel(first_sector, split, place, pairs, size, *refs):
    pieces, left_hbm = refs[:8], refs[8]
    outs = refs[9 : 9 + split]
    whole, left, sems, left_sem = refs[9 + split :]
    y, z, bond = place[0], place[1], place[2]
    count = whole.shape[0]
    copies = [pltpu.make_async_copy(left_hbm, left, left_sem)]
    for idx, piece in enumerate(pieces):
        upper, far = idx < SIDE, idx % SIDE
        for near in range(SIDE):
            step_y, step_z = (far, near) if upper else (near, far)
            owner = (y + SIDE - step_y) % SIDE * SIDE + (z + SIDE - step_z) % SIDE
            start = owner * 4 + (0 if upper else 2)
            copies.append(
                pltpu.make_async_copy(
                    piece.at[pl.ds(near * count, count)],
                    whole.at[:, pl.ds(start, 2)],
                    sems.at[len(copies) - 1],
                )
            )
    for copy in copies:
        copy.start()
    for copy in copies:
        copy.wait()
    lane = lax.broadcasted_iota(jnp.int32, (TILE, TILE), 1)
    strip_sectors = 8
    col_live = jnp.concatenate(
        [
            (lane[:1] < size[bond * strip_sectors + first_sector + s]).astype(F32)
            for s in range(count)
        ],
        axis=1,
    )
    terms, rows = left.shape[0], left.shape[1]
    zero = jnp.zeros((TILE, TILE), BF16)
    unroll = 8

    @pl.loop(0, terms * rows // unroll)
    def _(trip):
        for u in range(unroll):
            step = trip * unroll + u
            term, row = step // rows, step % rows
            low, high = pairs[step * 2], pairs[step * 2 + 1]
            lhs = jnp.concatenate(
                [
                    jnp.where(lane < size[low], left[term, row, 0], zero),
                    jnp.where(lane < size[high], left[term, row, 1], zero),
                ],
                axis=1,
            )
            rhs = jnp.concatenate(
                [
                    jnp.concatenate([whole[s, sector] for s in range(count)], axis=1)
                    for sector in (low, high)
                ],
                axis=0,
            )
            middle = (jnp.dot(lhs, rhs, preferred_element_type=F32) * col_live).astype(BF16)
            for s in range(count):
                value = middle[:, s * TILE : (s + 1) * TILE]
                if split == 1:
                    outs[0][row // 2, s, term, u % 2 * TILE : (u % 2 + 1) * TILE, :] = value
                else:
                    outs[u % 2][row // 2, s, term] = value


def left_stage(pieces, split, count, left_blocks, place, pairs, size, first_sector):
    terms = left_blocks.shape[0]
    shape = (8, count, terms, 2 * TILE // split, TILE)
    return pl.pallas_call(
        functools.partial(left_kernel, first_sector, split),
        out_shape=[jax.ShapeDtypeStruct(shape, BF16)] * split,
        grid_spec=pltpu.PrefetchScalarGridSpec(
            num_scalar_prefetch=3,
            grid=(1,),
            in_specs=[pl.BlockSpec(memory_space=pl.ANY)] * (len(pieces) + 1),
            out_specs=[pl.BlockSpec(shape, lambda i, *_: (0, 0, 0, 0, 0))] * split,
            scratch_shapes=[
                pltpu.VMEM((count, 64, TILE, TILE), BF16),
                pltpu.VMEM(left_blocks.shape, BF16),
                pltpu.SemaphoreType.DMA((32,)),
                pltpu.SemaphoreType.DMA(()),
            ],
        ),
        compiler_params=pltpu.CompilerParams(vmem_limit_bytes=60 << 20),
        cost_estimate=pl.CostEstimate(
            flops=2 * terms * 2048 * 256 * count * TILE,
            bytes_accessed=(2 << 20) + (terms * 2048 + 8192) * count * TILE * 2,
            transcendentals=0,
        ),
    )(place, pairs, size, *pieces, left_blocks)


def right_kernel(counts, half, place, pairs, size, *refs):
    arrived = refs[: len(counts)]
    right_hbm = refs[len(counts)]
    outs_a = refs[len(counts) + 1 : len(counts) + 5]
    outs_b = refs[len(counts) + 5 : len(counts) + 9]
    middle, right, sum_a, sum_b, sems, right_sems, out_sems = refs[len(counts) + 9 :]
    bond = place[2]
    rows, terms = middle.shape[2], middle.shape[1]
    copies = []
    first = 0
    for chunk, count in zip(arrived, counts):
        for source in range(8):
            block = chunk.at[source]
            if chunk.shape[3] != rows:
                block = block.at[:, :, half * rows : (half + 1) * rows]
            copies.append(
                pltpu.make_async_copy(
                    block, middle.at[pl.ds(source * 8 + first, count)], sems.at[len(copies)]
                )
            )
        first += count
    for copy in copies:
        copy.start()

    def owner_of(step_z, step_y):
        return (place[0] + step_y) % SIDE * SIDE + (place[1] + step_z) % SIDE

    def right_copy(step_z, step_y):
        return pltpu.make_async_copy(
            right_hbm.at[:, pl.ds(owner_of(step_z, step_y) * 4, 4)],
            right.at[step_z * SIDE + step_y],
            right_sems.at[step_z * SIDE + step_y],
        )

    for step_z in range(SIDE):
        for step_y in range(SIDE):
            right_copy(step_z, step_y).start()
    line = lax.broadcasted_iota(jnp.int32, (TILE, TILE), 0)
    lane = lax.broadcasted_iota(jnp.int32, (TILE, TILE), 1)
    row_live = line < size[bond * 2 + half]
    for copy in copies:
        copy.wait()
    sent = []
    for step_z in range(SIDE):

        @pl.loop(0, SIDE, step=2)
        def _(pair):
            for step_y in (pair, pair + 1):
                right_copy(step_z, step_y).wait()
            for step_y in (pair, pair + 1):
                owner = owner_of(step_z, step_y)
                blocks = right.at[step_z * SIDE + step_y]
                for q in range(4):
                    col = owner * 4 + q
                    lhs = jnp.concatenate(
                        [
                            middle[pairs[(term * 64 + col) * 2 + p], term]
                            for term in range(terms)
                            for p in range(2)
                        ],
                        axis=1,
                    )
                    rhs = jnp.concatenate(
                        [blocks[term, q, p] for term in range(terms) for p in range(2)], axis=0
                    )
                    product = jnp.dot(lhs, rhs, preferred_element_type=F32)
                    keep = row_live & (lane < size[col])
                    value = jnp.where(keep, product, 0.0).astype(BF16)
                    if q < 2:
                        sum_a[step_z, step_y, :, q * TILE : (q + 1) * TILE] = value
                    else:
                        sum_b[step_y, step_z, :, (q - 2) * TILE : (q - 1) * TILE] = value

        sent.append(
            pltpu.make_async_copy(sum_a.at[step_z], outs_a[step_z], out_sems.at[len(sent)])
        )
        sent[-1].start()
        for k in range(SIDE):
            sent.append(
                pltpu.make_async_copy(
                    sum_b.at[k, step_z], outs_b[k].at[step_z], out_sems.at[len(sent)]
                )
            )
            sent[-1].start()
    for copy in sent:
        copy.wait()


def right_stage(arrived, half, right_blocks, place, pairs, size):
    counts = tuple(a.shape[1] for a in arrived)
    terms, rows = arrived[0].shape[2], TILE
    shape = jax.ShapeDtypeStruct((SIDE, rows, 2 * TILE), BF16)
    anywhere = pl.BlockSpec(memory_space=pl.ANY)
    return pl.pallas_call(
        functools.partial(right_kernel, counts, half),
        out_shape=[shape] * 8,
        grid_spec=pltpu.PrefetchScalarGridSpec(
            num_scalar_prefetch=3,
            grid=(1,),
            in_specs=[anywhere] * (len(counts) + 1),
            out_specs=[anywhere] * 8,
            scratch_shapes=[
                pltpu.VMEM((64, terms, rows, TILE), BF16),
                pltpu.VMEM((GROUP, terms, 4, 2, TILE, TILE), BF16),
                pltpu.VMEM((SIDE, SIDE, rows, 2 * TILE), BF16),
                pltpu.VMEM((SIDE, SIDE, rows, 2 * TILE), BF16),
                pltpu.SemaphoreType.DMA((8 * len(counts),)),
                pltpu.SemaphoreType.DMA((GROUP,)),
                pltpu.SemaphoreType.DMA((SIDE * (SIDE + 1),)),
            ],
        ),
        compiler_params=pltpu.CompilerParams(vmem_limit_bytes=60 << 20),
        cost_estimate=pl.CostEstimate(
            flops=2 * terms * rows * 256 * 8192,
            bytes_accessed=(14 << 20),
            transcendentals=0,
        ),
    )(place, pairs, size, *arrived, right_blocks)


def sum_kernel(*refs):
    inputs, outputs = refs[:8], refs[8:]
    for half in range(2):
        mine = inputs[half * 4 : half * 4 + 4]
        total = mine[0][...].astype(F32)
        for other in mine[1:]:
            total = total + other[...].astype(F32)
        kept = outputs[half * 4 : half * 4 + 4]
        kept[0][...] = total[0]
        for k in range(1, SIDE):
            kept[k][...] = total[k].astype(BF16)


def sum_stage(pieces):
    rows, width = pieces[0].shape[1:]
    whole = pl.BlockSpec(memory_space=pltpu.VMEM)
    kinds = [F32, BF16, BF16, BF16]
    return pl.pallas_call(
        sum_kernel,
        name="near_sum",
        out_shape=[jax.ShapeDtypeStruct((rows, width), kind) for kind in kinds * 2],
        in_specs=[whole] * 8,
        out_specs=[whole] * 8,
        compiler_params=pltpu.CompilerParams(vmem_limit_bytes=16 << 20),
    )(*pieces)


def last_kernel(*refs):
    out = refs[-1]
    rows, width = refs[0].shape
    for block in range(len(refs) // SIDE):
        mine = refs[block * 4 : block * 4 + 4]
        total = mine[0][...]
        for other in mine[1:]:
            total = total + other[...].astype(F32)
        line, col = block // 2 * rows, block % 2 * width
        out[line : line + rows, col : col + width] = total


def last_stage(pieces):
    rows, width = pieces[0].shape
    whole = pl.BlockSpec(memory_space=pltpu.VMEM)
    return pl.pallas_call(
        last_kernel,
        name="far_sum",
        out_shape=jax.ShapeDtypeStruct((rows * len(pieces) // 8, 2 * width), F32),
        in_specs=[whole] * len(pieces),
        out_specs=whole,
        compiler_params=pltpu.CompilerParams(vmem_limit_bytes=16 << 20),
    )(*pieces)


def turn(value, d, along_y):
    return move(value, d, 0) if along_y else move(value, 0, d)


def apply_slab(wave_slab, left_blocks, right_blocks, sector_size, left_pairs, right_pairs):
    group = lax.axis_index("op")
    place = jnp.stack([group // SIDE, group % SIDE, lax.axis_index("bond")]).astype(jnp.int32)
    lefts, rights = left_pairs.reshape(-1), right_pairs.reshape(-1)
    chunk_count = len(CHUNKS)
    starts = [sum(CHUNKS[:chunk]) for chunk in range(chunk_count + 1)]
    wave = wave_slab.reshape(4, TILE, wave_slab.shape[1])
    ahead = min(2, chunk_count)

    def sent_both(values, y_first):
        return [
            [value] + [turn(value, d, (side == 0) == y_first) for d in range(1, SIDE)]
            for side, value in enumerate(values)
        ]

    units = range(starts[ahead])
    values = pack_stage(wave, [], [[(None, side, unit) for unit in units] for side in range(2)])
    got = sent_both(values, False)
    near = {chunk: ([got[0][1:], got[1][1:]], starts[chunk]) for chunk in range(ahead)}
    arrived = []
    for chunk in range(chunk_count):
        count = CHUNKS[chunk]
        after = chunk + ahead
        sources, offset = near[chunk]
        plans = []
        for side in range(2):
            plan = [(None, side, starts[chunk] + unit) for unit in range(count)]
            for d in range(SIDE - 1):
                plan += [(side * 3 + d, side, offset + unit) for unit in range(count)]
            if after < chunk_count:
                plan += [(None, 1 - side, starts[after] + unit) for unit in range(CHUNKS[after])]
            plans.append(plan)
        values = pack_stage(wave, sources[0] + sources[1], plans)
        got = sent_both(values, True)
        pieces = got[0] + got[1]
        if after < chunk_count:
            near[after] = ([got[1][1:], got[0][1:]], 4 * count)
        split = 2 if chunk == chunk_count - 1 else 1
        middles = left_stage(
            pieces, split, count, left_blocks, place, lefts, sector_size, starts[chunk]
        )
        for middle in middles:
            arrived.append(lax.all_to_all(middle, "bond", split_axis=0, concat_axis=0, tiled=True))
    finals = []
    for half in range(2):
        mine = arrived[: chunk_count - 1] + [arrived[chunk_count - 1 + half]]
        parts = right_stage(mine, half, right_blocks, place, rights, sector_size)
        got = [parts[0]] + [move(parts[d], 0, d) for d in range(1, SIDE)]
        got += [parts[4]] + [move(parts[4 + d], d, 0) for d in range(1, SIDE)]
        sums = sum_stage(got)
        finals += [sums[0]] + [move(sums[d], d, 0) for d in range(1, SIDE)]
        finals += [sums[4]] + [move(sums[4 + d], 0, d) for d in range(1, SIDE)]
    return last_stage(finals)


def solution(mesh):
    placed = (
        P("op", "bond"),
        P("op", None, None, None, None),
        P("op", None, None, None, None),
        P(),
        P("op", None, None),
        P("op", None, None),
    )
    return jax.shard_map(
        apply_slab, mesh=mesh, in_specs=placed, out_specs=P("bond", "op"), check_vma=False
    )
```

time: 302 us -> 340 us (1.13)
  waiting for transfers between devices: 112 us -> 151 us
  blocking collectives: 0 us -> 31.8 us
  local copies, waits for them, and re-layouts: 27.7 us -> 6.13 us
  starting transfers between devices: 112 us -> 92.8 us
  Pallas kernels: 45.8 us -> 55.9 us
    ppermute x54, waiting for transfers between devices: 85.9 us -> 130 us  [move(): return lax.ppermute(value, 'op', pairs)]
    all_to_all x0 -> x1, blocking collectives: none -> 31.8 us  [apply_slab(): lax.all_to_all(middle, 'bond', split_axis=0, concat_axis=0, tiled=True)]
    ppermute x54, starting transfers between devices: 95 us -> 75.9 us  [move(): return lax.ppermute(value, 'op', pairs)]
    another operation x13 -> x0, local copies, waits for them, and re-layouts: 14.8 us -> none  [apply_slab(): rows[chunk] = [jnp.stack([v[:, :, part] for v in side]) for side in both]]
    pallas_call x5 -> x11, Pallas kernels: 44.4 us -> 54.5 us  [the longest x4 26.9 us: left_stage(): pl.pallas_call(functools.partial(left_kernel, first_sector, split), out_s...]
    all_to_all x4, waiting for transfers between devices: 26.3 us -> 20.4 us  [apply_slab(): lax.all_to_all(middle, 'bond', split_axis=0, concat_axis=0, tiled=True)]
    unnamed x106 -> x82, local copies, waits for them, and re-layouts: 9.08 us -> 4.76 us
  transfers between devices with their start and end apart: 58 -> 58, of which waited for: 24 -> 25; matrix products, arithmetic and copies ran while one was open for 6% -> 1% of each run, Pallas kernels for 10% -> 15%
where the time goes in v1:
time: 340 us; the launch traced here: 339 us
  waiting for transfers between devices  151 us (44%)
  starting transfers between devices  92.8 us (27%)
  Pallas kernels  55.9 us (16%)
  blocking collectives  31.8 us (9%)
  local copies, waits for them, and re-layouts  6.13 us (2%)
    ppermute x54, waiting for transfers between devices, move(): return lax.ppermute(value, 'op', pairs)  130 us
    ppermute x54, starting transfers between devices, move(): return lax.ppermute(value, 'op', pairs)  75.9 us
    all_to_all x1, blocking collectives, apply_slab(): lax.all_to_all(middle, 'bond', split_axis=0, concat_axis=0, tiled=True)  31.8 us
    pallas_call x4, Pallas kernels, left_stage(): pl.pallas_call(functools.partial(left_kernel, first_sector, split), out_s...  26.9 us
    all_to_all x4, waiting for transfers between devices, apply_slab(): lax.all_to_all(middle, 'bond', split_axis=0, concat_axis=0, tiled=True)  20.4 us
    pallas_call x2, Pallas kernels, right_stage(): pl.pallas_call(functools.partial(right_kernel, counts, half), out_shape=[...  20.3 us
    all_to_all x4, starting transfers between devices, apply_slab(): lax.all_to_all(middle, 'bond', split_axis=0, concat_axis=0, tiled=True)  17 us
    pallas_call x5, Pallas kernels, pack_stage(): pl.pallas_call(functools.partial(pack_kernel, plans), out_shape=[jax.Shap...  7.31 us
  transfers between devices with their start and end apart: 58, of which 25 were waited for; matrix products, arithmetic and copies ran while one was open for 1% of the time, Pallas kernels for 15%

profile of v1, /device:TPU:0, one launch (start us, length us, event | category | flops | bytes accessed | tf_op | source)
XLA Modules:
  0.0 338.7 jit_solution(13659094967255098412)
XLA Ops:
  1.5 4.2 %collective-permute-start.2 = (bf16[4,2,128,128]{3,2,1,0:T(8,128)(2,1)S(1)}, bf16[4,2,128,128]{3,2,1,0:T(8,128)(2,1)S(1)}, u32[]{:S(2)}, u32[]{:S(2)}) collective-permute-start(bf16[4,2,128,128]{3,2,1,0:T(8,128)(2,1)S(1)} %get-tuple-element.49), channel_id=1, source_target_pairs={{0,3},{1,0},{2,1},{3,2},{4,7},{5,4},{6,5},{7,6},{8,11},{9,8},{10,9... | collective-permute-start | bytes 786440 | tf_op jit(solution)/shard_map/ppermute | solution.py:25
  6.9 3.0 collective-permute-start.5
  10.6 6.3 %collective-permute-done.2.refs_2_ = bf16[4,2,128,128]{3,2,1,0:T(8,128)(2,1)S(1)} collective-permute-done((bf16[4,2,128,128]{3,2,1,0:T(8,128)(2,1)S(1)}, bf16[4,2,128,128]{3,2,1,0:T(8,128)(2,1)S(1)}, u32[]{:S(2)}, u32[]{:S(2)}) %collective-permute-start.2) | collective-permute-done | bytes 262176 | tf_op jit(solution)/shard_map/ppermute | solution.py:25
  18.4 1.8 collective-permute-done.refs_0_
  20.3 4.9 %collective-permute-done.3.refs_3_ = bf16[4,2,128,128]{3,2,1,0:T(8,128)(2,1)S(1)} collective-permute-done((bf16[4,2,128,128]{3,2,1,0:T(8,128)(2,1)S(1)}, bf16[4,2,128,128]{3,2,1,0:T(8,128)(2,1)S(1)}, u32[]{:S(2)}, u32[]{:S(2)}) %collective-permute-start.3) | collective-permute-done | bytes 262176 | tf_op jit(solution)/shard_map/ppermute | solution.py:25
  30.0 3.8 %collective-permute-start.17 = (bf16[10,2,128,128]{3,2,1,0:T(8,128)(2,1)S(1)}, bf16[10,2,128,128]{3,2,1,0:T(8,128)(2,1)S(1)}, u32[]{:S(2)}, u32[]{:S(2)}) collective-permute-start(bf16[10,2,128,128]{3,2,1,0:T(8,128)(2,1)S(1)} %get-tuple-element.54.refs_4_), channel_id=1, source_target_pairs={{0,3},{1,0},{2,1},{3,2},{4,7},{5,4},{6,5},{7,6},{8,11},{9,8},{10,9... | collective-permute-start | bytes 1966088 | tf_op jit(solution)/shard_map/ppermute | solution.py:25
  33.8 10.4 %collective-permute-done.14.refs_3_.refs_5_ = bf16[10,2,128,128]{3,2,1,0:T(8,128)(2,1)S(1)} collective-permute-done((bf16[10,2,128,128]{3,2,1,0:T(8,128)(2,1)S(1)}, bf16[10,2,128,128]{3,2,1,0:T(8,128)(2,1)S(1)}, u32[]{:S(2)}, u32[]{:S(2)}) %collective-permute-start.14) | collective-permute-done | bytes 655392 | tf_op jit(solution)/shard_map/ppermute | solution.py:25
  45.3 2.2 collective-permute-done.13.refs_2_.refs_4_
  47.5 10.8 %collective-permute-done.12.refs_1_.refs_3_ = bf16[10,2,128,128]{3,2,1,0:T(8,128)(2,1)S(1)} collective-permute-done((bf16[10,2,128,128]{3,2,1,0:T(8,128)(2,1)S(1)}, bf16[10,2,128,128]{3,2,1,0:T(8,128)(2,1)S(1)}, u32[]{:S(2)}, u32[]{:S(2)}) %collective-permute-start.12) | collective-permute-done | bytes 655392 | tf_op jit(solution)/shard_map/ppermute | solution.py:25
  59.3 3.7 %collective-permute-done.15.refs_5_.refs_0_ = bf16[10,2,128,128]{3,2,1,0:T(8,128)(2,1)S(1)} collective-permute-done((bf16[10,2,128,128]{3,2,1,0:T(8,128)(2,1)S(1)}, bf16[10,2,128,128]{3,2,1,0:T(8,128)(2,1)S(1)}, u32[]{:S(2)}, u32[]{:S(2)}) %collective-permute-start.15) | collective-permute-done | bytes 655392 | tf_op jit(solution)/shard_map/ppermute | solution.py:25
  63.0 2.2 shard_map.71
  65.3 7.9 %collective-permute-start.26 = (bf16[8,2,128,128]{3,2,1,0:T(8,128)(2,1)}, bf16[8,2,128,128]{3,2,1,0:T(8,128)(2,1)S(1)}, u32[]{:S(2)}, u32[]{:S(2)}) collective-permute-start(bf16[8,2,128,128]{3,2,1,0:T(8,128)(2,1)} %get-tuple-element.57.refs_0_), channel_id=1, source_target_pairs={{0,12},{1,13},{2,14},{3,15},{4,0},{5,1},{6,2},{7,3},{8,4},{9,5},{1... | collective-permute-start | bytes 1572872 | tf_op jit(solution)/shard_map/ppermute | solution.py:25
  74.1 2.0 collective-permute-start.29
  76.1 15.5 %collective-permute-done.26.refs_3_ = bf16[8,2,128,128]{3,2,1,0:T(8,128)(2,1)S(1)} collective-permute-done((bf16[8,2,128,128]{3,2,1,0:T(8,128)(2,1)}, bf16[8,2,128,128]{3,2,1,0:T(8,128)(2,1)S(1)}, u32[]{:S(2)}, u32[]{:S(2)}) %collective-permute-start.26) | collective-permute-done | bytes 524320 | tf_op jit(solution)/shard_map/ppermute | solution.py:25
  91.7 2.4 shard_map.65
  94.1 3.7 %collective-permute-start.8 = (bf16[10,2,128,128]{3,2,1,0:T(8,128)(2,1)}, bf16[10,2,128,128]{3,2,1,0:T(8,128)(2,1)S(1)}, u32[]{:S(2)}, u32[]{:S(2)}) collective-permute-start(bf16[10,2,128,128]{3,2,1,0:T(8,128)(2,1)} %get-tuple-element.51.refs_0_), channel_id=1, source_target_pairs={{0,12},{1,13},{2,14},{3,15},{4,0},{5,1},{6,2},{7,3},{8,4},{9,5},{1... | collective-permute-start | bytes 1966088 | tf_op jit(solution)/shard_map/ppermute | solution.py:25
  99.2 3.2 collective-permute-done.27.refs_5_
  102.4 6.7 %shard_map.72 = (bf16[8,2,2,128,128]{4,3,2,1,0:T(8,128)(2,1)}, bf16[8,2,2,128,128]{4,3,2,1,0:T(8,128)(2,1)}) custom-call(s32[3]{0:T(128)} %pad_add_fusion.place, s32[64]{0:T(128)} %reshape.10.pairs, s32[64]{0:T(128)} %size.11, bf16[8,2,128,128]{3,2,1,0:T(8,128)(2,1)} %get-tuple-element.57.refs_0_, bf16[8,2,128,128]{3,2,1,0:T(8,128)(2,1)} %copy-done.34, ...), custom_call_target="tpu_custom_call" | custom-call | flops 536870912 | bytes 8388608 | tf_op jit(solution)/shard_map/pallas_call | solution.py:131
  109.1 4.3 %all-to-all-start.4 = ((bf16[8,2,2,128,128]{4,3,2,1,0:T(8,128)(2,1)}), bf16[8,2,2,128,128]{4,3,2,1,0:T(8,128)(2,1)}, u32[]{:S(2)}, u32[]{:S(2)}) async-start(bf16[8,2,2,128,128]{4,3,2,1,0:T(8,128)(2,1)} %get-tuple-element.76), calls=%async_computation.4 | async-start | bytes 2097152 | tf_op jit(solution)/shard_map/all_to_all | solution.py:373
  113.5 4.4 %collective-permute-start.6 = (bf16[10,2,128,128]{3,2,1,0:T(8,128)(2,1)}, bf16[10,2,128,128]{3,2,1,0:T(8,128)(2,1)S(1)}, u32[]{:S(2)}, u32[]{:S(2)}) collective-permute-start(bf16[10,2,128,128]{3,2,1,0:T(8,128)(2,1)} %get-tuple-element.51.refs_0_), channel_id=1, source_target_pairs={{0,4},{1,5},{2,6},{3,7},{4,8},{5,9},{6,10},{7,11},{8,12},{9,13},{1... | collective-permute-start | bytes 1966088 | tf_op jit(solution)/shard_map/ppermute | solution.py:25
  117.9 2.0 collective-permute-start.11
  120.8 12.1 %collective-permute-done.7.refs_2_.refs_4_ = bf16[10,2,128,128]{3,2,1,0:T(8,128)(2,1)S(1)} collective-permute-done((bf16[10,2,128,128]{3,2,1,0:T(8,128)(2,1)}, bf16[10,2,128,128]{3,2,1,0:T(8,128)(2,1)S(1)}, u32[]{:S(2)}, u32[]{:S(2)}) %collective-permute-start.7) | collective-permute-done | bytes 655392 | tf_op jit(solution)/shard_map/ppermute | solution.py:25
  132.9 13.5 %collective-permute-done.6.refs_1_.refs_3_ = bf16[10,2,128,128]{3,2,1,0:T(8,128)(2,1)S(1)} collective-permute-done((bf16[10,2,128,128]{3,2,1,0:T(8,128)(2,1)}, bf16[10,2,128,128]{3,2,1,0:T(8,128)(2,1)S(1)}, u32[]{:S(2)}, u32[]{:S(2)}) %collective-permute-start.6) | collective-permute-done | bytes 655392 | tf_op jit(solution)/shard_map/ppermute | solution.py:25
  146.3 2.0 collective-permute-done.11.refs_7_.refs_2_
  148.4 3.5 %collective-permute-done.9.refs_5_.refs_0_ = bf16[10,2,128,128]{3,2,1,0:T(8,128)(2,1)} collective-permute-done((bf16[10,2,128,128]{3,2,1,0:T(8,128)(2,1)}, bf16[10,2,128,128]{3,2,1,0:T(8,128)(2,1)}, u32[]{:S(2)}, u32[]{:S(2)}) %collective-permute-start.9) | collective-permute-done | bytes 655392 | tf_op jit(solution)/shard_map/ppermute | solution.py:25
  151.9 6.7 %shard_map.66 = bf16[8,2,2,256,128]{4,3,2,1,0:T(8,128)(2,1)} custom-call(s32[3]{0:T(128)} %pad_add_fusion.place, s32[64]{0:T(128)} %reshape.10.pairs, s32[64]{0:T(128)} %size.11, bf16[10,2,128,128]{3,2,1,0:T(8,128)(2,1)} %get-tuple-element.51.refs_0_, bf16[10,2,128,128]{3,2,1,0:T(8,128)(2,1)} %copy-done.12, bf16[10,2,128,128]{3,2,1,0:T(8,128)(2,1)} %copy-done.10, ...), custom_call_target="tpu_custom_call" | custom-call | flops 536870912 | bytes 8388608 | tf_op jit(solution)/shard_map/pallas_call | solution.py:131
  158.6 4.4 %all-to-all-start = ((bf16[8,2,2,256,128]{4,3,2,1,0:T(8,128)(2,1)}), bf16[8,2,2,256,128]{4,3,2,1,0:T(8,128)(2,1)}, u32[]{:S(2)}, u32[]{:S(2)}) async-start(bf16[8,2,2,256,128]{4,3,2,1,0:T(8,128)(2,1)} %shard_map.66), calls=%async_computation | async-start | bytes 4194304 | tf_op jit(solution)/shard_map/all_to_all | solution.py:373
  163.0 6.8 %shard_map.68 = bf16[8,2,2,256,128]{4,3,2,1,0:T(8,128)(2,1)} custom-call(s32[3]{0:T(128)} %pad_add_fusion.place, s32[64]{0:T(128)} %reshape.10.pairs, s32[64]{0:T(128)} %size.11, bf16[10,2,128,128]{3,2,1,0:T(8,128)(2,1)} %copy-done.18, bf16[10,2,128,128]{3,2,1,0:T(8,128)(2,1)} %copy-done.4, bf16[10,2,128,128]{3,2,1,0:T(8,128)(2,1)} %copy-done.3, ...), custom_call_target="tpu_custom_call" | custom-call | flops 536870912 | bytes 8388608 | tf_op jit(solution)/shard_map/pallas_call | solution.py:131
  169.9 20.4 %all-to-all-done.refs_0_ = bf16[8,2,2,256,128]{4,3,2,1,0:T(8,128)(2,1)} async-done(((bf16[8,2,2,256,128]{4,3,2,1,0:T(8,128)(2,1)}), bf16[8,2,2,256,128]{4,3,2,1,0:T(8,128)(2,1)}, u32[]{:S(2)}, u32[]{:S(2)}) %all-to-all-start) | async-done | bytes 2097184 | tf_op jit(solution)/shard_map/all_to_all | solution.py:373
  190.3 4.5 %all-to-all-start.1 = ((bf16[8,2,2,256,128]{4,3,2,1,0:T(8,128)(2,1)}), bf16[8,2,2,256,128]{4,3,2,1,0:T(8,128)(2,1)}, u32[]{:S(2)}, u32[]{:S(2)}) async-start(bf16[8,2,2,256,128]{4,3,2,1,0:T(8,128)(2,1)} %shard_map.68), calls=%async_computation.1 | async-start | bytes 4194304 | tf_op jit(solution)/shard_map/all_to_all | solution.py:373
  198.3 2.3 collective-permute-start.19
  201.8 11.3 %collective-permute-done.20.refs_3_ = bf16[8,2,128,128]{3,2,1,0:T(8,128)(2,1)S(1)} collective-permute-done((bf16[8,2,128,128]{3,2,1,0:T(8,128)(2,1)S(1)}, bf16[8,2,128,128]{3,2,1,0:T(8,128)(2,1)S(1)}, u32[]{:S(2)}, u32[]{:S(2)}) %collective-permute-start.20) | collective-permute-done | bytes 524320 | tf_op jit(solution)/shard_map/ppermute | solution.py:25
  214.7 10.4 %collective-permute-done.18.refs_1_ = bf16[8,2,128,128]{3,2,1,0:T(8,128)(2,1)S(1)} collective-permute-done((bf16[8,2,128,128]{3,2,1,0:T(8,128)(2,1)S(1)}, bf16[8,2,128,128]{3,2,1,0:T(8,128)(2,1)S(1)}, u32[]{:S(2)}, u32[]{:S(2)}) %collective-permute-start.18) | collective-permute-done | bytes 524320 | tf_op jit(solution)/shard_map/ppermute | solution.py:25
  225.1 3.0 collective-permute-done.21.refs_5_
  228.2 6.7 %shard_map.70 = bf16[8,2,2,256,128]{4,3,2,1,0:T(8,128)(2,1)} custom-call(s32[3]{0:T(128)} %pad_add_fusion.place, s32[64]{0:T(128)} %reshape.10.pairs, s32[64]{0:T(128)} %size.11, bf16[8,2,128,128]{3,2,1,0:T(8,128)(2,1)} %copy-done.20, bf16[8,2,128,128]{3,2,1,0:T(8,128)(2,1)} %copy-done.29, bf16[8,2,128,128]{3,2,1,0:T(8,128)(2,1)} %copy-done.28, ...), custom_call_target="tpu_custom_call" | custom-call | flops 536870912 | bytes 8388608 | tf_op jit(solution)/shard_map/pallas_call | solution.py:131
  234.9 31.8 %all_to_all.25.refs_2_ = bf16[8,2,2,256,128]{4,3,2,1,0:T(8,128)(2,1)} all-to-all(bf16[8,2,2,256,128]{4,3,2,1,0:T(8,128)(2,1)} %shard_map.70), channel_id=1, replica_groups=mesh['bond'=8,'op'=16] {'bond'}, dimensions={0} | all-to-all | bytes 4194304 | tf_op jit(solution)/shard_map/all_to_all | solution.py:373
  266.6 3.7 %all-to-all-start.3 = ((bf16[8,2,2,128,128]{4,3,2,1,0:T(8,128)(2,1)}), bf16[8,2,2,128,128]{4,3,2,1,0:T(8,128)(2,1)S(1)}, u32[]{:S(2)}, u32[]{:S(2)}) async-start(bf16[8,2,2,128,128]{4,3,2,1,0:T(8,128)(2,1)} %get-tuple-element.59), calls=%async_computation.3 | async-start | bytes 2097152 | tf_op jit(solution)/shard_map/all_to_all | solution.py:373
  271.2 10.1 %shard_map.74 = (bf16[4,128,256]{2,1,0:T(8,128)(2,1)}, bf16[4,128,256]{2,1,0:T(8,128)(2,1)}, bf16[4,128,256]{2,1,0:T(8,128)(2,1)}, bf16[4,128,256]{2,1,0:T(8,128...) custom-call(s32[3]{0:T(128)} %pad_add_fusion.place, ...), custom_call_target="tpu_custom_call" | custom-call | flops 1073741824 | bytes 14680064 | tf_op jit(solution)/shard_map/pallas_call | solution.py:248
  281.4 2.1 collective-permute-start.43
  285.5 3.2 collective-permute-start.46
  289.8 10.2 %shard_map.73 = (bf16[4,128,256]{2,1,0:T(8,128)(2,1)}, bf16[4,128,256]{2,1,0:T(8,128)(2,1)}, bf16[4,128,256]{2,1,0:T(8,128)(2,1)}, bf16[4,128,256]{2,1,0:T(8,128...) custom-call(s32[3]{0:T(128)} %pad_add_fusion.place, ...), custom_call_target="tpu_custom_call" | custom-call | flops 1073741824 | bytes 14680064 | tf_op jit(solution)/shard_map/pallas_call | solution.py:248
  303.0 1.8 collective-permute-start.31
  304.8 2.5 collective-permute-start.32
  309.0 7.0 %collective-permute-done.30.refs_1_ = bf16[4,128,256]{2,1,0:T(8,128)(2,1)S(1)} collective-permute-done((bf16[4,128,256]{2,1,0:T(8,128)(2,1)}, bf16[4,128,256]{2,1,0:T(8,128)(2,1)S(1)}, u32[]{:S(2)}, u32[]{:S(2)}) %collective-permute-start.30) | collective-permute-done | bytes 262176 | tf_op jit(solution)/shard_map/ppermute | solution.py:25
  319.1 2.8 collective-permute-done.33.refs_5_
  323.2 2.4 collective-permute-start.52
  327.5 3.1 collective-permute-start.37
  333.5 2.4 collective-permute-start.41
  (168 shorter events, 41.8 us)
Async XLA Ops:
  1.5 15.4 %collective-permute-start.2 = (bf16[4,2,128,128]{3,2,1,0:T(8,128)(2,1)S(1)}, bf16[4,2,128,128]{3,2,1,0:T(8,128)(2,1)S(1)}, u32[]{:S(2)}, u32[]{:S(2)}) collective-permute-start(bf16[4,2,128,128]{3,2,1,0:T(8,128)(2,1)S(1)} %get-tuple-element.49), channel_id=1, source_target_pairs={{0,3},{1,0},{2,1},{3,2},{4,7},{5,4},{6,5},{7,6},{8,11},{9,8},{10,9... | collective-permute-start | bytes 786440 | tf_op jit(solution)/shard_map/ppermute | solution.py:25
  5.7 12.8 %collective-permute-start.1 = (bf16[4,2,128,128]{3,2,1,0:T(8,128)(2,1)S(1)}, bf16[4,2,128,128]{3,2,1,0:T(8,128)(2,1)S(1)}, u32[]{:S(2)}, u32[]{:S(2)}) collective-permute-start(bf16[4,2,128,128]{3,2,1,0:T(8,128)(2,1)S(1)} %get-tuple-element.49), channel_id=1, source_target_pairs={{0,2},{1,3},{2,0},{3,1},{4,6},{5,7},{6,4},{7,5},{8,10},{9,11},{10,... | collective-permute-start | bytes 786440 | tf_op jit(solution)/shard_map/ppermute | solution.py:25
  5.7 14.6 %collective-permute-start = (bf16[4,2,128,128]{3,2,1,0:T(8,128)(2,1)S(1)}, bf16[4,2,128,128]{3,2,1,0:T(8,128)(2,1)S(1)}, u32[]{:S(2)}, u32[]{:S(2)}) collective-permute-start(bf16[4,2,128,128]{3,2,1,0:T(8,128)(2,1)S(1)} %get-tuple-element.49), channel_id=1, source_target_pairs={{0,1},{1,2},{2,3},{3,0},{4,5},{5,6},{6,7},{7,4},{8,9},{9,10},{10,1... | collective-permute-start | bytes 786440 | tf_op jit(solution)/shard_map/ppermute | solution.py:25
  6.9 13.4 %collective-permute-start.5 = (bf16[4,2,128,128]{3,2,1,0:T(8,128)(2,1)S(1)}, bf16[4,2,128,128]{3,2,1,0:T(8,128)(2,1)S(1)}, u32[]{:S(2)}, u32[]{:S(2)}) collective-permute-start(bf16[4,2,128,128]{3,2,1,0:T(8,128)(2,1)S(1)} %get-tuple-element.50), channel_id=1, source_target_pairs={{0,12},{1,13},{2,14},{3,15},{4,0},{5,1},{6,2},{7,3},{8,4},{9,5},{1... | collective-permute-start | bytes 786440 | tf_op jit(solution)/shard_map/ppermute | solution.py:25
  10.0 10.3 %collective-permute-start.4 = (bf16[4,2,128,128]{3,2,1,0:T(8,128)(2,1)S(1)}, bf16[4,2,128,128]{3,2,1,0:T(8,128)(2,1)S(1)}, u32[]{:S(2)}, u32[]{:S(2)}) collective-permute-start(bf16[4,2,128,128]{3,2,1,0:T(8,128)(2,1)S(1)} %get-tuple-element.50), channel_id=1, source_target_pairs={{0,8},{1,9},{2,10},{3,11},{4,12},{5,13},{6,14},{7,15},{8,0},{9,1},... | collective-permute-start | bytes 786440 | tf_op jit(solution)/shard_map/ppermute | solution.py:25
  16.9 8.3 %collective-permute-start.3 = (bf16[4,2,128,128]{3,2,1,0:T(8,128)(2,1)S(1)}, bf16[4,2,128,128]{3,2,1,0:T(8,128)(2,1)S(1)}, u32[]{:S(2)}, u32[]{:S(2)}) collective-permute-start(bf16[4,2,128,128]{3,2,1,0:T(8,128)(2,1)S(1)} %get-tuple-element.50), channel_id=1, source_target_pairs={{0,4},{1,5},{2,6},{3,7},{4,8},{5,9},{6,10},{7,11},{8,12},{9,13},{1... | collective-permute-start | bytes 786440 | tf_op jit(solution)/shard_map/ppermute | solution.py:25
  26.6 17.7 %collective-permute-start.14 = (bf16[10,2,128,128]{3,2,1,0:T(8,128)(2,1)S(1)}, bf16[10,2,128,128]{3,2,1,0:T(8,128)(2,1)S(1)}, u32[]{:S(2)}, u32[]{:S(2)}) collective-permute-start(bf16[10,2,128,128]{3,2,1,0:T(8,128)(2,1)S(1)} %get-tuple-element.53.refs_0_), channel_id=1, source_target_pairs={{0,12},{1,13},{2,14},{3,15},{4,0},{5,1},{6,2},{7,3},{8,4},{9,5},{1... | collective-permute-start | bytes 1966088 | tf_op jit(solution)/shard_map/ppermute | solution.py:25
  28.4 19.1 %collective-permute-start.13 = (bf16[10,2,128,128]{3,2,1,0:T(8,128)(2,1)S(1)}, bf16[10,2,128,128]{3,2,1,0:T(8,128)(2,1)S(1)}, u32[]{:S(2)}, u32[]{:S(2)}) collective-permute-start(bf16[10,2,128,128]{3,2,1,0:T(8,128)(2,1)S(1)} %get-tuple-element.53.refs_0_), channel_id=1, source_target_pairs={{0,8},{1,9},{2,10},{3,11},{4,12},{5,13},{6,14},{7,15},{8,0},{9,1},... | collective-permute-start | bytes 1966088 | tf_op jit(solution)/shard_map/ppermute | solution.py:25
  29.0 29.3 %collective-permute-start.12 = (bf16[10,2,128,128]{3,2,1,0:T(8,128)(2,1)S(1)}, bf16[10,2,128,128]{3,2,1,0:T(8,128)(2,1)S(1)}, u32[]{:S(2)}, u32[]{:S(2)}) collective-permute-start(bf16[10,2,128,128]{3,2,1,0:T(8,128)(2,1)S(1)} %get-tuple-element.53.refs_0_), channel_id=1, source_target_pairs={{0,4},{1,5},{2,6},{3,7},{4,8},{5,9},{6,10},{7,11},{8,12},{9,13},{1... | collective-permute-start | bytes 1966088 | tf_op jit(solution)/shard_map/ppermute | solution.py:25
  30.0 29.3 %collective-permute-start.17 = (bf16[10,2,128,128]{3,2,1,0:T(8,128)(2,1)S(1)}, bf16[10,2,128,128]{3,2,1,0:T(8,128)(2,1)S(1)}, u32[]{:S(2)}, u32[]{:S(2)}) collective-permute-start(bf16[10,2,128,128]{3,2,1,0:T(8,128)(2,1)S(1)} %get-tuple-element.54.refs_4_), channel_id=1, source_target_pairs={{0,3},{1,0},{2,1},{3,2},{4,7},{5,4},{6,5},{7,6},{8,11},{9,8},{10,9... | collective-permute-start | bytes 1966088 | tf_op jit(solution)/shard_map/ppermute | solution.py:25
  33.8 25.5 %collective-permute-start.16 = (bf16[10,2,128,128]{3,2,1,0:T(8,128)(2,1)S(1)}, bf16[10,2,128,128]{3,2,1,0:T(8,128)(2,1)S(1)}, u32[]{:S(2)}, u32[]{:S(2)}) collective-permute-start(bf16[10,2,128,128]{3,2,1,0:T(8,128)(2,1)S(1)} %get-tuple-element.54.refs_4_), channel_id=1, source_target_pairs={{0,2},{1,3},{2,0},{3,1},{4,6},{5,7},{6,4},{7,5},{8,10},{9,11},{10,... | collective-permute-start | bytes 1966088 | tf_op jit(solution)/shard_map/ppermute | solution.py:25
  44.2 18.8 %collective-permute-start.15 = (bf16[10,2,128,128]{3,2,1,0:T(8,128)(2,1)S(1)}, bf16[10,2,128,128]{3,2,1,0:T(8,128)(2,1)S(1)}, u32[]{:S(2)}, u32[]{:S(2)}) collective-permute-start(bf16[10,2,128,128]{3,2,1,0:T(8,128)(2,1)S(1)} %get-tuple-element.54.refs_4_), channel_id=1, source_target_pairs={{0,1},{1,2},{2,3},{3,0},{4,5},{5,6},{6,7},{7,4},{8,9},{9,10},{10,1... | collective-permute-start | bytes 1966088 | tf_op jit(solution)/shard_map/ppermute | solution.py:25
  65.3 26.4 %collective-permute-start.26 = (bf16[8,2,128,128]{3,2,1,0:T(8,128)(2,1)}, bf16[8,2,128,128]{3,2,1,0:T(8,128)(2,1)S(1)}, u32[]{:S(2)}, u32[]{:S(2)}) collective-permute-start(bf16[8,2,128,128]{3,2,1,0:T(8,128)(2,1)} %get-tuple-element.57.refs_0_), channel_id=1, source_target_pairs={{0,12},{1,13},{2,14},{3,15},{4,0},{5,1},{6,2},{7,3},{8,4},{9,5},{1... | collective-permute-start | bytes 1572872 | tf_op jit(solution)/shard_map/ppermute | solution.py:25
  73.2 21.0 %collective-permute-start.25 = (bf16[8,2,128,128]{3,2,1,0:T(8,128)(2,1)}, bf16[8,2,128,128]{3,2,1,0:T(8,128)(2,1)S(1)}, u32[]{:S(2)}, u32[]{:S(2)}) collective-permute-start(bf16[8,2,128,128]{3,2,1,0:T(8,128)(2,1)} %get-tuple-element.57.refs_0_), channel_id=1, source_target_pairs={{0,8},{1,9},{2,10},{3,11},{4,12},{5,13},{6,14},{7,15},{8,0},{9,1},... | collective-permute-start | bytes 1572872 | tf_op jit(solution)/shard_map/ppermute | solution.py:25
  73.2 26.0 %collective-permute-start.24 = (bf16[8,2,128,128]{3,2,1,0:T(8,128)(2,1)}, bf16[8,2,128,128]{3,2,1,0:T(8,128)(2,1)S(1)}, u32[]{:S(2)}, u32[]{:S(2)}) collective-permute-start(bf16[8,2,128,128]{3,2,1,0:T(8,128)(2,1)} %get-tuple-element.57.refs_0_), channel_id=1, source_target_pairs={{0,4},{1,5},{2,6},{3,7},{4,8},{5,9},{6,10},{7,11},{8,12},{9,13},{1... | collective-permute-start | bytes 1572872 | tf_op jit(solution)/shard_map/ppermute | solution.py:25
  74.1 25.0 %collective-permute-start.29 = (bf16[8,2,128,128]{3,2,1,0:T(8,128)(2,1)}, bf16[8,2,128,128]{3,2,1,0:T(8,128)(2,1)S(1)}, u32[]{:S(2)}, u32[]{:S(2)}) collective-permute-start(bf16[8,2,128,128]{3,2,1,0:T(8,128)(2,1)} %get-tuple-element.58.refs_4_), channel_id=1, source_target_pairs={{0,3},{1,0},{2,1},{3,2},{4,7},{5,4},{6,5},{7,6},{8,11},{9,8},{10,9... | collective-permute-start | bytes 1572872 | tf_op jit(solution)/shard_map/ppermute | solution.py:25
  76.1 23.0 %collective-permute-start.28 = (bf16[8,2,128,128]{3,2,1,0:T(8,128)(2,1)}, bf16[8,2,128,128]{3,2,1,0:T(8,128)(2,1)S(1)}, u32[]{:S(2)}, u32[]{:S(2)}) collective-permute-start(bf16[8,2,128,128]{3,2,1,0:T(8,128)(2,1)} %get-tuple-element.58.refs_4_), channel_id=1, source_target_pairs={{0,2},{1,3},{2,0},{3,1},{4,6},{5,7},{6,4},{7,5},{8,10},{9,11},{10,... | collective-permute-start | bytes 1572872 | tf_op jit(solution)/shard_map/ppermute | solution.py:25
  91.7 10.7 %collective-permute-start.27 = (bf16[8,2,128,128]{3,2,1,0:T(8,128)(2,1)}, bf16[8,2,128,128]{3,2,1,0:T(8,128)(2,1)}, u32[]{:S(2)}, u32[]{:S(2)}) collective-permute-start(bf16[8,2,128,128]{3,2,1,0:T(8,128)(2,1)} %get-tuple-element.58.refs_4_), channel_id=1, source_target_pairs={{0,1},{1,2},{2,3},{3,0},{4,5},{5,6},{6,7},{7,4},{8,9},{9,10},{10,1... | collective-permute-start | bytes 1572872 | tf_op jit(solution)/shard_map/ppermute | solution.py:25
  94.1 25.8 %collective-permute-start.8 = (bf16[10,2,128,128]{3,2,1,0:T(8,128)(2,1)}, bf16[10,2,128,128]{3,2,1,0:T(8,128)(2,1)S(1)}, u32[]{:S(2)}, u32[]{:S(2)}) collective-permute-start(bf16[10,2,128,128]{3,2,1,0:T(8,128)(2,1)} %get-tuple-element.51.refs_0_), channel_id=1, source_target_pairs={{0,12},{1,13},{2,14},{3,15},{4,0},{5,1},{6,2},{7,3},{8,4},{9,5},{1... | collective-permute-start | bytes 1966088 | tf_op jit(solution)/shard_map/ppermute | solution.py:25
  109.1 49.5 %all-to-all-start.4 = ((bf16[8,2,2,128,128]{4,3,2,1,0:T(8,128)(2,1)}), bf16[8,2,2,128,128]{4,3,2,1,0:T(8,128)(2,1)}, u32[]{:S(2)}, u32[]{:S(2)}) async-start(bf16[8,2,2,128,128]{4,3,2,1,0:T(8,128)(2,1)} %get-tuple-element.76), calls=%async_computation.4 | async-start | bytes 2097152 | tf_op jit(solution)/shard_map/all_to_all | solution.py:373
  113.4 19.4 %collective-permute-start.7 = (bf16[10,2,128,128]{3,2,1,0:T(8,128)(2,1)}, bf16[10,2,128,128]{3,2,1,0:T(8,128)(2,1)S(1)}, u32[]{:S(2)}, u32[]{:S(2)}) collective-permute-start(bf16[10,2,128,128]{3,2,1,0:T(8,128)(2,1)} %get-tuple-element.51.refs_0_), channel_id=1, source_target_pairs={{0,8},{1,9},{2,10},{3,11},{4,12},{5,13},{6,14},{7,15},{8,0},{9,1},... | collective-permute-start | bytes 1966088 | tf_op jit(solution)/shard_map/ppermute | solution.py:25
  113.5 32.8 %collective-permute-start.6 = (bf16[10,2,128,128]{3,2,1,0:T(8,128)(2,1)}, bf16[10,2,128,128]{3,2,1,0:T(8,128)(2,1)S(1)}, u32[]{:S(2)}, u32[]{:S(2)}) collective-permute-start(bf16[10,2,128,128]{3,2,1,0:T(8,128)(2,1)} %get-tuple-element.51.refs_0_), channel_id=1, source_target_pairs={{0,4},{1,5},{2,6},{3,7},{4,8},{5,9},{6,10},{7,11},{8,12},{9,13},{1... | collective-permute-start | bytes 1966088 | tf_op jit(solution)/shard_map/ppermute | solution.py:25
  117.9 30.4 %collective-permute-start.11 = (bf16[10,2,128,128]{3,2,1,0:T(8,128)(2,1)}, bf16[10,2,128,128]{3,2,1,0:T(8,128)(2,1)S(1)}, u32[]{:S(2)}, u32[]{:S(2)}) collective-permute-start(bf16[10,2,128,128]{3,2,1,0:T(8,128)(2,1)} %get-tuple-element.52.refs_4_), channel_id=1, source_target_pairs={{0,3},{1,0},{2,1},{3,2},{4,7},{5,4},{6,5},{7,6},{8,11},{9,8},{10,9... | collective-permute-start | bytes 1966088 | tf_op jit(solution)/shard_map/ppermute | solution.py:25
  119.9 28.4 %collective-permute-start.10 = (bf16[10,2,128,128]{3,2,1,0:T(8,128)(2,1)}, bf16[10,2,128,128]{3,2,1,0:T(8,128)(2,1)S(1)}, u32[]{:S(2)}, u32[]{:S(2)}) collective-permute-start(bf16[10,2,128,128]{3,2,1,0:T(8,128)(2,1)} %get-tuple-element.52.refs_4_), channel_id=1, source_target_pairs={{0,2},{1,3},{2,0},{3,1},{4,6},{5,7},{6,4},{7,5},{8,10},{9,11},{10,... | collective-permute-start | bytes 1966088 | tf_op jit(solution)/shard_map/ppermute | solution.py:25
  119.9 31.9 %collective-permute-start.9 = (bf16[10,2,128,128]{3,2,1,0:T(8,128)(2,1)}, bf16[10,2,128,128]{3,2,1,0:T(8,128)(2,1)}, u32[]{:S(2)}, u32[]{:S(2)}) collective-permute-start(bf16[10,2,128,128]{3,2,1,0:T(8,128)(2,1)} %get-tuple-element.52.refs_4_), channel_id=1, source_target_pairs={{0,1},{1,2},{2,3},{3,0},{4,5},{5,6},{6,7},{7,4},{8,9},{9,10},{10,1... | collective-permute-start | bytes 1966088 | tf_op jit(solution)/shard_map/ppermute | solution.py:25
  158.6 31.7 %all-to-all-start = ((bf16[8,2,2,256,128]{4,3,2,1,0:T(8,128)(2,1)}), bf16[8,2,2,256,128]{4,3,2,1,0:T(8,128)(2,1)}, u32[]{:S(2)}, u32[]{:S(2)}) async-start(bf16[8,2,2,256,128]{4,3,2,1,0:T(8,128)(2,1)} %shard_map.66), calls=%async_computation | async-start | bytes 4194304 | tf_op jit(solution)/shard_map/all_to_all | solution.py:373
  190.3 44.5 %all-to-all-start.1 = ((bf16[8,2,2,256,128]{4,3,2,1,0:T(8,128)(2,1)}), bf16[8,2,2,256,128]{4,3,2,1,0:T(8,128)(2,1)}, u32[]{:S(2)}, u32[]{:S(2)}) async-start(bf16[8,2,2,256,128]{4,3,2,1,0:T(8,128)(2,1)} %shard_map.68), calls=%async_computation.1 | async-start | bytes 4194304 | tf_op jit(solution)/shard_map/all_to_all | solution.py:373
  198.2 14.9 %collective-permute-start.20 = (bf16[8,2,128,128]{3,2,1,0:T(8,128)(2,1)S(1)}, bf16[8,2,128,128]{3,2,1,0:T(8,128)(2,1)S(1)}, u32[]{:S(2)}, u32[]{:S(2)}) collective-permute-start(bf16[8,2,128,128]{3,2,1,0:T(8,128)(2,1)S(1)} %get-tuple-element.55.refs_0_), channel_id=1, source_target_pairs={{0,12},{1,13},{2,14},{3,15},{4,0},{5,1},{6,2},{7,3},{8,4},{9,5},{1... | collective-permute-start | bytes 1572872 | tf_op jit(solution)/shard_map/ppermute | solution.py:25
  198.3 16.4 %collective-permute-start.19 = (bf16[8,2,128,128]{3,2,1,0:T(8,128)(2,1)S(1)}, bf16[8,2,128,128]{3,2,1,0:T(8,128)(2,1)S(1)}, u32[]{:S(2)}, u32[]{:S(2)}) collective-permute-start(bf16[8,2,128,128]{3,2,1,0:T(8,128)(2,1)S(1)} %get-tuple-element.55.refs_0_), channel_id=1, source_target_pairs={{0,8},{1,9},{2,10},{3,11},{4,12},{5,13},{6,14},{7,15},{8,0},{9,1},... | collective-permute-start | bytes 1572872 | tf_op jit(solution)/shard_map/ppermute | solution.py:25
  200.6 24.5 %collective-permute-start.18 = (bf16[8,2,128,128]{3,2,1,0:T(8,128)(2,1)S(1)}, bf16[8,2,128,128]{3,2,1,0:T(8,128)(2,1)S(1)}, u32[]{:S(2)}, u32[]{:S(2)}) collective-permute-start(bf16[8,2,128,128]{3,2,1,0:T(8,128)(2,1)S(1)} %get-tuple-element.55.refs_0_), channel_id=1, source_target_pairs={{0,4},{1,5},{2,6},{3,7},{4,8},{5,9},{6,10},{7,11},{8,12},{9,13},{1... | collective-permute-start | bytes 1572872 | tf_op jit(solution)/shard_map/ppermute | solution.py:25
  200.6 24.5 %collective-permute-start.23 = (bf16[8,2,128,128]{3,2,1,0:T(8,128)(2,1)S(1)}, bf16[8,2,128,128]{3,2,1,0:T(8,128)(2,1)S(1)}, u32[]{:S(2)}, u32[]{:S(2)}) collective-permute-start(bf16[8,2,128,128]{3,2,1,0:T(8,128)(2,1)S(1)} %get-tuple-element.56.refs_4_), channel_id=1, source_target_pairs={{0,3},{1,0},{2,1},{3,2},{4,7},{5,4},{6,5},{7,6},{8,11},{9,8},{10,9... | collective-permute-start | bytes 1572872 | tf_op jit(solution)/shard_map/ppermute | solution.py:25
  201.8 23.3 %collective-permute-start.22 = (bf16[8,2,128,128]{3,2,1,0:T(8,128)(2,1)S(1)}, bf16[8,2,128,128]{3,2,1,0:T(8,128)(2,1)S(1)}, u32[]{:S(2)}, u32[]{:S(2)}) collective-permute-start(bf16[8,2,128,128]{3,2,1,0:T(8,128)(2,1)S(1)} %get-tuple-element.56.refs_4_), channel_id=1, source_target_pairs={{0,2},{1,3},{2,0},{3,1},{4,6},{5,7},{6,4},{7,5},{8,10},{9,11},{10,... | collective-permute-start | bytes 1572872 | tf_op jit(solution)/shard_map/ppermute | solution.py:25
  213.1 15.0 %collective-permute-start.21 = (bf16[8,2,128,128]{3,2,1,0:T(8,128)(2,1)S(1)}, bf16[8,2,128,128]{3,2,1,0:T(8,128)(2,1)}, u32[]{:S(2)}, u32[]{:S(2)}) collective-permute-start(bf16[8,2,128,128]{3,2,1,0:T(8,128)(2,1)S(1)} %get-tuple-element.56.refs_4_), channel_id=1, source_target_pairs={{0,1},{1,2},{2,3},{3,0},{4,5},{5,6},{6,7},{7,4},{8,9},{9,10},{10,1... | collective-permute-start | bytes 1572872 | tf_op jit(solution)/shard_map/ppermute | solution.py:25
  266.6 22.1 %all-to-all-start.3 = ((bf16[8,2,2,128,128]{4,3,2,1,0:T(8,128)(2,1)}), bf16[8,2,2,128,128]{4,3,2,1,0:T(8,128)(2,1)S(1)}, u32[]{:S(2)}, u32[]{:S(2)}) async-start(bf16[8,2,2,128,128]{4,3,2,1,0:T(8,128)(2,1)} %get-tuple-element.59), calls=%async_computation.3 | async-start | bytes 2097152 | tf_op jit(solution)/shard_map/all_to_all | solution.py:373
  281.3 18.7 %collective-permute-start.42 = (bf16[4,128,256]{2,1,0:T(8,128)(2,1)}, bf16[4,128,256]{2,1,0:T(8,128)(2,1)S(1)}, u32[]{:S(2)}, u32[]{:S(2)}) collective-permute-start(bf16[4,128,256]{2,1,0:T(8,128)(2,1)} %get-tuple-element.78), channel_id=1, source_target_pairs={{0,1},{1,2},{2,3},{3,0},{4,5},{5,6},{6,7},{7,4},{8,9},{9,10},{10,1... | collective-permute-start | bytes 786440 | tf_op jit(solution)/shard_map/ppermute | solution.py:25
  281.4 20.4 %collective-permute-start.43 = (bf16[4,128,256]{2,1,0:T(8,128)(2,1)}, bf16[4,128,256]{2,1,0:T(8,128)(2,1)S(1)}, u32[]{:S(2)}, u32[]{:S(2)}) collective-permute-start(bf16[4,128,256]{2,1,0:T(8,128)(2,1)} %get-tuple-element.79), channel_id=1, source_target_pairs={{0,2},{1,3},{2,0},{3,1},{4,6},{5,7},{6,4},{7,5},{8,10},{9,11},{10,... | collective-permute-start | bytes 786440 | tf_op jit(solution)/shard_map/ppermute | solution.py:25
  283.5 19.5 %collective-permute-start.44 = (bf16[4,128,256]{2,1,0:T(8,128)(2,1)}, bf16[4,128,256]{2,1,0:T(8,128)(2,1)S(1)}, u32[]{:S(2)}, u32[]{:S(2)}) collective-permute-start(bf16[4,128,256]{2,1,0:T(8,128)(2,1)} %get-tuple-element.80), channel_id=1, source_target_pairs={{0,3},{1,0},{2,1},{3,2},{4,7},{5,4},{6,5},{7,6},{8,11},{9,8},{10,9... | collective-permute-start | bytes 786440 | tf_op jit(solution)/shard_map/ppermute | solution.py:25
  284.6 20.2 %collective-permute-start.45 = (bf16[4,128,256]{2,1,0:T(8,128)(2,1)}, bf16[4,128,256]{2,1,0:T(8,128)(2,1)S(1)}, u32[]{:S(2)}, u32[]{:S(2)}) collective-permute-start(bf16[4,128,256]{2,1,0:T(8,128)(2,1)} %get-tuple-element.82), channel_id=1, source_target_pairs={{0,4},{1,5},{2,6},{3,7},{4,8},{5,9},{6,10},{7,11},{8,12},{9,13},{1... | collective-permute-start | bytes 786440 | tf_op jit(solution)/shard_map/ppermute | solution.py:25
  285.5 21.8 %collective-permute-start.46 = (bf16[4,128,256]{2,1,0:T(8,128)(2,1)}, bf16[4,128,256]{2,1,0:T(8,128)(2,1)S(1)}, u32[]{:S(2)}, u32[]{:S(2)}) collective-permute-start(bf16[4,128,256]{2,1,0:T(8,128)(2,1)} %get-tuple-element.83), channel_id=1, source_target_pairs={{0,8},{1,9},{2,10},{3,11},{4,12},{5,13},{6,14},{7,15},{8,0},{9,1},... | collective-permute-start | bytes 786440 | tf_op jit(solution)/shard_map/ppermute | solution.py:25
  301.8 14.2 %collective-permute-start.30 = (bf16[4,128,256]{2,1,0:T(8,128)(2,1)}, bf16[4,128,256]{2,1,0:T(8,128)(2,1)S(1)}, u32[]{:S(2)}, u32[]{:S(2)}) collective-permute-start(bf16[4,128,256]{2,1,0:T(8,128)(2,1)} %get-tuple-element.61), channel_id=1, source_target_pairs={{0,1},{1,2},{2,3},{3,0},{4,5},{5,6},{6,7},{7,4},{8,9},{9,10},{10,1... | collective-permute-start | bytes 786440 | tf_op jit(solution)/shard_map/ppermute | solution.py:25
  303.0 13.7 %collective-permute-start.31 = (bf16[4,128,256]{2,1,0:T(8,128)(2,1)}, bf16[4,128,256]{2,1,0:T(8,128)(2,1)S(1)}, u32[]{:S(2)}, u32[]{:S(2)}) collective-permute-start(bf16[4,128,256]{2,1,0:T(8,128)(2,1)} %get-tuple-element.62), channel_id=1, source_target_pairs={{0,2},{1,3},{2,0},{3,1},{4,6},{5,7},{6,4},{7,5},{8,10},{9,11},{10,... | collective-permute-start | bytes 786440 | tf_op jit(solution)/shard_map/ppermute | solution.py:25
  304.8 13.6 %collective-permute-start.32 = (bf16[4,128,256]{2,1,0:T(8,128)(2,1)}, bf16[4,128,256]{2,1,0:T(8,128)(2,1)S(1)}, u32[]{:S(2)}, u32[]{:S(2)}) collective-permute-start(bf16[4,128,256]{2,1,0:T(8,128)(2,1)} %get-tuple-element.63), channel_id=1, source_target_pairs={{0,3},{1,0},{2,1},{3,2},{4,7},{5,4},{6,5},{7,6},{8,11},{9,8},{10,9... | collective-permute-start | bytes 786440 | tf_op jit(solution)/shard_map/ppermute | solution.py:25
  307.4 14.5 %collective-permute-start.33 = (bf16[4,128,256]{2,1,0:T(8,128)(2,1)}, bf16[4,128,256]{2,1,0:T(8,128)(2,1)S(1)}, u32[]{:S(2)}, u32[]{:S(2)}) collective-permute-start(bf16[4,128,256]{2,1,0:T(8,128)(2,1)} %get-tuple-element.65), channel_id=1, source_target_pairs={{0,4},{1,5},{2,6},{3,7},{4,8},{5,9},{6,10},{7,11},{8,12},{9,13},{1... | collective-permute-start | bytes 786440 | tf_op jit(solution)/shard_map/ppermute | solution.py:25
  307.7 14.2 %collective-permute-start.34 = (bf16[4,128,256]{2,1,0:T(8,128)(2,1)}, bf16[4,128,256]{2,1,0:T(8,128)(2,1)S(1)}, u32[]{:S(2)}, u32[]{:S(2)}) collective-permute-start(bf16[4,128,256]{2,1,0:T(8,128)(2,1)} %get-tuple-element.66), channel_id=1, source_target_pairs={{0,8},{1,9},{2,10},{3,11},{4,12},{5,13},{6,14},{7,15},{8,0},{9,1},... | collective-permute-start | bytes 786440 | tf_op jit(solution)/shard_map/ppermute | solution.py:25
  316.7 9.2 %collective-permute-start.48 = (bf16[128,256]{1,0:T(8,128)(2,1)S(1)}, bf16[128,256]{1,0:T(8,128)(2,1)S(1)}, u32[]{:S(2)}, u32[]{:S(2)}) collective-permute-start(bf16[128,256]{1,0:T(8,128)(2,1)S(1)} %get-tuple-element.86), channel_id=1, source_target_pairs={{0,4},{1,5},{2,6},{3,7},{4,8},{5,9},{6,10},{7,11},{8,12},{9,13},{1... | collective-permute-start | bytes 196616 | tf_op jit(solution)/shard_map/ppermute | solution.py:25
  318.4 8.5 %collective-permute-start.49 = (bf16[128,256]{1,0:T(8,128)(2,1)S(1)}, bf16[128,256]{1,0:T(8,128)(2,1)S(1)}, u32[]{:S(2)}, u32[]{:S(2)}) collective-permute-start(bf16[128,256]{1,0:T(8,128)(2,1)S(1)} %get-tuple-element.87), channel_id=1, source_target_pairs={{0,8},{1,9},{2,10},{3,11},{4,12},{5,13},{6,14},{7,15},{8,0},{9,1},... | collective-permute-start | bytes 196616 | tf_op jit(solution)/shard_map/ppermute | solution.py:25
  321.9 8.8 %collective-permute-start.51 = (bf16[128,256]{1,0:T(8,128)(2,1)S(1)}, bf16[128,256]{1,0:T(8,128)(2,1)S(1)}, u32[]{:S(2)}, u32[]{:S(2)}) collective-permute-start(bf16[128,256]{1,0:T(8,128)(2,1)S(1)} %get-tuple-element.90), channel_id=1, source_target_pairs={{0,1},{1,2},{2,3},{3,0},{4,5},{5,6},{6,7},{7,4},{8,9},{9,10},{10,1... | collective-permute-start | bytes 196616 | tf_op jit(solution)/shard_map/ppermute | solution.py:25
  327.5 8.3 %collective-permute-start.37 = (bf16[128,256]{1,0:T(8,128)(2,1)S(1)}, bf16[128,256]{1,0:T(8,128)(2,1)S(1)}, u32[]{:S(2)}, u32[]{:S(2)}) collective-permute-start(bf16[128,256]{1,0:T(8,128)(2,1)S(1)} %get-tuple-element.70), channel_id=1, source_target_pairs={{0,8},{1,9},{2,10},{3,11},{4,12},{5,13},{6,14},{7,15},{8,0},{9,1},... | collective-permute-start | bytes 196616 | tf_op jit(solution)/shard_map/ppermute | solution.py:25
  (50 other events, 650.5 us)

commit v2 on v1

--- a/solution.py
+++ b/solution.py
@@ -14,6 +14,7 @@
 BF16 = jnp.bfloat16
 F32 = jnp.float32
 CHUNKS = (2, 2, 2, 2)
+MODES = ((False,), (True,), (False,), (True, False))
 
 
 def move(value, step_y, step_z):
@@ -59,10 +60,11 @@
     )(wave, *gots)
 
 
-def left_kernel(first_sector, split, place, pairs, size, *refs):
+def left_kernel(first_sector, modes, place, pairs, size, *refs):
+    split = len(modes)
     pieces, left_hbm = refs[:8], refs[8]
-    outs = refs[9 : 9 + split]
-    whole, left, sems, left_sem = refs[9 + split :]
+    outs = list(refs[9:-5])
+    whole, left, done, sems, left_sem = refs[-5:]
     y, z, bond = place[0], place[1], place[2]
     count = whole.shape[0]
     copies = [pltpu.make_async_copy(left_hbm, left, left_sem)]
@@ -117,28 +119,47 @@
                 axis=0,
             )
             middle = (jnp.dot(lhs, rhs, preferred_element_type=F32) * col_live).astype(BF16)
+            target = row // 2
+            if modes[u % 2 % split]:
+                target = (target // 2 + SIDE - bond // 2) % SIDE * 2 + (target + bond) % 2
+            half, line = (0, u % 2 * TILE) if split == 1 else (u % 2, 0)
             for s in range(count):
-                value = middle[:, s * TILE : (s + 1) * TILE]
-                if split == 1:
-                    outs[0][row // 2, s, term, u % 2 * TILE : (u % 2 + 1) * TILE, :] = value
-                else:
-                    outs[u % 2][row // 2, s, term] = value
-
-
-def left_stage(pieces, split, count, left_blocks, place, pairs, size, first_sector):
+                done[half, target, s, term, line : line + TILE, :] = middle[
+                    :, s * TILE : (s + 1) * TILE
+                ]
+
+    sent = []
+    for half, turned in enumerate(modes):
+        for block in range(8):
+            out = outs.pop(0) if turned else outs[0].at[block]
+            sent.append(pltpu.make_async_copy(done.at[half, block], out, sems.at[len(sent)]))
+        if not turned:
+            outs.pop(0)
+    for copy in sent:
+        copy.start()
+    for copy in sent:
+        copy.wait()
+
+
+def left_stage(pieces, modes, count, left_blocks, place, pairs, size, first_sector):
     terms = left_blocks.shape[0]
-    shape = (8, count, terms, 2 * TILE // split, TILE)
-    return pl.pallas_call(
-        functools.partial(left_kernel, first_sector, split),
-        out_shape=[jax.ShapeDtypeStruct(shape, BF16)] * split,
+    block = (count, terms, 2 * TILE // len(modes), TILE)
+    shapes = []
+    for turned in modes:
+        shapes += [block] * 8 if turned else [(8, *block)]
+    anywhere = pl.BlockSpec(memory_space=pl.ANY)
+    results = pl.pallas_call(
+        functools.partial(left_kernel, first_sector, modes),
+        out_shape=[jax.ShapeDtypeStruct(shape, BF16) for shape in shapes],
         grid_spec=pltpu.PrefetchScalarGridSpec(
             num_scalar_prefetch=3,
             grid=(1,),
-            in_specs=[pl.BlockSpec(memory_space=pl.ANY)] * (len(pieces) + 1),
-            out_specs=[pl.BlockSpec(shape, lambda i, *_: (0, 0, 0, 0, 0))] * split,
+            in_specs=[anywhere] * (len(pieces) + 1),
+            out_specs=[anywhere] * len(shapes),
             scratch_shapes=[
                 pltpu.VMEM((count, 64, TILE, TILE), BF16),
                 pltpu.VMEM(left_blocks.shape, BF16),
+                pltpu.VMEM((len(modes), 8, *block), BF16),
                 pltpu.SemaphoreType.DMA((32,)),
                 pltpu.SemaphoreType.DMA(()),
             ],
@@ -150,26 +171,49 @@
             transcendentals=0,
         ),
     )(place, pairs, size, *pieces, left_blocks)
-
-
-def right_kernel(counts, half, place, pairs, size, *refs):
-    arrived = refs[: len(counts)]
-    right_hbm = refs[len(counts)]
-    outs_a = refs[len(counts) + 1 : len(counts) + 5]
-    outs_b = refs[len(counts) + 5 : len(counts) + 9]
-    middle, right, sum_a, sum_b, sems, right_sems, out_sems = refs[len(counts) + 9 :]
+    results = list(results)
+    grouped = []
+    for turned in modes:
+        grouped.append([results.pop(0) for _ in range(8 if turned else 1)])
+    return grouped
+
+
+def exchange(blocks):
+    if len(blocks) == 1:
+        return [lax.all_to_all(blocks[0], "bond", split_axis=0, concat_axis=0, tiled=True)]
+    got = [blocks[0]]
+    for turned in range(1, 8):
+        step_x, step_core = turned // 2, turned % 2
+        pairs = [
+            (x * 2 + core, (x + step_x) % SIDE * 2 + (core + step_core) % 2)
+            for x in range(SIDE)
+            for core in range(2)
+        ]
+        got.append(lax.ppermute(blocks[turned], "bond", pairs))
+    return got
+
+
+def right_kernel(layout, half, place, pairs, size, *refs):
+    total = sum(8 if turned else 1 for _, turned in layout)
+    arrived, right = list(refs[:total]), refs[total]
+    outs_a, outs_b = refs[total + 1 : total + 5], refs[total + 5 : total + 9]
+    middle, blocks, sum_a, sum_b, sems, right_sems, out_sems = refs[total + 9 :]
     bond = place[2]
     rows, terms = middle.shape[2], middle.shape[1]
     copies = []
     first = 0
-    for chunk, count in zip(arrived, counts):
-        for source in range(8):
-            block = chunk.at[source]
-            if chunk.shape[3] != rows:
-                block = block.at[:, :, half * rows : (half + 1) * rows]
+    for count, turned in layout:
+        whole = None if turned else arrived.pop(0)
+        for block in range(8):
+            source = block
+            piece = arrived.pop(0) if turned else whole.at[block]
+            if turned:
+                source = (bond // 2 + SIDE - block // 2) % SIDE * 2 + (bond + block) % 2
+            if piece.shape[2] != rows:
+                piece = piece.at[:, :, half * rows : (half + 1) * rows]
             copies.append(
                 pltpu.make_async_copy(
-                    block, middle.at[pl.ds(source * 8 + first, count)], sems.at[len(copies)]
+                    piece, middle.at[pl.ds(source * 8 + first, count)], sems.at[len(copies)]
                 )
             )
         first += count
@@ -181,19 +225,21 @@
 
     def right_copy(step_z, step_y):
         return pltpu.make_async_copy(
-            right_hbm.at[:, pl.ds(owner_of(step_z, step_y) * 4, 4)],
-            right.at[step_z * SIDE + step_y],
+            right.at[:, pl.ds(owner_of(step_z, step_y) * 4, 4)],
+            blocks.at[step_z * SIDE + step_y],
             right_sems.at[step_z * SIDE + step_y],
         )
 
-    for step_z in range(SIDE):
-        for step_y in range(SIDE):
-            right_copy(step_z, step_y).start()
+    for step_y in range(SIDE):
+        right_copy(0, step_y).start()
     line = lax.broadcasted_iota(jnp.int32, (TILE, TILE), 0)
     lane = lax.broadcasted_iota(jnp.int32, (TILE, TILE), 1)
     row_live = line < size[bond * 2 + half]
     for copy in copies:
         copy.wait()
+    for step_z in range(1, SIDE):
+        for step_y in range(SIDE):
+            right_copy(step_z, step_y).start()
     sent = []
     for step_z in range(SIDE):
 
@@ -203,7 +249,7 @@
                 right_copy(step_z, step_y).wait()
             for step_y in (pair, pair + 1):
                 owner = owner_of(step_z, step_y)
-                blocks = right.at[step_z * SIDE + step_y]
+                block = blocks.at[step_z * SIDE + step_y]
                 for q in range(4):
                     col = owner * 4 + q
                     lhs = jnp.concatenate(
@@ -215,7 +261,7 @@
                         axis=1,
                     )
                     rhs = jnp.concatenate(
-                        [blocks[term, q, p] for term in range(terms) for p in range(2)], axis=0
+                        [block[term, q, p] for term in range(terms) for p in range(2)], axis=0
                     )
                     product = jnp.dot(lhs, rhs, preferred_element_type=F32)
                     keep = row_live & (lane < size[col])
@@ -241,29 +287,30 @@
 
 
 def right_stage(arrived, half, right_blocks, place, pairs, size):
-    counts = tuple(a.shape[1] for a in arrived)
-    terms, rows = arrived[0].shape[2], TILE
+    layout = tuple((count, len(blocks) > 1) for count, blocks in zip(CHUNKS, arrived))
+    arrived = [block for blocks in arrived for block in blocks]
+    terms, rows = right_blocks.shape[0], TILE
     shape = jax.ShapeDtypeStruct((SIDE, rows, 2 * TILE), BF16)
     anywhere = pl.BlockSpec(memory_space=pl.ANY)
     return pl.pallas_call(
-        functools.partial(right_kernel, counts, half),
+        functools.partial(right_kernel, layout, half),
         out_shape=[shape] * 8,
         grid_spec=pltpu.PrefetchScalarGridSpec(
             num_scalar_prefetch=3,
             grid=(1,),
-            in_specs=[anywhere] * (len(counts) + 1),
+            in_specs=[anywhere] * (len(arrived) + 1),
             out_specs=[anywhere] * 8,
             scratch_shapes=[
                 pltpu.VMEM((64, terms, rows, TILE), BF16),
                 pltpu.VMEM((GROUP, terms, 4, 2, TILE, TILE), BF16),
                 pltpu.VMEM((SIDE, SIDE, rows, 2 * TILE), BF16),
                 pltpu.VMEM((SIDE, SIDE, rows, 2 * TILE), BF16),
-                pltpu.SemaphoreType.DMA((8 * len(counts),)),
+                pltpu.SemaphoreType.DMA((8 * len(layout),)),
                 pltpu.SemaphoreType.DMA((GROUP,)),
                 pltpu.SemaphoreType.DMA((SIDE * (SIDE + 1),)),
             ],
         ),
-        compiler_params=pltpu.CompilerParams(vmem_limit_bytes=60 << 20),
+        compiler_params=pltpu.CompilerParams(vmem_limit_bytes=58 << 20),
         cost_estimate=pl.CostEstimate(
             flops=2 * terms * rows * 256 * 8192,
             bytes_accessed=(14 << 20),
@@ -365,12 +412,11 @@
         pieces = got[0] + got[1]
         if after < chunk_count:
             near[after] = ([got[1][1:], got[0][1:]], 4 * count)
-        split = 2 if chunk == chunk_count - 1 else 1
         middles = left_stage(
-            pieces, split, count, left_blocks, place, lefts, sector_size, starts[chunk]
+            pieces, MODES[chunk], count, left_blocks, place, lefts, sector_size, starts[chunk]
         )
         for middle in middles:
-            arrived.append(lax.all_to_all(middle, "bond", split_axis=0, concat_axis=0, tiled=True))
+            arrived.append(exchange(middle))
     finals = []
     for half in range(2):
         mine = arrived[: chunk_count - 1] + [arrived[chunk_count - 1 + half]]

time: 340 us -> 339 us (level)
  blocking collectives: 31.8 us -> 0 us
  waiting for transfers between devices: 151 us -> 171 us
  starting transfers between devices: 92.8 us -> 107 us
    ppermute x0 -> x14, waiting for transfers between devices: none -> 32.8 us  [exchange(): got.append(lax.ppermute(blocks[turned], 'bond', pairs))]
    all_to_all x1 -> x0, blocking collectives: 31.8 us -> none  [apply_slab(): lax.all_to_all(middle, 'bond', split_axis=0, concat_axis=0, tiled=True)]
    all_to_all x4 -> x3, waiting for transfers between devices: 20.4 us -> 0.01 us  [exchange(): lax.all_to_all(blocks[0], 'bond', split_axis=0, concat_axis=0, tiled=True)]
    ppermute x0 -> x14, starting transfers between devices: none -> 16.7 us  [exchange(): got.append(lax.ppermute(blocks[turned], 'bond', pairs))]
    ppermute x54, waiting for transfers between devices: 130 us -> 138 us  [move(): return lax.ppermute(value, 'op', pairs)]
    all_to_all x4 -> x3, starting transfers between devices: 17 us -> 13.6 us  [exchange(): lax.all_to_all(blocks[0], 'bond', split_axis=0, concat_axis=0, tiled=True)]
  transfers between devices with their start and end apart: 58 -> 71, of which waited for: 25 -> 30; matrix products, arithmetic and copies ran while one was open for 1% -> 1% of each run, Pallas kernels for 15% -> 13%
where the time goes in v2:
time: 339 us; the launch traced here: 338 us
  waiting for transfers between devices  171 us (50%)
  starting transfers between devices  107 us (32%)
  Pallas kernels  53 us (16%)
  local copies, waits for them, and re-layouts  5.92 us (2%)
    ppermute x54, waiting for transfers between devices, move(): return lax.ppermute(value, 'op', pairs)  138 us
    ppermute x54, starting transfers between devices, move(): return lax.ppermute(value, 'op', pairs)  76.7 us
    ppermute x14, waiting for transfers between devices, exchange(): got.append(lax.ppermute(blocks[turned], 'bond', pairs))  32.8 us
    pallas_call x4, Pallas kernels, left_stage(): pl.pallas_call(functools.partial(left_kernel, first_sector, modes), out_s...  26.9 us
    pallas_call x2, Pallas kernels, right_stage(): pl.pallas_call(functools.partial(right_kernel, layout, half), out_shape=[...  17.4 us
    ppermute x14, starting transfers between devices, exchange(): got.append(lax.ppermute(blocks[turned], 'bond', pairs))  16.7 us
    all_to_all x3, starting transfers between devices, exchange(): lax.all_to_all(blocks[0], 'bond', split_axis=0, concat_axis=0, tiled=True)  13.6 us
    pallas_call x5, Pallas kernels, pack_stage(): pl.pallas_call(functools.partial(pack_kernel, plans), out_shape=[jax.Shap...  7.37 us
  transfers between devices with their start and end apart: 71, of which 30 were waited for; matrix products, arithmetic and copies ran while one was open for 1% of the time, Pallas kernels for 13%

profile of v2, /device:TPU:0, one launch (start us, length us, event | category | flops | bytes accessed | tf_op | source)
XLA Modules:
  0.0 338.4 jit_solution(11612649700465650231)
XLA Ops:
  1.5 4.2 %collective-permute-start.2 = (bf16[4,2,128,128]{3,2,1,0:T(8,128)(2,1)S(1)}, bf16[4,2,128,128]{3,2,1,0:T(8,128)(2,1)S(1)}, u32[]{:S(2)}, u32[]{:S(2)}) collective-permute-start(bf16[4,2,128,128]{3,2,1,0:T(8,128)(2,1)S(1)} %get-tuple-element.64), channel_id=1, source_target_pairs={{0,3},{1,0},{2,1},{3,2},{4,7},{5,4},{6,5},{7,6},{8,11},{9,8},{10,9... | collective-permute-start | bytes 786440 | tf_op jit(solution)/shard_map/ppermute | solution.py:26
  6.9 3.0 collective-permute-start.5
  10.6 6.3 %collective-permute-done.2.refs_2_ = bf16[4,2,128,128]{3,2,1,0:T(8,128)(2,1)S(1)} collective-permute-done((bf16[4,2,128,128]{3,2,1,0:T(8,128)(2,1)S(1)}, bf16[4,2,128,128]{3,2,1,0:T(8,128)(2,1)S(1)}, u32[]{:S(2)}, u32[]{:S(2)}) %collective-permute-start.2) | collective-permute-done | bytes 262176 | tf_op jit(solution)/shard_map/ppermute | solution.py:26
  20.3 4.9 %collective-permute-done.3.refs_3_ = bf16[4,2,128,128]{3,2,1,0:T(8,128)(2,1)S(1)} collective-permute-done((bf16[4,2,128,128]{3,2,1,0:T(8,128)(2,1)S(1)}, bf16[4,2,128,128]{3,2,1,0:T(8,128)(2,1)S(1)}, u32[]{:S(2)}, u32[]{:S(2)}) %collective-permute-start.3) | collective-permute-done | bytes 262176 | tf_op jit(solution)/shard_map/ppermute | solution.py:26
  25.2 2.4 shard_map.65
  31.0 3.8 %collective-permute-start.11 = (bf16[10,2,128,128]{3,2,1,0:T(8,128)(2,1)}, bf16[10,2,128,128]{3,2,1,0:T(8,128)(2,1)S(1)}, u32[]{:S(2)}, u32[]{:S(2)}) collective-permute-start(bf16[10,2,128,128]{3,2,1,0:T(8,128)(2,1)} %get-tuple-element.67.refs_4_), channel_id=1, source_target_pairs={{0,3},{1,0},{2,1},{3,2},{4,7},{5,4},{6,5},{7,6},{8,11},{9,8},{10,9... | collective-permute-start | bytes 1966088 | tf_op jit(solution)/shard_map/ppermute | solution.py:26
  34.9 10.6 %collective-permute-done.8.refs_3_.refs_5_ = bf16[10,2,128,128]{3,2,1,0:T(8,128)(2,1)S(1)} collective-permute-done((bf16[10,2,128,128]{3,2,1,0:T(8,128)(2,1)}, bf16[10,2,128,128]{3,2,1,0:T(8,128)(2,1)S(1)}, u32[]{:S(2)}, u32[]{:S(2)}) %collective-permute-start.8) | collective-permute-done | bytes 655392 | tf_op jit(solution)/shard_map/ppermute | solution.py:26
  48.7 10.8 %collective-permute-done.6.refs_1_.refs_3_ = bf16[10,2,128,128]{3,2,1,0:T(8,128)(2,1)S(1)} collective-permute-done((bf16[10,2,128,128]{3,2,1,0:T(8,128)(2,1)}, bf16[10,2,128,128]{3,2,1,0:T(8,128)(2,1)S(1)}, u32[]{:S(2)}, u32[]{:S(2)}) %collective-permute-start.6) | collective-permute-done | bytes 655392 | tf_op jit(solution)/shard_map/ppermute | solution.py:26
  60.7 3.7 %collective-permute-done.9.refs_5_.refs_0_ = bf16[10,2,128,128]{3,2,1,0:T(8,128)(2,1)} collective-permute-done((bf16[10,2,128,128]{3,2,1,0:T(8,128)(2,1)}, bf16[10,2,128,128]{3,2,1,0:T(8,128)(2,1)}, u32[]{:S(2)}, u32[]{:S(2)}) %collective-permute-start.9) | collective-permute-done | bytes 655392 | tf_op jit(solution)/shard_map/ppermute | solution.py:26
  64.4 6.7 %shard_map.66 = bf16[8,2,2,256,128]{4,3,2,1,0:T(8,128)(2,1)} custom-call(s32[3]{0:T(128)} %pad_add_fusion.place, s32[64]{0:T(128)} %reshape.10.pairs, s32[64]{0:T(128)} %size.11, bf16[10,2,128,128]{3,2,1,0:T(8,128)(2,1)} %get-tuple-element.66.refs_0_, bf16[10,2,128,128]{3,2,1,0:T(8,128)(2,1)} %copy-done.6, bf16[10,2,128,128]{3,2,1,0:T(8,128)(2,1)} %copy-done.4, ...), custom_call_target="tpu_custom_call" | custom-call | flops 536870912 | bytes 8388608 | tf_op jit(solution)/shard_map/pallas_call | solution.py:151
  71.2 4.6 %all-to-all-start = ((bf16[8,2,2,256,128]{4,3,2,1,0:T(8,128)(2,1)}), bf16[8,2,2,256,128]{4,3,2,1,0:T(8,128)(2,1)}, u32[]{:S(2)}, u32[]{:S(2)}) async-start(bf16[8,2,2,256,128]{4,3,2,1,0:T(8,128)(2,1)} %shard_map.66), calls=%async_computation | async-start | bytes 4194304 | tf_op jit(solution)/shard_map/all_to_all | solution.py:183
  78.2 8.1 %collective-permute-start.27 = (bf16[8,2,128,128]{3,2,1,0:T(8,128)(2,1)S(1)}, bf16[8,2,128,128]{3,2,1,0:T(8,128)(2,1)S(1)}, u32[]{:S(2)}, u32[]{:S(2)}) collective-permute-start(bf16[8,2,128,128]{3,2,1,0:T(8,128)(2,1)S(1)} %get-tuple-element.78.refs_0_), channel_id=1, source_target_pairs={{0,12},{1,13},{2,14},{3,15},{4,0},{5,1},{6,2},{7,3},{8,4},{9,5},{1... | collective-permute-start | bytes 1572872 | tf_op jit(solution)/shard_map/ppermute | solution.py:26
  86.3 2.3 shard_map.67
  88.7 1.9 collective-permute-start.25
  90.7 2.0 collective-permute-start.30
  92.7 17.1 %collective-permute-done.27.refs_3_ = bf16[8,2,128,128]{3,2,1,0:T(8,128)(2,1)S(1)} collective-permute-done((bf16[8,2,128,128]{3,2,1,0:T(8,128)(2,1)S(1)}, bf16[8,2,128,128]{3,2,1,0:T(8,128)(2,1)S(1)}, u32[]{:S(2)}, u32[]{:S(2)}) %collective-permute-start.27) | collective-permute-done | bytes 524320 | tf_op jit(solution)/shard_map/ppermute | solution.py:26
  113.0 13.2 %collective-permute-done.29.refs_6_ = bf16[8,2,128,128]{3,2,1,0:T(8,128)(2,1)S(1)} collective-permute-done((bf16[8,2,128,128]{3,2,1,0:T(8,128)(2,1)S(1)}, bf16[8,2,128,128]{3,2,1,0:T(8,128)(2,1)S(1)}, u32[]{:S(2)}, u32[]{:S(2)}) %collective-permute-start.29) | collective-permute-done | bytes 524320 | tf_op jit(solution)/shard_map/ppermute | solution.py:26
  127.0 8.5 %collective-permute-done.28.refs_5_ = bf16[8,2,128,128]{3,2,1,0:T(8,128)(2,1)} collective-permute-done((bf16[8,2,128,128]{3,2,1,0:T(8,128)(2,1)S(1)}, bf16[8,2,128,128]{3,2,1,0:T(8,128)(2,1)}, u32[]{:S(2)}, u32[]{:S(2)}) %collective-permute-start.28) | collective-permute-done | bytes 524320 | tf_op jit(solution)/shard_map/ppermute | solution.py:26
  135.5 6.7 %shard_map.70 = bf16[8,2,2,256,128]{4,3,2,1,0:T(8,128)(2,1)} custom-call(s32[3]{0:T(128)} %pad_add_fusion.place, s32[64]{0:T(128)} %reshape.10.pairs, s32[64]{0:T(128)} %size.11, bf16[8,2,128,128]{3,2,1,0:T(8,128)(2,1)} %copy-done.25, bf16[8,2,128,128]{3,2,1,0:T(8,128)(2,1)} %copy-done.43, bf16[8,2,128,128]{3,2,1,0:T(8,128)(2,1)} %copy-done.42, ...), custom_call_target="tpu_custom_call" | custom-call | flops 536870912 | bytes 8388608 | tf_op jit(solution)/shard_map/pallas_call | solution.py:151
  142.3 4.4 %all-to-all-start.1 = ((bf16[8,2,2,256,128]{4,3,2,1,0:T(8,128)(2,1)}), bf16[8,2,2,256,128]{4,3,2,1,0:T(8,128)(2,1)}, u32[]{:S(2)}, u32[]{:S(2)}) async-start(bf16[8,2,2,256,128]{4,3,2,1,0:T(8,128)(2,1)} %shard_map.70), calls=%async_computation.1 | async-start | bytes 4194304 | tf_op jit(solution)/shard_map/all_to_all | solution.py:183
  146.7 4.5 %collective-permute-start.12 = (bf16[10,2,128,128]{3,2,1,0:T(8,128)(2,1)}, bf16[10,2,128,128]{3,2,1,0:T(8,128)(2,1)S(1)}, u32[]{:S(2)}, u32[]{:S(2)}) collective-permute-start(bf16[10,2,128,128]{3,2,1,0:T(8,128)(2,1)} %get-tuple-element.68.refs_0_), channel_id=1, source_target_pairs={{0,4},{1,5},{2,6},{3,7},{4,8},{5,9},{6,10},{7,11},{8,12},{9,13},{1... | collective-permute-start | bytes 1966088 | tf_op jit(solution)/shard_map/ppermute | solution.py:26
  153.8 12.3 %collective-permute-done.13.refs_2_.refs_4_ = bf16[10,2,128,128]{3,2,1,0:T(8,128)(2,1)S(1)} collective-permute-done((bf16[10,2,128,128]{3,2,1,0:T(8,128)(2,1)}, bf16[10,2,128,128]{3,2,1,0:T(8,128)(2,1)S(1)}, u32[]{:S(2)}, u32[]{:S(2)}) %collective-permute-start.13) | collective-permute-done | bytes 655392 | tf_op jit(solution)/shard_map/ppermute | solution.py:26
  166.1 13.3 %collective-permute-done.12.refs_1_.refs_3_ = bf16[10,2,128,128]{3,2,1,0:T(8,128)(2,1)S(1)} collective-permute-done((bf16[10,2,128,128]{3,2,1,0:T(8,128)(2,1)}, bf16[10,2,128,128]{3,2,1,0:T(8,128)(2,1)S(1)}, u32[]{:S(2)}, u32[]{:S(2)}) %collective-permute-start.12) | collective-permute-done | bytes 655392 | tf_op jit(solution)/shard_map/ppermute | solution.py:26
  179.4 4.1 %collective-permute-done.15.refs_5_.refs_0_ = bf16[10,2,128,128]{3,2,1,0:T(8,128)(2,1)S(1)} collective-permute-done((bf16[10,2,128,128]{3,2,1,0:T(8,128)(2,1)S(1)}, bf16[10,2,128,128]{3,2,1,0:T(8,128)(2,1)S(1)}, u32[]{:S(2)}, u32[]{:S(2)}) %collective-permute-start.15) | collective-permute-done | bytes 655392 | tf_op jit(solution)/shard_map/ppermute | solution.py:26
  185.0 2.3 collective-permute-start.32
  188.9 10.8 %collective-permute-done.33.refs_3_ = bf16[8,2,128,128]{3,2,1,0:T(8,128)(2,1)S(1)} collective-permute-done((bf16[8,2,128,128]{3,2,1,0:T(8,128)(2,1)S(1)}, bf16[8,2,128,128]{3,2,1,0:T(8,128)(2,1)S(1)}, u32[]{:S(2)}, u32[]{:S(2)}) %collective-permute-start.33) | collective-permute-done | bytes 524320 | tf_op jit(solution)/shard_map/ppermute | solution.py:26
  199.7 6.7 %shard_map.68 = (bf16[2,2,256,128]{3,2,1,0:T(8,128)(2,1)}, bf16[2,2,256,128]{3,2,1,0:T(8,128)(2,1)}, bf16[2,2,256,128]{3,2,1,0:T(8,128)(2,1)}, bf16[2,2,256,128]...) custom-call(s32[3]{0:T(128)} %pad_add_fusion.place, ...), custom_call_target="tpu_custom_call" | custom-call | flops 536870912 | bytes 8388608 | tf_op jit(solution)/shard_map/pallas_call | solution.py:151
  206.6 5.2 %collective-permute-done.31.refs_1_ = bf16[8,2,128,128]{3,2,1,0:T(8,128)(2,1)S(1)} collective-permute-done((bf16[8,2,128,128]{3,2,1,0:T(8,128)(2,1)S(1)}, bf16[8,2,128,128]{3,2,1,0:T(8,128)(2,1)S(1)}, u32[]{:S(2)}, u32[]{:S(2)}) %collective-permute-start.31) | collective-permute-done | bytes 524320 | tf_op jit(solution)/shard_map/ppermute | solution.py:26
  214.4 6.7 %shard_map.72 = (bf16[2,2,128,128]{3,2,1,0:T(8,128)(2,1)}, bf16[2,2,128,128]{3,2,1,0:T(8,128)(2,1)}, bf16[2,2,128,128]{3,2,1,0:T(8,128)(2,1)}, bf16[2,2,128,128]...) custom-call(s32[3]{0:T(128)} %pad_add_fusion.place, ...), custom_call_target="tpu_custom_call" | custom-call | flops 536870912 | bytes 8388608 | tf_op jit(solution)/shard_map/pallas_call | solution.py:151
  221.2 4.6 %all-to-all-start.2 = ((bf16[8,2,2,128,128]{4,3,2,1,0:T(8,128)(2,1)}), bf16[8,2,2,128,128]{4,3,2,1,0:T(8,128)(2,1)S(1)}, u32[]{:S(2)}, u32[]{:S(2)}) async-start(bf16[8,2,2,128,128]{4,3,2,1,0:T(8,128)(2,1)} %get-tuple-element.106), calls=%async_computation.2 | async-start | bytes 2097152 | tf_op jit(solution)/shard_map/all_to_all | solution.py:183
  227.5 2.7 collective-permute-start.21
  233.7 12.9 %collective-permute-done.20.refs_4_ = bf16[2,2,256,128]{3,2,1,0:T(8,128)(2,1)S(1)} collective-permute-done((bf16[2,2,256,128]{3,2,1,0:T(8,128)(2,1)}, bf16[2,2,256,128]{3,2,1,0:T(8,128)(2,1)S(1)}, u32[]{:S(2)}, u32[]{:S(2)}) %collective-permute-start.20) | collective-permute-done | bytes 262176 | tf_op jit(solution)/shard_map/ppermute | solution.py:192
  247.1 6.5 %collective-permute-done.21.refs_5_ = bf16[2,2,256,128]{3,2,1,0:T(8,128)(2,1)S(1)} collective-permute-done((bf16[2,2,256,128]{3,2,1,0:T(8,128)(2,1)S(1)}, bf16[2,2,256,128]{3,2,1,0:T(8,128)(2,1)S(1)}, u32[]{:S(2)}, u32[]{:S(2)}) %collective-permute-start.21) | collective-permute-done | bytes 262176 | tf_op jit(solution)/shard_map/ppermute | solution.py:192
  253.6 4.6 %collective-permute-done.22.refs_6_ = bf16[2,2,256,128]{3,2,1,0:T(8,128)(2,1)S(1)} collective-permute-done((bf16[2,2,256,128]{3,2,1,0:T(8,128)(2,1)}, bf16[2,2,256,128]{3,2,1,0:T(8,128)(2,1)S(1)}, u32[]{:S(2)}, u32[]{:S(2)}) %collective-permute-start.22) | collective-permute-done | bytes 262176 | tf_op jit(solution)/shard_map/ppermute | solution.py:192
  258.2 2.2 collective-permute-start.40
  262.2 3.2 collective-permute-start.41
  267.4 2.0 collective-permute-done.41.refs_15_
  269.4 2.7 collective-permute-done.42.refs_16_
  272.1 2.3 collective-permute-done.43.refs_17_
  274.6 8.7 %shard_map.73 = (bf16[4,128,256]{2,1,0:T(8,128)(2,1)}, bf16[4,128,256]{2,1,0:T(8,128)(2,1)}, bf16[4,128,256]{2,1,0:T(8,128)(2,1)}, bf16[4,128,256]{2,1,0:T(8,128...) custom-call(s32[3]{0:T(128)} %pad_add_fusion.place, ...), custom_call_target="tpu_custom_call" | custom-call | flops 1073741824 | bytes 14680064 | tf_op jit(solution)/shard_map/pallas_call | solution.py:295
  287.6 3.1 collective-permute-start.48
  291.7 8.7 %shard_map.74 = (bf16[4,128,256]{2,1,0:T(8,128)(2,1)}, bf16[4,128,256]{2,1,0:T(8,128)(2,1)}, bf16[4,128,256]{2,1,0:T(8,128)(2,1)}, bf16[4,128,256]{2,1,0:T(8,128...) custom-call(s32[3]{0:T(128)} %pad_add_fusion.place, ...), custom_call_target="tpu_custom_call" | custom-call | flops 1073741824 | bytes 14680064 | tf_op jit(solution)/shard_map/pallas_call | solution.py:295
  304.7 2.5 collective-permute-start.58
  308.8 7.0 %collective-permute-done.56.refs_1_ = bf16[4,128,256]{2,1,0:T(8,128)(2,1)S(1)} collective-permute-done((bf16[4,128,256]{2,1,0:T(8,128)(2,1)}, bf16[4,128,256]{2,1,0:T(8,128)(2,1)S(1)}, u32[]{:S(2)}, u32[]{:S(2)}) %collective-permute-start.56) | collective-permute-done | bytes 262176 | tf_op jit(solution)/shard_map/ppermute | solution.py:26
  319.0 2.5 collective-permute-done.59.refs_5_
  322.4 2.5 collective-permute-start.54
  327.5 2.5 collective-permute-start.63
  333.0 2.4 collective-permute-start.67
  (229 shorter events, 62.7 us)
Async XLA Ops:
  1.5 15.4 %collective-permute-start.2 = (bf16[4,2,128,128]{3,2,1,0:T(8,128)(2,1)S(1)}, bf16[4,2,128,128]{3,2,1,0:T(8,128)(2,1)S(1)}, u32[]{:S(2)}, u32[]{:S(2)}) collective-permute-start(bf16[4,2,128,128]{3,2,1,0:T(8,128)(2,1)S(1)} %get-tuple-element.64), channel_id=1, source_target_pairs={{0,3},{1,0},{2,1},{3,2},{4,7},{5,4},{6,5},{7,6},{8,11},{9,8},{10,9... | collective-permute-start | bytes 786440 | tf_op jit(solution)/shard_map/ppermute | solution.py:26
  5.7 14.6 %collective-permute-start = (bf16[4,2,128,128]{3,2,1,0:T(8,128)(2,1)S(1)}, bf16[4,2,128,128]{3,2,1,0:T(8,128)(2,1)S(1)}, u32[]{:S(2)}, u32[]{:S(2)}) collective-permute-start(bf16[4,2,128,128]{3,2,1,0:T(8,128)(2,1)S(1)} %get-tuple-element.64), channel_id=1, source_target_pairs={{0,1},{1,2},{2,3},{3,0},{4,5},{5,6},{6,7},{7,4},{8,9},{9,10},{10,1... | collective-permute-start | bytes 786440 | tf_op jit(solution)/shard_map/ppermute | solution.py:26
  6.9 13.4 %collective-permute-start.5 = (bf16[4,2,128,128]{3,2,1,0:T(8,128)(2,1)S(1)}, bf16[4,2,128,128]{3,2,1,0:T(8,128)(2,1)S(1)}, u32[]{:S(2)}, u32[]{:S(2)}) collective-permute-start(bf16[4,2,128,128]{3,2,1,0:T(8,128)(2,1)S(1)} %get-tuple-element.65), channel_id=1, source_target_pairs={{0,12},{1,13},{2,14},{3,15},{4,0},{5,1},{6,2},{7,3},{8,4},{9,5},{1... | collective-permute-start | bytes 786440 | tf_op jit(solution)/shard_map/ppermute | solution.py:26
  27.6 17.9 %collective-permute-start.8 = (bf16[10,2,128,128]{3,2,1,0:T(8,128)(2,1)}, bf16[10,2,128,128]{3,2,1,0:T(8,128)(2,1)S(1)}, u32[]{:S(2)}, u32[]{:S(2)}) collective-permute-start(bf16[10,2,128,128]{3,2,1,0:T(8,128)(2,1)} %get-tuple-element.66.refs_0_), channel_id=1, source_target_pairs={{0,12},{1,13},{2,14},{3,15},{4,0},{5,1},{6,2},{7,3},{8,4},{9,5},{1... | collective-permute-start | bytes 1966088 | tf_op jit(solution)/shard_map/ppermute | solution.py:26
  29.4 19.3 %collective-permute-start.7 = (bf16[10,2,128,128]{3,2,1,0:T(8,128)(2,1)}, bf16[10,2,128,128]{3,2,1,0:T(8,128)(2,1)S(1)}, u32[]{:S(2)}, u32[]{:S(2)}) collective-permute-start(bf16[10,2,128,128]{3,2,1,0:T(8,128)(2,1)} %get-tuple-element.66.refs_0_), channel_id=1, source_target_pairs={{0,8},{1,9},{2,10},{3,11},{4,12},{5,13},{6,14},{7,15},{8,0},{9,1},... | collective-permute-start | bytes 1966088 | tf_op jit(solution)/shard_map/ppermute | solution.py:26
  30.1 29.5 %collective-permute-start.6 = (bf16[10,2,128,128]{3,2,1,0:T(8,128)(2,1)}, bf16[10,2,128,128]{3,2,1,0:T(8,128)(2,1)S(1)}, u32[]{:S(2)}, u32[]{:S(2)}) collective-permute-start(bf16[10,2,128,128]{3,2,1,0:T(8,128)(2,1)} %get-tuple-element.66.refs_0_), channel_id=1, source_target_pairs={{0,4},{1,5},{2,6},{3,7},{4,8},{5,9},{6,10},{7,11},{8,12},{9,13},{1... | collective-permute-start | bytes 1966088 | tf_op jit(solution)/shard_map/ppermute | solution.py:26
  31.0 29.6 %collective-permute-start.11 = (bf16[10,2,128,128]{3,2,1,0:T(8,128)(2,1)}, bf16[10,2,128,128]{3,2,1,0:T(8,128)(2,1)S(1)}, u32[]{:S(2)}, u32[]{:S(2)}) collective-permute-start(bf16[10,2,128,128]{3,2,1,0:T(8,128)(2,1)} %get-tuple-element.67.refs_4_), channel_id=1, source_target_pairs={{0,3},{1,0},{2,1},{3,2},{4,7},{5,4},{6,5},{7,6},{8,11},{9,8},{10,9... | collective-permute-start | bytes 1966088 | tf_op jit(solution)/shard_map/ppermute | solution.py:26
  34.9 25.8 %collective-permute-start.10 = (bf16[10,2,128,128]{3,2,1,0:T(8,128)(2,1)}, bf16[10,2,128,128]{3,2,1,0:T(8,128)(2,1)}, u32[]{:S(2)}, u32[]{:S(2)}) collective-permute-start(bf16[10,2,128,128]{3,2,1,0:T(8,128)(2,1)} %get-tuple-element.67.refs_4_), channel_id=1, source_target_pairs={{0,2},{1,3},{2,0},{3,1},{4,6},{5,7},{6,4},{7,5},{8,10},{9,11},{10,... | collective-permute-start | bytes 1966088 | tf_op jit(solution)/shard_map/ppermute | solution.py:26
  45.5 18.9 %collective-permute-start.9 = (bf16[10,2,128,128]{3,2,1,0:T(8,128)(2,1)}, bf16[10,2,128,128]{3,2,1,0:T(8,128)(2,1)}, u32[]{:S(2)}, u32[]{:S(2)}) collective-permute-start(bf16[10,2,128,128]{3,2,1,0:T(8,128)(2,1)} %get-tuple-element.67.refs_4_), channel_id=1, source_target_pairs={{0,1},{1,2},{2,3},{3,0},{4,5},{5,6},{6,7},{7,4},{8,9},{9,10},{10,1... | collective-permute-start | bytes 1966088 | tf_op jit(solution)/shard_map/ppermute | solution.py:26
  71.2 71.1 %all-to-all-start = ((bf16[8,2,2,256,128]{4,3,2,1,0:T(8,128)(2,1)}), bf16[8,2,2,256,128]{4,3,2,1,0:T(8,128)(2,1)}, u32[]{:S(2)}, u32[]{:S(2)}) async-start(bf16[8,2,2,256,128]{4,3,2,1,0:T(8,128)(2,1)} %shard_map.66), calls=%async_computation | async-start | bytes 4194304 | tf_op jit(solution)/shard_map/all_to_all | solution.py:183
  78.2 31.6 %collective-permute-start.27 = (bf16[8,2,128,128]{3,2,1,0:T(8,128)(2,1)S(1)}, bf16[8,2,128,128]{3,2,1,0:T(8,128)(2,1)S(1)}, u32[]{:S(2)}, u32[]{:S(2)}) collective-permute-start(bf16[8,2,128,128]{3,2,1,0:T(8,128)(2,1)S(1)} %get-tuple-element.78.refs_0_), channel_id=1, source_target_pairs={{0,12},{1,13},{2,14},{3,15},{4,0},{5,1},{6,2},{7,3},{8,4},{9,5},{1... | collective-permute-start | bytes 1572872 | tf_op jit(solution)/shard_map/ppermute | solution.py:26
  86.2 24.6 %collective-permute-start.26 = (bf16[8,2,128,128]{3,2,1,0:T(8,128)(2,1)S(1)}, bf16[8,2,128,128]{3,2,1,0:T(8,128)(2,1)S(1)}, u32[]{:S(2)}, u32[]{:S(2)}) collective-permute-start(bf16[8,2,128,128]{3,2,1,0:T(8,128)(2,1)S(1)} %get-tuple-element.78.refs_0_), channel_id=1, source_target_pairs={{0,8},{1,9},{2,10},{3,11},{4,12},{5,13},{6,14},{7,15},{8,0},{9,1},... | collective-permute-start | bytes 1572872 | tf_op jit(solution)/shard_map/ppermute | solution.py:26
  88.6 64.3 %collective-permute-start.14 = (bf16[10,2,128,128]{3,2,1,0:T(8,128)(2,1)}, bf16[10,2,128,128]{3,2,1,0:T(8,128)(2,1)S(1)}, u32[]{:S(2)}, u32[]{:S(2)}) collective-permute-start(bf16[10,2,128,128]{3,2,1,0:T(8,128)(2,1)} %get-tuple-element.68.refs_0_), channel_id=1, source_target_pairs={{0,12},{1,13},{2,14},{3,15},{4,0},{5,1},{6,2},{7,3},{8,4},{9,5},{1... | collective-permute-start | bytes 1966088 | tf_op jit(solution)/shard_map/ppermute | solution.py:26
  88.7 24.2 %collective-permute-start.25 = (bf16[8,2,128,128]{3,2,1,0:T(8,128)(2,1)S(1)}, bf16[8,2,128,128]{3,2,1,0:T(8,128)(2,1)S(1)}, u32[]{:S(2)}, u32[]{:S(2)}) collective-permute-start(bf16[8,2,128,128]{3,2,1,0:T(8,128)(2,1)S(1)} %get-tuple-element.78.refs_0_), channel_id=1, source_target_pairs={{0,4},{1,5},{2,6},{3,7},{4,8},{5,9},{6,10},{7,11},{8,12},{9,13},{1... | collective-permute-start | bytes 1572872 | tf_op jit(solution)/shard_map/ppermute | solution.py:26
  90.7 22.3 %collective-permute-start.30 = (bf16[8,2,128,128]{3,2,1,0:T(8,128)(2,1)S(1)}, bf16[8,2,128,128]{3,2,1,0:T(8,128)(2,1)S(1)}, u32[]{:S(2)}, u32[]{:S(2)}) collective-permute-start(bf16[8,2,128,128]{3,2,1,0:T(8,128)(2,1)S(1)} %get-tuple-element.79.refs_4_), channel_id=1, source_target_pairs={{0,3},{1,0},{2,1},{3,2},{4,7},{5,4},{6,5},{7,6},{8,11},{9,8},{10,9... | collective-permute-start | bytes 1572872 | tf_op jit(solution)/shard_map/ppermute | solution.py:26
  109.8 16.3 %collective-permute-start.29 = (bf16[8,2,128,128]{3,2,1,0:T(8,128)(2,1)S(1)}, bf16[8,2,128,128]{3,2,1,0:T(8,128)(2,1)S(1)}, u32[]{:S(2)}, u32[]{:S(2)}) collective-permute-start(bf16[8,2,128,128]{3,2,1,0:T(8,128)(2,1)S(1)} %get-tuple-element.79.refs_4_), channel_id=1, source_target_pairs={{0,2},{1,3},{2,0},{3,1},{4,6},{5,7},{6,4},{7,5},{8,10},{9,11},{10,... | collective-permute-start | bytes 1572872 | tf_op jit(solution)/shard_map/ppermute | solution.py:26
  110.8 24.7 %collective-permute-start.28 = (bf16[8,2,128,128]{3,2,1,0:T(8,128)(2,1)S(1)}, bf16[8,2,128,128]{3,2,1,0:T(8,128)(2,1)}, u32[]{:S(2)}, u32[]{:S(2)}) collective-permute-start(bf16[8,2,128,128]{3,2,1,0:T(8,128)(2,1)S(1)} %get-tuple-element.79.refs_4_), channel_id=1, source_target_pairs={{0,1},{1,2},{2,3},{3,0},{4,5},{5,6},{6,7},{7,4},{8,9},{9,10},{10,1... | collective-permute-start | bytes 1572872 | tf_op jit(solution)/shard_map/ppermute | solution.py:26
  142.3 78.9 %all-to-all-start.1 = ((bf16[8,2,2,256,128]{4,3,2,1,0:T(8,128)(2,1)}), bf16[8,2,2,256,128]{4,3,2,1,0:T(8,128)(2,1)}, u32[]{:S(2)}, u32[]{:S(2)}) async-start(bf16[8,2,2,256,128]{4,3,2,1,0:T(8,128)(2,1)} %shard_map.70), calls=%async_computation.1 | async-start | bytes 4194304 | tf_op jit(solution)/shard_map/all_to_all | solution.py:183
  146.6 19.4 %collective-permute-start.13 = (bf16[10,2,128,128]{3,2,1,0:T(8,128)(2,1)}, bf16[10,2,128,128]{3,2,1,0:T(8,128)(2,1)S(1)}, u32[]{:S(2)}, u32[]{:S(2)}) collective-permute-start(bf16[10,2,128,128]{3,2,1,0:T(8,128)(2,1)} %get-tuple-element.68.refs_0_), channel_id=1, source_target_pairs={{0,8},{1,9},{2,10},{3,11},{4,12},{5,13},{6,14},{7,15},{8,0},{9,1},... | collective-permute-start | bytes 1966088 | tf_op jit(solution)/shard_map/ppermute | solution.py:26
  146.7 32.7 %collective-permute-start.12 = (bf16[10,2,128,128]{3,2,1,0:T(8,128)(2,1)}, bf16[10,2,128,128]{3,2,1,0:T(8,128)(2,1)S(1)}, u32[]{:S(2)}, u32[]{:S(2)}) collective-permute-start(bf16[10,2,128,128]{3,2,1,0:T(8,128)(2,1)} %get-tuple-element.68.refs_0_), channel_id=1, source_target_pairs={{0,4},{1,5},{2,6},{3,7},{4,8},{5,9},{6,10},{7,11},{8,12},{9,13},{1... | collective-permute-start | bytes 1966088 | tf_op jit(solution)/shard_map/ppermute | solution.py:26
  151.3 28.2 %collective-permute-start.17 = (bf16[10,2,128,128]{3,2,1,0:T(8,128)(2,1)S(1)}, bf16[10,2,128,128]{3,2,1,0:T(8,128)(2,1)S(1)}, u32[]{:S(2)}, u32[]{:S(2)}) collective-permute-start(bf16[10,2,128,128]{3,2,1,0:T(8,128)(2,1)S(1)} %get-tuple-element.69.refs_4_), channel_id=1, source_target_pairs={{0,3},{1,0},{2,1},{3,2},{4,7},{5,4},{6,5},{7,6},{8,11},{9,8},{10,9... | collective-permute-start | bytes 1966088 | tf_op jit(solution)/shard_map/ppermute | solution.py:26
  151.9 27.5 %collective-permute-start.16 = (bf16[10,2,128,128]{3,2,1,0:T(8,128)(2,1)S(1)}, bf16[10,2,128,128]{3,2,1,0:T(8,128)(2,1)S(1)}, u32[]{:S(2)}, u32[]{:S(2)}) collective-permute-start(bf16[10,2,128,128]{3,2,1,0:T(8,128)(2,1)S(1)} %get-tuple-element.69.refs_4_), channel_id=1, source_target_pairs={{0,2},{1,3},{2,0},{3,1},{4,6},{5,7},{6,4},{7,5},{8,10},{9,11},{10,... | collective-permute-start | bytes 1966088 | tf_op jit(solution)/shard_map/ppermute | solution.py:26
  152.9 30.6 %collective-permute-start.15 = (bf16[10,2,128,128]{3,2,1,0:T(8,128)(2,1)S(1)}, bf16[10,2,128,128]{3,2,1,0:T(8,128)(2,1)S(1)}, u32[]{:S(2)}, u32[]{:S(2)}) collective-permute-start(bf16[10,2,128,128]{3,2,1,0:T(8,128)(2,1)S(1)} %get-tuple-element.69.refs_4_), channel_id=1, source_target_pairs={{0,1},{1,2},{2,3},{3,0},{4,5},{5,6},{6,7},{7,4},{8,9},{9,10},{10,1... | collective-permute-start | bytes 1966088 | tf_op jit(solution)/shard_map/ppermute | solution.py:26
  184.9 14.9 %collective-permute-start.33 = (bf16[8,2,128,128]{3,2,1,0:T(8,128)(2,1)S(1)}, bf16[8,2,128,128]{3,2,1,0:T(8,128)(2,1)S(1)}, u32[]{:S(2)}, u32[]{:S(2)}) collective-permute-start(bf16[8,2,128,128]{3,2,1,0:T(8,128)(2,1)S(1)} %get-tuple-element.80.refs_0_), channel_id=1, source_target_pairs={{0,12},{1,13},{2,14},{3,15},{4,0},{5,1},{6,2},{7,3},{8,4},{9,5},{1... | collective-permute-start | bytes 1572872 | tf_op jit(solution)/shard_map/ppermute | solution.py:26
  185.0 21.5 %collective-permute-start.32 = (bf16[8,2,128,128]{3,2,1,0:T(8,128)(2,1)S(1)}, bf16[8,2,128,128]{3,2,1,0:T(8,128)(2,1)S(1)}, u32[]{:S(2)}, u32[]{:S(2)}) collective-permute-start(bf16[8,2,128,128]{3,2,1,0:T(8,128)(2,1)S(1)} %get-tuple-element.80.refs_0_), channel_id=1, source_target_pairs={{0,8},{1,9},{2,10},{3,11},{4,12},{5,13},{6,14},{7,15},{8,0},{9,1},... | collective-permute-start | bytes 1572872 | tf_op jit(solution)/shard_map/ppermute | solution.py:26
  187.3 24.5 %collective-permute-start.31 = (bf16[8,2,128,128]{3,2,1,0:T(8,128)(2,1)S(1)}, bf16[8,2,128,128]{3,2,1,0:T(8,128)(2,1)S(1)}, u32[]{:S(2)}, u32[]{:S(2)}) collective-permute-start(bf16[8,2,128,128]{3,2,1,0:T(8,128)(2,1)S(1)} %get-tuple-element.80.refs_0_), channel_id=1, source_target_pairs={{0,4},{1,5},{2,6},{3,7},{4,8},{5,9},{6,10},{7,11},{8,12},{9,13},{1... | collective-permute-start | bytes 1572872 | tf_op jit(solution)/shard_map/ppermute | solution.py:26
  187.3 26.2 %collective-permute-start.36 = (bf16[8,2,128,128]{3,2,1,0:T(8,128)(2,1)S(1)}, bf16[8,2,128,128]{3,2,1,0:T(8,128)(2,1)S(1)}, u32[]{:S(2)}, u32[]{:S(2)}) collective-permute-start(bf16[8,2,128,128]{3,2,1,0:T(8,128)(2,1)S(1)} %get-tuple-element.81.refs_4_), channel_id=1, source_target_pairs={{0,3},{1,0},{2,1},{3,2},{4,7},{5,4},{6,5},{7,6},{8,11},{9,8},{10,9... | collective-permute-start | bytes 1572872 | tf_op jit(solution)/shard_map/ppermute | solution.py:26
  188.1 25.3 %collective-permute-start.35 = (bf16[8,2,128,128]{3,2,1,0:T(8,128)(2,1)S(1)}, bf16[8,2,128,128]{3,2,1,0:T(8,128)(2,1)}, u32[]{:S(2)}, u32[]{:S(2)}) collective-permute-start(bf16[8,2,128,128]{3,2,1,0:T(8,128)(2,1)S(1)} %get-tuple-element.81.refs_4_), channel_id=1, source_target_pairs={{0,2},{1,3},{2,0},{3,1},{4,6},{5,7},{6,4},{7,5},{8,10},{9,11},{10,... | collective-permute-start | bytes 1572872 | tf_op jit(solution)/shard_map/ppermute | solution.py:26
  199.7 14.7 %collective-permute-start.34 = (bf16[8,2,128,128]{3,2,1,0:T(8,128)(2,1)S(1)}, bf16[8,2,128,128]{3,2,1,0:T(8,128)(2,1)}, u32[]{:S(2)}, u32[]{:S(2)}) collective-permute-start(bf16[8,2,128,128]{3,2,1,0:T(8,128)(2,1)S(1)} %get-tuple-element.81.refs_4_), channel_id=1, source_target_pairs={{0,1},{1,2},{2,3},{3,0},{4,5},{5,6},{6,7},{7,4},{8,9},{9,10},{10,1... | collective-permute-start | bytes 1572872 | tf_op jit(solution)/shard_map/ppermute | solution.py:26
  206.5 24.3 %collective-permute-start.18 = (bf16[2,2,256,128]{3,2,1,0:T(8,128)(2,1)}, bf16[2,2,256,128]{3,2,1,0:T(8,128)(2,1)S(1)}, u32[]{:S(2)}, u32[]{:S(2)}) collective-permute-start(bf16[2,2,256,128]{3,2,1,0:T(8,128)(2,1)} %get-tuple-element.71), channel_id=1, source_target_pairs={{0,16},{16,0},{32,48},{48,32},{64,80},{80,64},{96,112},{112,96},{1... | collective-permute-start | bytes 786440 | tf_op jit(solution)/shard_map/ppermute | solution.py:192
  211.8 20.3 %collective-permute-start.19 = (bf16[2,2,256,128]{3,2,1,0:T(8,128)(2,1)}, bf16[2,2,256,128]{3,2,1,0:T(8,128)(2,1)S(1)}, u32[]{:S(2)}, u32[]{:S(2)}) collective-permute-start(bf16[2,2,256,128]{3,2,1,0:T(8,128)(2,1)} %get-tuple-element.72), channel_id=1, source_target_pairs={{0,32},{16,48},{32,64},{48,80},{64,96},{80,112},{96,0},{112,16},{1... | collective-permute-start | bytes 786440 | tf_op jit(solution)/shard_map/ppermute | solution.py:192
  221.2 69.5 %all-to-all-start.2 = ((bf16[8,2,2,128,128]{4,3,2,1,0:T(8,128)(2,1)}), bf16[8,2,2,128,128]{4,3,2,1,0:T(8,128)(2,1)S(1)}, u32[]{:S(2)}, u32[]{:S(2)}) async-start(bf16[8,2,2,128,128]{4,3,2,1,0:T(8,128)(2,1)} %get-tuple-element.106), calls=%async_computation.2 | async-start | bytes 2097152 | tf_op jit(solution)/shard_map/all_to_all | solution.py:183
  225.8 20.9 %collective-permute-start.20 = (bf16[2,2,256,128]{3,2,1,0:T(8,128)(2,1)}, bf16[2,2,256,128]{3,2,1,0:T(8,128)(2,1)S(1)}, u32[]{:S(2)}, u32[]{:S(2)}) collective-permute-start(bf16[2,2,256,128]{3,2,1,0:T(8,128)(2,1)} %get-tuple-element.73), channel_id=1, source_target_pairs={{0,48},{16,32},{32,80},{48,64},{64,112},{80,96},{96,16},{112,0},{1... | collective-permute-start | bytes 786440 | tf_op jit(solution)/shard_map/ppermute | solution.py:192
  227.5 26.0 %collective-permute-start.21 = (bf16[2,2,256,128]{3,2,1,0:T(8,128)(2,1)S(1)}, bf16[2,2,256,128]{3,2,1,0:T(8,128)(2,1)S(1)}, u32[]{:S(2)}, u32[]{:S(2)}) collective-permute-start(bf16[2,2,256,128]{3,2,1,0:T(8,128)(2,1)S(1)} %copy-done.56), channel_id=1, source_target_pairs={{0,64},{16,80},{32,96},{48,112},{64,0},{80,16},{96,32},{112,48},{1... | collective-permute-start | bytes 786440 | tf_op jit(solution)/shard_map/ppermute | solution.py:192
  230.2 27.9 %collective-permute-start.22 = (bf16[2,2,256,128]{3,2,1,0:T(8,128)(2,1)}, bf16[2,2,256,128]{3,2,1,0:T(8,128)(2,1)S(1)}, u32[]{:S(2)}, u32[]{:S(2)}) collective-permute-start(bf16[2,2,256,128]{3,2,1,0:T(8,128)(2,1)} %get-tuple-element.75), channel_id=1, source_target_pairs={{0,80},{16,64},{32,112},{48,96},{64,16},{80,0},{96,48},{112,32},{1... | collective-permute-start | bytes 786440 | tf_op jit(solution)/shard_map/ppermute | solution.py:192
  230.8 27.4 %collective-permute-start.23 = (bf16[2,2,256,128]{3,2,1,0:T(8,128)(2,1)}, bf16[2,2,256,128]{3,2,1,0:T(8,128)(2,1)S(1)}, u32[]{:S(2)}, u32[]{:S(2)}) collective-permute-start(bf16[2,2,256,128]{3,2,1,0:T(8,128)(2,1)} %get-tuple-element.76), channel_id=1, source_target_pairs={{0,96},{16,112},{32,0},{48,16},{64,32},{80,48},{96,64},{112,80},{1... | collective-permute-start | bytes 786440 | tf_op jit(solution)/shard_map/ppermute | solution.py:192
  232.1 30.1 %collective-permute-start.24 = (bf16[2,2,256,128]{3,2,1,0:T(8,128)(2,1)}, bf16[2,2,256,128]{3,2,1,0:T(8,128)(2,1)S(1)}, u32[]{:S(2)}, u32[]{:S(2)}) collective-permute-start(bf16[2,2,256,128]{3,2,1,0:T(8,128)(2,1)} %get-tuple-element.77), channel_id=1, source_target_pairs={{0,112},{16,96},{32,16},{48,0},{64,48},{80,32},{96,80},{112,64},{1... | collective-permute-start | bytes 786440 | tf_op jit(solution)/shard_map/ppermute | solution.py:192
  246.6 18.8 %collective-permute-start.37 = (bf16[2,2,128,128]{3,2,1,0:T(8,128)(2,1)}, bf16[2,2,128,128]{3,2,1,0:T(8,128)(2,1)S(1)}, u32[]{:S(2)}, u32[]{:S(2)}) collective-permute-start(bf16[2,2,128,128]{3,2,1,0:T(8,128)(2,1)} %get-tuple-element.83), channel_id=1, source_target_pairs={{0,16},{16,0},{32,48},{48,32},{64,80},{80,64},{96,112},{112,96},{1... | collective-permute-start | bytes 393224 | tf_op jit(solution)/shard_map/ppermute | solution.py:192
  283.3 17.1 %collective-permute-start.44 = (bf16[4,128,256]{2,1,0:T(8,128)(2,1)}, bf16[4,128,256]{2,1,0:T(8,128)(2,1)S(1)}, u32[]{:S(2)}, u32[]{:S(2)}) collective-permute-start(bf16[4,128,256]{2,1,0:T(8,128)(2,1)} %get-tuple-element.91), channel_id=1, source_target_pairs={{0,1},{1,2},{2,3},{3,0},{4,5},{5,6},{6,7},{7,4},{8,9},{9,10},{10,1... | collective-permute-start | bytes 786440 | tf_op jit(solution)/shard_map/ppermute | solution.py:26
  283.4 18.7 %collective-permute-start.45 = (bf16[4,128,256]{2,1,0:T(8,128)(2,1)}, bf16[4,128,256]{2,1,0:T(8,128)(2,1)S(1)}, u32[]{:S(2)}, u32[]{:S(2)}) collective-permute-start(bf16[4,128,256]{2,1,0:T(8,128)(2,1)} %get-tuple-element.92), channel_id=1, source_target_pairs={{0,2},{1,3},{2,0},{3,1},{4,6},{5,7},{6,4},{7,5},{8,10},{9,11},{10,... | collective-permute-start | bytes 786440 | tf_op jit(solution)/shard_map/ppermute | solution.py:26
  285.1 18.0 %collective-permute-start.46 = (bf16[4,128,256]{2,1,0:T(8,128)(2,1)}, bf16[4,128,256]{2,1,0:T(8,128)(2,1)S(1)}, u32[]{:S(2)}, u32[]{:S(2)}) collective-permute-start(bf16[4,128,256]{2,1,0:T(8,128)(2,1)} %get-tuple-element.93), channel_id=1, source_target_pairs={{0,3},{1,0},{2,1},{3,2},{4,7},{5,4},{6,5},{7,6},{8,11},{9,8},{10,9... | collective-permute-start | bytes 786440 | tf_op jit(solution)/shard_map/ppermute | solution.py:26
  286.6 18.1 %collective-permute-start.47 = (bf16[4,128,256]{2,1,0:T(8,128)(2,1)}, bf16[4,128,256]{2,1,0:T(8,128)(2,1)S(1)}, u32[]{:S(2)}, u32[]{:S(2)}) collective-permute-start(bf16[4,128,256]{2,1,0:T(8,128)(2,1)} %get-tuple-element.95), channel_id=1, source_target_pairs={{0,4},{1,5},{2,6},{3,7},{4,8},{5,9},{6,10},{7,11},{8,12},{9,13},{1... | collective-permute-start | bytes 786440 | tf_op jit(solution)/shard_map/ppermute | solution.py:26
  287.6 19.6 %collective-permute-start.48 = (bf16[4,128,256]{2,1,0:T(8,128)(2,1)}, bf16[4,128,256]{2,1,0:T(8,128)(2,1)S(1)}, u32[]{:S(2)}, u32[]{:S(2)}) collective-permute-start(bf16[4,128,256]{2,1,0:T(8,128)(2,1)} %get-tuple-element.96), channel_id=1, source_target_pairs={{0,8},{1,9},{2,10},{3,11},{4,12},{5,13},{6,14},{7,15},{8,0},{9,1},... | collective-permute-start | bytes 786440 | tf_op jit(solution)/shard_map/ppermute | solution.py:26
  302.0 13.7 %collective-permute-start.56 = (bf16[4,128,256]{2,1,0:T(8,128)(2,1)}, bf16[4,128,256]{2,1,0:T(8,128)(2,1)S(1)}, u32[]{:S(2)}, u32[]{:S(2)}) collective-permute-start(bf16[4,128,256]{2,1,0:T(8,128)(2,1)} %get-tuple-element.108), channel_id=1, source_target_pairs={{0,1},{1,2},{2,3},{3,0},{4,5},{5,6},{6,7},{7,4},{8,9},{9,10},{10,1... | collective-permute-start | bytes 786440 | tf_op jit(solution)/shard_map/ppermute | solution.py:26
  303.1 13.3 %collective-permute-start.57 = (bf16[4,128,256]{2,1,0:T(8,128)(2,1)}, bf16[4,128,256]{2,1,0:T(8,128)(2,1)S(1)}, u32[]{:S(2)}, u32[]{:S(2)}) collective-permute-start(bf16[4,128,256]{2,1,0:T(8,128)(2,1)} %get-tuple-element.109), channel_id=1, source_target_pairs={{0,2},{1,3},{2,0},{3,1},{4,6},{5,7},{6,4},{7,5},{8,10},{9,11},{10,... | collective-permute-start | bytes 786440 | tf_op jit(solution)/shard_map/ppermute | solution.py:26
  304.7 13.4 %collective-permute-start.58 = (bf16[4,128,256]{2,1,0:T(8,128)(2,1)}, bf16[4,128,256]{2,1,0:T(8,128)(2,1)S(1)}, u32[]{:S(2)}, u32[]{:S(2)}) collective-permute-start(bf16[4,128,256]{2,1,0:T(8,128)(2,1)} %get-tuple-element.110), channel_id=1, source_target_pairs={{0,3},{1,0},{2,1},{3,2},{4,7},{5,4},{6,5},{7,6},{8,11},{9,8},{10,9... | collective-permute-start | bytes 786440 | tf_op jit(solution)/shard_map/ppermute | solution.py:26
  307.2 14.3 %collective-permute-start.59 = (bf16[4,128,256]{2,1,0:T(8,128)(2,1)}, bf16[4,128,256]{2,1,0:T(8,128)(2,1)S(1)}, u32[]{:S(2)}, u32[]{:S(2)}) collective-permute-start(bf16[4,128,256]{2,1,0:T(8,128)(2,1)} %get-tuple-element.112), channel_id=1, source_target_pairs={{0,4},{1,5},{2,6},{3,7},{4,8},{5,9},{6,10},{7,11},{8,12},{9,13},{1... | collective-permute-start | bytes 786440 | tf_op jit(solution)/shard_map/ppermute | solution.py:26
  308.1 13.5 %collective-permute-start.60 = (bf16[4,128,256]{2,1,0:T(8,128)(2,1)}, bf16[4,128,256]{2,1,0:T(8,128)(2,1)S(1)}, u32[]{:S(2)}, u32[]{:S(2)}) collective-permute-start(bf16[4,128,256]{2,1,0:T(8,128)(2,1)} %get-tuple-element.113), channel_id=1, source_target_pairs={{0,8},{1,9},{2,10},{3,11},{4,12},{5,13},{6,14},{7,15},{8,0},{9,1},... | collective-permute-start | bytes 786440 | tf_op jit(solution)/shard_map/ppermute | solution.py:26
  (81 other events, 1173.6 us)

commit v3 on v2

--- a/solution.py
+++ b/solution.py
@@ -60,27 +60,25 @@
     )(wave, *gots)
 
 
-def left_kernel(first_sector, modes, place, pairs, size, *refs):
+def left_kernel(first_sector, modes, plan, place, pairs, size, *refs):
     split = len(modes)
-    pieces, left_hbm = refs[:8], refs[8]
-    outs = list(refs[9:-5])
+    total = 1 + max(entry[0] for entry in plan)
+    pieces, left_hbm = refs[:total], refs[total]
+    outs = list(refs[total + 1 : -5])
     whole, left, done, sems, left_sem = refs[-5:]
     y, z, bond = place[0], place[1], place[2]
     count = whole.shape[0]
     copies = [pltpu.make_async_copy(left_hbm, left, left_sem)]
-    for idx, piece in enumerate(pieces):
-        upper, far = idx < SIDE, idx % SIDE
-        for near in range(SIDE):
-            step_y, step_z = (far, near) if upper else (near, far)
-            owner = (y + SIDE - step_y) % SIDE * SIDE + (z + SIDE - step_z) % SIDE
-            start = owner * 4 + (0 if upper else 2)
-            copies.append(
-                pltpu.make_async_copy(
-                    piece.at[pl.ds(near * count, count)],
-                    whole.at[:, pl.ds(start, 2)],
-                    sems.at[len(copies) - 1],
-                )
+    for source, offset, side, far, near in plan:
+        step_y, step_z = (far, near) if side == 0 else (near, far)
+        owner = (y + SIDE - step_y) % SIDE * SIDE + (z + SIDE - step_z) % SIDE
+        copies.append(
+            pltpu.make_async_copy(
+                pieces[source].at[offset : offset + count],
+                whole.at[:, pl.ds(owner * 4 + 2 * side, 2)],
+                sems.at[len(copies) - 1],
             )
+        )
     for copy in copies:
         copy.start()
     for copy in copies:
@@ -141,7 +139,7 @@
         copy.wait()
 
 
-def left_stage(pieces, modes, count, left_blocks, place, pairs, size, first_sector):
+def left_stage(pieces, plan, modes, count, left_blocks, place, pairs, size, first_sector):
     terms = left_blocks.shape[0]
     block = (count, terms, 2 * TILE // len(modes), TILE)
     shapes = []
@@ -149,7 +147,7 @@
         shapes += [block] * 8 if turned else [(8, *block)]
     anywhere = pl.BlockSpec(memory_space=pl.ANY)
     results = pl.pallas_call(
-        functools.partial(left_kernel, first_sector, modes),
+        functools.partial(left_kernel, first_sector, modes, plan),
         out_shape=[jax.ShapeDtypeStruct(shape, BF16) for shape in shapes],
         grid_spec=pltpu.PrefetchScalarGridSpec(
             num_scalar_prefetch=3,
@@ -241,10 +239,11 @@
         for step_y in range(SIDE):
             right_copy(step_z, step_y).start()
     sent = []
-    for step_z in range(SIDE):
-
-        @pl.loop(0, SIDE, step=2)
-        def _(pair):
+    for step_zs in ((0, 1), (2, 3)):
+
+        @pl.loop(0, SIDE)
+        def _(trip):
+            step_z, pair = step_zs[0] + trip // 2, trip % 2 * 2
             for step_y in (pair, pair + 1):
                 right_copy(step_z, step_y).wait()
             for step_y in (pair, pair + 1):
@@ -271,17 +270,18 @@
                     else:
                         sum_b[step_y, step_z, :, (q - 2) * TILE : (q - 1) * TILE] = value
 
-        sent.append(
-            pltpu.make_async_copy(sum_a.at[step_z], outs_a[step_z], out_sems.at[len(sent)])
-        )
-        sent[-1].start()
-        for k in range(SIDE):
+        for step_z in step_zs:
             sent.append(
-                pltpu.make_async_copy(
-                    sum_b.at[k, step_z], outs_b[k].at[step_z], out_sems.at[len(sent)]
-                )
+                pltpu.make_async_copy(sum_a.at[step_z], outs_a[step_z], out_sems.at[len(sent)])
             )
             sent[-1].start()
+            for k in range(SIDE):
+                sent.append(
+                    pltpu.make_async_copy(
+                        sum_b.at[k, step_z], outs_b[k].at[step_z], out_sems.at[len(sent)]
+                    )
+                )
+                sent[-1].start()
     for copy in sent:
         copy.wait()
 
@@ -393,27 +393,51 @@
     units = range(starts[ahead])
     values = pack_stage(wave, [], [[(None, side, unit) for unit in units] for side in range(2)])
     got = sent_both(values, False)
+    first = sent_both(values, True)
     near = {chunk: ([got[0][1:], got[1][1:]], starts[chunk]) for chunk in range(ahead)}
     arrived = []
     for chunk in range(chunk_count):
         count = CHUNKS[chunk]
         after = chunk + ahead
         sources, offset = near[chunk]
-        plans = []
+        early = chunk < ahead
+        packs = []
         for side in range(2):
-            plan = [(None, side, starts[chunk] + unit) for unit in range(count)]
+            pack = []
+            if not early:
+                pack += [(None, side, starts[chunk] + unit) for unit in range(count)]
             for d in range(SIDE - 1):
-                plan += [(side * 3 + d, side, offset + unit) for unit in range(count)]
+                pack += [(side * 3 + d, side, offset + unit) for unit in range(count)]
             if after < chunk_count:
-                plan += [(None, 1 - side, starts[after] + unit) for unit in range(CHUNKS[after])]
-            plans.append(plan)
-        values = pack_stage(wave, sources[0] + sources[1], plans)
+                pack += [(None, 1 - side, starts[after] + unit) for unit in range(CHUNKS[after])]
+            packs.append(pack)
+        values = pack_stage(wave, sources[0] + sources[1], packs)
         got = sent_both(values, True)
-        pieces = got[0] + got[1]
+        pieces, plan = [], []
+        for side in range(2):
+            for far in range(SIDE):
+                slots = range(1, SIDE) if early else range(SIDE)
+                plan += [
+                    (len(pieces), place_of * count, side, far, slot)
+                    for place_of, slot in enumerate(slots)
+                ]
+                pieces.append(got[side][far])
+                if early:
+                    plan.append((len(pieces), starts[chunk], side, far, 0))
+                    pieces.append(first[side][far])
         if after < chunk_count:
-            near[after] = ([got[1][1:], got[0][1:]], 4 * count)
+            skip = (SIDE - 1 if early else SIDE) * count
+            near[after] = ([got[1][1:], got[0][1:]], skip)
         middles = left_stage(
-            pieces, MODES[chunk], count, left_blocks, place, lefts, sector_size, starts[chunk]
+            pieces,
+            tuple(plan),
+            MODES[chunk],
+            count,
+            left_blocks,
+            place,
+            lefts,
+            sector_size,
+            starts[chunk],
         )
         for middle in middles:
             arrived.append(exchange(middle))

time: 339 us -> 333 us (0.982)
  waiting for transfers between devices: 171 us -> 146 us
  starting transfers between devices: 107 us -> 121 us
  local copies, waits for them, and re-layouts: 5.92 us -> 9.4 us
    ppermute x54 -> x60, waiting for transfers between devices: 138 us -> 113 us  [move(): return lax.ppermute(value, 'op', pairs)]
    ppermute x54 -> x60, starting transfers between devices: 76.7 us -> 90.2 us  [move(): return lax.ppermute(value, 'op', pairs)]
    unnamed x118 -> x150, local copies, waits for them, and re-layouts: 4.55 us -> 7.98 us
  transfers between devices with their start and end apart: 71 -> 77, of which waited for: 30 -> 30; matrix products, arithmetic and copies ran while one was open for 1% -> 1% of each run, Pallas kernels for 13% -> 14%
where the time goes in v3:
time: 333 us; the launch traced here: 332 us
  waiting for transfers between devices  146 us (44%)
  starting transfers between devices  121 us (36%)
  Pallas kernels  54.3 us (16%)
  local copies, waits for them, and re-layouts  9.4 us (3%)
    ppermute x60, waiting for transfers between devices, move(): return lax.ppermute(value, 'op', pairs)  113 us
    ppermute x60, starting transfers between devices, move(): return lax.ppermute(value, 'op', pairs)  90.2 us
    ppermute x14, waiting for transfers between devices, exchange(): got.append(lax.ppermute(blocks[turned], 'bond', pairs))  32.8 us
    pallas_call x4, Pallas kernels, left_stage(): pl.pallas_call(functools.partial(left_kernel, first_sector, modes, plan),...  26.8 us
    pallas_call x2, Pallas kernels, right_stage(): pl.pallas_call(functools.partial(right_kernel, layout, half), out_shape=[...  17.8 us
    ppermute x14, starting transfers between devices, exchange(): got.append(lax.ppermute(blocks[turned], 'bond', pairs))  16.7 us
    all_to_all x3, starting transfers between devices, exchange(): lax.all_to_all(blocks[0], 'bond', split_axis=0, concat_axis=0, tiled=True)  13.6 us
    pallas_call x5, Pallas kernels, pack_stage(): pl.pallas_call(functools.partial(pack_kernel, plans), out_shape=[jax.Shap...  8.2 us
  transfers between devices with their start and end apart: 77, of which 30 were waited for; matrix products, arithmetic and copies ran while one was open for 1% of the time, Pallas kernels for 14%

profile of v3, /device:TPU:0, one launch (start us, length us, event | category | flops | bytes accessed | tf_op | source)
XLA Modules:
  0.0 331.7 jit_solution(8792149006425833783)
XLA Ops:
  1.5 4.2 %collective-permute-start.2 = (bf16[4,2,128,128]{3,2,1,0:T(8,128)(2,1)S(1)}, bf16[4,2,128,128]{3,2,1,0:T(8,128)(2,1)S(1)}, u32[]{:S(2)}, u32[]{:S(2)}) collective-permute-start(bf16[4,2,128,128]{3,2,1,0:T(8,128)(2,1)S(1)} %get-tuple-element.64.refs_1_), channel_id=1, source_target_pairs={{0,3},{1,0},{2,1},{3,2},{4,7},{5,4},{6,5},{7,6},{8,11},{9,8},{10,9... | collective-permute-start | bytes 786440 | tf_op jit(solution)/shard_map/ppermute | solution.py:26
  7.0 3.0 collective-permute-start.5
  10.6 6.3 %collective-permute-done.2.refs_2_ = bf16[4,2,128,128]{3,2,1,0:T(8,128)(2,1)S(1)} collective-permute-done((bf16[4,2,128,128]{3,2,1,0:T(8,128)(2,1)S(1)}, bf16[4,2,128,128]{3,2,1,0:T(8,128)(2,1)S(1)}, u32[]{:S(2)}, u32[]{:S(2)}) %collective-permute-start.2) | collective-permute-done | bytes 262176 | tf_op jit(solution)/shard_map/ppermute | solution.py:26
  20.3 3.2 collective-permute-start.9
  23.5 2.6 collective-permute-done.3.refs_3_
  28.4 3.0 collective-permute-start.10
  31.4 3.7 %collective-permute-start.17 = (bf16[4,2,128,128]{3,2,1,0:T(8,128)(2,1)S(1)}, bf16[4,2,128,128]{3,2,1,0:T(8,128)(2,1)S(1)}, u32[]{:S(2)}, u32[]{:S(2)}) collective-permute-start(bf16[4,2,128,128]{3,2,1,0:T(8,128)(2,1)S(1)} %get-tuple-element.65.refs_9_), channel_id=1, source_target_pairs={{0,3},{1,0},{2,1},{3,2},{4,7},{5,4},{6,5},{7,6},{8,11},{9,8},{10,9... | collective-permute-start | bytes 786440 | tf_op jit(solution)/shard_map/ppermute | solution.py:26
  36.0 2.9 collective-permute-done.7.refs_3_
  40.8 3.2 collective-permute-done.17.refs_15_
  44.0 2.4 collective-permute-start.6
  46.4 4.2 %collective-permute-start.16 = (bf16[8,2,128,128]{3,2,1,0:T(8,128)(2,1)}, bf16[8,2,128,128]{3,2,1,0:T(8,128)(2,1)S(1)}, u32[]{:S(2)}, u32[]{:S(2)}) collective-permute-start(bf16[8,2,128,128]{3,2,1,0:T(8,128)(2,1)} %get-tuple-element.67.refs_8_), channel_id=1, source_target_pairs={{0,3},{1,0},{2,1},{3,2},{4,7},{5,4},{6,5},{7,6},{8,11},{9,8},{10,9... | collective-permute-start | bytes 1572872 | tf_op jit(solution)/shard_map/ppermute | solution.py:26
  50.6 3.5 %collective-permute-done.10.refs_6_.refs_5_ = bf16[8,2,128,128]{3,2,1,0:T(8,128)(2,1)S(1)} collective-permute-done((bf16[8,2,128,128]{3,2,1,0:T(8,128)(2,1)}, bf16[8,2,128,128]{3,2,1,0:T(8,128)(2,1)S(1)}, u32[]{:S(2)}, u32[]{:S(2)}) %collective-permute-start.10) | collective-permute-done | bytes 524320 | tf_op jit(solution)/shard_map/ppermute | solution.py:26
  57.8 4.0 %collective-permute-done.6.refs_2_.refs_3_ = bf16[8,2,128,128]{3,2,1,0:T(8,128)(2,1)S(1)} collective-permute-done((bf16[8,2,128,128]{3,2,1,0:T(8,128)(2,1)}, bf16[8,2,128,128]{3,2,1,0:T(8,128)(2,1)S(1)}, u32[]{:S(2)}, u32[]{:S(2)}) %collective-permute-start.6) | collective-permute-done | bytes 524320 | tf_op jit(solution)/shard_map/ppermute | solution.py:26
  61.9 5.4 %collective-permute-done.16.refs_14_.refs_2_ = bf16[8,2,128,128]{3,2,1,0:T(8,128)(2,1)S(1)} collective-permute-done((bf16[8,2,128,128]{3,2,1,0:T(8,128)(2,1)}, bf16[8,2,128,128]{3,2,1,0:T(8,128)(2,1)S(1)}, u32[]{:S(2)}, u32[]{:S(2)}) %collective-permute-start.16) | collective-permute-done | bytes 524320 | tf_op jit(solution)/shard_map/ppermute | solution.py:26
  67.3 3.6 %collective-permute-done.12.refs_10_.refs_0_ = bf16[8,2,128,128]{3,2,1,0:T(8,128)(2,1)S(1)} collective-permute-done((bf16[8,2,128,128]{3,2,1,0:T(8,128)(2,1)}, bf16[8,2,128,128]{3,2,1,0:T(8,128)(2,1)S(1)}, u32[]{:S(2)}, u32[]{:S(2)}) %collective-permute-start.12) | collective-permute-done | bytes 524320 | tf_op jit(solution)/shard_map/ppermute | solution.py:26
  71.7 6.7 %shard_map.66 = bf16[8,2,2,256,128]{4,3,2,1,0:T(8,128)(2,1)} custom-call(s32[3]{0:T(128)} %pad_add_fusion.place, s32[64]{0:T(128)} %reshape.10.pairs, s32[64]{0:T(128)} %size.11, bf16[8,2,128,128]{3,2,1,0:T(8,128)(2,1)} %get-tuple-element.66.refs_0_, bf16[4,2,128,128]{3,2,1,0:T(8,128)(2,1)} %copy-done.20, bf16[8,2,128,128]{3,2,1,0:T(8,128)(2,1)} %copy-done.7, ...), custom_call_target="tpu_custom_call" | custom-call | flops 536870912 | bytes 8388608 | tf_op jit(solution)/shard_map/pallas_call | solution.py:149
  78.5 4.6 %all-to-all-start = ((bf16[8,2,2,256,128]{4,3,2,1,0:T(8,128)(2,1)}), bf16[8,2,2,256,128]{4,3,2,1,0:T(8,128)(2,1)}, u32[]{:S(2)}, u32[]{:S(2)}) async-start(bf16[8,2,2,256,128]{4,3,2,1,0:T(8,128)(2,1)} %shard_map.66), calls=%async_computation | async-start | bytes 4194304 | tf_op jit(solution)/shard_map/all_to_all | solution.py:181
  86.6 5.8 %collective-permute-start.33 = (bf16[8,2,128,128]{3,2,1,0:T(8,128)(2,1)S(1)}, bf16[8,2,128,128]{3,2,1,0:T(8,128)(2,1)S(1)}, u32[]{:S(2)}, u32[]{:S(2)}) collective-permute-start(bf16[8,2,128,128]{3,2,1,0:T(8,128)(2,1)S(1)} %get-tuple-element.78.refs_0_), channel_id=1, source_target_pairs={{0,12},{1,13},{2,14},{3,15},{4,0},{5,1},{6,2},{7,3},{8,4},{9,5},{1... | collective-permute-start | bytes 1572872 | tf_op jit(solution)/shard_map/ppermute | solution.py:26
  93.4 22.1 %collective-permute-done.33.refs_3_ = bf16[8,2,128,128]{3,2,1,0:T(8,128)(2,1)S(1)} collective-permute-done((bf16[8,2,128,128]{3,2,1,0:T(8,128)(2,1)S(1)}, bf16[8,2,128,128]{3,2,1,0:T(8,128)(2,1)S(1)}, u32[]{:S(2)}, u32[]{:S(2)}) %collective-permute-start.33) | collective-permute-done | bytes 524320 | tf_op jit(solution)/shard_map/ppermute | solution.py:26
  117.8 3.8 %collective-permute-start.20 = (bf16[8,2,128,128]{3,2,1,0:T(8,128)(2,1)}, bf16[8,2,128,128]{3,2,1,0:T(8,128)(2,1)S(1)}, u32[]{:S(2)}, u32[]{:S(2)}) collective-permute-start(bf16[8,2,128,128]{3,2,1,0:T(8,128)(2,1)} %get-tuple-element.68.refs_0_), channel_id=1, source_target_pairs={{0,12},{1,13},{2,14},{3,15},{4,0},{5,1},{6,2},{7,3},{8,4},{9,5},{1... | collective-permute-start | bytes 1572872 | tf_op jit(solution)/shard_map/ppermute | solution.py:26
  123.3 6.9 %collective-permute-done.34.refs_5_ = bf16[8,2,128,128]{3,2,1,0:T(8,128)(2,1)} collective-permute-done((bf16[8,2,128,128]{3,2,1,0:T(8,128)(2,1)S(1)}, bf16[8,2,128,128]{3,2,1,0:T(8,128)(2,1)}, u32[]{:S(2)}, u32[]{:S(2)}) %collective-permute-start.34) | collective-permute-done | bytes 524320 | tf_op jit(solution)/shard_map/ppermute | solution.py:26
  130.2 6.8 %shard_map.70 = bf16[8,2,2,256,128]{4,3,2,1,0:T(8,128)(2,1)} custom-call(s32[3]{0:T(128)} %pad_add_fusion.place, s32[64]{0:T(128)} %reshape.10.pairs, s32[64]{0:T(128)} %size.11, bf16[8,2,128,128]{3,2,1,0:T(8,128)(2,1)} %copy-done.34, bf16[8,2,128,128]{3,2,1,0:T(8,128)(2,1)} %copy-done.56, bf16[8,2,128,128]{3,2,1,0:T(8,128)(2,1)} %copy-done.55, ...), custom_call_target="tpu_custom_call" | custom-call | flops 536870912 | bytes 8388608 | tf_op jit(solution)/shard_map/pallas_call | solution.py:149
  137.0 4.4 %all-to-all-start.1 = ((bf16[8,2,2,256,128]{4,3,2,1,0:T(8,128)(2,1)}), bf16[8,2,2,256,128]{4,3,2,1,0:T(8,128)(2,1)}, u32[]{:S(2)}, u32[]{:S(2)}) async-start(bf16[8,2,2,256,128]{4,3,2,1,0:T(8,128)(2,1)} %shard_map.70), calls=%async_computation.1 | async-start | bytes 4194304 | tf_op jit(solution)/shard_map/all_to_all | solution.py:181
  141.5 4.5 %collective-permute-start.18 = (bf16[8,2,128,128]{3,2,1,0:T(8,128)(2,1)}, bf16[8,2,128,128]{3,2,1,0:T(8,128)(2,1)S(1)}, u32[]{:S(2)}, u32[]{:S(2)}) collective-permute-start(bf16[8,2,128,128]{3,2,1,0:T(8,128)(2,1)} %get-tuple-element.68.refs_0_), channel_id=1, source_target_pairs={{0,4},{1,5},{2,6},{3,7},{4,8},{5,9},{6,10},{7,11},{8,12},{9,13},{1... | collective-permute-start | bytes 1572872 | tf_op jit(solution)/shard_map/ppermute | solution.py:26
  148.2 9.9 %collective-permute-done.19.refs_4_ = bf16[8,2,128,128]{3,2,1,0:T(8,128)(2,1)S(1)} collective-permute-done((bf16[8,2,128,128]{3,2,1,0:T(8,128)(2,1)}, bf16[8,2,128,128]{3,2,1,0:T(8,128)(2,1)S(1)}, u32[]{:S(2)}, u32[]{:S(2)}) %collective-permute-start.19) | collective-permute-done | bytes 524320 | tf_op jit(solution)/shard_map/ppermute | solution.py:26
  158.1 10.5 %collective-permute-done.18.refs_2_.refs_3_ = bf16[8,2,128,128]{3,2,1,0:T(8,128)(2,1)S(1)} collective-permute-done((bf16[8,2,128,128]{3,2,1,0:T(8,128)(2,1)}, bf16[8,2,128,128]{3,2,1,0:T(8,128)(2,1)S(1)}, u32[]{:S(2)}, u32[]{:S(2)}) %collective-permute-start.18) | collective-permute-done | bytes 524320 | tf_op jit(solution)/shard_map/ppermute | solution.py:26
  168.6 4.0 %collective-permute-done.21.refs_10_.refs_0_ = bf16[8,2,128,128]{3,2,1,0:T(8,128)(2,1)S(1)} collective-permute-done((bf16[8,2,128,128]{3,2,1,0:T(8,128)(2,1)}, bf16[8,2,128,128]{3,2,1,0:T(8,128)(2,1)S(1)}, u32[]{:S(2)}, u32[]{:S(2)}) %collective-permute-start.21) | collective-permute-done | bytes 524320 | tf_op jit(solution)/shard_map/ppermute | solution.py:26
  175.0 2.3 collective-permute-start.38
  178.8 11.2 %collective-permute-done.39.refs_3_ = bf16[8,2,128,128]{3,2,1,0:T(8,128)(2,1)S(1)} collective-permute-done((bf16[8,2,128,128]{3,2,1,0:T(8,128)(2,1)}, bf16[8,2,128,128]{3,2,1,0:T(8,128)(2,1)S(1)}, u32[]{:S(2)}, u32[]{:S(2)}) %collective-permute-start.39) | collective-permute-done | bytes 524320 | tf_op jit(solution)/shard_map/ppermute | solution.py:26
  190.0 6.6 %shard_map.68 = (bf16[2,2,256,128]{3,2,1,0:T(8,128)(2,1)}, bf16[2,2,256,128]{3,2,1,0:T(8,128)(2,1)}, bf16[2,2,256,128]{3,2,1,0:T(8,128)(2,1)}, bf16[2,2,256,128]...) custom-call(s32[3]{0:T(128)} %pad_add_fusion.place, ...), custom_call_target="tpu_custom_call" | custom-call | flops 536870912 | bytes 8388608 | tf_op jit(solution)/shard_map/pallas_call | solution.py:149
  196.7 5.1 %collective-permute-done.37.refs_1_ = bf16[8,2,128,128]{3,2,1,0:T(8,128)(2,1)S(1)} collective-permute-done((bf16[8,2,128,128]{3,2,1,0:T(8,128)(2,1)}, bf16[8,2,128,128]{3,2,1,0:T(8,128)(2,1)S(1)}, u32[]{:S(2)}, u32[]{:S(2)}) %collective-permute-start.37) | collective-permute-done | bytes 524320 | tf_op jit(solution)/shard_map/ppermute | solution.py:26
  205.4 6.7 %shard_map.72 = (bf16[2,2,128,128]{3,2,1,0:T(8,128)(2,1)}, bf16[2,2,128,128]{3,2,1,0:T(8,128)(2,1)}, bf16[2,2,128,128]{3,2,1,0:T(8,128)(2,1)}, bf16[2,2,128,128]...) custom-call(s32[3]{0:T(128)} %pad_add_fusion.place, ...), custom_call_target="tpu_custom_call" | custom-call | flops 536870912 | bytes 8388608 | tf_op jit(solution)/shard_map/pallas_call | solution.py:149
  212.2 4.6 %all-to-all-start.2 = ((bf16[8,2,2,128,128]{4,3,2,1,0:T(8,128)(2,1)}), bf16[8,2,2,128,128]{4,3,2,1,0:T(8,128)(2,1)S(1)}, u32[]{:S(2)}, u32[]{:S(2)}) async-start(bf16[8,2,2,128,128]{4,3,2,1,0:T(8,128)(2,1)} %get-tuple-element.106), calls=%async_computation.2 | async-start | bytes 2097152 | tf_op jit(solution)/shard_map/all_to_all | solution.py:181
  218.5 2.7 collective-permute-start.27
  224.7 12.9 %collective-permute-done.26.refs_4_ = bf16[2,2,256,128]{3,2,1,0:T(8,128)(2,1)S(1)} collective-permute-done((bf16[2,2,256,128]{3,2,1,0:T(8,128)(2,1)S(1)}, bf16[2,2,256,128]{3,2,1,0:T(8,128)(2,1)S(1)}, u32[]{:S(2)}, u32[]{:S(2)}) %collective-permute-start.26) | collective-permute-done | bytes 262176 | tf_op jit(solution)/shard_map/ppermute | solution.py:190
  238.1 6.5 %collective-permute-done.27.refs_5_ = bf16[2,2,256,128]{3,2,1,0:T(8,128)(2,1)S(1)} collective-permute-done((bf16[2,2,256,128]{3,2,1,0:T(8,128)(2,1)}, bf16[2,2,256,128]{3,2,1,0:T(8,128)(2,1)S(1)}, u32[]{:S(2)}, u32[]{:S(2)}) %collective-permute-start.27) | collective-permute-done | bytes 262176 | tf_op jit(solution)/shard_map/ppermute | solution.py:190
  244.6 4.6 %collective-permute-done.28.refs_6_ = bf16[2,2,256,128]{3,2,1,0:T(8,128)(2,1)S(1)} collective-permute-done((bf16[2,2,256,128]{3,2,1,0:T(8,128)(2,1)S(1)}, bf16[2,2,256,128]{3,2,1,0:T(8,128)(2,1)S(1)}, u32[]{:S(2)}, u32[]{:S(2)}) %collective-permute-start.28) | collective-permute-done | bytes 262176 | tf_op jit(solution)/shard_map/ppermute | solution.py:190
  253.1 3.2 collective-permute-start.47
  260.4 2.7 collective-permute-done.48.refs_16_
  263.1 2.3 collective-permute-done.49.refs_17_
  265.6 8.9 %shard_map.73 = (bf16[4,128,256]{2,1,0:T(8,128)(2,1)}, bf16[4,128,256]{2,1,0:T(8,128)(2,1)}, bf16[4,128,256]{2,1,0:T(8,128)(2,1)}, bf16[4,128,256]{2,1,0:T(8,128...) custom-call(s32[3]{0:T(128)} %pad_add_fusion.place, ...), custom_call_target="tpu_custom_call" | custom-call | flops 1073741824 | bytes 14680064 | tf_op jit(solution)/shard_map/pallas_call | solution.py:295
  277.8 5.0 %collective-permute-start.53 = (bf16[4,128,256]{2,1,0:T(8,128)(2,1)}, bf16[4,128,256]{2,1,0:T(8,128)(2,1)S(1)}, u32[]{:S(2)}, u32[]{:S(2)}) collective-permute-start(bf16[4,128,256]{2,1,0:T(8,128)(2,1)} %get-tuple-element.95), channel_id=1, source_target_pairs={{0,4},{1,5},{2,6},{3,7},{4,8},{5,9},{6,10},{7,11},{8,12},{9,13},{1... | collective-permute-start | bytes 786440 | tf_op jit(solution)/shard_map/ppermute | solution.py:26
  283.8 8.9 %shard_map.74 = (bf16[4,128,256]{2,1,0:T(8,128)(2,1)}, bf16[4,128,256]{2,1,0:T(8,128)(2,1)}, bf16[4,128,256]{2,1,0:T(8,128)(2,1)}, bf16[4,128,256]{2,1,0:T(8,128...) custom-call(s32[3]{0:T(128)} %pad_add_fusion.place, ...), custom_call_target="tpu_custom_call" | custom-call | flops 1073741824 | bytes 14680064 | tf_op jit(solution)/shard_map/pallas_call | solution.py:295
  292.7 2.8 collective-permute-start.55
  300.3 3.0 collective-permute-start.66
  303.3 6.3 %collective-permute-done.62.refs_1_ = bf16[4,128,256]{2,1,0:T(8,128)(2,1)S(1)} collective-permute-done((bf16[4,128,256]{2,1,0:T(8,128)(2,1)}, bf16[4,128,256]{2,1,0:T(8,128)(2,1)S(1)}, u32[]{:S(2)}, u32[]{:S(2)}) %collective-permute-start.62) | collective-permute-done | bytes 262176 | tf_op jit(solution)/shard_map/ppermute | solution.py:26
  320.8 2.4 collective-permute-start.69
  326.5 2.4 collective-permute-start.73
  (273 shorter events, 74.3 us)
Async XLA Ops:
  1.5 15.4 %collective-permute-start.2 = (bf16[4,2,128,128]{3,2,1,0:T(8,128)(2,1)S(1)}, bf16[4,2,128,128]{3,2,1,0:T(8,128)(2,1)S(1)}, u32[]{:S(2)}, u32[]{:S(2)}) collective-permute-start(bf16[4,2,128,128]{3,2,1,0:T(8,128)(2,1)S(1)} %get-tuple-element.64.refs_1_), channel_id=1, source_target_pairs={{0,3},{1,0},{2,1},{3,2},{4,7},{5,4},{6,5},{7,6},{8,11},{9,8},{10,9... | collective-permute-start | bytes 786440 | tf_op jit(solution)/shard_map/ppermute | solution.py:26
  5.7 14.6 %collective-permute-start = (bf16[4,2,128,128]{3,2,1,0:T(8,128)(2,1)S(1)}, bf16[4,2,128,128]{3,2,1,0:T(8,128)(2,1)S(1)}, u32[]{:S(2)}, u32[]{:S(2)}) collective-permute-start(bf16[4,2,128,128]{3,2,1,0:T(8,128)(2,1)S(1)} %get-tuple-element.64.refs_1_), channel_id=1, source_target_pairs={{0,1},{1,2},{2,3},{3,0},{4,5},{5,6},{6,7},{7,4},{8,9},{9,10},{10,1... | collective-permute-start | bytes 786440 | tf_op jit(solution)/shard_map/ppermute | solution.py:26
  7.0 16.5 %collective-permute-start.5 = (bf16[4,2,128,128]{3,2,1,0:T(8,128)(2,1)S(1)}, bf16[4,2,128,128]{3,2,1,0:T(8,128)(2,1)S(1)}, u32[]{:S(2)}, u32[]{:S(2)}) collective-permute-start(bf16[4,2,128,128]{3,2,1,0:T(8,128)(2,1)S(1)} %get-tuple-element.65.refs_9_), channel_id=1, source_target_pairs={{0,12},{1,13},{2,14},{3,15},{4,0},{5,1},{6,2},{7,3},{8,4},{9,5},{1... | collective-permute-start | bytes 786440 | tf_op jit(solution)/shard_map/ppermute | solution.py:26
  18.5 16.6 %collective-permute-start.11 = (bf16[4,2,128,128]{3,2,1,0:T(8,128)(2,1)S(1)}, bf16[4,2,128,128]{3,2,1,0:T(8,128)(2,1)S(1)}, u32[]{:S(2)}, u32[]{:S(2)}) collective-permute-start(bf16[4,2,128,128]{3,2,1,0:T(8,128)(2,1)S(1)} %get-tuple-element.64.refs_1_), channel_id=1, source_target_pairs={{0,12},{1,13},{2,14},{3,15},{4,0},{5,1},{6,2},{7,3},{8,4},{9,5},{1... | collective-permute-start | bytes 786440 | tf_op jit(solution)/shard_map/ppermute | solution.py:26
  20.3 15.2 %collective-permute-start.9 = (bf16[4,2,128,128]{3,2,1,0:T(8,128)(2,1)S(1)}, bf16[4,2,128,128]{3,2,1,0:T(8,128)(2,1)S(1)}, u32[]{:S(2)}, u32[]{:S(2)}) collective-permute-start(bf16[4,2,128,128]{3,2,1,0:T(8,128)(2,1)S(1)} %get-tuple-element.64.refs_1_), channel_id=1, source_target_pairs={{0,8},{1,9},{2,10},{3,11},{4,12},{5,13},{6,14},{7,15},{8,0},{9,1},... | collective-permute-start | bytes 786440 | tf_op jit(solution)/shard_map/ppermute | solution.py:26
  28.4 25.8 %collective-permute-start.10 = (bf16[8,2,128,128]{3,2,1,0:T(8,128)(2,1)}, bf16[8,2,128,128]{3,2,1,0:T(8,128)(2,1)S(1)}, u32[]{:S(2)}, u32[]{:S(2)}) collective-permute-start(bf16[8,2,128,128]{3,2,1,0:T(8,128)(2,1)} %get-tuple-element.66.refs_0_), channel_id=1, source_target_pairs={{0,12},{1,13},{2,14},{3,15},{4,0},{5,1},{6,2},{7,3},{8,4},{9,5},{1... | collective-permute-start | bytes 1572872 | tf_op jit(solution)/shard_map/ppermute | solution.py:26
  35.5 15.1 %collective-permute-start.13 = (bf16[4,2,128,128]{3,2,1,0:T(8,128)(2,1)S(1)}, bf16[4,2,128,128]{3,2,1,0:T(8,128)(2,1)S(1)}, u32[]{:S(2)}, u32[]{:S(2)}) collective-permute-start(bf16[4,2,128,128]{3,2,1,0:T(8,128)(2,1)S(1)} %get-tuple-element.65.refs_9_), channel_id=1, source_target_pairs={{0,1},{1,2},{2,3},{3,0},{4,5},{5,6},{6,7},{7,4},{8,9},{9,10},{10,1... | collective-permute-start | bytes 786440 | tf_op jit(solution)/shard_map/ppermute | solution.py:26
  39.0 18.9 %collective-permute-start.8 = (bf16[8,2,128,128]{3,2,1,0:T(8,128)(2,1)}, bf16[8,2,128,128]{3,2,1,0:T(8,128)(2,1)S(1)}, u32[]{:S(2)}, u32[]{:S(2)}) collective-permute-start(bf16[8,2,128,128]{3,2,1,0:T(8,128)(2,1)} %get-tuple-element.66.refs_0_), channel_id=1, source_target_pairs={{0,8},{1,9},{2,10},{3,11},{4,12},{5,13},{6,14},{7,15},{8,0},{9,1},... | collective-permute-start | bytes 1572872 | tf_op jit(solution)/shard_map/ppermute | solution.py:26
  44.0 17.9 %collective-permute-start.6 = (bf16[8,2,128,128]{3,2,1,0:T(8,128)(2,1)}, bf16[8,2,128,128]{3,2,1,0:T(8,128)(2,1)S(1)}, u32[]{:S(2)}, u32[]{:S(2)}) collective-permute-start(bf16[8,2,128,128]{3,2,1,0:T(8,128)(2,1)} %get-tuple-element.66.refs_0_), channel_id=1, source_target_pairs={{0,4},{1,5},{2,6},{3,7},{4,8},{5,9},{6,10},{7,11},{8,12},{9,13},{1... | collective-permute-start | bytes 1572872 | tf_op jit(solution)/shard_map/ppermute | solution.py:26
  46.4 20.9 %collective-permute-start.16 = (bf16[8,2,128,128]{3,2,1,0:T(8,128)(2,1)}, bf16[8,2,128,128]{3,2,1,0:T(8,128)(2,1)S(1)}, u32[]{:S(2)}, u32[]{:S(2)}) collective-permute-start(bf16[8,2,128,128]{3,2,1,0:T(8,128)(2,1)} %get-tuple-element.67.refs_8_), channel_id=1, source_target_pairs={{0,3},{1,0},{2,1},{3,2},{4,7},{5,4},{6,5},{7,6},{8,11},{9,8},{10,9... | collective-permute-start | bytes 1572872 | tf_op jit(solution)/shard_map/ppermute | solution.py:26
  50.6 16.6 %collective-permute-start.14 = (bf16[8,2,128,128]{3,2,1,0:T(8,128)(2,1)}, bf16[8,2,128,128]{3,2,1,0:T(8,128)(2,1)S(1)}, u32[]{:S(2)}, u32[]{:S(2)}) collective-permute-start(bf16[8,2,128,128]{3,2,1,0:T(8,128)(2,1)} %get-tuple-element.67.refs_8_), channel_id=1, source_target_pairs={{0,2},{1,3},{2,0},{3,1},{4,6},{5,7},{6,4},{7,5},{8,10},{9,11},{10,... | collective-permute-start | bytes 1572872 | tf_op jit(solution)/shard_map/ppermute | solution.py:26
  54.1 16.7 %collective-permute-start.12 = (bf16[8,2,128,128]{3,2,1,0:T(8,128)(2,1)}, bf16[8,2,128,128]{3,2,1,0:T(8,128)(2,1)S(1)}, u32[]{:S(2)}, u32[]{:S(2)}) collective-permute-start(bf16[8,2,128,128]{3,2,1,0:T(8,128)(2,1)} %get-tuple-element.67.refs_8_), channel_id=1, source_target_pairs={{0,1},{1,2},{2,3},{3,0},{4,5},{5,6},{6,7},{7,4},{8,9},{9,10},{10,1... | collective-permute-start | bytes 1572872 | tf_op jit(solution)/shard_map/ppermute | solution.py:26
  78.5 58.5 %all-to-all-start = ((bf16[8,2,2,256,128]{4,3,2,1,0:T(8,128)(2,1)}), bf16[8,2,2,256,128]{4,3,2,1,0:T(8,128)(2,1)}, u32[]{:S(2)}, u32[]{:S(2)}) async-start(bf16[8,2,2,256,128]{4,3,2,1,0:T(8,128)(2,1)} %shard_map.66), calls=%async_computation | async-start | bytes 4194304 | tf_op jit(solution)/shard_map/all_to_all | solution.py:181
  86.6 28.9 %collective-permute-start.33 = (bf16[8,2,128,128]{3,2,1,0:T(8,128)(2,1)S(1)}, bf16[8,2,128,128]{3,2,1,0:T(8,128)(2,1)S(1)}, u32[]{:S(2)}, u32[]{:S(2)}) collective-permute-start(bf16[8,2,128,128]{3,2,1,0:T(8,128)(2,1)S(1)} %get-tuple-element.78.refs_0_), channel_id=1, source_target_pairs={{0,12},{1,13},{2,14},{3,15},{4,0},{5,1},{6,2},{7,3},{8,4},{9,5},{1... | collective-permute-start | bytes 1572872 | tf_op jit(solution)/shard_map/ppermute | solution.py:26
  92.4 25.4 %collective-permute-start.32 = (bf16[8,2,128,128]{3,2,1,0:T(8,128)(2,1)S(1)}, bf16[8,2,128,128]{3,2,1,0:T(8,128)(2,1)S(1)}, u32[]{:S(2)}, u32[]{:S(2)}) collective-permute-start(bf16[8,2,128,128]{3,2,1,0:T(8,128)(2,1)S(1)} %get-tuple-element.78.refs_0_), channel_id=1, source_target_pairs={{0,8},{1,9},{2,10},{3,11},{4,12},{5,13},{6,14},{7,15},{8,0},{9,1},... | collective-permute-start | bytes 1572872 | tf_op jit(solution)/shard_map/ppermute | solution.py:26
  92.4 29.1 %collective-permute-start.31 = (bf16[8,2,128,128]{3,2,1,0:T(8,128)(2,1)S(1)}, bf16[8,2,128,128]{3,2,1,0:T(8,128)(2,1)S(1)}, u32[]{:S(2)}, u32[]{:S(2)}) collective-permute-start(bf16[8,2,128,128]{3,2,1,0:T(8,128)(2,1)S(1)} %get-tuple-element.78.refs_0_), channel_id=1, source_target_pairs={{0,4},{1,5},{2,6},{3,7},{4,8},{5,9},{6,10},{7,11},{8,12},{9,13},{1... | collective-permute-start | bytes 1572872 | tf_op jit(solution)/shard_map/ppermute | solution.py:26
  93.4 28.2 %collective-permute-start.36 = (bf16[8,2,128,128]{3,2,1,0:T(8,128)(2,1)S(1)}, bf16[8,2,128,128]{3,2,1,0:T(8,128)(2,1)S(1)}, u32[]{:S(2)}, u32[]{:S(2)}) collective-permute-start(bf16[8,2,128,128]{3,2,1,0:T(8,128)(2,1)S(1)} %get-tuple-element.79.refs_4_), channel_id=1, source_target_pairs={{0,3},{1,0},{2,1},{3,2},{4,7},{5,4},{6,5},{7,6},{8,11},{9,8},{10,9... | collective-permute-start | bytes 1572872 | tf_op jit(solution)/shard_map/ppermute | solution.py:26
  93.4 28.2 %collective-permute-start.35 = (bf16[8,2,128,128]{3,2,1,0:T(8,128)(2,1)S(1)}, bf16[8,2,128,128]{3,2,1,0:T(8,128)(2,1)S(1)}, u32[]{:S(2)}, u32[]{:S(2)}) collective-permute-start(bf16[8,2,128,128]{3,2,1,0:T(8,128)(2,1)S(1)} %get-tuple-element.79.refs_4_), channel_id=1, source_target_pairs={{0,2},{1,3},{2,0},{3,1},{4,6},{5,7},{6,4},{7,5},{8,10},{9,11},{10,... | collective-permute-start | bytes 1572872 | tf_op jit(solution)/shard_map/ppermute | solution.py:26
  115.5 14.7 %collective-permute-start.34 = (bf16[8,2,128,128]{3,2,1,0:T(8,128)(2,1)S(1)}, bf16[8,2,128,128]{3,2,1,0:T(8,128)(2,1)}, u32[]{:S(2)}, u32[]{:S(2)}) collective-permute-start(bf16[8,2,128,128]{3,2,1,0:T(8,128)(2,1)S(1)} %get-tuple-element.79.refs_4_), channel_id=1, source_target_pairs={{0,1},{1,2},{2,3},{3,0},{4,5},{5,6},{6,7},{7,4},{8,9},{9,10},{10,1... | collective-permute-start | bytes 1572872 | tf_op jit(solution)/shard_map/ppermute | solution.py:26
  117.8 29.4 %collective-permute-start.20 = (bf16[8,2,128,128]{3,2,1,0:T(8,128)(2,1)}, bf16[8,2,128,128]{3,2,1,0:T(8,128)(2,1)S(1)}, u32[]{:S(2)}, u32[]{:S(2)}) collective-permute-start(bf16[8,2,128,128]{3,2,1,0:T(8,128)(2,1)} %get-tuple-element.68.refs_0_), channel_id=1, source_target_pairs={{0,12},{1,13},{2,14},{3,15},{4,0},{5,1},{6,2},{7,3},{8,4},{9,5},{1... | collective-permute-start | bytes 1572872 | tf_op jit(solution)/shard_map/ppermute | solution.py:26
  137.0 75.2 %all-to-all-start.1 = ((bf16[8,2,2,256,128]{4,3,2,1,0:T(8,128)(2,1)}), bf16[8,2,2,256,128]{4,3,2,1,0:T(8,128)(2,1)}, u32[]{:S(2)}, u32[]{:S(2)}) async-start(bf16[8,2,2,256,128]{4,3,2,1,0:T(8,128)(2,1)} %shard_map.70), calls=%async_computation.1 | async-start | bytes 4194304 | tf_op jit(solution)/shard_map/all_to_all | solution.py:181
  141.4 16.6 %collective-permute-start.19 = (bf16[8,2,128,128]{3,2,1,0:T(8,128)(2,1)}, bf16[8,2,128,128]{3,2,1,0:T(8,128)(2,1)S(1)}, u32[]{:S(2)}, u32[]{:S(2)}) collective-permute-start(bf16[8,2,128,128]{3,2,1,0:T(8,128)(2,1)} %get-tuple-element.68.refs_0_), channel_id=1, source_target_pairs={{0,8},{1,9},{2,10},{3,11},{4,12},{5,13},{6,14},{7,15},{8,0},{9,1},... | collective-permute-start | bytes 1572872 | tf_op jit(solution)/shard_map/ppermute | solution.py:26
  141.5 27.1 %collective-permute-start.18 = (bf16[8,2,128,128]{3,2,1,0:T(8,128)(2,1)}, bf16[8,2,128,128]{3,2,1,0:T(8,128)(2,1)S(1)}, u32[]{:S(2)}, u32[]{:S(2)}) collective-permute-start(bf16[8,2,128,128]{3,2,1,0:T(8,128)(2,1)} %get-tuple-element.68.refs_0_), channel_id=1, source_target_pairs={{0,4},{1,5},{2,6},{3,7},{4,8},{5,9},{6,10},{7,11},{8,12},{9,13},{1... | collective-permute-start | bytes 1572872 | tf_op jit(solution)/shard_map/ppermute | solution.py:26
  146.0 22.5 %collective-permute-start.23 = (bf16[8,2,128,128]{3,2,1,0:T(8,128)(2,1)}, bf16[8,2,128,128]{3,2,1,0:T(8,128)(2,1)S(1)}, u32[]{:S(2)}, u32[]{:S(2)}) collective-permute-start(bf16[8,2,128,128]{3,2,1,0:T(8,128)(2,1)} %get-tuple-element.69.refs_8_), channel_id=1, source_target_pairs={{0,3},{1,0},{2,1},{3,2},{4,7},{5,4},{6,5},{7,6},{8,11},{9,8},{10,9... | collective-permute-start | bytes 1572872 | tf_op jit(solution)/shard_map/ppermute | solution.py:26
  146.0 22.5 %collective-permute-start.22 = (bf16[8,2,128,128]{3,2,1,0:T(8,128)(2,1)}, bf16[8,2,128,128]{3,2,1,0:T(8,128)(2,1)S(1)}, u32[]{:S(2)}, u32[]{:S(2)}) collective-permute-start(bf16[8,2,128,128]{3,2,1,0:T(8,128)(2,1)} %get-tuple-element.69.refs_8_), channel_id=1, source_target_pairs={{0,2},{1,3},{2,0},{3,1},{4,6},{5,7},{6,4},{7,5},{8,10},{9,11},{10,... | collective-permute-start | bytes 1572872 | tf_op jit(solution)/shard_map/ppermute | solution.py:26
  147.2 25.4 %collective-permute-start.21 = (bf16[8,2,128,128]{3,2,1,0:T(8,128)(2,1)}, bf16[8,2,128,128]{3,2,1,0:T(8,128)(2,1)S(1)}, u32[]{:S(2)}, u32[]{:S(2)}) collective-permute-start(bf16[8,2,128,128]{3,2,1,0:T(8,128)(2,1)} %get-tuple-element.69.refs_8_), channel_id=1, source_target_pairs={{0,1},{1,2},{2,3},{3,0},{4,5},{5,6},{6,7},{7,4},{8,9},{9,10},{10,1... | collective-permute-start | bytes 1572872 | tf_op jit(solution)/shard_map/ppermute | solution.py:26
  174.9 15.1 %collective-permute-start.39 = (bf16[8,2,128,128]{3,2,1,0:T(8,128)(2,1)}, bf16[8,2,128,128]{3,2,1,0:T(8,128)(2,1)S(1)}, u32[]{:S(2)}, u32[]{:S(2)}) collective-permute-start(bf16[8,2,128,128]{3,2,1,0:T(8,128)(2,1)} %get-tuple-element.80.refs_0_), channel_id=1, source_target_pairs={{0,12},{1,13},{2,14},{3,15},{4,0},{5,1},{6,2},{7,3},{8,4},{9,5},{1... | collective-permute-start | bytes 1572872 | tf_op jit(solution)/shard_map/ppermute | solution.py:26
  175.0 21.6 %collective-permute-start.38 = (bf16[8,2,128,128]{3,2,1,0:T(8,128)(2,1)}, bf16[8,2,128,128]{3,2,1,0:T(8,128)(2,1)S(1)}, u32[]{:S(2)}, u32[]{:S(2)}) collective-permute-start(bf16[8,2,128,128]{3,2,1,0:T(8,128)(2,1)} %get-tuple-element.80.refs_0_), channel_id=1, source_target_pairs={{0,8},{1,9},{2,10},{3,11},{4,12},{5,13},{6,14},{7,15},{8,0},{9,1},... | collective-permute-start | bytes 1572872 | tf_op jit(solution)/shard_map/ppermute | solution.py:26
  177.3 24.5 %collective-permute-start.37 = (bf16[8,2,128,128]{3,2,1,0:T(8,128)(2,1)}, bf16[8,2,128,128]{3,2,1,0:T(8,128)(2,1)S(1)}, u32[]{:S(2)}, u32[]{:S(2)}) collective-permute-start(bf16[8,2,128,128]{3,2,1,0:T(8,128)(2,1)} %get-tuple-element.80.refs_0_), channel_id=1, source_target_pairs={{0,4},{1,5},{2,6},{3,7},{4,8},{5,9},{6,10},{7,11},{8,12},{9,13},{1... | collective-permute-start | bytes 1572872 | tf_op jit(solution)/shard_map/ppermute | solution.py:26
  177.3 26.2 %collective-permute-start.42 = (bf16[8,2,128,128]{3,2,1,0:T(8,128)(2,1)}, bf16[8,2,128,128]{3,2,1,0:T(8,128)(2,1)S(1)}, u32[]{:S(2)}, u32[]{:S(2)}) collective-permute-start(bf16[8,2,128,128]{3,2,1,0:T(8,128)(2,1)} %get-tuple-element.81.refs_4_), channel_id=1, source_target_pairs={{0,3},{1,0},{2,1},{3,2},{4,7},{5,4},{6,5},{7,6},{8,11},{9,8},{10,9... | collective-permute-start | bytes 1572872 | tf_op jit(solution)/shard_map/ppermute | solution.py:26
  178.5 25.0 %collective-permute-start.41 = (bf16[8,2,128,128]{3,2,1,0:T(8,128)(2,1)}, bf16[8,2,128,128]{3,2,1,0:T(8,128)(2,1)S(1)}, u32[]{:S(2)}, u32[]{:S(2)}) collective-permute-start(bf16[8,2,128,128]{3,2,1,0:T(8,128)(2,1)} %get-tuple-element.81.refs_4_), channel_id=1, source_target_pairs={{0,2},{1,3},{2,0},{3,1},{4,6},{5,7},{6,4},{7,5},{8,10},{9,11},{10,... | collective-permute-start | bytes 1572872 | tf_op jit(solution)/shard_map/ppermute | solution.py:26
  190.0 14.7 %collective-permute-start.40 = (bf16[8,2,128,128]{3,2,1,0:T(8,128)(2,1)}, bf16[8,2,128,128]{3,2,1,0:T(8,128)(2,1)S(1)}, u32[]{:S(2)}, u32[]{:S(2)}) collective-permute-start(bf16[8,2,128,128]{3,2,1,0:T(8,128)(2,1)} %get-tuple-element.81.refs_4_), channel_id=1, source_target_pairs={{0,1},{1,2},{2,3},{3,0},{4,5},{5,6},{6,7},{7,4},{8,9},{9,10},{10,1... | collective-permute-start | bytes 1572872 | tf_op jit(solution)/shard_map/ppermute | solution.py:26
  196.6 25.1 %collective-permute-start.24 = (bf16[2,2,256,128]{3,2,1,0:T(8,128)(2,1)}, bf16[2,2,256,128]{3,2,1,0:T(8,128)(2,1)S(1)}, u32[]{:S(2)}, u32[]{:S(2)}) collective-permute-start(bf16[2,2,256,128]{3,2,1,0:T(8,128)(2,1)} %get-tuple-element.71), channel_id=1, source_target_pairs={{0,16},{16,0},{32,48},{48,32},{64,80},{80,64},{96,112},{112,96},{1... | collective-permute-start | bytes 786440 | tf_op jit(solution)/shard_map/ppermute | solution.py:190
  201.8 21.2 %collective-permute-start.25 = (bf16[2,2,256,128]{3,2,1,0:T(8,128)(2,1)}, bf16[2,2,256,128]{3,2,1,0:T(8,128)(2,1)S(1)}, u32[]{:S(2)}, u32[]{:S(2)}) collective-permute-start(bf16[2,2,256,128]{3,2,1,0:T(8,128)(2,1)} %get-tuple-element.72), channel_id=1, source_target_pairs={{0,32},{16,48},{32,64},{48,80},{64,96},{80,112},{96,0},{112,16},{1... | collective-permute-start | bytes 786440 | tf_op jit(solution)/shard_map/ppermute | solution.py:190
  212.2 70.6 %all-to-all-start.2 = ((bf16[8,2,2,128,128]{4,3,2,1,0:T(8,128)(2,1)}), bf16[8,2,2,128,128]{4,3,2,1,0:T(8,128)(2,1)S(1)}, u32[]{:S(2)}, u32[]{:S(2)}) async-start(bf16[8,2,2,128,128]{4,3,2,1,0:T(8,128)(2,1)} %get-tuple-element.106), calls=%async_computation.2 | async-start | bytes 2097152 | tf_op jit(solution)/shard_map/all_to_all | solution.py:181
  216.8 20.9 %collective-permute-start.26 = (bf16[2,2,256,128]{3,2,1,0:T(8,128)(2,1)S(1)}, bf16[2,2,256,128]{3,2,1,0:T(8,128)(2,1)S(1)}, u32[]{:S(2)}, u32[]{:S(2)}) collective-permute-start(bf16[2,2,256,128]{3,2,1,0:T(8,128)(2,1)S(1)} %copy-done.72), channel_id=1, source_target_pairs={{0,48},{16,32},{32,80},{48,64},{64,112},{80,96},{96,16},{112,0},{1... | collective-permute-start | bytes 786440 | tf_op jit(solution)/shard_map/ppermute | solution.py:190
  218.5 26.0 %collective-permute-start.27 = (bf16[2,2,256,128]{3,2,1,0:T(8,128)(2,1)}, bf16[2,2,256,128]{3,2,1,0:T(8,128)(2,1)S(1)}, u32[]{:S(2)}, u32[]{:S(2)}) collective-permute-start(bf16[2,2,256,128]{3,2,1,0:T(8,128)(2,1)} %get-tuple-element.74), channel_id=1, source_target_pairs={{0,64},{16,80},{32,96},{48,112},{64,0},{80,16},{96,32},{112,48},{1... | collective-permute-start | bytes 786440 | tf_op jit(solution)/shard_map/ppermute | solution.py:190
  221.2 27.9 %collective-permute-start.28 = (bf16[2,2,256,128]{3,2,1,0:T(8,128)(2,1)S(1)}, bf16[2,2,256,128]{3,2,1,0:T(8,128)(2,1)S(1)}, u32[]{:S(2)}, u32[]{:S(2)}) collective-permute-start(bf16[2,2,256,128]{3,2,1,0:T(8,128)(2,1)S(1)} %copy-done.71), channel_id=1, source_target_pairs={{0,80},{16,64},{32,112},{48,96},{64,16},{80,0},{96,48},{112,32},{1... | collective-permute-start | bytes 786440 | tf_op jit(solution)/shard_map/ppermute | solution.py:190
  221.8 27.4 %collective-permute-start.29 = (bf16[2,2,256,128]{3,2,1,0:T(8,128)(2,1)}, bf16[2,2,256,128]{3,2,1,0:T(8,128)(2,1)S(1)}, u32[]{:S(2)}, u32[]{:S(2)}) collective-permute-start(bf16[2,2,256,128]{3,2,1,0:T(8,128)(2,1)} %get-tuple-element.76), channel_id=1, source_target_pairs={{0,96},{16,112},{32,0},{48,16},{64,32},{80,48},{96,64},{112,80},{1... | collective-permute-start | bytes 786440 | tf_op jit(solution)/shard_map/ppermute | solution.py:190
  223.1 30.1 %collective-permute-start.30 = (bf16[2,2,256,128]{3,2,1,0:T(8,128)(2,1)}, bf16[2,2,256,128]{3,2,1,0:T(8,128)(2,1)S(1)}, u32[]{:S(2)}, u32[]{:S(2)}) collective-permute-start(bf16[2,2,256,128]{3,2,1,0:T(8,128)(2,1)} %get-tuple-element.77), channel_id=1, source_target_pairs={{0,112},{16,96},{32,16},{48,0},{64,48},{80,32},{96,80},{112,64},{1... | collective-permute-start | bytes 786440 | tf_op jit(solution)/shard_map/ppermute | solution.py:190
  237.6 18.8 %collective-permute-start.43 = (bf16[2,2,128,128]{3,2,1,0:T(8,128)(2,1)}, bf16[2,2,128,128]{3,2,1,0:T(8,128)(2,1)S(1)}, u32[]{:S(2)}, u32[]{:S(2)}) collective-permute-start(bf16[2,2,128,128]{3,2,1,0:T(8,128)(2,1)} %get-tuple-element.83), channel_id=1, source_target_pairs={{0,16},{16,0},{32,48},{48,32},{64,80},{80,64},{96,112},{112,96},{1... | collective-permute-start | bytes 393224 | tf_op jit(solution)/shard_map/ppermute | solution.py:190
  274.5 18.2 %collective-permute-start.50 = (bf16[4,128,256]{2,1,0:T(8,128)(2,1)}, bf16[4,128,256]{2,1,0:T(8,128)(2,1)S(1)}, u32[]{:S(2)}, u32[]{:S(2)}) collective-permute-start(bf16[4,128,256]{2,1,0:T(8,128)(2,1)} %get-tuple-element.91), channel_id=1, source_target_pairs={{0,1},{1,2},{2,3},{3,0},{4,5},{5,6},{6,7},{7,4},{8,9},{9,10},{10,1... | collective-permute-start | bytes 786440 | tf_op jit(solution)/shard_map/ppermute | solution.py:26
  274.6 21.0 %collective-permute-start.51 = (bf16[4,128,256]{2,1,0:T(8,128)(2,1)}, bf16[4,128,256]{2,1,0:T(8,128)(2,1)S(1)}, u32[]{:S(2)}, u32[]{:S(2)}) collective-permute-start(bf16[4,128,256]{2,1,0:T(8,128)(2,1)} %get-tuple-element.92), channel_id=1, source_target_pairs={{0,2},{1,3},{2,0},{3,1},{4,6},{5,7},{6,4},{7,5},{8,10},{9,11},{10,... | collective-permute-start | bytes 786440 | tf_op jit(solution)/shard_map/ppermute | solution.py:26
  276.9 18.7 %collective-permute-start.52 = (bf16[4,128,256]{2,1,0:T(8,128)(2,1)}, bf16[4,128,256]{2,1,0:T(8,128)(2,1)S(1)}, u32[]{:S(2)}, u32[]{:S(2)}) collective-permute-start(bf16[4,128,256]{2,1,0:T(8,128)(2,1)} %get-tuple-element.93), channel_id=1, source_target_pairs={{0,3},{1,0},{2,1},{3,2},{4,7},{5,4},{6,5},{7,6},{8,11},{9,8},{10,9... | collective-permute-start | bytes 786440 | tf_op jit(solution)/shard_map/ppermute | solution.py:26
  277.8 19.2 %collective-permute-start.53 = (bf16[4,128,256]{2,1,0:T(8,128)(2,1)}, bf16[4,128,256]{2,1,0:T(8,128)(2,1)S(1)}, u32[]{:S(2)}, u32[]{:S(2)}) collective-permute-start(bf16[4,128,256]{2,1,0:T(8,128)(2,1)} %get-tuple-element.95), channel_id=1, source_target_pairs={{0,4},{1,5},{2,6},{3,7},{4,8},{5,9},{6,10},{7,11},{8,12},{9,13},{1... | collective-permute-start | bytes 786440 | tf_op jit(solution)/shard_map/ppermute | solution.py:26
  282.8 16.1 %collective-permute-start.54 = (bf16[4,128,256]{2,1,0:T(8,128)(2,1)}, bf16[4,128,256]{2,1,0:T(8,128)(2,1)S(1)}, u32[]{:S(2)}, u32[]{:S(2)}) collective-permute-start(bf16[4,128,256]{2,1,0:T(8,128)(2,1)} %get-tuple-element.96), channel_id=1, source_target_pairs={{0,8},{1,9},{2,10},{3,11},{4,12},{5,13},{6,14},{7,15},{8,0},{9,1},... | collective-permute-start | bytes 786440 | tf_op jit(solution)/shard_map/ppermute | solution.py:26
  295.6 15.3 %collective-permute-start.63 = (bf16[4,128,256]{2,1,0:T(8,128)(2,1)}, bf16[4,128,256]{2,1,0:T(8,128)(2,1)S(1)}, u32[]{:S(2)}, u32[]{:S(2)}) collective-permute-start(bf16[4,128,256]{2,1,0:T(8,128)(2,1)} %get-tuple-element.109), channel_id=1, source_target_pairs={{0,2},{1,3},{2,0},{3,1},{4,6},{5,7},{6,4},{7,5},{8,10},{9,11},{10,... | collective-permute-start | bytes 786440 | tf_op jit(solution)/shard_map/ppermute | solution.py:26
  297.1 14.8 %collective-permute-start.64 = (bf16[4,128,256]{2,1,0:T(8,128)(2,1)}, bf16[4,128,256]{2,1,0:T(8,128)(2,1)S(1)}, u32[]{:S(2)}, u32[]{:S(2)}) collective-permute-start(bf16[4,128,256]{2,1,0:T(8,128)(2,1)} %get-tuple-element.110), channel_id=1, source_target_pairs={{0,3},{1,0},{2,1},{3,2},{4,7},{5,4},{6,5},{7,6},{8,11},{9,8},{10,9... | collective-permute-start | bytes 786440 | tf_op jit(solution)/shard_map/ppermute | solution.py:26
  (103 other events, 1575.5 us)

commit v4 on v3

--- a/solution.py
+++ b/solution.py
@@ -14,7 +14,7 @@
 BF16 = jnp.bfloat16
 F32 = jnp.float32
 CHUNKS = (2, 2, 2, 2)
-MODES = ((False,), (True,), (False,), (True, False))
+TURNED = (False, True, False, True)
 
 
 def move(value, step_y, step_z):
@@ -55,20 +55,24 @@
             out_specs=[pl.BlockSpec(shape, lambda i: (0, 0, 0, 0)) for shape in shapes],
             scratch_shapes=[pltpu.SemaphoreType.DMA((sum(len(plan) for plan in plans),))],
         ),
-        compiler_params=pltpu.CompilerParams(vmem_limit_bytes=8 << 20),
+        compiler_params=pltpu.CompilerParams(vmem_limit_bytes=60 << 20),
         cost_estimate=pl.CostEstimate(flops=0, bytes_accessed=3 << 20, transcendentals=0),
     )(wave, *gots)
 
 
-def left_kernel(first_sector, modes, plan, place, pairs, size, *refs):
-    split = len(modes)
+def left_kernel(first_sector, turned, plan, place, pairs, size, *refs):
     total = 1 + max(entry[0] for entry in plan)
     pieces, left_hbm = refs[:total], refs[total]
-    outs = list(refs[total + 1 : -5])
-    whole, left, done, sems, left_sem = refs[-5:]
+    outs = refs[total + 1 : -6]
+    whole, left, done, sems, left_sem, out_sems = refs[-6:]
     y, z, bond = place[0], place[1], place[2]
     count = whole.shape[0]
-    copies = [pltpu.make_async_copy(left_hbm, left, left_sem)]
+
+    def left_copy(trip):
+        part = pl.ds(trip * 4, 4)
+        return pltpu.make_async_copy(left_hbm.at[:, part], left.at[:, part], left_sem.at[trip])
+
+    copies = []
     for source, offset, side, far, near in plan:
         step_y, step_z = (far, near) if side == 0 else (near, far)
         owner = (y + SIDE - step_y) % SIDE * SIDE + (z + SIDE - step_z) % SIDE
@@ -76,13 +80,13 @@
             pltpu.make_async_copy(
                 pieces[source].at[offset : offset + count],
                 whole.at[:, pl.ds(owner * 4 + 2 * side, 2)],
-                sems.at[len(copies) - 1],
+                sems.at[len(copies)],
             )
         )
     for copy in copies:
         copy.start()
-    for copy in copies:
-        copy.wait()
+    for trip in range(4):
+        left_copy(trip).start()
     lane = lax.broadcasted_iota(jnp.int32, (TILE, TILE), 1)
     strip_sectors = 8
     col_live = jnp.concatenate(
@@ -94,14 +98,20 @@
     )
     terms, rows = left.shape[0], left.shape[1]
     zero = jnp.zeros((TILE, TILE), BF16)
-    unroll = 8
-
-    @pl.loop(0, terms * rows // unroll)
+
+    def out_copy(block):
+        return pltpu.make_async_copy(done.at[block], outs[0].at[block], out_sems.at[block])
+
+    for copy in copies:
+        copy.wait()
+
+    @pl.loop(0, rows // 4)
     def _(trip):
-        for u in range(unroll):
-            step = trip * unroll + u
-            term, row = step // rows, step % rows
-            low, high = pairs[step * 2], pairs[step * 2 + 1]
+        left_copy(trip).wait()
+        for u in range(4 * terms):
+            row, term = trip * 4 + u // terms, u % terms
+            entry = (term * rows + row) * 2
+            low, high = pairs[entry], pairs[entry + 1]
             lhs = jnp.concatenate(
                 [
                     jnp.where(lane < size[low], left[term, row, 0], zero),
@@ -118,36 +128,37 @@
             )
             middle = (jnp.dot(lhs, rhs, preferred_element_type=F32) * col_live).astype(BF16)
             target = row // 2
-            if modes[u % 2 % split]:
+            if turned:
                 target = (target // 2 + SIDE - bond // 2) % SIDE * 2 + (target + bond) % 2
-            half, line = (0, u % 2 * TILE) if split == 1 else (u % 2, 0)
+            line = u // terms % 2 * TILE
             for s in range(count):
-                done[half, target, s, term, line : line + TILE, :] = middle[
+                done[target, s, term, line : line + TILE, :] = middle[
                     :, s * TILE : (s + 1) * TILE
                 ]
-
-    sent = []
-    for half, turned in enumerate(modes):
-        for block in range(8):
-            out = outs.pop(0) if turned else outs[0].at[block]
-            sent.append(pltpu.make_async_copy(done.at[half, block], out, sems.at[len(sent)]))
         if not turned:
-            outs.pop(0)
-    for copy in sent:
-        copy.start()
+            out_copy(trip * 2).start()
+            out_copy(trip * 2 + 1).start()
+
+    if turned:
+        sent = [
+            pltpu.make_async_copy(done.at[block], outs[block], out_sems.at[block])
+            for block in range(8)
+        ]
+        for copy in sent:
+            copy.start()
+    else:
+        sent = [out_copy(block) for block in range(8)]
     for copy in sent:
         copy.wait()
 
 
-def left_stage(pieces, plan, modes, count, left_blocks, place, pairs, size, first_sector):
+def left_stage(pieces, plan, turned, count, left_blocks, place, pairs, size, first_sector):
     terms = left_blocks.shape[0]
-    block = (count, terms, 2 * TILE // len(modes), TILE)
-    shapes = []
-    for turned in modes:
-        shapes += [block] * 8 if turned else [(8, *block)]
+    block = (count, terms, 2 * TILE, TILE)
+    shapes = [block] * 8 if turned else [(8, *block)]
     anywhere = pl.BlockSpec(memory_space=pl.ANY)
-    results = pl.pallas_call(
-        functools.partial(left_kernel, first_sector, modes, plan),
+    return pl.pallas_call(
+        functools.partial(left_kernel, first_sector, turned, plan),
         out_shape=[jax.ShapeDtypeStruct(shape, BF16) for shape in shapes],
         grid_spec=pltpu.PrefetchScalarGridSpec(
             num_scalar_prefetch=3,
@@ -157,9 +168,10 @@
             scratch_shapes=[
                 pltpu.VMEM((count, 64, TILE, TILE), BF16),
                 pltpu.VMEM(left_blocks.shape, BF16),
-                pltpu.VMEM((len(modes), 8, *block), BF16),
+                pltpu.VMEM((8, *block), BF16),
                 pltpu.SemaphoreType.DMA((32,)),
-                pltpu.SemaphoreType.DMA(()),
+                pltpu.SemaphoreType.DMA((4,)),
+                pltpu.SemaphoreType.DMA((8,)),
             ],
         ),
         compiler_params=pltpu.CompilerParams(vmem_limit_bytes=60 << 20),
@@ -169,11 +181,6 @@
             transcendentals=0,
         ),
     )(place, pairs, size, *pieces, left_blocks)
-    results = list(results)
-    grouped = []
-    for turned in modes:
-        grouped.append([results.pop(0) for _ in range(8 if turned else 1)])
-    return grouped
 
 
 def exchange(blocks):
@@ -191,7 +198,7 @@
     return got
 
 
-def right_kernel(layout, half, place, pairs, size, *refs):
+def right_kernel(layout, place, pairs, size, *refs):
     total = sum(8 if turned else 1 for _, turned in layout)
     arrived, right = list(refs[:total]), refs[total]
     outs_a, outs_b = refs[total + 1 : total + 5], refs[total + 5 : total + 9]
@@ -207,8 +214,6 @@
             piece = arrived.pop(0) if turned else whole.at[block]
             if turned:
                 source = (bond // 2 + SIDE - block // 2) % SIDE * 2 + (bond + block) % 2
-            if piece.shape[2] != rows:
-                piece = piece.at[:, :, half * rows : (half + 1) * rows]
             copies.append(
                 pltpu.make_async_copy(
                     piece, middle.at[pl.ds(source * 8 + first, count)], sems.at[len(copies)]
@@ -232,7 +237,8 @@
         right_copy(0, step_y).start()
     line = lax.broadcasted_iota(jnp.int32, (TILE, TILE), 0)
     lane = lax.broadcasted_iota(jnp.int32, (TILE, TILE), 1)
-    row_live = line < size[bond * 2 + half]
+    row_live = jnp.concatenate([line < size[bond * 2 + h] for h in range(rows // TILE)], axis=0)
+    lanes = jnp.concatenate([lane] * (rows // TILE), axis=0)
     for copy in copies:
         copy.wait()
     for step_z in range(1, SIDE):
@@ -263,7 +269,7 @@
                         [block[term, q, p] for term in range(terms) for p in range(2)], axis=0
                     )
                     product = jnp.dot(lhs, rhs, preferred_element_type=F32)
-                    keep = row_live & (lane < size[col])
+                    keep = row_live & (lanes < size[col])
                     value = jnp.where(keep, product, 0.0).astype(BF16)
                     if q < 2:
                         sum_a[step_z, step_y, :, q * TILE : (q + 1) * TILE] = value
@@ -286,14 +292,15 @@
         copy.wait()
 
 
-def right_stage(arrived, half, right_blocks, place, pairs, size):
+def right_stage(arrived, right_blocks, place, pairs, size):
     layout = tuple((count, len(blocks) > 1) for count, blocks in zip(CHUNKS, arrived))
     arrived = [block for blocks in arrived for block in blocks]
-    terms, rows = right_blocks.shape[0], TILE
+    terms, rows = right_blocks.shape[0], 2 * TILE
     shape = jax.ShapeDtypeStruct((SIDE, rows, 2 * TILE), BF16)
     anywhere = pl.BlockSpec(memory_space=pl.ANY)
     return pl.pallas_call(
-        functools.partial(right_kernel, layout, half),
+        functools.partial(right_kernel, layout),
+        name="right",
         out_shape=[shape] * 8,
         grid_spec=pltpu.PrefetchScalarGridSpec(
             num_scalar_prefetch=3,
@@ -310,10 +317,10 @@
                 pltpu.SemaphoreType.DMA((SIDE * (SIDE + 1),)),
             ],
         ),
-        compiler_params=pltpu.CompilerParams(vmem_limit_bytes=58 << 20),
+        compiler_params=pltpu.CompilerParams(vmem_limit_bytes=60 << 20),
         cost_estimate=pl.CostEstimate(
             flops=2 * terms * rows * 256 * 8192,
-            bytes_accessed=(14 << 20),
+            bytes_accessed=(20 << 20),
             transcendentals=0,
         ),
     )(place, pairs, size, *arrived, right_blocks)
@@ -431,7 +438,7 @@
         middles = left_stage(
             pieces,
             tuple(plan),
-            MODES[chunk],
+            TURNED[chunk],
             count,
             left_blocks,
             place,
@@ -439,17 +446,13 @@
             sector_size,
             starts[chunk],
         )
-        for middle in middles:
-            arrived.append(exchange(middle))
-    finals = []
-    for half in range(2):
-        mine = arrived[: chunk_count - 1] + [arrived[chunk_count - 1 + half]]
-        parts = right_stage(mine, half, right_blocks, place, rights, sector_size)
-        got = [parts[0]] + [move(parts[d], 0, d) for d in range(1, SIDE)]
-        got += [parts[4]] + [move(parts[4 + d], d, 0) for d in range(1, SIDE)]
-        sums = sum_stage(got)
-        finals += [sums[0]] + [move(sums[d], d, 0) for d in range(1, SIDE)]
-        finals += [sums[4]] + [move(sums[4 + d], 0, d) for d in range(1, SIDE)]
+        arrived.append(exchange(middles))
+    parts = right_stage(arrived, right_blocks, place, rights, sector_size)
+    got = [parts[0]] + [move(parts[d], 0, d) for d in range(1, SIDE)]
+    got += [parts[4]] + [move(parts[4 + d], d, 0) for d in range(1, SIDE)]
+    sums = sum_stage(got)
+    finals = [sums[0]] + [move(sums[d], d, 0) for d in range(1, SIDE)]
+    finals += [sums[4]] + [move(sums[4 + d], 0, d) for d in range(1, SIDE)]
     return last_stage(finals)
 
 

time: 333 us -> 318 us (0.955)
  starting transfers between devices: 121 us -> 108 us
  Pallas kernels: 54.3 us -> 49.6 us
  waiting for transfers between devices: 146 us -> 150 us
    ppermute x60 -> x48, waiting for transfers between devices: 113 us -> 121 us  [move(): return lax.ppermute(value, 'op', pairs)]
    pallas_call x6 -> x5, Pallas kernels: 44.7 us -> 36.8 us  [the longest x4 24.9 us: left_stage(): pl.pallas_call(functools.partial(left_kernel, first_sector, turned, plan)...]
    all_to_all x3 -> x2, starting transfers between devices: 13.6 us -> 8.73 us  [exchange(): lax.all_to_all(blocks[0], 'bond', split_axis=0, concat_axis=0, tiled=True)]
    ppermute x60 -> x48, starting transfers between devices: 90.2 us -> 85.5 us  [move(): return lax.ppermute(value, 'op', pairs)]
    ppermute x14, waiting for transfers between devices: 32.8 us -> 29.1 us  [exchange(): got.append(lax.ppermute(blocks[turned], 'bond', pairs))]
    unnamed x150 -> x94, local copies, waits for them, and re-layouts: 7.98 us -> 6.72 us
  transfers between devices with their start and end apart: 77 -> 64, of which waited for: 30 -> 27; matrix products, arithmetic and copies ran while one was open for 1% -> 1% of each run, Pallas kernels for 14% -> 9%
where the time goes in v4:
time: 318 us; the launch traced here: 317 us
  waiting for transfers between devices  150 us (47%)
  starting transfers between devices  108 us (34%)
  Pallas kernels  49.6 us (16%)
  local copies, waits for them, and re-layouts  8.07 us (3%)
    ppermute x48, waiting for transfers between devices, move(): return lax.ppermute(value, 'op', pairs)  121 us
    ppermute x48, starting transfers between devices, move(): return lax.ppermute(value, 'op', pairs)  85.5 us
    ppermute x14, waiting for transfers between devices, exchange(): got.append(lax.ppermute(blocks[turned], 'bond', pairs))  29.1 us
    pallas_call x4, Pallas kernels, left_stage(): pl.pallas_call(functools.partial(left_kernel, first_sector, turned, plan)...  24.9 us
    ppermute x14, starting transfers between devices, exchange(): got.append(lax.ppermute(blocks[turned], 'bond', pairs))  14.1 us
    pallas_call x1, Pallas kernels, right_stage(): pl.pallas_call(functools.partial(right_kernel, layout), name='right', out...  11.9 us
    pallas_call x5, Pallas kernels, pack_stage(): pl.pallas_call(functools.partial(pack_kernel, plans), out_shape=[jax.Shap...  11.4 us
    all_to_all x2, starting transfers between devices, exchange(): lax.all_to_all(blocks[0], 'bond', split_axis=0, concat_axis=0, tiled=True)  8.73 us
  transfers between devices with their start and end apart: 64, of which 27 were waited for; matrix products, arithmetic and copies ran while one was open for 1% of the time, Pallas kernels for 9%

profile of v4, /device:TPU:0, one launch (start us, length us, event | category | flops | bytes accessed | tf_op | source)
XLA Modules:
  0.0 317.4 jit_solution(13727905171896842715)
XLA Ops:
  2.1 4.2 %collective-permute-start.2 = (bf16[4,2,128,128]{3,2,1,0:T(8,128)(2,1)}, bf16[4,2,128,128]{3,2,1,0:T(8,128)(2,1)S(1)}, u32[]{:S(2)}, u32[]{:S(2)}) collective-permute-start(bf16[4,2,128,128]{3,2,1,0:T(8,128)(2,1)} %get-tuple-element.47.refs_1_), channel_id=1, source_target_pairs={{0,3},{1,0},{2,1},{3,2},{4,7},{5,4},{6,5},{7,6},{8,11},{9,8},{10,9... | collective-permute-start | bytes 786440 | tf_op jit(solution)/shard_map/ppermute | solution.py:26
  7.5 3.0 collective-permute-start.5
  11.2 6.6 %collective-permute-done.2.refs_2_ = bf16[4,2,128,128]{3,2,1,0:T(8,128)(2,1)S(1)} collective-permute-done((bf16[4,2,128,128]{3,2,1,0:T(8,128)(2,1)}, bf16[4,2,128,128]{3,2,1,0:T(8,128)(2,1)S(1)}, u32[]{:S(2)}, u32[]{:S(2)}) %collective-permute-start.2) | collective-permute-done | bytes 262176 | tf_op jit(solution)/shard_map/ppermute | solution.py:26
  21.1 3.2 %collective-permute-start.9 = (bf16[4,2,128,128]{3,2,1,0:T(8,128)(2,1)}, bf16[4,2,128,128]{3,2,1,0:T(8,128)(2,1)S(1)}, u32[]{:S(2)}, u32[]{:S(2)}) collective-permute-start(bf16[4,2,128,128]{3,2,1,0:T(8,128)(2,1)} %get-tuple-element.47.refs_1_), channel_id=1, source_target_pairs={{0,8},{1,9},{2,10},{3,11},{4,12},{5,13},{6,14},{7,15},{8,0},{9,1},... | collective-permute-start | bytes 786440 | tf_op jit(solution)/shard_map/ppermute | solution.py:26
  24.3 2.9 collective-permute-done.3.refs_3_
  30.3 3.0 collective-permute-start.10
  33.4 3.7 %collective-permute-start.17 = (bf16[4,2,128,128]{3,2,1,0:T(8,128)(2,1)S(1)}, bf16[4,2,128,128]{3,2,1,0:T(8,128)(2,1)}, u32[]{:S(2)}, u32[]{:S(2)}) collective-permute-start(bf16[4,2,128,128]{3,2,1,0:T(8,128)(2,1)S(1)} %copy-done.12), channel_id=1, source_target_pairs={{0,3},{1,0},{2,1},{3,2},{4,7},{5,4},{6,5},{7,6},{8,11},{9,8},{10,9... | collective-permute-start | bytes 786440 | tf_op jit(solution)/shard_map/ppermute | solution.py:26
  38.0 8.8 %collective-permute-done.7.refs_3_ = bf16[4,2,128,128]{3,2,1,0:T(8,128)(2,1)S(1)} collective-permute-done((bf16[4,2,128,128]{3,2,1,0:T(8,128)(2,1)S(1)}, bf16[4,2,128,128]{3,2,1,0:T(8,128)(2,1)S(1)}, u32[]{:S(2)}, u32[]{:S(2)}) %collective-permute-start.7) | collective-permute-done | bytes 262176 | tf_op jit(solution)/shard_map/ppermute | solution.py:26
  49.2 6.2 %collective-permute-start.16 = (bf16[8,2,128,128]{3,2,1,0:T(8,128)(2,1)}, bf16[8,2,128,128]{3,2,1,0:T(8,128)(2,1)S(1)}, u32[]{:S(2)}, u32[]{:S(2)}) collective-permute-start(bf16[8,2,128,128]{3,2,1,0:T(8,128)(2,1)} %get-tuple-element.50.refs_8_), channel_id=1, source_target_pairs={{0,3},{1,0},{2,1},{3,2},{4,7},{5,4},{6,5},{7,6},{8,11},{9,8},{10,9... | collective-permute-start | bytes 1572872 | tf_op jit(solution)/shard_map/ppermute | solution.py:26
  58.6 4.8 %collective-permute-done.6.refs_2_.refs_3_ = bf16[8,2,128,128]{3,2,1,0:T(8,128)(2,1)S(1)} collective-permute-done((bf16[8,2,128,128]{3,2,1,0:T(8,128)(2,1)}, bf16[8,2,128,128]{3,2,1,0:T(8,128)(2,1)S(1)}, u32[]{:S(2)}, u32[]{:S(2)}) %collective-permute-start.6) | collective-permute-done | bytes 524320 | tf_op jit(solution)/shard_map/ppermute | solution.py:26
  63.4 5.9 %collective-permute-done.16.refs_14_.refs_2_ = bf16[8,2,128,128]{3,2,1,0:T(8,128)(2,1)S(1)} collective-permute-done((bf16[8,2,128,128]{3,2,1,0:T(8,128)(2,1)}, bf16[8,2,128,128]{3,2,1,0:T(8,128)(2,1)S(1)}, u32[]{:S(2)}, u32[]{:S(2)}) %collective-permute-start.16) | collective-permute-done | bytes 524320 | tf_op jit(solution)/shard_map/ppermute | solution.py:26
  69.3 3.2 %collective-permute-done.12.refs_10_.refs_0_ = bf16[8,2,128,128]{3,2,1,0:T(8,128)(2,1)S(1)} collective-permute-done((bf16[8,2,128,128]{3,2,1,0:T(8,128)(2,1)}, bf16[8,2,128,128]{3,2,1,0:T(8,128)(2,1)S(1)}, u32[]{:S(2)}, u32[]{:S(2)}) %collective-permute-start.12) | collective-permute-done | bytes 524320 | tf_op jit(solution)/shard_map/ppermute | solution.py:26
  73.4 6.1 %shard_map.66 = bf16[8,2,2,256,128]{4,3,2,1,0:T(8,128)(2,1)} custom-call(s32[3]{0:T(128)} %pad_add_fusion.place, s32[64]{0:T(128)} %reshape.10.pairs, s32[64]{0:T(128)} %size.9, bf16[8,2,128,128]{3,2,1,0:T(8,128)(2,1)} %get-tuple-element.49.refs_0_, bf16[4,2,128,128]{3,2,1,0:T(8,128)(2,1)} %get-tuple-element.47.refs_1_, bf16[8,2,128,128]{3,2,1,0:T(8,128)(2,1)} %copy-done.6, ...), custom_call_target="tpu_custom_call" | custom-call | flops 536870912 | bytes 8388608 | tf_op jit(solution)/shard_map/pallas_call | solution.py:160
  79.5 4.3 %all-to-all-start = ((bf16[8,2,2,256,128]{4,3,2,1,0:T(8,128)(2,1)}), bf16[8,2,2,256,128]{4,3,2,1,0:T(8,128)(2,1)S(1)}, u32[]{:S(2)}, u32[]{:S(2)}) async-start(bf16[8,2,2,256,128]{4,3,2,1,0:T(8,128)(2,1)} %shard_map.66), calls=%async_computation | async-start | bytes 4194304 | tf_op jit(solution)/shard_map/all_to_all | solution.py:188
  83.8 2.4 shard_map.67
  86.2 4.5 %collective-permute-start.20 = (bf16[8,2,128,128]{3,2,1,0:T(8,128)(2,1)}, bf16[8,2,128,128]{3,2,1,0:T(8,128)(2,1)S(1)}, u32[]{:S(2)}, u32[]{:S(2)}) collective-permute-start(bf16[8,2,128,128]{3,2,1,0:T(8,128)(2,1)} %get-tuple-element.51.refs_0_), channel_id=1, source_target_pairs={{0,12},{1,13},{2,14},{3,15},{4,0},{5,1},{6,2},{7,3},{8,4},{9,5},{1... | collective-permute-start | bytes 1572872 | tf_op jit(solution)/shard_map/ppermute | solution.py:26
  95.7 7.6 %collective-permute-done.20.refs_6_.refs_5_ = bf16[8,2,128,128]{3,2,1,0:T(8,128)(2,1)S(1)} collective-permute-done((bf16[8,2,128,128]{3,2,1,0:T(8,128)(2,1)}, bf16[8,2,128,128]{3,2,1,0:T(8,128)(2,1)S(1)}, u32[]{:S(2)}, u32[]{:S(2)}) %collective-permute-start.20) | collective-permute-done | bytes 524320 | tf_op jit(solution)/shard_map/ppermute | solution.py:26
  103.3 3.1 collective-permute-start.35
  106.4 18.9 %collective-permute-done.33.refs_3_ = bf16[8,2,128,128]{3,2,1,0:T(8,128)(2,1)S(1)} collective-permute-done((bf16[8,2,128,128]{3,2,1,0:T(8,128)(2,1)}, bf16[8,2,128,128]{3,2,1,0:T(8,128)(2,1)S(1)}, u32[]{:S(2)}, u32[]{:S(2)}) %collective-permute-start.33) | collective-permute-done | bytes 524320 | tf_op jit(solution)/shard_map/ppermute | solution.py:26
  125.3 2.4 collective-permute-start.34
  127.7 4.4 %collective-permute-start.18 = (bf16[8,2,128,128]{3,2,1,0:T(8,128)(2,1)}, bf16[8,2,128,128]{3,2,1,0:T(8,128)(2,1)}, u32[]{:S(2)}, u32[]{:S(2)}) collective-permute-start(bf16[8,2,128,128]{3,2,1,0:T(8,128)(2,1)} %get-tuple-element.51.refs_0_), channel_id=1, source_target_pairs={{0,4},{1,5},{2,6},{3,7},{4,8},{5,9},{6,10},{7,11},{8,12},{9,13},{1... | collective-permute-start | bytes 1572872 | tf_op jit(solution)/shard_map/ppermute | solution.py:26
  134.9 6.2 %collective-permute-done.34.refs_5_ = bf16[8,2,128,128]{3,2,1,0:T(8,128)(2,1)} collective-permute-done((bf16[8,2,128,128]{3,2,1,0:T(8,128)(2,1)}, bf16[8,2,128,128]{3,2,1,0:T(8,128)(2,1)}, u32[]{:S(2)}, u32[]{:S(2)}) %collective-permute-start.34) | collective-permute-done | bytes 524320 | tf_op jit(solution)/shard_map/ppermute | solution.py:26
  142.8 6.0 %shard_map.70 = bf16[8,2,2,256,128]{4,3,2,1,0:T(8,128)(2,1)} custom-call(s32[3]{0:T(128)} %pad_add_fusion.place, s32[64]{0:T(128)} %reshape.10.pairs, s32[64]{0:T(128)} %size.9, bf16[8,2,128,128]{3,2,1,0:T(8,128)(2,1)} %get-tuple-element.61.refs_0_, bf16[8,2,128,128]{3,2,1,0:T(8,128)(2,1)} %collective-permute-done.31.refs_1_, ...), custom_call_target="tpu_custom_call" | custom-call | flops 536870912 | bytes 8388608 | tf_op jit(solution)/shard_map/pallas_call | solution.py:160
  150.1 4.4 %all-to-all-start.1 = ((bf16[8,2,2,256,128]{4,3,2,1,0:T(8,128)(2,1)}), bf16[8,2,2,256,128]{4,3,2,1,0:T(8,128)(2,1)}, u32[]{:S(2)}, u32[]{:S(2)}) async-start(bf16[8,2,2,256,128]{4,3,2,1,0:T(8,128)(2,1)} %shard_map.70), calls=%async_computation.1 | async-start | bytes 4194304 | tf_op jit(solution)/shard_map/all_to_all | solution.py:188
  154.6 8.4 %collective-permute-done.21.refs_10_.refs_0_ = bf16[8,2,128,128]{3,2,1,0:T(8,128)(2,1)} collective-permute-done((bf16[8,2,128,128]{3,2,1,0:T(8,128)(2,1)}, bf16[8,2,128,128]{3,2,1,0:T(8,128)(2,1)}, u32[]{:S(2)}, u32[]{:S(2)}) %collective-permute-start.21) | collective-permute-done | bytes 524320 | tf_op jit(solution)/shard_map/ppermute | solution.py:26
  165.3 3.7 %collective-permute-start.39 = (bf16[8,2,128,128]{3,2,1,0:T(8,128)(2,1)}, bf16[8,2,128,128]{3,2,1,0:T(8,128)(2,1)S(1)}, u32[]{:S(2)}, u32[]{:S(2)}) collective-permute-start(bf16[8,2,128,128]{3,2,1,0:T(8,128)(2,1)} %get-tuple-element.63.refs_0_), channel_id=1, source_target_pairs={{0,12},{1,13},{2,14},{3,15},{4,0},{5,1},{6,2},{7,3},{8,4},{9,5},{1... | collective-permute-start | bytes 1572872 | tf_op jit(solution)/shard_map/ppermute | solution.py:26
  170.5 2.5 collective-permute-start.41
  173.0 18.9 %collective-permute-done.39.refs_3_ = bf16[8,2,128,128]{3,2,1,0:T(8,128)(2,1)S(1)} collective-permute-done((bf16[8,2,128,128]{3,2,1,0:T(8,128)(2,1)}, bf16[8,2,128,128]{3,2,1,0:T(8,128)(2,1)S(1)}, u32[]{:S(2)}, u32[]{:S(2)}) %collective-permute-start.39) | collective-permute-done | bytes 524320 | tf_op jit(solution)/shard_map/ppermute | solution.py:26
  191.9 6.4 %shard_map.68 = (bf16[2,2,256,128]{3,2,1,0:T(8,128)(2,1)}, bf16[2,2,256,128]{3,2,1,0:T(8,128)(2,1)}, bf16[2,2,256,128]{3,2,1,0:T(8,128)(2,1)}, bf16[2,2,256,128]...) custom-call(s32[3]{0:T(128)} %pad_add_fusion.place, ...), custom_call_target="tpu_custom_call" | custom-call | flops 536870912 | bytes 8388608 | tf_op jit(solution)/shard_map/pallas_call | solution.py:160
  203.0 3.2 %collective-permute-done.40.refs_5_ = bf16[8,2,128,128]{3,2,1,0:T(8,128)(2,1)S(1)} collective-permute-done((bf16[8,2,128,128]{3,2,1,0:T(8,128)(2,1)}, bf16[8,2,128,128]{3,2,1,0:T(8,128)(2,1)S(1)}, u32[]{:S(2)}, u32[]{:S(2)}) %collective-permute-start.40) | collective-permute-done | bytes 524320 | tf_op jit(solution)/shard_map/ppermute | solution.py:26
  207.0 6.4 %shard_map.72 = (bf16[2,2,256,128]{3,2,1,0:T(8,128)(2,1)}, bf16[2,2,256,128]{3,2,1,0:T(8,128)(2,1)}, bf16[2,2,256,128]{3,2,1,0:T(8,128)(2,1)}, bf16[2,2,256,128]...) custom-call(s32[3]{0:T(128)} %pad_add_fusion.place, ...), custom_call_target="tpu_custom_call" | custom-call | flops 536870912 | bytes 8388608 | tf_op jit(solution)/shard_map/pallas_call | solution.py:160
  213.4 2.5 collective-permute-start.29
  217.0 4.2 %collective-permute-done.27.refs_5_ = bf16[2,2,256,128]{3,2,1,0:T(8,128)(2,1)} collective-permute-done((bf16[2,2,256,128]{3,2,1,0:T(8,128)(2,1)}, bf16[2,2,256,128]{3,2,1,0:T(8,128)(2,1)}, u32[]{:S(2)}, u32[]{:S(2)}) %collective-permute-start.27) | collective-permute-done | bytes 262176 | tf_op jit(solution)/shard_map/ppermute | solution.py:197
  221.2 4.6 %collective-permute-done.28.refs_6_ = bf16[2,2,256,128]{3,2,1,0:T(8,128)(2,1)} collective-permute-done((bf16[2,2,256,128]{3,2,1,0:T(8,128)(2,1)}, bf16[2,2,256,128]{3,2,1,0:T(8,128)(2,1)}, u32[]{:S(2)}, u32[]{:S(2)}) %collective-permute-start.28) | collective-permute-done | bytes 262176 | tf_op jit(solution)/shard_map/ppermute | solution.py:197
  233.6 3.7 %collective-permute-done.45.refs_13_ = bf16[2,2,256,128]{3,2,1,0:T(8,128)(2,1)S(1)} collective-permute-done((bf16[2,2,256,128]{3,2,1,0:T(8,128)(2,1)}, bf16[2,2,256,128]{3,2,1,0:T(8,128)(2,1)S(1)}, u32[]{:S(2)}, u32[]{:S(2)}) %collective-permute-start.45) | collective-permute-done | bytes 262176 | tf_op jit(solution)/shard_map/ppermute | solution.py:197
  237.3 6.2 %collective-permute-done.46.refs_14_ = bf16[2,2,256,128]{3,2,1,0:T(8,128)(2,1)S(1)} collective-permute-done((bf16[2,2,256,128]{3,2,1,0:T(8,128)(2,1)}, bf16[2,2,256,128]{3,2,1,0:T(8,128)(2,1)S(1)}, u32[]{:S(2)}, u32[]{:S(2)}) %collective-permute-start.46) | collective-permute-done | bytes 262176 | tf_op jit(solution)/shard_map/ppermute | solution.py:197
  243.5 4.5 %collective-permute-done.47.refs_15_ = bf16[2,2,256,128]{3,2,1,0:T(8,128)(2,1)S(1)} collective-permute-done((bf16[2,2,256,128]{3,2,1,0:T(8,128)(2,1)}, bf16[2,2,256,128]{3,2,1,0:T(8,128)(2,1)S(1)}, u32[]{:S(2)}, u32[]{:S(2)}) %collective-permute-start.47) | collective-permute-done | bytes 262176 | tf_op jit(solution)/shard_map/ppermute | solution.py:197
  248.9 3.4 %collective-permute-done.49.refs_17_ = bf16[2,2,256,128]{3,2,1,0:T(8,128)(2,1)S(1)} collective-permute-done((bf16[2,2,256,128]{3,2,1,0:T(8,128)(2,1)}, bf16[2,2,256,128]{3,2,1,0:T(8,128)(2,1)S(1)}, u32[]{:S(2)}, u32[]{:S(2)}) %collective-permute-start.49) | collective-permute-done | bytes 262176 | tf_op jit(solution)/shard_map/ppermute | solution.py:197
  253.0 11.9 %right.1 = (bf16[4,256,256]{2,1,0:T(8,128)(2,1)}, bf16[4,256,256]{2,1,0:T(8,128)(2,1)}, bf16[4,256,256]{2,1,0:T(8,128)(2,1)}, bf16[4,256,256]{2,1,0:T(8,128)(2,1...) custom-call(s32[3]{0:T(128)} %pad_add_fusion.place, ...), custom_call_target="tpu_custom_call" | custom-call | flops 2147483648 | bytes 20971520 | tf_op jit(solution)/shard_map/right/pallas_call | solution.py:301
  266.3 3.4 %collective-permute-start.51 = (bf16[4,256,256]{2,1,0:T(8,128)(2,1)}, bf16[4,256,256]{2,1,0:T(8,128)(2,1)S(1)}, u32[]{:S(2)}, u32[]{:S(2)}) collective-permute-start(bf16[4,256,256]{2,1,0:T(8,128)(2,1)} %get-tuple-element.75), channel_id=1, source_target_pairs={{0,2},{1,3},{2,0},{3,1},{4,6},{5,7},{6,4},{7,5},{8,10},{9,11},{10,... | collective-permute-start | bytes 1572872 | tf_op jit(solution)/shard_map/ppermute | solution.py:26
  269.7 5.0 %collective-permute-start.54 = (bf16[4,256,256]{2,1,0:T(8,128)(2,1)}, bf16[4,256,256]{2,1,0:T(8,128)(2,1)S(1)}, u32[]{:S(2)}, u32[]{:S(2)}) collective-permute-start(bf16[4,256,256]{2,1,0:T(8,128)(2,1)} %get-tuple-element.79), channel_id=1, source_target_pairs={{0,8},{1,9},{2,10},{3,11},{4,12},{5,13},{6,14},{7,15},{8,0},{9,1},... | collective-permute-start | bytes 1572872 | tf_op jit(solution)/shard_map/ppermute | solution.py:26
  274.7 6.4 %collective-permute-done.50.refs_1_ = bf16[4,256,256]{2,1,0:T(8,128)(2,1)S(1)} collective-permute-done((bf16[4,256,256]{2,1,0:T(8,128)(2,1)}, bf16[4,256,256]{2,1,0:T(8,128)(2,1)S(1)}, u32[]{:S(2)}, u32[]{:S(2)}) %collective-permute-start.50) | collective-permute-done | bytes 524320 | tf_op jit(solution)/shard_map/ppermute | solution.py:26
  281.1 3.6 %collective-permute-start.55 = (bf16[4,256,256]{2,1,0:T(8,128)(2,1)}, bf16[4,256,256]{2,1,0:T(8,128)(2,1)S(1)}, u32[]{:S(2)}, u32[]{:S(2)}) collective-permute-start(bf16[4,256,256]{2,1,0:T(8,128)(2,1)} %get-tuple-element.80), channel_id=1, source_target_pairs={{0,12},{1,13},{2,14},{3,15},{4,0},{5,1},{6,2},{7,3},{8,4},{9,5},{1... | collective-permute-start | bytes 1572872 | tf_op jit(solution)/shard_map/ppermute | solution.py:26
  284.7 9.0 %collective-permute-done.51.refs_2_ = bf16[4,256,256]{2,1,0:T(8,128)(2,1)S(1)} collective-permute-done((bf16[4,256,256]{2,1,0:T(8,128)(2,1)}, bf16[4,256,256]{2,1,0:T(8,128)(2,1)S(1)}, u32[]{:S(2)}, u32[]{:S(2)}) %collective-permute-start.51) | collective-permute-done | bytes 524320 | tf_op jit(solution)/shard_map/ppermute | solution.py:26
  293.7 4.5 %collective-permute-done.54.refs_6_ = bf16[4,256,256]{2,1,0:T(8,128)(2,1)S(1)} collective-permute-done((bf16[4,256,256]{2,1,0:T(8,128)(2,1)}, bf16[4,256,256]{2,1,0:T(8,128)(2,1)S(1)}, u32[]{:S(2)}, u32[]{:S(2)}) %collective-permute-start.54) | collective-permute-done | bytes 524320 | tf_op jit(solution)/shard_map/ppermute | solution.py:26
  301.2 2.4 collective-permute-start.56
  305.5 2.5 collective-permute-start.58
  311.3 4.4 %collective-permute-done.59.refs_5_ = bf16[256,256]{1,0:T(8,128)(2,1)S(1)} collective-permute-done((bf16[256,256]{1,0:T(8,128)(2,1)S(1)}, bf16[256,256]{1,0:T(8,128)(2,1)S(1)}, u32[]{:S(2)}, u32[]{:S(2)}) %collective-permute-start.59) | collective-permute-done | bytes 131104 | tf_op jit(solution)/shard_map/ppermute | solution.py:26
  (189 shorter events, 59.4 us)
Async XLA Ops:
  2.1 15.7 %collective-permute-start.2 = (bf16[4,2,128,128]{3,2,1,0:T(8,128)(2,1)}, bf16[4,2,128,128]{3,2,1,0:T(8,128)(2,1)S(1)}, u32[]{:S(2)}, u32[]{:S(2)}) collective-permute-start(bf16[4,2,128,128]{3,2,1,0:T(8,128)(2,1)} %get-tuple-element.47.refs_1_), channel_id=1, source_target_pairs={{0,3},{1,0},{2,1},{3,2},{4,7},{5,4},{6,5},{7,6},{8,11},{9,8},{10,9... | collective-permute-start | bytes 786440 | tf_op jit(solution)/shard_map/ppermute | solution.py:26
  6.3 14.8 %collective-permute-start = (bf16[4,2,128,128]{3,2,1,0:T(8,128)(2,1)}, bf16[4,2,128,128]{3,2,1,0:T(8,128)(2,1)S(1)}, u32[]{:S(2)}, u32[]{:S(2)}) collective-permute-start(bf16[4,2,128,128]{3,2,1,0:T(8,128)(2,1)} %get-tuple-element.47.refs_1_), channel_id=1, source_target_pairs={{0,1},{1,2},{2,3},{3,0},{4,5},{5,6},{6,7},{7,4},{8,9},{9,10},{10,1... | collective-permute-start | bytes 786440 | tf_op jit(solution)/shard_map/ppermute | solution.py:26
  7.5 16.7 %collective-permute-start.5 = (bf16[4,2,128,128]{3,2,1,0:T(8,128)(2,1)}, bf16[4,2,128,128]{3,2,1,0:T(8,128)(2,1)S(1)}, u32[]{:S(2)}, u32[]{:S(2)}) collective-permute-start(bf16[4,2,128,128]{3,2,1,0:T(8,128)(2,1)} %get-tuple-element.48.refs_9_), channel_id=1, source_target_pairs={{0,12},{1,13},{2,14},{3,15},{4,0},{5,1},{6,2},{7,3},{8,4},{9,5},{1... | collective-permute-start | bytes 786440 | tf_op jit(solution)/shard_map/ppermute | solution.py:26
  10.5 13.7 %collective-permute-start.4 = (bf16[4,2,128,128]{3,2,1,0:T(8,128)(2,1)}, bf16[4,2,128,128]{3,2,1,0:T(8,128)(2,1)S(1)}, u32[]{:S(2)}, u32[]{:S(2)}) collective-permute-start(bf16[4,2,128,128]{3,2,1,0:T(8,128)(2,1)} %get-tuple-element.48.refs_9_), channel_id=1, source_target_pairs={{0,8},{1,9},{2,10},{3,11},{4,12},{5,13},{6,14},{7,15},{8,0},{9,1},... | collective-permute-start | bytes 786440 | tf_op jit(solution)/shard_map/ppermute | solution.py:26
  19.4 17.7 %collective-permute-start.11 = (bf16[4,2,128,128]{3,2,1,0:T(8,128)(2,1)}, bf16[4,2,128,128]{3,2,1,0:T(8,128)(2,1)S(1)}, u32[]{:S(2)}, u32[]{:S(2)}) collective-permute-start(bf16[4,2,128,128]{3,2,1,0:T(8,128)(2,1)} %get-tuple-element.47.refs_1_), channel_id=1, source_target_pairs={{0,12},{1,13},{2,14},{3,15},{4,0},{5,1},{6,2},{7,3},{8,4},{9,5},{1... | collective-permute-start | bytes 786440 | tf_op jit(solution)/shard_map/ppermute | solution.py:26
  21.1 15.9 %collective-permute-start.9 = (bf16[4,2,128,128]{3,2,1,0:T(8,128)(2,1)}, bf16[4,2,128,128]{3,2,1,0:T(8,128)(2,1)S(1)}, u32[]{:S(2)}, u32[]{:S(2)}) collective-permute-start(bf16[4,2,128,128]{3,2,1,0:T(8,128)(2,1)} %get-tuple-element.47.refs_1_), channel_id=1, source_target_pairs={{0,8},{1,9},{2,10},{3,11},{4,12},{5,13},{6,14},{7,15},{8,0},{9,1},... | collective-permute-start | bytes 786440 | tf_op jit(solution)/shard_map/ppermute | solution.py:26
  30.3 25.1 %collective-permute-start.10 = (bf16[8,2,128,128]{3,2,1,0:T(8,128)(2,1)}, bf16[8,2,128,128]{3,2,1,0:T(8,128)(2,1)S(1)}, u32[]{:S(2)}, u32[]{:S(2)}) collective-permute-start(bf16[8,2,128,128]{3,2,1,0:T(8,128)(2,1)} %get-tuple-element.49.refs_0_), channel_id=1, source_target_pairs={{0,12},{1,13},{2,14},{3,15},{4,0},{5,1},{6,2},{7,3},{8,4},{9,5},{1... | collective-permute-start | bytes 1572872 | tf_op jit(solution)/shard_map/ppermute | solution.py:26
  37.0 18.4 %collective-permute-start.13 = (bf16[4,2,128,128]{3,2,1,0:T(8,128)(2,1)S(1)}, bf16[4,2,128,128]{3,2,1,0:T(8,128)(2,1)}, u32[]{:S(2)}, u32[]{:S(2)}) collective-permute-start(bf16[4,2,128,128]{3,2,1,0:T(8,128)(2,1)S(1)} %copy-done.12), channel_id=1, source_target_pairs={{0,1},{1,2},{2,3},{3,0},{4,5},{5,6},{6,7},{7,4},{8,9},{9,10},{10,1... | collective-permute-start | bytes 786440 | tf_op jit(solution)/shard_map/ppermute | solution.py:26
  46.8 16.6 %collective-permute-start.6 = (bf16[8,2,128,128]{3,2,1,0:T(8,128)(2,1)}, bf16[8,2,128,128]{3,2,1,0:T(8,128)(2,1)S(1)}, u32[]{:S(2)}, u32[]{:S(2)}) collective-permute-start(bf16[8,2,128,128]{3,2,1,0:T(8,128)(2,1)} %get-tuple-element.49.refs_0_), channel_id=1, source_target_pairs={{0,4},{1,5},{2,6},{3,7},{4,8},{5,9},{6,10},{7,11},{8,12},{9,13},{1... | collective-permute-start | bytes 1572872 | tf_op jit(solution)/shard_map/ppermute | solution.py:26
  49.2 20.1 %collective-permute-start.16 = (bf16[8,2,128,128]{3,2,1,0:T(8,128)(2,1)}, bf16[8,2,128,128]{3,2,1,0:T(8,128)(2,1)S(1)}, u32[]{:S(2)}, u32[]{:S(2)}) collective-permute-start(bf16[8,2,128,128]{3,2,1,0:T(8,128)(2,1)} %get-tuple-element.50.refs_8_), channel_id=1, source_target_pairs={{0,3},{1,0},{2,1},{3,2},{4,7},{5,4},{6,5},{7,6},{8,11},{9,8},{10,9... | collective-permute-start | bytes 1572872 | tf_op jit(solution)/shard_map/ppermute | solution.py:26
  55.4 13.9 %collective-permute-start.14 = (bf16[8,2,128,128]{3,2,1,0:T(8,128)(2,1)}, bf16[8,2,128,128]{3,2,1,0:T(8,128)(2,1)S(1)}, u32[]{:S(2)}, u32[]{:S(2)}) collective-permute-start(bf16[8,2,128,128]{3,2,1,0:T(8,128)(2,1)} %get-tuple-element.50.refs_8_), channel_id=1, source_target_pairs={{0,2},{1,3},{2,0},{3,1},{4,6},{5,7},{6,4},{7,5},{8,10},{9,11},{10,... | collective-permute-start | bytes 1572872 | tf_op jit(solution)/shard_map/ppermute | solution.py:26
  55.5 17.1 %collective-permute-start.12 = (bf16[8,2,128,128]{3,2,1,0:T(8,128)(2,1)}, bf16[8,2,128,128]{3,2,1,0:T(8,128)(2,1)S(1)}, u32[]{:S(2)}, u32[]{:S(2)}) collective-permute-start(bf16[8,2,128,128]{3,2,1,0:T(8,128)(2,1)} %get-tuple-element.50.refs_8_), channel_id=1, source_target_pairs={{0,1},{1,2},{2,3},{3,0},{4,5},{5,6},{6,7},{7,4},{8,9},{9,10},{10,1... | collective-permute-start | bytes 1572872 | tf_op jit(solution)/shard_map/ppermute | solution.py:26
  79.5 69.3 %all-to-all-start = ((bf16[8,2,2,256,128]{4,3,2,1,0:T(8,128)(2,1)}), bf16[8,2,2,256,128]{4,3,2,1,0:T(8,128)(2,1)S(1)}, u32[]{:S(2)}, u32[]{:S(2)}) async-start(bf16[8,2,2,256,128]{4,3,2,1,0:T(8,128)(2,1)} %shard_map.66), calls=%async_computation | async-start | bytes 4194304 | tf_op jit(solution)/shard_map/all_to_all | solution.py:188
  86.2 17.1 %collective-permute-start.20 = (bf16[8,2,128,128]{3,2,1,0:T(8,128)(2,1)}, bf16[8,2,128,128]{3,2,1,0:T(8,128)(2,1)S(1)}, u32[]{:S(2)}, u32[]{:S(2)}) collective-permute-start(bf16[8,2,128,128]{3,2,1,0:T(8,128)(2,1)} %get-tuple-element.51.refs_0_), channel_id=1, source_target_pairs={{0,12},{1,13},{2,14},{3,15},{4,0},{5,1},{6,2},{7,3},{8,4},{9,5},{1... | collective-permute-start | bytes 1572872 | tf_op jit(solution)/shard_map/ppermute | solution.py:26
  93.0 32.3 %collective-permute-start.33 = (bf16[8,2,128,128]{3,2,1,0:T(8,128)(2,1)}, bf16[8,2,128,128]{3,2,1,0:T(8,128)(2,1)S(1)}, u32[]{:S(2)}, u32[]{:S(2)}) collective-permute-start(bf16[8,2,128,128]{3,2,1,0:T(8,128)(2,1)} %get-tuple-element.61.refs_0_), channel_id=1, source_target_pairs={{0,12},{1,13},{2,14},{3,15},{4,0},{5,1},{6,2},{7,3},{8,4},{9,5},{1... | collective-permute-start | bytes 1572872 | tf_op jit(solution)/shard_map/ppermute | solution.py:26
  93.9 33.8 %collective-permute-start.32 = (bf16[8,2,128,128]{3,2,1,0:T(8,128)(2,1)}, bf16[8,2,128,128]{3,2,1,0:T(8,128)(2,1)}, u32[]{:S(2)}, u32[]{:S(2)}) collective-permute-start(bf16[8,2,128,128]{3,2,1,0:T(8,128)(2,1)} %get-tuple-element.61.refs_0_), channel_id=1, source_target_pairs={{0,8},{1,9},{2,10},{3,11},{4,12},{5,13},{6,14},{7,15},{8,0},{9,1},... | collective-permute-start | bytes 1572872 | tf_op jit(solution)/shard_map/ppermute | solution.py:26
  93.9 33.8 %collective-permute-start.31 = (bf16[8,2,128,128]{3,2,1,0:T(8,128)(2,1)}, bf16[8,2,128,128]{3,2,1,0:T(8,128)(2,1)}, u32[]{:S(2)}, u32[]{:S(2)}) collective-permute-start(bf16[8,2,128,128]{3,2,1,0:T(8,128)(2,1)} %get-tuple-element.61.refs_0_), channel_id=1, source_target_pairs={{0,4},{1,5},{2,6},{3,7},{4,8},{5,9},{6,10},{7,11},{8,12},{9,13},{1... | collective-permute-start | bytes 1572872 | tf_op jit(solution)/shard_map/ppermute | solution.py:26
  95.1 37.0 %collective-permute-start.36 = (bf16[8,2,128,128]{3,2,1,0:T(8,128)(2,1)}, bf16[8,2,128,128]{3,2,1,0:T(8,128)(2,1)}, u32[]{:S(2)}, u32[]{:S(2)}) collective-permute-start(bf16[8,2,128,128]{3,2,1,0:T(8,128)(2,1)} %get-tuple-element.62.refs_4_), channel_id=1, source_target_pairs={{0,3},{1,0},{2,1},{3,2},{4,7},{5,4},{6,5},{7,6},{8,11},{9,8},{10,9... | collective-permute-start | bytes 1572872 | tf_op jit(solution)/shard_map/ppermute | solution.py:26
  103.3 29.7 %collective-permute-start.35 = (bf16[8,2,128,128]{3,2,1,0:T(8,128)(2,1)}, bf16[8,2,128,128]{3,2,1,0:T(8,128)(2,1)}, u32[]{:S(2)}, u32[]{:S(2)}) collective-permute-start(bf16[8,2,128,128]{3,2,1,0:T(8,128)(2,1)} %get-tuple-element.62.refs_4_), channel_id=1, source_target_pairs={{0,2},{1,3},{2,0},{3,1},{4,6},{5,7},{6,4},{7,5},{8,10},{9,11},{10,... | collective-permute-start | bytes 1572872 | tf_op jit(solution)/shard_map/ppermute | solution.py:26
  125.3 15.9 %collective-permute-start.34 = (bf16[8,2,128,128]{3,2,1,0:T(8,128)(2,1)}, bf16[8,2,128,128]{3,2,1,0:T(8,128)(2,1)}, u32[]{:S(2)}, u32[]{:S(2)}) collective-permute-start(bf16[8,2,128,128]{3,2,1,0:T(8,128)(2,1)} %get-tuple-element.62.refs_4_), channel_id=1, source_target_pairs={{0,1},{1,2},{2,3},{3,0},{4,5},{5,6},{6,7},{7,4},{8,9},{9,10},{10,1... | collective-permute-start | bytes 1572872 | tf_op jit(solution)/shard_map/ppermute | solution.py:26
  127.7 26.9 %collective-permute-start.19 = (bf16[8,2,128,128]{3,2,1,0:T(8,128)(2,1)}, bf16[8,2,128,128]{3,2,1,0:T(8,128)(2,1)S(1)}, u32[]{:S(2)}, u32[]{:S(2)}) collective-permute-start(bf16[8,2,128,128]{3,2,1,0:T(8,128)(2,1)} %get-tuple-element.51.refs_0_), channel_id=1, source_target_pairs={{0,8},{1,9},{2,10},{3,11},{4,12},{5,13},{6,14},{7,15},{8,0},{9,1},... | collective-permute-start | bytes 1572872 | tf_op jit(solution)/shard_map/ppermute | solution.py:26
  127.7 26.9 %collective-permute-start.18 = (bf16[8,2,128,128]{3,2,1,0:T(8,128)(2,1)}, bf16[8,2,128,128]{3,2,1,0:T(8,128)(2,1)}, u32[]{:S(2)}, u32[]{:S(2)}) collective-permute-start(bf16[8,2,128,128]{3,2,1,0:T(8,128)(2,1)} %get-tuple-element.51.refs_0_), channel_id=1, source_target_pairs={{0,4},{1,5},{2,6},{3,7},{4,8},{5,9},{6,10},{7,11},{8,12},{9,13},{1... | collective-permute-start | bytes 1572872 | tf_op jit(solution)/shard_map/ppermute | solution.py:26
  132.1 22.4 %collective-permute-start.23 = (bf16[8,2,128,128]{3,2,1,0:T(8,128)(2,1)}, bf16[8,2,128,128]{3,2,1,0:T(8,128)(2,1)}, u32[]{:S(2)}, u32[]{:S(2)}) collective-permute-start(bf16[8,2,128,128]{3,2,1,0:T(8,128)(2,1)} %get-tuple-element.52.refs_8_), channel_id=1, source_target_pairs={{0,3},{1,0},{2,1},{3,2},{4,7},{5,4},{6,5},{7,6},{8,11},{9,8},{10,9... | collective-permute-start | bytes 1572872 | tf_op jit(solution)/shard_map/ppermute | solution.py:26
  133.0 21.6 %collective-permute-start.22 = (bf16[8,2,128,128]{3,2,1,0:T(8,128)(2,1)}, bf16[8,2,128,128]{3,2,1,0:T(8,128)(2,1)}, u32[]{:S(2)}, u32[]{:S(2)}) collective-permute-start(bf16[8,2,128,128]{3,2,1,0:T(8,128)(2,1)} %get-tuple-element.52.refs_8_), channel_id=1, source_target_pairs={{0,2},{1,3},{2,0},{3,1},{4,6},{5,7},{6,4},{7,5},{8,10},{9,11},{10,... | collective-permute-start | bytes 1572872 | tf_op jit(solution)/shard_map/ppermute | solution.py:26
  141.2 21.8 %collective-permute-start.21 = (bf16[8,2,128,128]{3,2,1,0:T(8,128)(2,1)}, bf16[8,2,128,128]{3,2,1,0:T(8,128)(2,1)}, u32[]{:S(2)}, u32[]{:S(2)}) collective-permute-start(bf16[8,2,128,128]{3,2,1,0:T(8,128)(2,1)} %get-tuple-element.52.refs_8_), channel_id=1, source_target_pairs={{0,1},{1,2},{2,3},{3,0},{4,5},{5,6},{6,7},{7,4},{8,9},{9,10},{10,1... | collective-permute-start | bytes 1572872 | tf_op jit(solution)/shard_map/ppermute | solution.py:26
  150.1 102.2 %all-to-all-start.1 = ((bf16[8,2,2,256,128]{4,3,2,1,0:T(8,128)(2,1)}), bf16[8,2,2,256,128]{4,3,2,1,0:T(8,128)(2,1)}, u32[]{:S(2)}, u32[]{:S(2)}) async-start(bf16[8,2,2,256,128]{4,3,2,1,0:T(8,128)(2,1)} %shard_map.70), calls=%async_computation.1 | async-start | bytes 4194304 | tf_op jit(solution)/shard_map/all_to_all | solution.py:188
  165.3 26.6 %collective-permute-start.39 = (bf16[8,2,128,128]{3,2,1,0:T(8,128)(2,1)}, bf16[8,2,128,128]{3,2,1,0:T(8,128)(2,1)S(1)}, u32[]{:S(2)}, u32[]{:S(2)}) collective-permute-start(bf16[8,2,128,128]{3,2,1,0:T(8,128)(2,1)} %get-tuple-element.63.refs_0_), channel_id=1, source_target_pairs={{0,12},{1,13},{2,14},{3,15},{4,0},{5,1},{6,2},{7,3},{8,4},{9,5},{1... | collective-permute-start | bytes 1572872 | tf_op jit(solution)/shard_map/ppermute | solution.py:26
  169.0 29.3 %collective-permute-start.38 = (bf16[8,2,128,128]{3,2,1,0:T(8,128)(2,1)}, bf16[8,2,128,128]{3,2,1,0:T(8,128)(2,1)S(1)}, u32[]{:S(2)}, u32[]{:S(2)}) collective-permute-start(bf16[8,2,128,128]{3,2,1,0:T(8,128)(2,1)} %get-tuple-element.63.refs_0_), channel_id=1, source_target_pairs={{0,8},{1,9},{2,10},{3,11},{4,12},{5,13},{6,14},{7,15},{8,0},{9,1},... | collective-permute-start | bytes 1572872 | tf_op jit(solution)/shard_map/ppermute | solution.py:26
  169.0 29.4 %collective-permute-start.37 = (bf16[8,2,128,128]{3,2,1,0:T(8,128)(2,1)}, bf16[8,2,128,128]{3,2,1,0:T(8,128)(2,1)S(1)}, u32[]{:S(2)}, u32[]{:S(2)}) collective-permute-start(bf16[8,2,128,128]{3,2,1,0:T(8,128)(2,1)} %get-tuple-element.63.refs_0_), channel_id=1, source_target_pairs={{0,4},{1,5},{2,6},{3,7},{4,8},{5,9},{6,10},{7,11},{8,12},{9,13},{1... | collective-permute-start | bytes 1572872 | tf_op jit(solution)/shard_map/ppermute | solution.py:26
  169.9 29.8 %collective-permute-start.42 = (bf16[8,2,128,128]{3,2,1,0:T(8,128)(2,1)}, bf16[8,2,128,128]{3,2,1,0:T(8,128)(2,1)S(1)}, u32[]{:S(2)}, u32[]{:S(2)}) collective-permute-start(bf16[8,2,128,128]{3,2,1,0:T(8,128)(2,1)} %get-tuple-element.64.refs_4_), channel_id=1, source_target_pairs={{0,3},{1,0},{2,1},{3,2},{4,7},{5,4},{6,5},{7,6},{8,11},{9,8},{10,9... | collective-permute-start | bytes 1572872 | tf_op jit(solution)/shard_map/ppermute | solution.py:26
  170.5 30.4 %collective-permute-start.41 = (bf16[8,2,128,128]{3,2,1,0:T(8,128)(2,1)}, bf16[8,2,128,128]{3,2,1,0:T(8,128)(2,1)S(1)}, u32[]{:S(2)}, u32[]{:S(2)}) collective-permute-start(bf16[8,2,128,128]{3,2,1,0:T(8,128)(2,1)} %get-tuple-element.64.refs_4_), channel_id=1, source_target_pairs={{0,2},{1,3},{2,0},{3,1},{4,6},{5,7},{6,4},{7,5},{8,10},{9,11},{10,... | collective-permute-start | bytes 1572872 | tf_op jit(solution)/shard_map/ppermute | solution.py:26
  191.9 14.3 %collective-permute-start.40 = (bf16[8,2,128,128]{3,2,1,0:T(8,128)(2,1)}, bf16[8,2,128,128]{3,2,1,0:T(8,128)(2,1)S(1)}, u32[]{:S(2)}, u32[]{:S(2)}) collective-permute-start(bf16[8,2,128,128]{3,2,1,0:T(8,128)(2,1)} %get-tuple-element.64.refs_4_), channel_id=1, source_target_pairs={{0,1},{1,2},{2,3},{3,0},{4,5},{5,6},{6,7},{7,4},{8,9},{9,10},{10,1... | collective-permute-start | bytes 1572872 | tf_op jit(solution)/shard_map/ppermute | solution.py:26
  198.3 15.1 %collective-permute-start.24 = (bf16[2,2,256,128]{3,2,1,0:T(8,128)(2,1)}, bf16[2,2,256,128]{3,2,1,0:T(8,128)(2,1)S(1)}, u32[]{:S(2)}, u32[]{:S(2)}) collective-permute-start(bf16[2,2,256,128]{3,2,1,0:T(8,128)(2,1)} %get-tuple-element.54), channel_id=1, source_target_pairs={{0,16},{16,0},{32,48},{48,32},{64,80},{80,64},{96,112},{112,96},{1... | collective-permute-start | bytes 786440 | tf_op jit(solution)/shard_map/ppermute | solution.py:197
  198.4 17.5 %collective-permute-start.25 = (bf16[2,2,256,128]{3,2,1,0:T(8,128)(2,1)}, bf16[2,2,256,128]{3,2,1,0:T(8,128)(2,1)S(1)}, u32[]{:S(2)}, u32[]{:S(2)}) collective-permute-start(bf16[2,2,256,128]{3,2,1,0:T(8,128)(2,1)} %get-tuple-element.55), channel_id=1, source_target_pairs={{0,32},{16,48},{32,64},{48,80},{64,96},{80,112},{96,0},{112,16},{1... | collective-permute-start | bytes 786440 | tf_op jit(solution)/shard_map/ppermute | solution.py:197
  199.8 16.8 %collective-permute-start.26 = (bf16[2,2,256,128]{3,2,1,0:T(8,128)(2,1)}, bf16[2,2,256,128]{3,2,1,0:T(8,128)(2,1)S(1)}, u32[]{:S(2)}, u32[]{:S(2)}) collective-permute-start(bf16[2,2,256,128]{3,2,1,0:T(8,128)(2,1)} %get-tuple-element.56), channel_id=1, source_target_pairs={{0,48},{16,32},{32,80},{48,64},{64,112},{80,96},{96,16},{112,0},{1... | collective-permute-start | bytes 786440 | tf_op jit(solution)/shard_map/ppermute | solution.py:197
  201.0 20.2 %collective-permute-start.27 = (bf16[2,2,256,128]{3,2,1,0:T(8,128)(2,1)}, bf16[2,2,256,128]{3,2,1,0:T(8,128)(2,1)}, u32[]{:S(2)}, u32[]{:S(2)}) collective-permute-start(bf16[2,2,256,128]{3,2,1,0:T(8,128)(2,1)} %get-tuple-element.57), channel_id=1, source_target_pairs={{0,64},{16,80},{32,96},{48,112},{64,0},{80,16},{96,32},{112,48},{1... | collective-permute-start | bytes 786440 | tf_op jit(solution)/shard_map/ppermute | solution.py:197
  206.2 19.6 %collective-permute-start.28 = (bf16[2,2,256,128]{3,2,1,0:T(8,128)(2,1)}, bf16[2,2,256,128]{3,2,1,0:T(8,128)(2,1)}, u32[]{:S(2)}, u32[]{:S(2)}) collective-permute-start(bf16[2,2,256,128]{3,2,1,0:T(8,128)(2,1)} %get-tuple-element.58), channel_id=1, source_target_pairs={{0,80},{16,64},{32,112},{48,96},{64,16},{80,0},{96,48},{112,32},{1... | collective-permute-start | bytes 786440 | tf_op jit(solution)/shard_map/ppermute | solution.py:197
  216.6 13.6 %collective-permute-start.43 = (bf16[2,2,256,128]{3,2,1,0:T(8,128)(2,1)}, bf16[2,2,256,128]{3,2,1,0:T(8,128)(2,1)S(1)}, u32[]{:S(2)}, u32[]{:S(2)}) collective-permute-start(bf16[2,2,256,128]{3,2,1,0:T(8,128)(2,1)} %get-tuple-element.66), channel_id=1, source_target_pairs={{0,16},{16,0},{32,48},{48,32},{64,80},{80,64},{96,112},{112,96},{1... | collective-permute-start | bytes 786440 | tf_op jit(solution)/shard_map/ppermute | solution.py:197
  225.8 17.8 %collective-permute-start.46 = (bf16[2,2,256,128]{3,2,1,0:T(8,128)(2,1)}, bf16[2,2,256,128]{3,2,1,0:T(8,128)(2,1)S(1)}, u32[]{:S(2)}, u32[]{:S(2)}) collective-permute-start(bf16[2,2,256,128]{3,2,1,0:T(8,128)(2,1)} %get-tuple-element.69), channel_id=1, source_target_pairs={{0,64},{16,80},{32,96},{48,112},{64,0},{80,16},{96,32},{112,48},{1... | collective-permute-start | bytes 786440 | tf_op jit(solution)/shard_map/ppermute | solution.py:197
  228.3 19.7 %collective-permute-start.47 = (bf16[2,2,256,128]{3,2,1,0:T(8,128)(2,1)}, bf16[2,2,256,128]{3,2,1,0:T(8,128)(2,1)S(1)}, u32[]{:S(2)}, u32[]{:S(2)}) collective-permute-start(bf16[2,2,256,128]{3,2,1,0:T(8,128)(2,1)} %get-tuple-element.70), channel_id=1, source_target_pairs={{0,80},{16,64},{32,112},{48,96},{64,16},{80,0},{96,48},{112,32},{1... | collective-permute-start | bytes 786440 | tf_op jit(solution)/shard_map/ppermute | solution.py:197
  230.1 18.8 %collective-permute-start.48 = (bf16[2,2,256,128]{3,2,1,0:T(8,128)(2,1)}, bf16[2,2,256,128]{3,2,1,0:T(8,128)(2,1)S(1)}, u32[]{:S(2)}, u32[]{:S(2)}) collective-permute-start(bf16[2,2,256,128]{3,2,1,0:T(8,128)(2,1)} %get-tuple-element.71), channel_id=1, source_target_pairs={{0,96},{16,112},{32,0},{48,16},{64,32},{80,48},{96,64},{112,80},{1... | collective-permute-start | bytes 786440 | tf_op jit(solution)/shard_map/ppermute | solution.py:197
  232.0 20.3 %collective-permute-start.49 = (bf16[2,2,256,128]{3,2,1,0:T(8,128)(2,1)}, bf16[2,2,256,128]{3,2,1,0:T(8,128)(2,1)S(1)}, u32[]{:S(2)}, u32[]{:S(2)}) collective-permute-start(bf16[2,2,256,128]{3,2,1,0:T(8,128)(2,1)} %get-tuple-element.72), channel_id=1, source_target_pairs={{0,112},{16,96},{32,16},{48,0},{64,48},{80,32},{96,80},{112,64},{1... | collective-permute-start | bytes 786440 | tf_op jit(solution)/shard_map/ppermute | solution.py:197
  264.9 16.2 %collective-permute-start.50 = (bf16[4,256,256]{2,1,0:T(8,128)(2,1)}, bf16[4,256,256]{2,1,0:T(8,128)(2,1)S(1)}, u32[]{:S(2)}, u32[]{:S(2)}) collective-permute-start(bf16[4,256,256]{2,1,0:T(8,128)(2,1)} %get-tuple-element.74), channel_id=1, source_target_pairs={{0,1},{1,2},{2,3},{3,0},{4,5},{5,6},{6,7},{7,4},{8,9},{9,10},{10,1... | collective-permute-start | bytes 1572872 | tf_op jit(solution)/shard_map/ppermute | solution.py:26
  266.3 27.4 %collective-permute-start.51 = (bf16[4,256,256]{2,1,0:T(8,128)(2,1)}, bf16[4,256,256]{2,1,0:T(8,128)(2,1)S(1)}, u32[]{:S(2)}, u32[]{:S(2)}) collective-permute-start(bf16[4,256,256]{2,1,0:T(8,128)(2,1)} %get-tuple-element.75), channel_id=1, source_target_pairs={{0,2},{1,3},{2,0},{3,1},{4,6},{5,7},{6,4},{7,5},{8,10},{9,11},{10,... | collective-permute-start | bytes 1572872 | tf_op jit(solution)/shard_map/ppermute | solution.py:26
  269.7 24.0 %collective-permute-start.52 = (bf16[4,256,256]{2,1,0:T(8,128)(2,1)}, bf16[4,256,256]{2,1,0:T(8,128)(2,1)S(1)}, u32[]{:S(2)}, u32[]{:S(2)}) collective-permute-start(bf16[4,256,256]{2,1,0:T(8,128)(2,1)} %get-tuple-element.76), channel_id=1, source_target_pairs={{0,3},{1,0},{2,1},{3,2},{4,7},{5,4},{6,5},{7,6},{8,11},{9,8},{10,9... | collective-permute-start | bytes 1572872 | tf_op jit(solution)/shard_map/ppermute | solution.py:26
  269.7 24.0 %collective-permute-start.53 = (bf16[4,256,256]{2,1,0:T(8,128)(2,1)}, bf16[4,256,256]{2,1,0:T(8,128)(2,1)S(1)}, u32[]{:S(2)}, u32[]{:S(2)}) collective-permute-start(bf16[4,256,256]{2,1,0:T(8,128)(2,1)} %get-tuple-element.78), channel_id=1, source_target_pairs={{0,4},{1,5},{2,6},{3,7},{4,8},{5,9},{6,10},{7,11},{8,12},{9,13},{1... | collective-permute-start | bytes 1572872 | tf_op jit(solution)/shard_map/ppermute | solution.py:26
  269.7 28.5 %collective-permute-start.54 = (bf16[4,256,256]{2,1,0:T(8,128)(2,1)}, bf16[4,256,256]{2,1,0:T(8,128)(2,1)S(1)}, u32[]{:S(2)}, u32[]{:S(2)}) collective-permute-start(bf16[4,256,256]{2,1,0:T(8,128)(2,1)} %get-tuple-element.79), channel_id=1, source_target_pairs={{0,8},{1,9},{2,10},{3,11},{4,12},{5,13},{6,14},{7,15},{8,0},{9,1},... | collective-permute-start | bytes 1572872 | tf_op jit(solution)/shard_map/ppermute | solution.py:26
  281.1 17.5 %collective-permute-start.55 = (bf16[4,256,256]{2,1,0:T(8,128)(2,1)}, bf16[4,256,256]{2,1,0:T(8,128)(2,1)S(1)}, u32[]{:S(2)}, u32[]{:S(2)}) collective-permute-start(bf16[4,256,256]{2,1,0:T(8,128)(2,1)} %get-tuple-element.80), channel_id=1, source_target_pairs={{0,12},{1,13},{2,14},{3,15},{4,0},{5,1},{6,2},{7,3},{8,4},{9,5},{1... | collective-permute-start | bytes 1572872 | tf_op jit(solution)/shard_map/ppermute | solution.py:26
  (62 other events, 764.6 us)

commit v5 on v4

--- a/solution.py
+++ b/solution.py
@@ -14,7 +14,13 @@
 BF16 = jnp.bfloat16
 F32 = jnp.float32
 CHUNKS = (2, 2, 2, 2)
-TURNED = (False, True, False, True)
+SPLIT = (192, 64)
+MODES = (
+    ((False, 0, 256),),
+    ((True, 0, 256),),
+    ((False, 0, 256),),
+    ((True, 0, SPLIT[0]), (False, SPLIT[0], SPLIT[1])),
+)
 
 
 def move(value, step_y, step_z):
@@ -55,16 +61,22 @@
             out_specs=[pl.BlockSpec(shape, lambda i: (0, 0, 0, 0)) for shape in shapes],
             scratch_shapes=[pltpu.SemaphoreType.DMA((sum(len(plan) for plan in plans),))],
         ),
-        compiler_params=pltpu.CompilerParams(vmem_limit_bytes=60 << 20),
+        compiler_params=pltpu.CompilerParams(vmem_limit_bytes=8 << 20),
         cost_estimate=pl.CostEstimate(flops=0, bytes_accessed=3 << 20, transcendentals=0),
     )(wave, *gots)
 
 
-def left_kernel(first_sector, turned, plan, place, pairs, size, *refs):
+def left_kernel(first_sector, modes, plan, place, pairs, size, *refs):
     total = 1 + max(entry[0] for entry in plan)
     pieces, left_hbm = refs[:total], refs[total]
-    outs = refs[total + 1 : -6]
-    whole, left, done, sems, left_sem, out_sems = refs[-6:]
+    rest = refs[total + 1 :]
+    out_count = sum(8 if turned else 1 for turned, _, _ in modes)
+    outs, rest = list(rest[:out_count]), rest[out_count:]
+    whole, left, sems, left_sem, out_sems = rest[:5]
+    dones = rest[5:]
+    targets = []
+    for turned, _, _ in modes:
+        targets.append([outs.pop(0) for _ in range(8 if turned else 1)])
     y, z, bond = place[0], place[1], place[2]
     count = whole.shape[0]
 
@@ -99,8 +111,10 @@
     terms, rows = left.shape[0], left.shape[1]
     zero = jnp.zeros((TILE, TILE), BF16)
 
-    def out_copy(block):
-        return pltpu.make_async_copy(done.at[block], outs[0].at[block], out_sems.at[block])
+    def out_copy(mode, block):
+        target = targets[mode]
+        ref = target[block] if len(target) == 8 else target[0].at[block]
+        return pltpu.make_async_copy(dones[mode].at[block], ref, out_sems.at[mode, block])
 
     for copy in copies:
         copy.wait()
@@ -127,38 +141,42 @@
                 axis=0,
             )
             middle = (jnp.dot(lhs, rhs, preferred_element_type=F32) * col_live).astype(BF16)
-            target = row // 2
-            if turned:
-                target = (target // 2 + SIDE - bond // 2) % SIDE * 2 + (target + bond) % 2
-            line = u // terms % 2 * TILE
-            for s in range(count):
-                done[target, s, term, line : line + TILE, :] = middle[
-                    :, s * TILE : (s + 1) * TILE
-                ]
-        if not turned:
-            out_copy(trip * 2).start()
-            out_copy(trip * 2 + 1).start()
-
-    if turned:
-        sent = [
-            pltpu.make_async_copy(done.at[block], outs[block], out_sems.at[block])
-            for block in range(8)
-        ]
-        for copy in sent:
-            copy.start()
-    else:
-        sent = [out_copy(block) for block in range(8)]
-    for copy in sent:
-        copy.wait()
-
-
-def left_stage(pieces, plan, turned, count, left_blocks, place, pairs, size, first_sector):
+            for mode, (turned, start, length) in enumerate(modes):
+                low_row = max(start, u // terms % 2 * TILE)
+                high_row = min(start + length, u // terms % 2 * TILE + TILE)
+                if low_row >= high_row:
+                    continue
+                target = row // 2
+                if turned:
+                    target = (target // 2 + SIDE - bond // 2) % SIDE * 2 + (target + bond) % 2
+                shift = u // terms % 2 * TILE
+                for s in range(count):
+                    dones[mode][target, s, term, low_row - start : high_row - start, :] = middle[
+                        low_row - shift : high_row - shift, s * TILE : (s + 1) * TILE
+                    ]
+        for mode, (turned, _, _) in enumerate(modes):
+            if not turned:
+                out_copy(mode, trip * 2).start()
+                out_copy(mode, trip * 2 + 1).start()
+
+    for mode, (turned, _, _) in enumerate(modes):
+        if turned:
+            for block in range(8):
+                out_copy(mode, block).start()
+    for mode in range(len(modes)):
+        for block in range(8):
+            out_copy(mode, block).wait()
+
+
+def left_stage(pieces, plan, modes, count, left_blocks, place, pairs, size, first_sector):
     terms = left_blocks.shape[0]
-    block = (count, terms, 2 * TILE, TILE)
-    shapes = [block] * 8 if turned else [(8, *block)]
+    blocks = [(count, terms, length, TILE) for _, _, length in modes]
+    shapes = []
+    for (turned, _, _), block in zip(modes, blocks):
+        shapes += [block] * 8 if turned else [(8, *block)]
     anywhere = pl.BlockSpec(memory_space=pl.ANY)
-    return pl.pallas_call(
-        functools.partial(left_kernel, first_sector, turned, plan),
+    results = pl.pallas_call(
+        functools.partial(left_kernel, first_sector, modes, plan),
         out_shape=[jax.ShapeDtypeStruct(shape, BF16) for shape in shapes],
         grid_spec=pltpu.PrefetchScalarGridSpec(
             num_scalar_prefetch=3,
@@ -168,11 +186,11 @@
             scratch_shapes=[
                 pltpu.VMEM((count, 64, TILE, TILE), BF16),
                 pltpu.VMEM(left_blocks.shape, BF16),
-                pltpu.VMEM((8, *block), BF16),
                 pltpu.SemaphoreType.DMA((32,)),
                 pltpu.SemaphoreType.DMA((4,)),
-                pltpu.SemaphoreType.DMA((8,)),
-            ],
+                pltpu.SemaphoreType.DMA((len(modes), 8)),
+            ]
+            + [pltpu.VMEM((8, *block), BF16) for block in blocks],
         ),
         compiler_params=pltpu.CompilerParams(vmem_limit_bytes=60 << 20),
         cost_estimate=pl.CostEstimate(
@@ -181,6 +199,8 @@
             transcendentals=0,
         ),
     )(place, pairs, size, *pieces, left_blocks)
+    results = list(results)
+    return [[results.pop(0) for _ in range(8 if turned else 1)] for turned, _, _ in modes]
 
 
 def exchange(blocks):
@@ -198,11 +218,16 @@
     return got
 
 
-def right_kernel(layout, place, pairs, size, *refs):
+def right_kernel(layout, half, place, pairs, size, *refs):
     total = sum(8 if turned else 1 for _, turned in layout)
     arrived, right = list(refs[:total]), refs[total]
-    outs_a, outs_b = refs[total + 1 : total + 5], refs[total + 5 : total + 9]
-    middle, blocks, sum_a, sum_b, sems, right_sems, out_sems = refs[total + 9 :]
+    rest = refs[total + 1 :]
+    if half == 0:
+        outs_a, outs_b, rest = rest[:4], rest[4:8], rest[8:]
+    else:
+        out, rest = rest[0], rest[1:]
+    middle, blocks, sum_a, sum_b, sems, right_sems, out_sems = rest
+    first_row = sum(SPLIT[:half])
     bond = place[2]
     rows, terms = middle.shape[2], middle.shape[1]
     copies = []
@@ -214,6 +239,8 @@
             piece = arrived.pop(0) if turned else whole.at[block]
             if turned:
                 source = (bond // 2 + SIDE - block // 2) % SIDE * 2 + (bond + block) % 2
+            if piece.shape[2] != rows:
+                piece = piece.at[:, :, first_row : first_row + rows]
             copies.append(
                 pltpu.make_async_copy(
                     piece, middle.at[pl.ds(source * 8 + first, count)], sems.at[len(copies)]
@@ -235,10 +262,14 @@
 
     for step_y in range(SIDE):
         right_copy(0, step_y).start()
-    line = lax.broadcasted_iota(jnp.int32, (TILE, TILE), 0)
-    lane = lax.broadcasted_iota(jnp.int32, (TILE, TILE), 1)
-    row_live = jnp.concatenate([line < size[bond * 2 + h] for h in range(rows // TILE)], axis=0)
-    lanes = jnp.concatenate([lane] * (rows // TILE), axis=0)
+    lane = lax.broadcasted_iota(jnp.int32, (rows, TILE), 1)
+    lives = []
+    for h in range(2):
+        low, high = max(first_row, h * TILE), min(first_row + rows, (h + 1) * TILE)
+        if low < high:
+            line = lax.broadcasted_iota(jnp.int32, (high - low, TILE), 0) + (low - h * TILE)
+            lives.append(line < size[bond * 2 + h])
+    row_live = jnp.concatenate(lives, axis=0)
     for copy in copies:
         copy.wait()
     for step_z in range(1, SIDE):
@@ -269,14 +300,16 @@
                         [block[term, q, p] for term in range(terms) for p in range(2)], axis=0
                     )
                     product = jnp.dot(lhs, rhs, preferred_element_type=F32)
-                    keep = row_live & (lanes < size[col])
+                    keep = row_live & (lane < size[col])
                     value = jnp.where(keep, product, 0.0).astype(BF16)
-                    if q < 2:
+                    if half == 1:
+                        sum_a[owner, :, q * TILE : (q + 1) * TILE] = value
+                    elif q < 2:
                         sum_a[step_z, step_y, :, q * TILE : (q + 1) * TILE] = value
                     else:
                         sum_b[step_y, step_z, :, (q - 2) * TILE : (q - 1) * TILE] = value
 
-        for step_z in step_zs:
+        for step_z in step_zs if half == 0 else ():
             sent.append(
                 pltpu.make_async_copy(sum_a.at[step_z], outs_a[step_z], out_sems.at[len(sent)])
             )
@@ -288,39 +321,45 @@
                     )
                 )
                 sent[-1].start()
+    if half == 1:
+        sent.append(pltpu.make_async_copy(sum_a, out, out_sems.at[0]))
+        sent[-1].start()
     for copy in sent:
         copy.wait()
 
 
-def right_stage(arrived, right_blocks, place, pairs, size):
+def right_stage(arrived, half, right_blocks, place, pairs, size):
     layout = tuple((count, len(blocks) > 1) for count, blocks in zip(CHUNKS, arrived))
     arrived = [block for blocks in arrived for block in blocks]
-    terms, rows = right_blocks.shape[0], 2 * TILE
-    shape = jax.ShapeDtypeStruct((SIDE, rows, 2 * TILE), BF16)
+    terms, rows = right_blocks.shape[0], SPLIT[half]
+    if half == 0:
+        shapes = [jax.ShapeDtypeStruct((SIDE, rows, 2 * TILE), BF16)] * 8
+        scratch = [pltpu.VMEM((SIDE, SIDE, rows, 2 * TILE), BF16)] * 2
+    else:
+        shapes = [jax.ShapeDtypeStruct((GROUP, rows, 4 * TILE), BF16)]
+        scratch = [pltpu.VMEM(shapes[0].shape, BF16), pltpu.VMEM((16, TILE), BF16)]
     anywhere = pl.BlockSpec(memory_space=pl.ANY)
     return pl.pallas_call(
-        functools.partial(right_kernel, layout),
-        name="right",
-        out_shape=[shape] * 8,
+        functools.partial(right_kernel, layout, half),
+        out_shape=shapes,
         grid_spec=pltpu.PrefetchScalarGridSpec(
             num_scalar_prefetch=3,
             grid=(1,),
             in_specs=[anywhere] * (len(arrived) + 1),
-            out_specs=[anywhere] * 8,
+            out_specs=[anywhere] * len(shapes),
             scratch_shapes=[
                 pltpu.VMEM((64, terms, rows, TILE), BF16),
                 pltpu.VMEM((GROUP, terms, 4, 2, TILE, TILE), BF16),
-                pltpu.VMEM((SIDE, SIDE, rows, 2 * TILE), BF16),
-                pltpu.VMEM((SIDE, SIDE, rows, 2 * TILE), BF16),
+                *scratch,
                 pltpu.SemaphoreType.DMA((8 * len(layout),)),
                 pltpu.SemaphoreType.DMA((GROUP,)),
                 pltpu.SemaphoreType.DMA((SIDE * (SIDE + 1),)),
             ],
         ),
-        compiler_params=pltpu.CompilerParams(vmem_limit_bytes=60 << 20),
+        compiler_params=pltpu.CompilerParams(vmem_limit_bytes=58 << 20),
         cost_estimate=pl.CostEstimate(
             flops=2 * terms * rows * 256 * 8192,
-            bytes_accessed=(20 << 20),
+            bytes_accessed=(14 << 20),
             transcendentals=0,
         ),
     )(place, pairs, size, *arrived, right_blocks)
@@ -354,24 +393,27 @@
 
 
 def last_kernel(*refs):
-    out = refs[-1]
+    block, out = refs[-2], refs[-1]
     rows, width = refs[0].shape
-    for block in range(len(refs) // SIDE):
-        mine = refs[block * 4 : block * 4 + 4]
+    for side in range(2):
+        mine = refs[side * 4 : side * 4 + 4]
         total = mine[0][...]
         for other in mine[1:]:
             total = total + other[...].astype(F32)
-        line, col = block // 2 * rows, block % 2 * width
-        out[line : line + rows, col : col + width] = total
+        out[:rows, side * width : (side + 1) * width] = total
+    total = block[0].astype(F32)
+    for source in range(1, GROUP):
+        total = total + block[source].astype(F32)
+    out[rows:, :] = total
 
 
 def last_stage(pieces):
-    rows, width = pieces[0].shape
+    rows, width = sum(SPLIT), 4 * TILE
     whole = pl.BlockSpec(memory_space=pltpu.VMEM)
     return pl.pallas_call(
         last_kernel,
         name="far_sum",
-        out_shape=jax.ShapeDtypeStruct((rows * len(pieces) // 8, 2 * width), F32),
+        out_shape=jax.ShapeDtypeStruct((rows, width), F32),
         in_specs=[whole] * len(pieces),
         out_specs=whole,
         compiler_params=pltpu.CompilerParams(vmem_limit_bytes=16 << 20),
@@ -438,7 +480,7 @@
         middles = left_stage(
             pieces,
             tuple(plan),
-            TURNED[chunk],
+            MODES[chunk],
             count,
             left_blocks,
             place,
@@ -446,13 +488,20 @@
             sector_size,
             starts[chunk],
         )
-        arrived.append(exchange(middles))
-    parts = right_stage(arrived, right_blocks, place, rights, sector_size)
+        for middle in middles:
+            arrived.append(exchange(middle))
+    parts = []
+    for half in range(2):
+        mine = arrived[: chunk_count - 1] + [arrived[chunk_count - 1 + half]]
+        parts.append(right_stage(mine, half, right_blocks, place, rights, sector_size))
+    block = lax.all_to_all(parts[1][0], "op", split_axis=0, concat_axis=0, tiled=True)
+    parts = parts[0]
     got = [parts[0]] + [move(parts[d], 0, d) for d in range(1, SIDE)]
     got += [parts[4]] + [move(parts[4 + d], d, 0) for d in range(1, SIDE)]
     sums = sum_stage(got)
     finals = [sums[0]] + [move(sums[d], d, 0) for d in range(1, SIDE)]
     finals += [sums[4]] + [move(sums[4 + d], 0, d) for d in range(1, SIDE)]
+    finals.append(block)
     return last_stage(finals)
 
 

time: 318 us -> 331 us (1.041)
  starting transfers between devices: 108 us -> 115 us
  local copies, waits for them, and re-layouts: 8.07 us -> 12.1 us
    ppermute x14, waiting for transfers between devices: 29.1 us -> 20.6 us  [exchange(): got.append(lax.ppermute(blocks[turned], 'bond', pairs))]
    ppermute x48, starting transfers between devices: 85.5 us -> 77.3 us  [move(): return lax.ppermute(value, 'op', pairs)]
    ppermute x48, waiting for transfers between devices: 121 us -> 129 us  [move(): return lax.ppermute(value, 'op', pairs)]
    pallas_call x5 -> x6, Pallas kernels: 36.8 us -> 42.9 us  [the longest x4 25 us: left_stage(): pl.pallas_call(functools.partial(left_kernel, first_sector, modes, plan),...]
    all_to_all x0 -> x1, starting transfers between devices: none -> 5.44 us  [apply_slab(): lax.all_to_all(parts[1][0], 'op', split_axis=0, concat_axis=0, tiled=True)]
    ppermute x14, starting transfers between devices: 14.1 us -> 18.7 us  [exchange(): got.append(lax.ppermute(blocks[turned], 'bond', pairs))]
    all_to_all x2 -> x3, starting transfers between devices: 8.73 us -> 13.1 us  [exchange(): lax.all_to_all(blocks[0], 'bond', split_axis=0, concat_axis=0, tiled=True)]
    unnamed x94 -> x156, local copies, waits for them, and re-layouts: 6.72 us -> 10.6 us
  transfers between devices with their start and end apart: 64 -> 66, of which waited for: 27 -> 29; matrix products, arithmetic and copies ran while one was open for 1% -> 1% of each run, Pallas kernels for 9% -> 14%
where the time goes in v5:
time: 331 us; the launch traced here: 329 us
  waiting for transfers between devices  149 us (45%)
  starting transfers between devices  115 us (35%)
  Pallas kernels  52.3 us (16%)
  local copies, waits for them, and re-layouts  12.1 us (4%)
    ppermute x48, waiting for transfers between devices, move(): return lax.ppermute(value, 'op', pairs)  129 us
    ppermute x48, starting transfers between devices, move(): return lax.ppermute(value, 'op', pairs)  77.3 us
    pallas_call x4, Pallas kernels, left_stage(): pl.pallas_call(functools.partial(left_kernel, first_sector, modes, plan),...  25 us
    ppermute x14, waiting for transfers between devices, exchange(): got.append(lax.ppermute(blocks[turned], 'bond', pairs))  20.6 us
    ppermute x14, starting transfers between devices, exchange(): got.append(lax.ppermute(blocks[turned], 'bond', pairs))  18.7 us
    pallas_call x2, Pallas kernels, right_stage(): pl.pallas_call(functools.partial(right_kernel, layout, half), out_shape=s...  17.9 us
    all_to_all x3, starting transfers between devices, exchange(): lax.all_to_all(blocks[0], 'bond', split_axis=0, concat_axis=0, tiled=True)  13.1 us
    unnamed x156, local copies, waits for them, and re-layouts  10.6 us
  transfers between devices with their start and end apart: 66, of which 29 were waited for; matrix products, arithmetic and copies ran while one was open for 1% of the time, Pallas kernels for 14%

profile of v5, /device:TPU:0, one launch (start us, length us, event | category | flops | bytes accessed | tf_op | source)
XLA Modules:
  0.0 329.5 jit_solution(16857320647949936734)
XLA Ops:
  1.5 4.2 %collective-permute-start.2 = (bf16[4,2,128,128]{3,2,1,0:T(8,128)(2,1)S(1)}, bf16[4,2,128,128]{3,2,1,0:T(8,128)(2,1)S(1)}, u32[]{:S(2)}, u32[]{:S(2)}) collective-permute-start(bf16[4,2,128,128]{3,2,1,0:T(8,128)(2,1)S(1)} %get-tuple-element.48.refs_1_), channel_id=1, source_target_pairs={{0,3},{1,0},{2,1},{3,2},{4,7},{5,4},{6,5},{7,6},{8,11},{9,8},{10,9... | collective-permute-start | bytes 786440 | tf_op jit(solution)/shard_map/ppermute | solution.py:32
  7.0 3.0 collective-permute-start.5
  10.6 6.3 %collective-permute-done.2.refs_2_ = bf16[4,2,128,128]{3,2,1,0:T(8,128)(2,1)S(1)} collective-permute-done((bf16[4,2,128,128]{3,2,1,0:T(8,128)(2,1)S(1)}, bf16[4,2,128,128]{3,2,1,0:T(8,128)(2,1)S(1)}, u32[]{:S(2)}, u32[]{:S(2)}) %collective-permute-start.2) | collective-permute-done | bytes 262176 | tf_op jit(solution)/shard_map/ppermute | solution.py:32
  20.3 3.2 collective-permute-start.9
  23.5 2.6 collective-permute-done.3.refs_3_
  28.4 3.0 collective-permute-start.10
  31.4 3.7 %collective-permute-start.17 = (bf16[4,2,128,128]{3,2,1,0:T(8,128)(2,1)S(1)}, bf16[4,2,128,128]{3,2,1,0:T(8,128)(2,1)S(1)}, u32[]{:S(2)}, u32[]{:S(2)}) collective-permute-start(bf16[4,2,128,128]{3,2,1,0:T(8,128)(2,1)S(1)} %get-tuple-element.49.refs_9_), channel_id=1, source_target_pairs={{0,3},{1,0},{2,1},{3,2},{4,7},{5,4},{6,5},{7,6},{8,11},{9,8},{10,9... | collective-permute-start | bytes 786440 | tf_op jit(solution)/shard_map/ppermute | solution.py:32
  36.0 2.9 collective-permute-done.7.refs_3_
  40.8 3.2 collective-permute-done.17.refs_15_
  44.0 2.4 collective-permute-start.6
  46.4 4.2 %collective-permute-start.16 = (bf16[8,2,128,128]{3,2,1,0:T(8,128)(2,1)}, bf16[8,2,128,128]{3,2,1,0:T(8,128)(2,1)S(1)}, u32[]{:S(2)}, u32[]{:S(2)}) collective-permute-start(bf16[8,2,128,128]{3,2,1,0:T(8,128)(2,1)} %get-tuple-element.51.refs_8_), channel_id=1, source_target_pairs={{0,3},{1,0},{2,1},{3,2},{4,7},{5,4},{6,5},{7,6},{8,11},{9,8},{10,9... | collective-permute-start | bytes 1572872 | tf_op jit(solution)/shard_map/ppermute | solution.py:32
  50.6 3.5 %collective-permute-done.10.refs_6_.refs_5_ = bf16[8,2,128,128]{3,2,1,0:T(8,128)(2,1)S(1)} collective-permute-done((bf16[8,2,128,128]{3,2,1,0:T(8,128)(2,1)}, bf16[8,2,128,128]{3,2,1,0:T(8,128)(2,1)S(1)}, u32[]{:S(2)}, u32[]{:S(2)}) %collective-permute-start.10) | collective-permute-done | bytes 524320 | tf_op jit(solution)/shard_map/ppermute | solution.py:32
  57.8 4.0 %collective-permute-done.6.refs_2_.refs_3_ = bf16[8,2,128,128]{3,2,1,0:T(8,128)(2,1)S(1)} collective-permute-done((bf16[8,2,128,128]{3,2,1,0:T(8,128)(2,1)}, bf16[8,2,128,128]{3,2,1,0:T(8,128)(2,1)S(1)}, u32[]{:S(2)}, u32[]{:S(2)}) %collective-permute-start.6) | collective-permute-done | bytes 524320 | tf_op jit(solution)/shard_map/ppermute | solution.py:32
  61.8 5.4 %collective-permute-done.16.refs_14_.refs_2_ = bf16[8,2,128,128]{3,2,1,0:T(8,128)(2,1)S(1)} collective-permute-done((bf16[8,2,128,128]{3,2,1,0:T(8,128)(2,1)}, bf16[8,2,128,128]{3,2,1,0:T(8,128)(2,1)S(1)}, u32[]{:S(2)}, u32[]{:S(2)}) %collective-permute-start.16) | collective-permute-done | bytes 524320 | tf_op jit(solution)/shard_map/ppermute | solution.py:32
  67.3 3.6 %collective-permute-done.12.refs_10_.refs_0_ = bf16[8,2,128,128]{3,2,1,0:T(8,128)(2,1)S(1)} collective-permute-done((bf16[8,2,128,128]{3,2,1,0:T(8,128)(2,1)}, bf16[8,2,128,128]{3,2,1,0:T(8,128)(2,1)S(1)}, u32[]{:S(2)}, u32[]{:S(2)}) %collective-permute-start.12) | collective-permute-done | bytes 524320 | tf_op jit(solution)/shard_map/ppermute | solution.py:32
  71.7 6.1 %shard_map.66 = bf16[8,2,2,256,128]{4,3,2,1,0:T(8,128)(2,1)} custom-call(s32[3]{0:T(128)} %pad_add_fusion.place, s32[64]{0:T(128)} %reshape.10.pairs, s32[64]{0:T(128)} %size.11, bf16[8,2,128,128]{3,2,1,0:T(8,128)(2,1)} %get-tuple-element.50.refs_0_, bf16[4,2,128,128]{3,2,1,0:T(8,128)(2,1)} %copy-done.20, bf16[8,2,128,128]{3,2,1,0:T(8,128)(2,1)} %copy-done.6, ...), custom_call_target="tpu_custom_call" | custom-call | flops 536870912 | bytes 8388608 | tf_op jit(solution)/shard_map/pallas_call | solution.py:178
  77.9 4.6 %all-to-all-start = ((bf16[8,2,2,256,128]{4,3,2,1,0:T(8,128)(2,1)}), bf16[8,2,2,256,128]{4,3,2,1,0:T(8,128)(2,1)}, u32[]{:S(2)}, u32[]{:S(2)}) async-start(bf16[8,2,2,256,128]{4,3,2,1,0:T(8,128)(2,1)} %shard_map.66), calls=%async_computation | async-start | bytes 4194304 | tf_op jit(solution)/shard_map/all_to_all | solution.py:208
  86.0 5.8 %collective-permute-start.33 = (bf16[8,2,128,128]{3,2,1,0:T(8,128)(2,1)S(1)}, bf16[8,2,128,128]{3,2,1,0:T(8,128)(2,1)S(1)}, u32[]{:S(2)}, u32[]{:S(2)}) collective-permute-start(bf16[8,2,128,128]{3,2,1,0:T(8,128)(2,1)S(1)} %get-tuple-element.62.refs_0_), channel_id=1, source_target_pairs={{0,12},{1,13},{2,14},{3,15},{4,0},{5,1},{6,2},{7,3},{8,4},{9,5},{1... | collective-permute-start | bytes 1572872 | tf_op jit(solution)/shard_map/ppermute | solution.py:32
  92.8 22.1 %collective-permute-done.33.refs_3_ = bf16[8,2,128,128]{3,2,1,0:T(8,128)(2,1)S(1)} collective-permute-done((bf16[8,2,128,128]{3,2,1,0:T(8,128)(2,1)S(1)}, bf16[8,2,128,128]{3,2,1,0:T(8,128)(2,1)S(1)}, u32[]{:S(2)}, u32[]{:S(2)}) %collective-permute-start.33) | collective-permute-done | bytes 524320 | tf_op jit(solution)/shard_map/ppermute | solution.py:32
  117.2 3.8 %collective-permute-start.20 = (bf16[8,2,128,128]{3,2,1,0:T(8,128)(2,1)}, bf16[8,2,128,128]{3,2,1,0:T(8,128)(2,1)S(1)}, u32[]{:S(2)}, u32[]{:S(2)}) collective-permute-start(bf16[8,2,128,128]{3,2,1,0:T(8,128)(2,1)} %get-tuple-element.52.refs_0_), channel_id=1, source_target_pairs={{0,12},{1,13},{2,14},{3,15},{4,0},{5,1},{6,2},{7,3},{8,4},{9,5},{1... | collective-permute-start | bytes 1572872 | tf_op jit(solution)/shard_map/ppermute | solution.py:32
  122.7 6.9 %collective-permute-done.34.refs_5_ = bf16[8,2,128,128]{3,2,1,0:T(8,128)(2,1)} collective-permute-done((bf16[8,2,128,128]{3,2,1,0:T(8,128)(2,1)S(1)}, bf16[8,2,128,128]{3,2,1,0:T(8,128)(2,1)}, u32[]{:S(2)}, u32[]{:S(2)}) %collective-permute-start.34) | collective-permute-done | bytes 524320 | tf_op jit(solution)/shard_map/ppermute | solution.py:32
  129.6 6.0 %shard_map.70 = bf16[8,2,2,256,128]{4,3,2,1,0:T(8,128)(2,1)} custom-call(s32[3]{0:T(128)} %pad_add_fusion.place, s32[64]{0:T(128)} %reshape.10.pairs, s32[64]{0:T(128)} %size.11, bf16[8,2,128,128]{3,2,1,0:T(8,128)(2,1)} %copy-done.34, bf16[8,2,128,128]{3,2,1,0:T(8,128)(2,1)} %copy-done.56, bf16[8,2,128,128]{3,2,1,0:T(8,128)(2,1)} %copy-done.55, ...), custom_call_target="tpu_custom_call" | custom-call | flops 536870912 | bytes 8388608 | tf_op jit(solution)/shard_map/pallas_call | solution.py:178
  135.7 4.4 %all-to-all-start.1 = ((bf16[8,2,2,256,128]{4,3,2,1,0:T(8,128)(2,1)}), bf16[8,2,2,256,128]{4,3,2,1,0:T(8,128)(2,1)}, u32[]{:S(2)}, u32[]{:S(2)}) async-start(bf16[8,2,2,256,128]{4,3,2,1,0:T(8,128)(2,1)} %shard_map.70), calls=%async_computation.1 | async-start | bytes 4194304 | tf_op jit(solution)/shard_map/all_to_all | solution.py:208
  140.1 4.5 %collective-permute-start.18 = (bf16[8,2,128,128]{3,2,1,0:T(8,128)(2,1)}, bf16[8,2,128,128]{3,2,1,0:T(8,128)(2,1)S(1)}, u32[]{:S(2)}, u32[]{:S(2)}) collective-permute-start(bf16[8,2,128,128]{3,2,1,0:T(8,128)(2,1)} %get-tuple-element.52.refs_0_), channel_id=1, source_target_pairs={{0,4},{1,5},{2,6},{3,7},{4,8},{5,9},{6,10},{7,11},{8,12},{9,13},{1... | collective-permute-start | bytes 1572872 | tf_op jit(solution)/shard_map/ppermute | solution.py:32
  146.8 9.9 %collective-permute-done.19.refs_4_ = bf16[8,2,128,128]{3,2,1,0:T(8,128)(2,1)S(1)} collective-permute-done((bf16[8,2,128,128]{3,2,1,0:T(8,128)(2,1)}, bf16[8,2,128,128]{3,2,1,0:T(8,128)(2,1)S(1)}, u32[]{:S(2)}, u32[]{:S(2)}) %collective-permute-start.19) | collective-permute-done | bytes 524320 | tf_op jit(solution)/shard_map/ppermute | solution.py:32
  156.7 10.5 %collective-permute-done.18.refs_2_.refs_3_ = bf16[8,2,128,128]{3,2,1,0:T(8,128)(2,1)S(1)} collective-permute-done((bf16[8,2,128,128]{3,2,1,0:T(8,128)(2,1)}, bf16[8,2,128,128]{3,2,1,0:T(8,128)(2,1)S(1)}, u32[]{:S(2)}, u32[]{:S(2)}) %collective-permute-start.18) | collective-permute-done | bytes 524320 | tf_op jit(solution)/shard_map/ppermute | solution.py:32
  167.2 4.0 %collective-permute-done.21.refs_10_.refs_0_ = bf16[8,2,128,128]{3,2,1,0:T(8,128)(2,1)S(1)} collective-permute-done((bf16[8,2,128,128]{3,2,1,0:T(8,128)(2,1)}, bf16[8,2,128,128]{3,2,1,0:T(8,128)(2,1)S(1)}, u32[]{:S(2)}, u32[]{:S(2)}) %collective-permute-start.21) | collective-permute-done | bytes 524320 | tf_op jit(solution)/shard_map/ppermute | solution.py:32
  174.1 6.5 %shard_map.68 = (bf16[2,2,256,128]{3,2,1,0:T(8,128)(2,1)}, bf16[2,2,256,128]{3,2,1,0:T(8,128)(2,1)}, bf16[2,2,256,128]{3,2,1,0:T(8,128)(2,1)}, bf16[2,2,256,128]...) custom-call(s32[3]{0:T(128)} %pad_add_fusion.place, ...), custom_call_target="tpu_custom_call" | custom-call | flops 536870912 | bytes 8388608 | tf_op jit(solution)/shard_map/pallas_call | solution.py:178
  185.9 4.9 %collective-permute-done.25.refs_3_ = bf16[2,2,256,128]{3,2,1,0:T(8,128)(2,1)S(1)} collective-permute-done((bf16[2,2,256,128]{3,2,1,0:T(8,128)(2,1)}, bf16[2,2,256,128]{3,2,1,0:T(8,128)(2,1)S(1)}, u32[]{:S(2)}, u32[]{:S(2)}) %collective-permute-start.25) | collective-permute-done | bytes 262176 | tf_op jit(solution)/shard_map/ppermute | solution.py:217
  192.9 6.1 %collective-permute-done.38.refs_2_ = bf16[8,2,128,128]{3,2,1,0:T(8,128)(2,1)S(1)} collective-permute-done((bf16[8,2,128,128]{3,2,1,0:T(8,128)(2,1)}, bf16[8,2,128,128]{3,2,1,0:T(8,128)(2,1)S(1)}, u32[]{:S(2)}, u32[]{:S(2)}) %collective-permute-start.38) | collective-permute-done | bytes 524320 | tf_op jit(solution)/shard_map/ppermute | solution.py:32
  199.0 10.4 %collective-permute-done.37.refs_1_ = bf16[8,2,128,128]{3,2,1,0:T(8,128)(2,1)S(1)} collective-permute-done((bf16[8,2,128,128]{3,2,1,0:T(8,128)(2,1)}, bf16[8,2,128,128]{3,2,1,0:T(8,128)(2,1)S(1)}, u32[]{:S(2)}, u32[]{:S(2)}) %collective-permute-start.37) | collective-permute-done | bytes 524320 | tf_op jit(solution)/shard_map/ppermute | solution.py:32
  210.1 2.7 collective-permute-start.27
  219.1 6.3 %shard_map.72 = (bf16[2,2,192,128]{3,2,1,0:T(8,128)(2,1)}, bf16[2,2,192,128]{3,2,1,0:T(8,128)(2,1)}, bf16[2,2,192,128]{3,2,1,0:T(8,128)(2,1)}, bf16[2,2,192,128]...) custom-call(s32[3]{0:T(128)} %pad_add_fusion.place, ...), custom_call_target="tpu_custom_call" | custom-call | flops 536870912 | bytes 8388608 | tf_op jit(solution)/shard_map/pallas_call | solution.py:178
  226.4 4.1 %all-to-all-start.2 = ((bf16[8,2,2,64,128]{4,3,2,1,0:T(8,128)(2,1)}), bf16[8,2,2,64,128]{4,3,2,1,0:T(8,128)(2,1)S(1)}, u32[]{:S(2)}, u32[]{:S(2)}) async-start(bf16[8,2,2,64,128]{4,3,2,1,0:T(8,128)(2,1)} %get-tuple-element.90), calls=%async_computation.2 | async-start | bytes 1048576 | tf_op jit(solution)/shard_map/all_to_all | solution.py:208
  232.4 2.7 collective-permute-start.46
  235.7 4.1 %collective-permute-start.47 = (bf16[2,2,192,128]{3,2,1,0:T(8,128)(2,1)}, bf16[2,2,192,128]{3,2,1,0:T(8,128)(2,1)S(1)}, u32[]{:S(2)}, u32[]{:S(2)}) collective-permute-start(bf16[2,2,192,128]{3,2,1,0:T(8,128)(2,1)} %get-tuple-element.71), channel_id=1, source_target_pairs={{0,80},{16,64},{32,112},{48,96},{64,16},{80,0},{96,48},{112,32},{1... | collective-permute-start | bytes 589832 | tf_op jit(solution)/shard_map/ppermute | solution.py:217
  244.4 5.5 %collective-permute-done.46.refs_14_ = bf16[2,2,192,128]{3,2,1,0:T(8,128)(2,1)S(1)} collective-permute-done((bf16[2,2,192,128]{3,2,1,0:T(8,128)(2,1)}, bf16[2,2,192,128]{3,2,1,0:T(8,128)(2,1)S(1)}, u32[]{:S(2)}, u32[]{:S(2)}) %collective-permute-start.46) | collective-permute-done | bytes 196640 | tf_op jit(solution)/shard_map/ppermute | solution.py:217
  249.9 3.1 collective-permute-done.47.refs_15_
  258.1 10.3 %shard_map.73 = (bf16[4,192,256]{2,1,0:T(8,128)(2,1)}, bf16[4,192,256]{2,1,0:T(8,128)(2,1)}, bf16[4,192,256]{2,1,0:T(8,128)(2,1)}, bf16[4,192,256]{2,1,0:T(8,128...) custom-call(s32[3]{0:T(128)} %pad_add_fusion.place, ...), custom_call_target="tpu_custom_call" | custom-call | flops 1610612736 | bytes 14680064 | tf_op jit(solution)/shard_map/pallas_call | solution.py:342
  269.6 7.6 %shard_map.74 = bf16[16,64,512]{2,1,0:T(8,128)(2,1)} custom-call(s32[3]{0:T(128)} %pad_add_fusion.place, s32[256]{0:T(256)} %reshape.9.pairs, s32[64]{0:T(128)} %size.11, bf16[8,2,2,256,128]{4,3,2,1,0:T(8,128)(2,1)} %all-to-all-done.refs_0_, bf16[2,2,256,128]{3,2,1,0:T(8,128)(2,1)} %get-tuple-element.54.refs_1_, bf16[2,2,256,128]{3,2,1,0:T(8,128)(2,1)} %copy-done.41, ...), custom_call_target="tpu_custom_call" | custom-call | flops 536870912 | bytes 14680064 | tf_op jit(solution)/shard_map/pallas_call | solution.py:342
  277.2 5.4 %all-to-all-start.3 = ((bf16[16,64,512]{2,1,0:T(8,128)(2,1)}), bf16[16,64,512]{2,1,0:T(8,128)(2,1)S(1)}, u32[]{:S(2)}, u32[]{:S(2)}) async-start(bf16[16,64,512]{2,1,0:T(8,128)(2,1)} %shard_map.74), calls=%async_computation.3 | async-start | bytes 2097152 | tf_op jit(solution)/shard_map/all_to_all | solution.py:497
  282.6 3.4 %collective-permute-start.51 = (bf16[4,192,256]{2,1,0:T(8,128)(2,1)}, bf16[4,192,256]{2,1,0:T(8,128)(2,1)S(1)}, u32[]{:S(2)}, u32[]{:S(2)}) collective-permute-start(bf16[4,192,256]{2,1,0:T(8,128)(2,1)} %get-tuple-element.76), channel_id=1, source_target_pairs={{0,2},{1,3},{2,0},{3,1},{4,6},{5,7},{6,4},{7,5},{8,10},{9,11},{10,... | collective-permute-start | bytes 1179656 | tf_op jit(solution)/shard_map/ppermute | solution.py:32
  288.7 2.7 collective-permute-start.54
  292.9 14.1 %collective-permute-done.51.refs_2_ = bf16[4,192,256]{2,1,0:T(8,128)(2,1)S(1)} collective-permute-done((bf16[4,192,256]{2,1,0:T(8,128)(2,1)}, bf16[4,192,256]{2,1,0:T(8,128)(2,1)S(1)}, u32[]{:S(2)}, u32[]{:S(2)}) %collective-permute-start.51) | collective-permute-done | bytes 393248 | tf_op jit(solution)/shard_map/ppermute | solution.py:32
  306.9 7.4 %collective-permute-done.52.refs_3_ = bf16[4,192,256]{2,1,0:T(8,128)(2,1)S(1)} collective-permute-done((bf16[4,192,256]{2,1,0:T(8,128)(2,1)}, bf16[4,192,256]{2,1,0:T(8,128)(2,1)S(1)}, u32[]{:S(2)}, u32[]{:S(2)}) %collective-permute-start.52) | collective-permute-done | bytes 393248 | tf_op jit(solution)/shard_map/ppermute | solution.py:32
  316.0 2.4 collective-permute-start.57
  318.4 2.3 collective-permute-start.58
  321.2 2.6 collective-permute-start.60
  (256 shorter events, 70.1 us)
Async XLA Ops:
  1.5 15.4 %collective-permute-start.2 = (bf16[4,2,128,128]{3,2,1,0:T(8,128)(2,1)S(1)}, bf16[4,2,128,128]{3,2,1,0:T(8,128)(2,1)S(1)}, u32[]{:S(2)}, u32[]{:S(2)}) collective-permute-start(bf16[4,2,128,128]{3,2,1,0:T(8,128)(2,1)S(1)} %get-tuple-element.48.refs_1_), channel_id=1, source_target_pairs={{0,3},{1,0},{2,1},{3,2},{4,7},{5,4},{6,5},{7,6},{8,11},{9,8},{10,9... | collective-permute-start | bytes 786440 | tf_op jit(solution)/shard_map/ppermute | solution.py:32
  7.0 16.5 %collective-permute-start.5 = (bf16[4,2,128,128]{3,2,1,0:T(8,128)(2,1)S(1)}, bf16[4,2,128,128]{3,2,1,0:T(8,128)(2,1)S(1)}, u32[]{:S(2)}, u32[]{:S(2)}) collective-permute-start(bf16[4,2,128,128]{3,2,1,0:T(8,128)(2,1)S(1)} %get-tuple-element.49.refs_9_), channel_id=1, source_target_pairs={{0,12},{1,13},{2,14},{3,15},{4,0},{5,1},{6,2},{7,3},{8,4},{9,5},{1... | collective-permute-start | bytes 786440 | tf_op jit(solution)/shard_map/ppermute | solution.py:32
  18.5 16.6 %collective-permute-start.11 = (bf16[4,2,128,128]{3,2,1,0:T(8,128)(2,1)S(1)}, bf16[4,2,128,128]{3,2,1,0:T(8,128)(2,1)S(1)}, u32[]{:S(2)}, u32[]{:S(2)}) collective-permute-start(bf16[4,2,128,128]{3,2,1,0:T(8,128)(2,1)S(1)} %get-tuple-element.48.refs_1_), channel_id=1, source_target_pairs={{0,12},{1,13},{2,14},{3,15},{4,0},{5,1},{6,2},{7,3},{8,4},{9,5},{1... | collective-permute-start | bytes 786440 | tf_op jit(solution)/shard_map/ppermute | solution.py:32
  20.3 15.2 %collective-permute-start.9 = (bf16[4,2,128,128]{3,2,1,0:T(8,128)(2,1)S(1)}, bf16[4,2,128,128]{3,2,1,0:T(8,128)(2,1)S(1)}, u32[]{:S(2)}, u32[]{:S(2)}) collective-permute-start(bf16[4,2,128,128]{3,2,1,0:T(8,128)(2,1)S(1)} %get-tuple-element.48.refs_1_), channel_id=1, source_target_pairs={{0,8},{1,9},{2,10},{3,11},{4,12},{5,13},{6,14},{7,15},{8,0},{9,1},... | collective-permute-start | bytes 786440 | tf_op jit(solution)/shard_map/ppermute | solution.py:32
  28.4 25.8 %collective-permute-start.10 = (bf16[8,2,128,128]{3,2,1,0:T(8,128)(2,1)}, bf16[8,2,128,128]{3,2,1,0:T(8,128)(2,1)S(1)}, u32[]{:S(2)}, u32[]{:S(2)}) collective-permute-start(bf16[8,2,128,128]{3,2,1,0:T(8,128)(2,1)} %get-tuple-element.50.refs_0_), channel_id=1, source_target_pairs={{0,12},{1,13},{2,14},{3,15},{4,0},{5,1},{6,2},{7,3},{8,4},{9,5},{1... | collective-permute-start | bytes 1572872 | tf_op jit(solution)/shard_map/ppermute | solution.py:32
  35.5 15.1 %collective-permute-start.13 = (bf16[4,2,128,128]{3,2,1,0:T(8,128)(2,1)S(1)}, bf16[4,2,128,128]{3,2,1,0:T(8,128)(2,1)S(1)}, u32[]{:S(2)}, u32[]{:S(2)}) collective-permute-start(bf16[4,2,128,128]{3,2,1,0:T(8,128)(2,1)S(1)} %get-tuple-element.49.refs_9_), channel_id=1, source_target_pairs={{0,1},{1,2},{2,3},{3,0},{4,5},{5,6},{6,7},{7,4},{8,9},{9,10},{10,1... | collective-permute-start | bytes 786440 | tf_op jit(solution)/shard_map/ppermute | solution.py:32
  38.9 18.9 %collective-permute-start.8 = (bf16[8,2,128,128]{3,2,1,0:T(8,128)(2,1)}, bf16[8,2,128,128]{3,2,1,0:T(8,128)(2,1)S(1)}, u32[]{:S(2)}, u32[]{:S(2)}) collective-permute-start(bf16[8,2,128,128]{3,2,1,0:T(8,128)(2,1)} %get-tuple-element.50.refs_0_), channel_id=1, source_target_pairs={{0,8},{1,9},{2,10},{3,11},{4,12},{5,13},{6,14},{7,15},{8,0},{9,1},... | collective-permute-start | bytes 1572872 | tf_op jit(solution)/shard_map/ppermute | solution.py:32
  44.0 17.9 %collective-permute-start.6 = (bf16[8,2,128,128]{3,2,1,0:T(8,128)(2,1)}, bf16[8,2,128,128]{3,2,1,0:T(8,128)(2,1)S(1)}, u32[]{:S(2)}, u32[]{:S(2)}) collective-permute-start(bf16[8,2,128,128]{3,2,1,0:T(8,128)(2,1)} %get-tuple-element.50.refs_0_), channel_id=1, source_target_pairs={{0,4},{1,5},{2,6},{3,7},{4,8},{5,9},{6,10},{7,11},{8,12},{9,13},{1... | collective-permute-start | bytes 1572872 | tf_op jit(solution)/shard_map/ppermute | solution.py:32
  46.4 20.9 %collective-permute-start.16 = (bf16[8,2,128,128]{3,2,1,0:T(8,128)(2,1)}, bf16[8,2,128,128]{3,2,1,0:T(8,128)(2,1)S(1)}, u32[]{:S(2)}, u32[]{:S(2)}) collective-permute-start(bf16[8,2,128,128]{3,2,1,0:T(8,128)(2,1)} %get-tuple-element.51.refs_8_), channel_id=1, source_target_pairs={{0,3},{1,0},{2,1},{3,2},{4,7},{5,4},{6,5},{7,6},{8,11},{9,8},{10,9... | collective-permute-start | bytes 1572872 | tf_op jit(solution)/shard_map/ppermute | solution.py:32
  50.6 16.7 %collective-permute-start.14 = (bf16[8,2,128,128]{3,2,1,0:T(8,128)(2,1)}, bf16[8,2,128,128]{3,2,1,0:T(8,128)(2,1)S(1)}, u32[]{:S(2)}, u32[]{:S(2)}) collective-permute-start(bf16[8,2,128,128]{3,2,1,0:T(8,128)(2,1)} %get-tuple-element.51.refs_8_), channel_id=1, source_target_pairs={{0,2},{1,3},{2,0},{3,1},{4,6},{5,7},{6,4},{7,5},{8,10},{9,11},{10,... | collective-permute-start | bytes 1572872 | tf_op jit(solution)/shard_map/ppermute | solution.py:32
  54.1 16.7 %collective-permute-start.12 = (bf16[8,2,128,128]{3,2,1,0:T(8,128)(2,1)}, bf16[8,2,128,128]{3,2,1,0:T(8,128)(2,1)S(1)}, u32[]{:S(2)}, u32[]{:S(2)}) collective-permute-start(bf16[8,2,128,128]{3,2,1,0:T(8,128)(2,1)} %get-tuple-element.51.refs_8_), channel_id=1, source_target_pairs={{0,1},{1,2},{2,3},{3,0},{4,5},{5,6},{6,7},{7,4},{8,9},{9,10},{10,1... | collective-permute-start | bytes 1572872 | tf_op jit(solution)/shard_map/ppermute | solution.py:32
  77.9 57.7 %all-to-all-start = ((bf16[8,2,2,256,128]{4,3,2,1,0:T(8,128)(2,1)}), bf16[8,2,2,256,128]{4,3,2,1,0:T(8,128)(2,1)}, u32[]{:S(2)}, u32[]{:S(2)}) async-start(bf16[8,2,2,256,128]{4,3,2,1,0:T(8,128)(2,1)} %shard_map.66), calls=%async_computation | async-start | bytes 4194304 | tf_op jit(solution)/shard_map/all_to_all | solution.py:208
  86.0 28.9 %collective-permute-start.33 = (bf16[8,2,128,128]{3,2,1,0:T(8,128)(2,1)S(1)}, bf16[8,2,128,128]{3,2,1,0:T(8,128)(2,1)S(1)}, u32[]{:S(2)}, u32[]{:S(2)}) collective-permute-start(bf16[8,2,128,128]{3,2,1,0:T(8,128)(2,1)S(1)} %get-tuple-element.62.refs_0_), channel_id=1, source_target_pairs={{0,12},{1,13},{2,14},{3,15},{4,0},{5,1},{6,2},{7,3},{8,4},{9,5},{1... | collective-permute-start | bytes 1572872 | tf_op jit(solution)/shard_map/ppermute | solution.py:32
  91.8 25.4 %collective-permute-start.32 = (bf16[8,2,128,128]{3,2,1,0:T(8,128)(2,1)S(1)}, bf16[8,2,128,128]{3,2,1,0:T(8,128)(2,1)S(1)}, u32[]{:S(2)}, u32[]{:S(2)}) collective-permute-start(bf16[8,2,128,128]{3,2,1,0:T(8,128)(2,1)S(1)} %get-tuple-element.62.refs_0_), channel_id=1, source_target_pairs={{0,8},{1,9},{2,10},{3,11},{4,12},{5,13},{6,14},{7,15},{8,0},{9,1},... | collective-permute-start | bytes 1572872 | tf_op jit(solution)/shard_map/ppermute | solution.py:32
  91.8 29.2 %collective-permute-start.31 = (bf16[8,2,128,128]{3,2,1,0:T(8,128)(2,1)S(1)}, bf16[8,2,128,128]{3,2,1,0:T(8,128)(2,1)S(1)}, u32[]{:S(2)}, u32[]{:S(2)}) collective-permute-start(bf16[8,2,128,128]{3,2,1,0:T(8,128)(2,1)S(1)} %get-tuple-element.62.refs_0_), channel_id=1, source_target_pairs={{0,4},{1,5},{2,6},{3,7},{4,8},{5,9},{6,10},{7,11},{8,12},{9,13},{1... | collective-permute-start | bytes 1572872 | tf_op jit(solution)/shard_map/ppermute | solution.py:32
  92.8 28.2 %collective-permute-start.36 = (bf16[8,2,128,128]{3,2,1,0:T(8,128)(2,1)S(1)}, bf16[8,2,128,128]{3,2,1,0:T(8,128)(2,1)S(1)}, u32[]{:S(2)}, u32[]{:S(2)}) collective-permute-start(bf16[8,2,128,128]{3,2,1,0:T(8,128)(2,1)S(1)} %get-tuple-element.63.refs_4_), channel_id=1, source_target_pairs={{0,3},{1,0},{2,1},{3,2},{4,7},{5,4},{6,5},{7,6},{8,11},{9,8},{10,9... | collective-permute-start | bytes 1572872 | tf_op jit(solution)/shard_map/ppermute | solution.py:32
  92.8 28.3 %collective-permute-start.35 = (bf16[8,2,128,128]{3,2,1,0:T(8,128)(2,1)S(1)}, bf16[8,2,128,128]{3,2,1,0:T(8,128)(2,1)S(1)}, u32[]{:S(2)}, u32[]{:S(2)}) collective-permute-start(bf16[8,2,128,128]{3,2,1,0:T(8,128)(2,1)S(1)} %get-tuple-element.63.refs_4_), channel_id=1, source_target_pairs={{0,2},{1,3},{2,0},{3,1},{4,6},{5,7},{6,4},{7,5},{8,10},{9,11},{10,... | collective-permute-start | bytes 1572872 | tf_op jit(solution)/shard_map/ppermute | solution.py:32
  117.2 28.6 %collective-permute-start.20 = (bf16[8,2,128,128]{3,2,1,0:T(8,128)(2,1)}, bf16[8,2,128,128]{3,2,1,0:T(8,128)(2,1)S(1)}, u32[]{:S(2)}, u32[]{:S(2)}) collective-permute-start(bf16[8,2,128,128]{3,2,1,0:T(8,128)(2,1)} %get-tuple-element.52.refs_0_), channel_id=1, source_target_pairs={{0,12},{1,13},{2,14},{3,15},{4,0},{5,1},{6,2},{7,3},{8,4},{9,5},{1... | collective-permute-start | bytes 1572872 | tf_op jit(solution)/shard_map/ppermute | solution.py:32
  135.7 90.7 %all-to-all-start.1 = ((bf16[8,2,2,256,128]{4,3,2,1,0:T(8,128)(2,1)}), bf16[8,2,2,256,128]{4,3,2,1,0:T(8,128)(2,1)}, u32[]{:S(2)}, u32[]{:S(2)}) async-start(bf16[8,2,2,256,128]{4,3,2,1,0:T(8,128)(2,1)} %shard_map.70), calls=%async_computation.1 | async-start | bytes 4194304 | tf_op jit(solution)/shard_map/all_to_all | solution.py:208
  140.0 16.6 %collective-permute-start.19 = (bf16[8,2,128,128]{3,2,1,0:T(8,128)(2,1)}, bf16[8,2,128,128]{3,2,1,0:T(8,128)(2,1)S(1)}, u32[]{:S(2)}, u32[]{:S(2)}) collective-permute-start(bf16[8,2,128,128]{3,2,1,0:T(8,128)(2,1)} %get-tuple-element.52.refs_0_), channel_id=1, source_target_pairs={{0,8},{1,9},{2,10},{3,11},{4,12},{5,13},{6,14},{7,15},{8,0},{9,1},... | collective-permute-start | bytes 1572872 | tf_op jit(solution)/shard_map/ppermute | solution.py:32
  140.1 27.1 %collective-permute-start.18 = (bf16[8,2,128,128]{3,2,1,0:T(8,128)(2,1)}, bf16[8,2,128,128]{3,2,1,0:T(8,128)(2,1)S(1)}, u32[]{:S(2)}, u32[]{:S(2)}) collective-permute-start(bf16[8,2,128,128]{3,2,1,0:T(8,128)(2,1)} %get-tuple-element.52.refs_0_), channel_id=1, source_target_pairs={{0,4},{1,5},{2,6},{3,7},{4,8},{5,9},{6,10},{7,11},{8,12},{9,13},{1... | collective-permute-start | bytes 1572872 | tf_op jit(solution)/shard_map/ppermute | solution.py:32
  144.7 22.5 %collective-permute-start.23 = (bf16[8,2,128,128]{3,2,1,0:T(8,128)(2,1)}, bf16[8,2,128,128]{3,2,1,0:T(8,128)(2,1)S(1)}, u32[]{:S(2)}, u32[]{:S(2)}) collective-permute-start(bf16[8,2,128,128]{3,2,1,0:T(8,128)(2,1)} %get-tuple-element.53.refs_8_), channel_id=1, source_target_pairs={{0,3},{1,0},{2,1},{3,2},{4,7},{5,4},{6,5},{7,6},{8,11},{9,8},{10,9... | collective-permute-start | bytes 1572872 | tf_op jit(solution)/shard_map/ppermute | solution.py:32
  144.7 22.5 %collective-permute-start.22 = (bf16[8,2,128,128]{3,2,1,0:T(8,128)(2,1)}, bf16[8,2,128,128]{3,2,1,0:T(8,128)(2,1)S(1)}, u32[]{:S(2)}, u32[]{:S(2)}) collective-permute-start(bf16[8,2,128,128]{3,2,1,0:T(8,128)(2,1)} %get-tuple-element.53.refs_8_), channel_id=1, source_target_pairs={{0,2},{1,3},{2,0},{3,1},{4,6},{5,7},{6,4},{7,5},{8,10},{9,11},{10,... | collective-permute-start | bytes 1572872 | tf_op jit(solution)/shard_map/ppermute | solution.py:32
  145.8 25.4 %collective-permute-start.21 = (bf16[8,2,128,128]{3,2,1,0:T(8,128)(2,1)}, bf16[8,2,128,128]{3,2,1,0:T(8,128)(2,1)S(1)}, u32[]{:S(2)}, u32[]{:S(2)}) collective-permute-start(bf16[8,2,128,128]{3,2,1,0:T(8,128)(2,1)} %get-tuple-element.53.refs_8_), channel_id=1, source_target_pairs={{0,1},{1,2},{2,3},{3,0},{4,5},{5,6},{6,7},{7,4},{8,9},{9,10},{10,1... | collective-permute-start | bytes 1572872 | tf_op jit(solution)/shard_map/ppermute | solution.py:32
  174.1 17.6 %collective-permute-start.39 = (bf16[8,2,128,128]{3,2,1,0:T(8,128)(2,1)}, bf16[8,2,128,128]{3,2,1,0:T(8,128)(2,1)S(1)}, u32[]{:S(2)}, u32[]{:S(2)}) collective-permute-start(bf16[8,2,128,128]{3,2,1,0:T(8,128)(2,1)} %get-tuple-element.64.refs_0_), channel_id=1, source_target_pairs={{0,12},{1,13},{2,14},{3,15},{4,0},{5,1},{6,2},{7,3},{8,4},{9,5},{1... | collective-permute-start | bytes 1572872 | tf_op jit(solution)/shard_map/ppermute | solution.py:32
  182.4 16.6 %collective-permute-start.38 = (bf16[8,2,128,128]{3,2,1,0:T(8,128)(2,1)}, bf16[8,2,128,128]{3,2,1,0:T(8,128)(2,1)S(1)}, u32[]{:S(2)}, u32[]{:S(2)}) collective-permute-start(bf16[8,2,128,128]{3,2,1,0:T(8,128)(2,1)} %get-tuple-element.64.refs_0_), channel_id=1, source_target_pairs={{0,8},{1,9},{2,10},{3,11},{4,12},{5,13},{6,14},{7,15},{8,0},{9,1},... | collective-permute-start | bytes 1572872 | tf_op jit(solution)/shard_map/ppermute | solution.py:32
  184.6 24.7 %collective-permute-start.37 = (bf16[8,2,128,128]{3,2,1,0:T(8,128)(2,1)}, bf16[8,2,128,128]{3,2,1,0:T(8,128)(2,1)S(1)}, u32[]{:S(2)}, u32[]{:S(2)}) collective-permute-start(bf16[8,2,128,128]{3,2,1,0:T(8,128)(2,1)} %get-tuple-element.64.refs_0_), channel_id=1, source_target_pairs={{0,4},{1,5},{2,6},{3,7},{4,8},{5,9},{6,10},{7,11},{8,12},{9,13},{1... | collective-permute-start | bytes 1572872 | tf_op jit(solution)/shard_map/ppermute | solution.py:32
  184.7 28.2 %collective-permute-start.42 = (bf16[8,2,128,128]{3,2,1,0:T(8,128)(2,1)S(1)}, bf16[8,2,128,128]{3,2,1,0:T(8,128)(2,1)S(1)}, u32[]{:S(2)}, u32[]{:S(2)}) collective-permute-start(bf16[8,2,128,128]{3,2,1,0:T(8,128)(2,1)S(1)} %copy-done.37), channel_id=1, source_target_pairs={{0,3},{1,0},{2,1},{3,2},{4,7},{5,4},{6,5},{7,6},{8,11},{9,8},{10,9... | collective-permute-start | bytes 1572872 | tf_op jit(solution)/shard_map/ppermute | solution.py:32
  190.8 22.2 %collective-permute-start.41 = (bf16[8,2,128,128]{3,2,1,0:T(8,128)(2,1)S(1)}, bf16[8,2,128,128]{3,2,1,0:T(8,128)(2,1)S(1)}, u32[]{:S(2)}, u32[]{:S(2)}) collective-permute-start(bf16[8,2,128,128]{3,2,1,0:T(8,128)(2,1)S(1)} %copy-done.37), channel_id=1, source_target_pairs={{0,2},{1,3},{2,0},{3,1},{4,6},{5,7},{6,4},{7,5},{8,10},{9,11},{10,... | collective-permute-start | bytes 1572872 | tf_op jit(solution)/shard_map/ppermute | solution.py:32
  191.7 25.3 %collective-permute-start.40 = (bf16[8,2,128,128]{3,2,1,0:T(8,128)(2,1)S(1)}, bf16[8,2,128,128]{3,2,1,0:T(8,128)(2,1)S(1)}, u32[]{:S(2)}, u32[]{:S(2)}) collective-permute-start(bf16[8,2,128,128]{3,2,1,0:T(8,128)(2,1)S(1)} %copy-done.37), channel_id=1, source_target_pairs={{0,1},{1,2},{2,3},{3,0},{4,5},{5,6},{6,7},{7,4},{8,9},{9,10},{10,1... | collective-permute-start | bytes 1572872 | tf_op jit(solution)/shard_map/ppermute | solution.py:32
  199.0 26.5 %collective-permute-start.26 = (bf16[2,2,256,128]{3,2,1,0:T(8,128)(2,1)}, bf16[2,2,256,128]{3,2,1,0:T(8,128)(2,1)S(1)}, u32[]{:S(2)}, u32[]{:S(2)}) collective-permute-start(bf16[2,2,256,128]{3,2,1,0:T(8,128)(2,1)} %get-tuple-element.57), channel_id=1, source_target_pairs={{0,48},{16,32},{32,80},{48,64},{64,112},{80,96},{96,16},{112,0},{1... | collective-permute-start | bytes 786440 | tf_op jit(solution)/shard_map/ppermute | solution.py:217
  210.1 15.9 %collective-permute-start.27 = (bf16[2,2,256,128]{3,2,1,0:T(8,128)(2,1)}, bf16[2,2,256,128]{3,2,1,0:T(8,128)(2,1)S(1)}, u32[]{:S(2)}, u32[]{:S(2)}) collective-permute-start(bf16[2,2,256,128]{3,2,1,0:T(8,128)(2,1)} %get-tuple-element.58), channel_id=1, source_target_pairs={{0,64},{16,80},{32,96},{48,112},{64,0},{80,16},{96,32},{112,48},{1... | collective-permute-start | bytes 786440 | tf_op jit(solution)/shard_map/ppermute | solution.py:217
  212.8 17.7 %collective-permute-start.28 = (bf16[2,2,256,128]{3,2,1,0:T(8,128)(2,1)}, bf16[2,2,256,128]{3,2,1,0:T(8,128)(2,1)S(1)}, u32[]{:S(2)}, u32[]{:S(2)}) collective-permute-start(bf16[2,2,256,128]{3,2,1,0:T(8,128)(2,1)} %get-tuple-element.59), channel_id=1, source_target_pairs={{0,80},{16,64},{32,112},{48,96},{64,16},{80,0},{96,48},{112,32},{1... | collective-permute-start | bytes 786440 | tf_op jit(solution)/shard_map/ppermute | solution.py:217
  213.7 18.7 %collective-permute-start.29 = (bf16[2,2,256,128]{3,2,1,0:T(8,128)(2,1)}, bf16[2,2,256,128]{3,2,1,0:T(8,128)(2,1)S(1)}, u32[]{:S(2)}, u32[]{:S(2)}) collective-permute-start(bf16[2,2,256,128]{3,2,1,0:T(8,128)(2,1)} %get-tuple-element.60), channel_id=1, source_target_pairs={{0,96},{16,112},{32,0},{48,16},{64,32},{80,48},{96,64},{112,80},{1... | collective-permute-start | bytes 786440 | tf_op jit(solution)/shard_map/ppermute | solution.py:217
  217.8 17.9 %collective-permute-start.30 = (bf16[2,2,256,128]{3,2,1,0:T(8,128)(2,1)}, bf16[2,2,256,128]{3,2,1,0:T(8,128)(2,1)S(1)}, u32[]{:S(2)}, u32[]{:S(2)}) collective-permute-start(bf16[2,2,256,128]{3,2,1,0:T(8,128)(2,1)} %get-tuple-element.61), channel_id=1, source_target_pairs={{0,112},{16,96},{32,16},{48,0},{64,48},{80,32},{96,80},{112,64},{1... | collective-permute-start | bytes 786440 | tf_op jit(solution)/shard_map/ppermute | solution.py:217
  226.0 15.5 %collective-permute-start.44 = (bf16[2,2,192,128]{3,2,1,0:T(8,128)(2,1)}, bf16[2,2,192,128]{3,2,1,0:T(8,128)(2,1)S(1)}, u32[]{:S(2)}, u32[]{:S(2)}) collective-permute-start(bf16[2,2,192,128]{3,2,1,0:T(8,128)(2,1)} %get-tuple-element.68), channel_id=1, source_target_pairs={{0,32},{16,48},{32,64},{48,80},{64,96},{80,112},{96,0},{112,16},{1... | collective-permute-start | bytes 589832 | tf_op jit(solution)/shard_map/ppermute | solution.py:217
  226.4 42.4 %all-to-all-start.2 = ((bf16[8,2,2,64,128]{4,3,2,1,0:T(8,128)(2,1)}), bf16[8,2,2,64,128]{4,3,2,1,0:T(8,128)(2,1)S(1)}, u32[]{:S(2)}, u32[]{:S(2)}) async-start(bf16[8,2,2,64,128]{4,3,2,1,0:T(8,128)(2,1)} %get-tuple-element.90), calls=%async_computation.2 | async-start | bytes 1048576 | tf_op jit(solution)/shard_map/all_to_all | solution.py:208
  232.4 17.5 %collective-permute-start.46 = (bf16[2,2,192,128]{3,2,1,0:T(8,128)(2,1)}, bf16[2,2,192,128]{3,2,1,0:T(8,128)(2,1)S(1)}, u32[]{:S(2)}, u32[]{:S(2)}) collective-permute-start(bf16[2,2,192,128]{3,2,1,0:T(8,128)(2,1)} %get-tuple-element.70), channel_id=1, source_target_pairs={{0,64},{16,80},{32,96},{48,112},{64,0},{80,16},{96,32},{112,48},{1... | collective-permute-start | bytes 589832 | tf_op jit(solution)/shard_map/ppermute | solution.py:217
  235.7 17.3 %collective-permute-start.47 = (bf16[2,2,192,128]{3,2,1,0:T(8,128)(2,1)}, bf16[2,2,192,128]{3,2,1,0:T(8,128)(2,1)S(1)}, u32[]{:S(2)}, u32[]{:S(2)}) collective-permute-start(bf16[2,2,192,128]{3,2,1,0:T(8,128)(2,1)} %get-tuple-element.71), channel_id=1, source_target_pairs={{0,80},{16,64},{32,112},{48,96},{64,16},{80,0},{96,48},{112,32},{1... | collective-permute-start | bytes 589832 | tf_op jit(solution)/shard_map/ppermute | solution.py:217
  239.7 15.4 %collective-permute-start.48 = (bf16[2,2,192,128]{3,2,1,0:T(8,128)(2,1)}, bf16[2,2,192,128]{3,2,1,0:T(8,128)(2,1)S(1)}, u32[]{:S(2)}, u32[]{:S(2)}) collective-permute-start(bf16[2,2,192,128]{3,2,1,0:T(8,128)(2,1)} %get-tuple-element.72), channel_id=1, source_target_pairs={{0,96},{16,112},{32,0},{48,16},{64,32},{80,48},{96,64},{112,80},{1... | collective-permute-start | bytes 589832 | tf_op jit(solution)/shard_map/ppermute | solution.py:217
  241.5 16.0 %collective-permute-start.49 = (bf16[2,2,192,128]{3,2,1,0:T(8,128)(2,1)}, bf16[2,2,192,128]{3,2,1,0:T(8,128)(2,1)S(1)}, u32[]{:S(2)}, u32[]{:S(2)}) collective-permute-start(bf16[2,2,192,128]{3,2,1,0:T(8,128)(2,1)} %get-tuple-element.73), channel_id=1, source_target_pairs={{0,112},{16,96},{32,16},{48,0},{64,48},{80,32},{96,80},{112,64},{1... | collective-permute-start | bytes 589832 | tf_op jit(solution)/shard_map/ppermute | solution.py:217
  268.5 22.9 %collective-permute-start.50 = (bf16[4,192,256]{2,1,0:T(8,128)(2,1)}, bf16[4,192,256]{2,1,0:T(8,128)(2,1)S(1)}, u32[]{:S(2)}, u32[]{:S(2)}) collective-permute-start(bf16[4,192,256]{2,1,0:T(8,128)(2,1)} %get-tuple-element.75), channel_id=1, source_target_pairs={{0,1},{1,2},{2,3},{3,0},{4,5},{5,6},{6,7},{7,4},{8,9},{9,10},{10,1... | collective-permute-start | bytes 1179656 | tf_op jit(solution)/shard_map/ppermute | solution.py:32
  277.2 51.3 %all-to-all-start.3 = ((bf16[16,64,512]{2,1,0:T(8,128)(2,1)}), bf16[16,64,512]{2,1,0:T(8,128)(2,1)S(1)}, u32[]{:S(2)}, u32[]{:S(2)}) async-start(bf16[16,64,512]{2,1,0:T(8,128)(2,1)} %shard_map.74), calls=%async_computation.3 | async-start | bytes 2097152 | tf_op jit(solution)/shard_map/all_to_all | solution.py:497
  282.6 24.3 %collective-permute-start.51 = (bf16[4,192,256]{2,1,0:T(8,128)(2,1)}, bf16[4,192,256]{2,1,0:T(8,128)(2,1)S(1)}, u32[]{:S(2)}, u32[]{:S(2)}) collective-permute-start(bf16[4,192,256]{2,1,0:T(8,128)(2,1)} %get-tuple-element.76), channel_id=1, source_target_pairs={{0,2},{1,3},{2,0},{3,1},{4,6},{5,7},{6,4},{7,5},{8,10},{9,11},{10,... | collective-permute-start | bytes 1179656 | tf_op jit(solution)/shard_map/ppermute | solution.py:32
  286.1 28.2 %collective-permute-start.52 = (bf16[4,192,256]{2,1,0:T(8,128)(2,1)}, bf16[4,192,256]{2,1,0:T(8,128)(2,1)S(1)}, u32[]{:S(2)}, u32[]{:S(2)}) collective-permute-start(bf16[4,192,256]{2,1,0:T(8,128)(2,1)} %get-tuple-element.77), channel_id=1, source_target_pairs={{0,3},{1,0},{2,1},{3,2},{4,7},{5,4},{6,5},{7,6},{8,11},{9,8},{10,9... | collective-permute-start | bytes 1179656 | tf_op jit(solution)/shard_map/ppermute | solution.py:32
  287.2 27.1 %collective-permute-start.53 = (bf16[4,192,256]{2,1,0:T(8,128)(2,1)S(1)}, bf16[4,192,256]{2,1,0:T(8,128)(2,1)S(1)}, u32[]{:S(2)}, u32[]{:S(2)}) collective-permute-start(bf16[4,192,256]{2,1,0:T(8,128)(2,1)S(1)} %copy-done.76), channel_id=1, source_target_pairs={{0,4},{1,5},{2,6},{3,7},{4,8},{5,9},{6,10},{7,11},{8,12},{9,13},{1... | collective-permute-start | bytes 1179656 | tf_op jit(solution)/shard_map/ppermute | solution.py:32
  288.7 26.5 %collective-permute-start.54 = (bf16[4,192,256]{2,1,0:T(8,128)(2,1)S(1)}, bf16[4,192,256]{2,1,0:T(8,128)(2,1)S(1)}, u32[]{:S(2)}, u32[]{:S(2)}) collective-permute-start(bf16[4,192,256]{2,1,0:T(8,128)(2,1)S(1)} %copy-done.75), channel_id=1, source_target_pairs={{0,8},{1,9},{2,10},{3,11},{4,12},{5,13},{6,14},{7,15},{8,0},{9,1},... | collective-permute-start | bytes 1179656 | tf_op jit(solution)/shard_map/ppermute | solution.py:32
  291.4 23.8 %collective-permute-start.55 = (bf16[4,192,256]{2,1,0:T(8,128)(2,1)S(1)}, bf16[4,192,256]{2,1,0:T(8,128)(2,1)S(1)}, u32[]{:S(2)}, u32[]{:S(2)}) collective-permute-start(bf16[4,192,256]{2,1,0:T(8,128)(2,1)S(1)} %copy-done.74), channel_id=1, source_target_pairs={{0,12},{1,13},{2,14},{3,15},{4,0},{5,1},{6,2},{7,3},{8,4},{9,5},{1... | collective-permute-start | bytes 1179656 | tf_op jit(solution)/shard_map/ppermute | solution.py:32
  (95 other events, 1568.1 us)

commit v6 on v5

--- a/solution.py
+++ b/solution.py
@@ -14,7 +14,7 @@
 BF16 = jnp.bfloat16
 F32 = jnp.float32
 CHUNKS = (2, 2, 2, 2)
-SPLIT = (192, 64)
+SPLIT = (160, 96)
 MODES = (
     ((False, 0, 256),),
     ((True, 0, 256),),
@@ -270,11 +270,12 @@
             line = lax.broadcasted_iota(jnp.int32, (high - low, TILE), 0) + (low - h * TILE)
             lives.append(line < size[bond * 2 + h])
     row_live = jnp.concatenate(lives, axis=0)
-    for copy in copies:
-        copy.wait()
-    for step_z in range(1, SIDE):
-        for step_y in range(SIDE):
-            right_copy(step_z, step_y).start()
+    for batch, step_zs in enumerate(((1,), (2, 3))):
+        for copy in copies[batch * 16 : batch * 16 + 16]:
+            copy.wait()
+        for step_z in step_zs:
+            for step_y in range(SIDE):
+                right_copy(step_z, step_y).start()
     sent = []
     for step_zs in ((0, 1), (2, 3)):
 
@@ -373,19 +374,17 @@
         for other in mine[1:]:
             total = total + other[...].astype(F32)
         kept = outputs[half * 4 : half * 4 + 4]
-        kept[0][...] = total[0]
-        for k in range(1, SIDE):
+        for k in range(SIDE):
             kept[k][...] = total[k].astype(BF16)
 
 
 def sum_stage(pieces):
     rows, width = pieces[0].shape[1:]
     whole = pl.BlockSpec(memory_space=pltpu.VMEM)
-    kinds = [F32, BF16, BF16, BF16]
     return pl.pallas_call(
         sum_kernel,
         name="near_sum",
-        out_shape=[jax.ShapeDtypeStruct((rows, width), kind) for kind in kinds * 2],
+        out_shape=[jax.ShapeDtypeStruct((rows, width), BF16)] * 8,
         in_specs=[whole] * 8,
         out_specs=[whole] * 8,
         compiler_params=pltpu.CompilerParams(vmem_limit_bytes=16 << 20),
@@ -397,7 +396,7 @@
     rows, width = refs[0].shape
     for side in range(2):
         mine = refs[side * 4 : side * 4 + 4]
-        total = mine[0][...]
+        total = mine[0][...].astype(F32)
         for other in mine[1:]:
             total = total + other[...].astype(F32)
         out[:rows, side * width : (side + 1) * width] = total

time: 331 us -> 351 us (1.060)
  starting transfers between devices: 115 us -> 133 us
  waiting for transfers between devices: 149 us -> 156 us
    ppermute x14, waiting for transfers between devices: 20.6 us -> 44.9 us  [exchange(): got.append(lax.ppermute(blocks[turned], 'bond', pairs))]
    ppermute x48, starting transfers between devices: 77.3 us -> 98.2 us  [move(): return lax.ppermute(value, 'op', pairs)]
    ppermute x48, waiting for transfers between devices: 129 us -> 111 us  [move(): return lax.ppermute(value, 'op', pairs)]
    ppermute x14, starting transfers between devices: 18.7 us -> 15.1 us  [exchange(): got.append(lax.ppermute(blocks[turned], 'bond', pairs))]
    unnamed x156 -> x132, local copies, waits for them, and re-layouts: 10.6 us -> 10.1 us
  transfers between devices with their start and end apart: 66 -> 66, of which waited for: 29 -> 30; matrix products, arithmetic and copies ran while one was open for 1% -> 1% of each run, Pallas kernels for 14% -> 11%
where the time goes in v6:
time: 351 us
  waiting for transfers between devices  156 us (44%)
  starting transfers between devices  133 us (38%)
  Pallas kernels  49.5 us (14%)
  local copies, waits for them, and re-layouts  11.4 us (3%)
    ppermute x48, waiting for transfers between devices, move(): return lax.ppermute(value, 'op', pairs)  111 us
    ppermute x48, starting transfers between devices, move(): return lax.ppermute(value, 'op', pairs)  98.2 us
    ppermute x14, waiting for transfers between devices, exchange(): got.append(lax.ppermute(blocks[turned], 'bond', pairs))  44.9 us
    pallas_call x4, Pallas kernels, left_stage(): pl.pallas_call(functools.partial(left_kernel, first_sector, modes, plan),...  24.8 us
    pallas_call x2, Pallas kernels, right_stage(): pl.pallas_call(functools.partial(right_kernel, layout, half), out_shape=s...  17.3 us
    ppermute x14, starting transfers between devices, exchange(): got.append(lax.ppermute(blocks[turned], 'bond', pairs))  15.1 us
    all_to_all x3, starting transfers between devices, exchange(): lax.all_to_all(blocks[0], 'bond', split_axis=0, concat_axis=0, tiled=True)  13.5 us
    unnamed x132, local copies, waits for them, and re-layouts  10.1 us
  transfers between devices with their start and end apart: 66, of which 30 were waited for; matrix products, arithmetic and copies ran while one was open for 1% of the time, Pallas kernels for 11%

profile of v6, /device:TPU:0, one launch (start us, length us, event | category | flops | bytes accessed | tf_op | source)
XLA Modules:
  0.0 350.7 jit_solution(9451354323440700372)
XLA Ops:
  1.5 4.2 %collective-permute-start.2 = (bf16[4,2,128,128]{3,2,1,0:T(8,128)(2,1)S(1)}, bf16[4,2,128,128]{3,2,1,0:T(8,128)(2,1)S(1)}, u32[]{:S(2)}, u32[]{:S(2)}) collective-permute-start(bf16[4,2,128,128]{3,2,1,0:T(8,128)(2,1)S(1)} %get-tuple-element.48.refs_1_), channel_id=1, source_target_pairs={{0,3},{1,0},{2,1},{3,2},{4,7},{5,4},{6,5},{7,6},{8,11},{9,8},{10,9... | collective-permute-start | bytes 786440 | tf_op jit(solution)/shard_map/ppermute | solution.py:32
  7.0 3.0 collective-permute-start.5
  10.6 6.3 %collective-permute-done.2.refs_2_ = bf16[4,2,128,128]{3,2,1,0:T(8,128)(2,1)S(1)} collective-permute-done((bf16[4,2,128,128]{3,2,1,0:T(8,128)(2,1)S(1)}, bf16[4,2,128,128]{3,2,1,0:T(8,128)(2,1)S(1)}, u32[]{:S(2)}, u32[]{:S(2)}) %collective-permute-start.2) | collective-permute-done | bytes 262176 | tf_op jit(solution)/shard_map/ppermute | solution.py:32
  20.3 4.9 %collective-permute-done.3.refs_3_ = bf16[4,2,128,128]{3,2,1,0:T(8,128)(2,1)S(1)} collective-permute-done((bf16[4,2,128,128]{3,2,1,0:T(8,128)(2,1)S(1)}, bf16[4,2,128,128]{3,2,1,0:T(8,128)(2,1)S(1)}, u32[]{:S(2)}, u32[]{:S(2)}) %collective-permute-start.3) | collective-permute-done | bytes 262176 | tf_op jit(solution)/shard_map/ppermute | solution.py:32
  29.9 3.8 %collective-permute-start.23 = (bf16[8,2,128,128]{3,2,1,0:T(8,128)(2,1)S(1)}, bf16[8,2,128,128]{3,2,1,0:T(8,128)(2,1)S(1)}, u32[]{:S(2)}, u32[]{:S(2)}) collective-permute-start(bf16[8,2,128,128]{3,2,1,0:T(8,128)(2,1)S(1)} %get-tuple-element.53.refs_8_), channel_id=1, source_target_pairs={{0,3},{1,0},{2,1},{3,2},{4,7},{5,4},{6,5},{7,6},{8,11},{9,8},{10,9... | collective-permute-start | bytes 1572872 | tf_op jit(solution)/shard_map/ppermute | solution.py:32
  33.7 7.6 %collective-permute-done.20.refs_6_.refs_5_ = bf16[8,2,128,128]{3,2,1,0:T(8,128)(2,1)S(1)} collective-permute-done((bf16[8,2,128,128]{3,2,1,0:T(8,128)(2,1)S(1)}, bf16[8,2,128,128]{3,2,1,0:T(8,128)(2,1)S(1)}, u32[]{:S(2)}, u32[]{:S(2)}) %collective-permute-start.20) | collective-permute-done | bytes 524320 | tf_op jit(solution)/shard_map/ppermute | solution.py:32
  44.6 8.0 %collective-permute-done.18.refs_2_.refs_3_ = bf16[8,2,128,128]{3,2,1,0:T(8,128)(2,1)S(1)} collective-permute-done((bf16[8,2,128,128]{3,2,1,0:T(8,128)(2,1)S(1)}, bf16[8,2,128,128]{3,2,1,0:T(8,128)(2,1)S(1)}, u32[]{:S(2)}, u32[]{:S(2)}) %collective-permute-start.18) | collective-permute-done | bytes 524320 | tf_op jit(solution)/shard_map/ppermute | solution.py:32
  53.6 3.7 %collective-permute-done.21.refs_10_.refs_0_ = bf16[8,2,128,128]{3,2,1,0:T(8,128)(2,1)S(1)} collective-permute-done((bf16[8,2,128,128]{3,2,1,0:T(8,128)(2,1)S(1)}, bf16[8,2,128,128]{3,2,1,0:T(8,128)(2,1)S(1)}, u32[]{:S(2)}, u32[]{:S(2)}) %collective-permute-start.21) | collective-permute-done | bytes 524320 | tf_op jit(solution)/shard_map/ppermute | solution.py:32
  58.6 6.5 %collective-permute-start.39 = (bf16[8,2,128,128]{3,2,1,0:T(8,128)(2,1)S(1)}, bf16[8,2,128,128]{3,2,1,0:T(8,128)(2,1)S(1)}, u32[]{:S(2)}, u32[]{:S(2)}) collective-permute-start(bf16[8,2,128,128]{3,2,1,0:T(8,128)(2,1)S(1)} %get-tuple-element.64.refs_0_), channel_id=1, source_target_pairs={{0,12},{1,13},{2,14},{3,15},{4,0},{5,1},{6,2},{7,3},{8,4},{9,5},{1... | collective-permute-start | bytes 1572872 | tf_op jit(solution)/shard_map/ppermute | solution.py:32
  65.2 3.5 %collective-permute-start.38 = (bf16[8,2,128,128]{3,2,1,0:T(8,128)(2,1)S(1)}, bf16[8,2,128,128]{3,2,1,0:T(8,128)(2,1)S(1)}, u32[]{:S(2)}, u32[]{:S(2)}) collective-permute-start(bf16[8,2,128,128]{3,2,1,0:T(8,128)(2,1)S(1)} %get-tuple-element.64.refs_0_), channel_id=1, source_target_pairs={{0,8},{1,9},{2,10},{3,11},{4,12},{5,13},{6,14},{7,15},{8,0},{9,1},... | collective-permute-start | bytes 1572872 | tf_op jit(solution)/shard_map/ppermute | solution.py:32
  70.6 8.5 %collective-permute-done.11.refs_7_ = bf16[4,2,128,128]{3,2,1,0:T(8,128)(2,1)S(1)} collective-permute-done((bf16[4,2,128,128]{3,2,1,0:T(8,128)(2,1)S(1)}, bf16[4,2,128,128]{3,2,1,0:T(8,128)(2,1)S(1)}, u32[]{:S(2)}, u32[]{:S(2)}) %collective-permute-start.11) | collective-permute-done | bytes 262176 | tf_op jit(solution)/shard_map/ppermute | solution.py:32
  79.7 15.5 %collective-permute-start.41 = (bf16[8,2,128,128]{3,2,1,0:T(8,128)(2,1)S(1)}, bf16[8,2,128,128]{3,2,1,0:T(8,128)(2,1)}, u32[]{:S(2)}, u32[]{:S(2)}) collective-permute-start(bf16[8,2,128,128]{3,2,1,0:T(8,128)(2,1)S(1)} %get-tuple-element.65.refs_4_), channel_id=1, source_target_pairs={{0,2},{1,3},{2,0},{3,1},{4,6},{5,7},{6,4},{7,5},{8,10},{9,11},{10,... | collective-permute-start | bytes 1572872 | tf_op jit(solution)/shard_map/ppermute | solution.py:32
  99.5 3.7 %collective-permute-start.10 = (bf16[8,2,128,128]{3,2,1,0:T(8,128)(2,1)}, bf16[8,2,128,128]{3,2,1,0:T(8,128)(2,1)S(1)}, u32[]{:S(2)}, u32[]{:S(2)}) collective-permute-start(bf16[8,2,128,128]{3,2,1,0:T(8,128)(2,1)} %get-tuple-element.50.refs_0_), channel_id=1, source_target_pairs={{0,12},{1,13},{2,14},{3,15},{4,0},{5,1},{6,2},{7,3},{8,4},{9,5},{1... | collective-permute-start | bytes 1572872 | tf_op jit(solution)/shard_map/ppermute | solution.py:32
  103.9 2.4 collective-permute-start.17
  106.3 3.7 %collective-permute-start.15 = (bf16[4,2,128,128]{3,2,1,0:T(8,128)(2,1)S(1)}, bf16[4,2,128,128]{3,2,1,0:T(8,128)(2,1)}, u32[]{:S(2)}, u32[]{:S(2)}) collective-permute-start(bf16[4,2,128,128]{3,2,1,0:T(8,128)(2,1)S(1)} %get-tuple-element.49.refs_9_), channel_id=1, source_target_pairs={{0,2},{1,3},{2,0},{3,1},{4,6},{5,7},{6,4},{7,5},{8,10},{9,11},{10,... | collective-permute-start | bytes 786440 | tf_op jit(solution)/shard_map/ppermute | solution.py:32
  110.0 3.7 %collective-permute-done.40.refs_5_ = bf16[8,2,128,128]{3,2,1,0:T(8,128)(2,1)} collective-permute-done((bf16[8,2,128,128]{3,2,1,0:T(8,128)(2,1)S(1)}, bf16[8,2,128,128]{3,2,1,0:T(8,128)(2,1)}, u32[]{:S(2)}, u32[]{:S(2)}) %collective-permute-start.40) | collective-permute-done | bytes 524320 | tf_op jit(solution)/shard_map/ppermute | solution.py:32
  116.4 6.3 %shard_map.72 = (bf16[2,2,160,128]{3,2,1,0:T(8,128)(2,1)}, bf16[2,2,160,128]{3,2,1,0:T(8,128)(2,1)}, bf16[2,2,160,128]{3,2,1,0:T(8,128)(2,1)}, bf16[2,2,160,128]...) custom-call(s32[3]{0:T(128)} %pad_add_fusion.place, ...), custom_call_target="tpu_custom_call" | custom-call | flops 536870912 | bytes 8388608 | tf_op jit(solution)/shard_map/pallas_call | solution.py:178
  122.7 4.3 %all-to-all-start.2 = ((bf16[8,2,2,96,128]{4,3,2,1,0:T(8,128)(2,1)}), bf16[8,2,2,96,128]{4,3,2,1,0:T(8,128)(2,1)}, u32[]{:S(2)}, u32[]{:S(2)}) async-start(bf16[8,2,2,96,128]{4,3,2,1,0:T(8,128)(2,1)} %get-tuple-element.90), calls=%async_computation.2 | async-start | bytes 1572864 | tf_op jit(solution)/shard_map/all_to_all | solution.py:208
  127.2 4.5 %collective-permute-start.6 = (bf16[8,2,128,128]{3,2,1,0:T(8,128)(2,1)}, bf16[8,2,128,128]{3,2,1,0:T(8,128)(2,1)S(1)}, u32[]{:S(2)}, u32[]{:S(2)}) collective-permute-start(bf16[8,2,128,128]{3,2,1,0:T(8,128)(2,1)} %get-tuple-element.50.refs_0_), channel_id=1, source_target_pairs={{0,4},{1,5},{2,6},{3,7},{4,8},{5,9},{6,10},{7,11},{8,12},{9,13},{1... | collective-permute-start | bytes 1572872 | tf_op jit(solution)/shard_map/ppermute | solution.py:32
  131.6 2.4 collective-permute-start.16
  136.9 6.8 %collective-permute-done.8.refs_4_ = bf16[8,2,128,128]{3,2,1,0:T(8,128)(2,1)S(1)} collective-permute-done((bf16[8,2,128,128]{3,2,1,0:T(8,128)(2,1)}, bf16[8,2,128,128]{3,2,1,0:T(8,128)(2,1)S(1)}, u32[]{:S(2)}, u32[]{:S(2)}) %collective-permute-start.8) | collective-permute-done | bytes 524320 | tf_op jit(solution)/shard_map/ppermute | solution.py:32
  143.7 10.7 %collective-permute-done.6.refs_2_.refs_3_ = bf16[8,2,128,128]{3,2,1,0:T(8,128)(2,1)S(1)} collective-permute-done((bf16[8,2,128,128]{3,2,1,0:T(8,128)(2,1)}, bf16[8,2,128,128]{3,2,1,0:T(8,128)(2,1)S(1)}, u32[]{:S(2)}, u32[]{:S(2)}) %collective-permute-start.6) | collective-permute-done | bytes 524320 | tf_op jit(solution)/shard_map/ppermute | solution.py:32
  156.6 3.7 %collective-permute-done.12.refs_10_.refs_0_ = bf16[8,2,128,128]{3,2,1,0:T(8,128)(2,1)S(1)} collective-permute-done((bf16[8,2,128,128]{3,2,1,0:T(8,128)(2,1)S(1)}, bf16[8,2,128,128]{3,2,1,0:T(8,128)(2,1)S(1)}, u32[]{:S(2)}, u32[]{:S(2)}) %collective-permute-start.12) | collective-permute-done | bytes 524320 | tf_op jit(solution)/shard_map/ppermute | solution.py:32
  161.1 6.2 %shard_map.66 = bf16[8,2,2,256,128]{4,3,2,1,0:T(8,128)(2,1)} custom-call(s32[3]{0:T(128)} %pad_add_fusion.place, s32[64]{0:T(128)} %reshape.10.pairs, s32[64]{0:T(128)} %size.11, bf16[8,2,128,128]{3,2,1,0:T(8,128)(2,1)} %get-tuple-element.50.refs_0_, bf16[4,2,128,128]{3,2,1,0:T(8,128)(2,1)} %copy-done.20, bf16[8,2,128,128]{3,2,1,0:T(8,128)(2,1)} %copy-done.12, ...), custom_call_target="tpu_custom_call" | custom-call | flops 536870912 | bytes 8388608 | tf_op jit(solution)/shard_map/pallas_call | solution.py:178
  167.4 4.7 %all-to-all-start = ((bf16[8,2,2,256,128]{4,3,2,1,0:T(8,128)(2,1)}), bf16[8,2,2,256,128]{4,3,2,1,0:T(8,128)(2,1)}, u32[]{:S(2)}, u32[]{:S(2)}) async-start(bf16[8,2,2,256,128]{4,3,2,1,0:T(8,128)(2,1)} %shard_map.66), calls=%async_computation | async-start | bytes 4194304 | tf_op jit(solution)/shard_map/all_to_all | solution.py:208
  175.5 2.4 collective-permute-start.32
  180.6 9.7 %collective-permute-done.33.refs_3_ = bf16[8,2,128,128]{3,2,1,0:T(8,128)(2,1)S(1)} collective-permute-done((bf16[8,2,128,128]{3,2,1,0:T(8,128)(2,1)S(1)}, bf16[8,2,128,128]{3,2,1,0:T(8,128)(2,1)S(1)}, u32[]{:S(2)}, u32[]{:S(2)}) %collective-permute-start.33) | collective-permute-done | bytes 524320 | tf_op jit(solution)/shard_map/ppermute | solution.py:32
  192.0 10.7 %collective-permute-done.31.refs_1_ = bf16[8,2,128,128]{3,2,1,0:T(8,128)(2,1)S(1)} collective-permute-done((bf16[8,2,128,128]{3,2,1,0:T(8,128)(2,1)S(1)}, bf16[8,2,128,128]{3,2,1,0:T(8,128)(2,1)S(1)}, u32[]{:S(2)}, u32[]{:S(2)}) %collective-permute-start.31) | collective-permute-done | bytes 524320 | tf_op jit(solution)/shard_map/ppermute | solution.py:32
  202.7 2.8 collective-permute-done.34.refs_5_
  206.4 6.0 %shard_map.70 = bf16[8,2,2,256,128]{4,3,2,1,0:T(8,128)(2,1)} custom-call(s32[3]{0:T(128)} %pad_add_fusion.place, s32[64]{0:T(128)} %reshape.10.pairs, s32[64]{0:T(128)} %size.11, bf16[8,2,128,128]{3,2,1,0:T(8,128)(2,1)} %copy-done.25, bf16[8,2,128,128]{3,2,1,0:T(8,128)(2,1)} %copy-done.43, bf16[8,2,128,128]{3,2,1,0:T(8,128)(2,1)} %copy-done.42, ...), custom_call_target="tpu_custom_call" | custom-call | flops 536870912 | bytes 8388608 | tf_op jit(solution)/shard_map/pallas_call | solution.py:178
  212.3 4.4 %all-to-all-start.1 = ((bf16[8,2,2,256,128]{4,3,2,1,0:T(8,128)(2,1)}), bf16[8,2,2,256,128]{4,3,2,1,0:T(8,128)(2,1)S(1)}, u32[]{:S(2)}, u32[]{:S(2)}) async-start(bf16[8,2,2,256,128]{4,3,2,1,0:T(8,128)(2,1)} %shard_map.70), calls=%async_computation.1 | async-start | bytes 4194304 | tf_op jit(solution)/shard_map/all_to_all | solution.py:208
  216.8 6.4 %shard_map.68 = (bf16[2,2,256,128]{3,2,1,0:T(8,128)(2,1)}, bf16[2,2,256,128]{3,2,1,0:T(8,128)(2,1)}, bf16[2,2,256,128]{3,2,1,0:T(8,128)(2,1)}, bf16[2,2,256,128]...) custom-call(s32[3]{0:T(128)} %pad_add_fusion.place, ...), custom_call_target="tpu_custom_call" | custom-call | flops 536870912 | bytes 8388608 | tf_op jit(solution)/shard_map/pallas_call | solution.py:178
  231.7 17.9 %collective-permute-done.25.refs_3_ = bf16[2,2,256,128]{3,2,1,0:T(8,128)(2,1)S(1)} collective-permute-done((bf16[2,2,256,128]{3,2,1,0:T(8,128)(2,1)}, bf16[2,2,256,128]{3,2,1,0:T(8,128)(2,1)S(1)}, u32[]{:S(2)}, u32[]{:S(2)}) %collective-permute-start.25) | collective-permute-done | bytes 262176 | tf_op jit(solution)/shard_map/ppermute | solution.py:217
  250.5 4.0 %collective-permute-done.26.refs_4_ = bf16[2,2,256,128]{3,2,1,0:T(8,128)(2,1)S(1)} collective-permute-done((bf16[2,2,256,128]{3,2,1,0:T(8,128)(2,1)}, bf16[2,2,256,128]{3,2,1,0:T(8,128)(2,1)S(1)}, u32[]{:S(2)}, u32[]{:S(2)}) %collective-permute-start.26) | collective-permute-done | bytes 262176 | tf_op jit(solution)/shard_map/ppermute | solution.py:217
  254.5 6.9 %collective-permute-done.27.refs_5_ = bf16[2,2,256,128]{3,2,1,0:T(8,128)(2,1)S(1)} collective-permute-done((bf16[2,2,256,128]{3,2,1,0:T(8,128)(2,1)}, bf16[2,2,256,128]{3,2,1,0:T(8,128)(2,1)S(1)}, u32[]{:S(2)}, u32[]{:S(2)}) %collective-permute-start.27) | collective-permute-done | bytes 262176 | tf_op jit(solution)/shard_map/ppermute | solution.py:217
  261.4 4.5 %collective-permute-done.28.refs_6_ = bf16[2,2,256,128]{3,2,1,0:T(8,128)(2,1)S(1)} collective-permute-done((bf16[2,2,256,128]{3,2,1,0:T(8,128)(2,1)}, bf16[2,2,256,128]{3,2,1,0:T(8,128)(2,1)S(1)}, u32[]{:S(2)}, u32[]{:S(2)}) %collective-permute-start.28) | collective-permute-done | bytes 262176 | tf_op jit(solution)/shard_map/ppermute | solution.py:217
  267.3 7.9 %shard_map.74 = bf16[16,96,512]{2,1,0:T(8,128)(2,1)} custom-call(s32[3]{0:T(128)} %pad_add_fusion.place, s32[256]{0:T(256)} %reshape.9.pairs, s32[64]{0:T(128)} %size.11, bf16[8,2,2,256,128]{4,3,2,1,0:T(8,128)(2,1)} %all-to-all-done.refs_0_, bf16[2,2,256,128]{3,2,1,0:T(8,128)(2,1)} %get-tuple-element.54.refs_1_, bf16[2,2,256,128]{3,2,1,0:T(8,128)(2,1)} %copy-done.32, ...), custom_call_target="tpu_custom_call" | custom-call | flops 805306368 | bytes 14680064 | tf_op jit(solution)/shard_map/pallas_call | solution.py:343
  275.3 5.7 %all-to-all-start.3 = ((bf16[16,96,512]{2,1,0:T(8,128)(2,1)}), bf16[16,96,512]{2,1,0:T(8,128)(2,1)S(1)}, u32[]{:S(2)}, u32[]{:S(2)}) async-start(bf16[16,96,512]{2,1,0:T(8,128)(2,1)} %shard_map.74), calls=%async_computation.3 | async-start | bytes 3145728 | tf_op jit(solution)/shard_map/all_to_all | solution.py:496
  282.1 3.5 %collective-permute-start.46 = (bf16[2,2,160,128]{3,2,1,0:T(8,128)(2,1)S(1)}, bf16[2,2,160,128]{3,2,1,0:T(8,128)(2,1)S(1)}, u32[]{:S(2)}, u32[]{:S(2)}) collective-permute-start(bf16[2,2,160,128]{3,2,1,0:T(8,128)(2,1)S(1)} %copy-done.61), channel_id=1, source_target_pairs={{0,64},{16,80},{32,96},{48,112},{64,0},{80,16},{96,32},{112,48},{1... | collective-permute-start | bytes 491528 | tf_op jit(solution)/shard_map/ppermute | solution.py:217
  289.6 9.3 %collective-permute-done.45.refs_13_ = bf16[2,2,160,128]{3,2,1,0:T(8,128)(2,1)S(1)} collective-permute-done((bf16[2,2,160,128]{3,2,1,0:T(8,128)(2,1)S(1)}, bf16[2,2,160,128]{3,2,1,0:T(8,128)(2,1)S(1)}, u32[]{:S(2)}, u32[]{:S(2)}) %collective-permute-start.45) | collective-permute-done | bytes 163872 | tf_op jit(solution)/shard_map/ppermute | solution.py:217
  300.0 9.3 %shard_map.73 = (bf16[4,160,256]{2,1,0:T(8,128)(2,1)}, bf16[4,160,256]{2,1,0:T(8,128)(2,1)}, bf16[4,160,256]{2,1,0:T(8,128)(2,1)}, bf16[4,160,256]{2,1,0:T(8,128...) custom-call(s32[3]{0:T(128)} %pad_add_fusion.place, ...), custom_call_target="tpu_custom_call" | custom-call | flops 1342177280 | bytes 14680064 | tf_op jit(solution)/shard_map/pallas_call | solution.py:343
  311.4 2.7 collective-permute-start.51
  317.0 2.7 collective-permute-start.54
  321.2 3.3 collective-permute-start.55
  324.6 5.2 %collective-permute-done.51.refs_2_ = bf16[4,160,256]{2,1,0:T(8,128)(2,1)S(1)} collective-permute-done((bf16[4,160,256]{2,1,0:T(8,128)(2,1)}, bf16[4,160,256]{2,1,0:T(8,128)(2,1)S(1)}, u32[]{:S(2)}, u32[]{:S(2)}) %collective-permute-start.51) | collective-permute-done | bytes 327712 | tf_op jit(solution)/shard_map/ppermute | solution.py:32
  329.8 4.5 %collective-permute-done.54.refs_6_ = bf16[4,160,256]{2,1,0:T(8,128)(2,1)S(1)} collective-permute-done((bf16[4,160,256]{2,1,0:T(8,128)(2,1)}, bf16[4,160,256]{2,1,0:T(8,128)(2,1)S(1)}, u32[]{:S(2)}, u32[]{:S(2)}) %collective-permute-start.54) | collective-permute-done | bytes 327712 | tf_op jit(solution)/shard_map/ppermute | solution.py:32
  336.6 2.4 collective-permute-start.56
  345.5 3.4 collective-permute-done.59.refs_5_
  (232 shorter events, 75.6 us)
Async XLA Ops:
  1.5 15.4 %collective-permute-start.2 = (bf16[4,2,128,128]{3,2,1,0:T(8,128)(2,1)S(1)}, bf16[4,2,128,128]{3,2,1,0:T(8,128)(2,1)S(1)}, u32[]{:S(2)}, u32[]{:S(2)}) collective-permute-start(bf16[4,2,128,128]{3,2,1,0:T(8,128)(2,1)S(1)} %get-tuple-element.48.refs_1_), channel_id=1, source_target_pairs={{0,3},{1,0},{2,1},{3,2},{4,7},{5,4},{6,5},{7,6},{8,11},{9,8},{10,9... | collective-permute-start | bytes 786440 | tf_op jit(solution)/shard_map/ppermute | solution.py:32
  5.7 14.6 %collective-permute-start = (bf16[4,2,128,128]{3,2,1,0:T(8,128)(2,1)S(1)}, bf16[4,2,128,128]{3,2,1,0:T(8,128)(2,1)S(1)}, u32[]{:S(2)}, u32[]{:S(2)}) collective-permute-start(bf16[4,2,128,128]{3,2,1,0:T(8,128)(2,1)S(1)} %get-tuple-element.48.refs_1_), channel_id=1, source_target_pairs={{0,1},{1,2},{2,3},{3,0},{4,5},{5,6},{6,7},{7,4},{8,9},{9,10},{10,1... | collective-permute-start | bytes 786440 | tf_op jit(solution)/shard_map/ppermute | solution.py:32
  26.5 14.9 %collective-permute-start.20 = (bf16[8,2,128,128]{3,2,1,0:T(8,128)(2,1)S(1)}, bf16[8,2,128,128]{3,2,1,0:T(8,128)(2,1)S(1)}, u32[]{:S(2)}, u32[]{:S(2)}) collective-permute-start(bf16[8,2,128,128]{3,2,1,0:T(8,128)(2,1)S(1)} %get-tuple-element.52.refs_0_), channel_id=1, source_target_pairs={{0,12},{1,13},{2,14},{3,15},{4,0},{5,1},{6,2},{7,3},{8,4},{9,5},{1... | collective-permute-start | bytes 1572872 | tf_op jit(solution)/shard_map/ppermute | solution.py:32
  28.3 16.3 %collective-permute-start.19 = (bf16[8,2,128,128]{3,2,1,0:T(8,128)(2,1)S(1)}, bf16[8,2,128,128]{3,2,1,0:T(8,128)(2,1)S(1)}, u32[]{:S(2)}, u32[]{:S(2)}) collective-permute-start(bf16[8,2,128,128]{3,2,1,0:T(8,128)(2,1)S(1)} %get-tuple-element.52.refs_0_), channel_id=1, source_target_pairs={{0,8},{1,9},{2,10},{3,11},{4,12},{5,13},{6,14},{7,15},{8,0},{9,1},... | collective-permute-start | bytes 1572872 | tf_op jit(solution)/shard_map/ppermute | solution.py:32
  28.9 23.6 %collective-permute-start.18 = (bf16[8,2,128,128]{3,2,1,0:T(8,128)(2,1)S(1)}, bf16[8,2,128,128]{3,2,1,0:T(8,128)(2,1)S(1)}, u32[]{:S(2)}, u32[]{:S(2)}) collective-permute-start(bf16[8,2,128,128]{3,2,1,0:T(8,128)(2,1)S(1)} %get-tuple-element.52.refs_0_), channel_id=1, source_target_pairs={{0,4},{1,5},{2,6},{3,7},{4,8},{5,9},{6,10},{7,11},{8,12},{9,13},{1... | collective-permute-start | bytes 1572872 | tf_op jit(solution)/shard_map/ppermute | solution.py:32
  29.9 23.7 %collective-permute-start.23 = (bf16[8,2,128,128]{3,2,1,0:T(8,128)(2,1)S(1)}, bf16[8,2,128,128]{3,2,1,0:T(8,128)(2,1)S(1)}, u32[]{:S(2)}, u32[]{:S(2)}) collective-permute-start(bf16[8,2,128,128]{3,2,1,0:T(8,128)(2,1)S(1)} %get-tuple-element.53.refs_8_), channel_id=1, source_target_pairs={{0,3},{1,0},{2,1},{3,2},{4,7},{5,4},{6,5},{7,6},{8,11},{9,8},{10,9... | collective-permute-start | bytes 1572872 | tf_op jit(solution)/shard_map/ppermute | solution.py:32
  33.7 19.9 %collective-permute-start.22 = (bf16[8,2,128,128]{3,2,1,0:T(8,128)(2,1)S(1)}, bf16[8,2,128,128]{3,2,1,0:T(8,128)(2,1)S(1)}, u32[]{:S(2)}, u32[]{:S(2)}) collective-permute-start(bf16[8,2,128,128]{3,2,1,0:T(8,128)(2,1)S(1)} %get-tuple-element.53.refs_8_), channel_id=1, source_target_pairs={{0,2},{1,3},{2,0},{3,1},{4,6},{5,7},{6,4},{7,5},{8,10},{9,11},{10,... | collective-permute-start | bytes 1572872 | tf_op jit(solution)/shard_map/ppermute | solution.py:32
  41.3 16.0 %collective-permute-start.21 = (bf16[8,2,128,128]{3,2,1,0:T(8,128)(2,1)S(1)}, bf16[8,2,128,128]{3,2,1,0:T(8,128)(2,1)S(1)}, u32[]{:S(2)}, u32[]{:S(2)}) collective-permute-start(bf16[8,2,128,128]{3,2,1,0:T(8,128)(2,1)S(1)} %get-tuple-element.53.refs_8_), channel_id=1, source_target_pairs={{0,1},{1,2},{2,3},{3,0},{4,5},{5,6},{6,7},{7,4},{8,9},{9,10},{10,1... | collective-permute-start | bytes 1572872 | tf_op jit(solution)/shard_map/ppermute | solution.py:32
  58.6 36.6 %collective-permute-start.39 = (bf16[8,2,128,128]{3,2,1,0:T(8,128)(2,1)S(1)}, bf16[8,2,128,128]{3,2,1,0:T(8,128)(2,1)S(1)}, u32[]{:S(2)}, u32[]{:S(2)}) collective-permute-start(bf16[8,2,128,128]{3,2,1,0:T(8,128)(2,1)S(1)} %get-tuple-element.64.refs_0_), channel_id=1, source_target_pairs={{0,12},{1,13},{2,14},{3,15},{4,0},{5,1},{6,2},{7,3},{8,4},{9,5},{1... | collective-permute-start | bytes 1572872 | tf_op jit(solution)/shard_map/ppermute | solution.py:32
  65.1 14.0 %collective-permute-start.11 = (bf16[4,2,128,128]{3,2,1,0:T(8,128)(2,1)S(1)}, bf16[4,2,128,128]{3,2,1,0:T(8,128)(2,1)S(1)}, u32[]{:S(2)}, u32[]{:S(2)}) collective-permute-start(bf16[4,2,128,128]{3,2,1,0:T(8,128)(2,1)S(1)} %get-tuple-element.48.refs_1_), channel_id=1, source_target_pairs={{0,12},{1,13},{2,14},{3,15},{4,0},{5,1},{6,2},{7,3},{8,4},{9,5},{1... | collective-permute-start | bytes 786440 | tf_op jit(solution)/shard_map/ppermute | solution.py:32
  65.2 14.5 %collective-permute-start.9 = (bf16[4,2,128,128]{3,2,1,0:T(8,128)(2,1)S(1)}, bf16[4,2,128,128]{3,2,1,0:T(8,128)(2,1)S(1)}, u32[]{:S(2)}, u32[]{:S(2)}) collective-permute-start(bf16[4,2,128,128]{3,2,1,0:T(8,128)(2,1)S(1)} %get-tuple-element.48.refs_1_), channel_id=1, source_target_pairs={{0,8},{1,9},{2,10},{3,11},{4,12},{5,13},{6,14},{7,15},{8,0},{9,1},... | collective-permute-start | bytes 786440 | tf_op jit(solution)/shard_map/ppermute | solution.py:32
  65.2 33.5 %collective-permute-start.38 = (bf16[8,2,128,128]{3,2,1,0:T(8,128)(2,1)S(1)}, bf16[8,2,128,128]{3,2,1,0:T(8,128)(2,1)S(1)}, u32[]{:S(2)}, u32[]{:S(2)}) collective-permute-start(bf16[8,2,128,128]{3,2,1,0:T(8,128)(2,1)S(1)} %get-tuple-element.64.refs_0_), channel_id=1, source_target_pairs={{0,8},{1,9},{2,10},{3,11},{4,12},{5,13},{6,14},{7,15},{8,0},{9,1},... | collective-permute-start | bytes 1572872 | tf_op jit(solution)/shard_map/ppermute | solution.py:32
  68.7 35.2 %collective-permute-start.37 = (bf16[8,2,128,128]{3,2,1,0:T(8,128)(2,1)S(1)}, bf16[8,2,128,128]{3,2,1,0:T(8,128)(2,1)}, u32[]{:S(2)}, u32[]{:S(2)}) collective-permute-start(bf16[8,2,128,128]{3,2,1,0:T(8,128)(2,1)S(1)} %get-tuple-element.64.refs_0_), channel_id=1, source_target_pairs={{0,4},{1,5},{2,6},{3,7},{4,8},{5,9},{6,10},{7,11},{8,12},{9,13},{1... | collective-permute-start | bytes 1572872 | tf_op jit(solution)/shard_map/ppermute | solution.py:32
  79.1 24.8 %collective-permute-start.42 = (bf16[8,2,128,128]{3,2,1,0:T(8,128)(2,1)S(1)}, bf16[8,2,128,128]{3,2,1,0:T(8,128)(2,1)}, u32[]{:S(2)}, u32[]{:S(2)}) collective-permute-start(bf16[8,2,128,128]{3,2,1,0:T(8,128)(2,1)S(1)} %get-tuple-element.65.refs_4_), channel_id=1, source_target_pairs={{0,3},{1,0},{2,1},{3,2},{4,7},{5,4},{6,5},{7,6},{8,11},{9,8},{10,9... | collective-permute-start | bytes 1572872 | tf_op jit(solution)/shard_map/ppermute | solution.py:32
  79.7 26.6 %collective-permute-start.41 = (bf16[8,2,128,128]{3,2,1,0:T(8,128)(2,1)S(1)}, bf16[8,2,128,128]{3,2,1,0:T(8,128)(2,1)}, u32[]{:S(2)}, u32[]{:S(2)}) collective-permute-start(bf16[8,2,128,128]{3,2,1,0:T(8,128)(2,1)S(1)} %get-tuple-element.65.refs_4_), channel_id=1, source_target_pairs={{0,2},{1,3},{2,0},{3,1},{4,6},{5,7},{6,4},{7,5},{8,10},{9,11},{10,... | collective-permute-start | bytes 1572872 | tf_op jit(solution)/shard_map/ppermute | solution.py:32
  95.2 18.5 %collective-permute-start.40 = (bf16[8,2,128,128]{3,2,1,0:T(8,128)(2,1)S(1)}, bf16[8,2,128,128]{3,2,1,0:T(8,128)(2,1)}, u32[]{:S(2)}, u32[]{:S(2)}) collective-permute-start(bf16[8,2,128,128]{3,2,1,0:T(8,128)(2,1)S(1)} %get-tuple-element.65.refs_4_), channel_id=1, source_target_pairs={{0,1},{1,2},{2,3},{3,0},{4,5},{5,6},{6,7},{7,4},{8,9},{9,10},{10,1... | collective-permute-start | bytes 1572872 | tf_op jit(solution)/shard_map/ppermute | solution.py:32
  99.5 36.6 %collective-permute-start.10 = (bf16[8,2,128,128]{3,2,1,0:T(8,128)(2,1)}, bf16[8,2,128,128]{3,2,1,0:T(8,128)(2,1)S(1)}, u32[]{:S(2)}, u32[]{:S(2)}) collective-permute-start(bf16[8,2,128,128]{3,2,1,0:T(8,128)(2,1)} %get-tuple-element.50.refs_0_), channel_id=1, source_target_pairs={{0,12},{1,13},{2,14},{3,15},{4,0},{5,1},{6,2},{7,3},{8,4},{9,5},{1... | collective-permute-start | bytes 1572872 | tf_op jit(solution)/shard_map/ppermute | solution.py:32
  103.9 23.2 %collective-permute-start.7 = (bf16[4,2,128,128]{3,2,1,0:T(8,128)(2,1)S(1)}, bf16[4,2,128,128]{3,2,1,0:T(8,128)(2,1)S(1)}, u32[]{:S(2)}, u32[]{:S(2)}) collective-permute-start(bf16[4,2,128,128]{3,2,1,0:T(8,128)(2,1)S(1)} %get-tuple-element.48.refs_1_), channel_id=1, source_target_pairs={{0,4},{1,5},{2,6},{3,7},{4,8},{5,9},{6,10},{7,11},{8,12},{9,13},{1... | collective-permute-start | bytes 786440 | tf_op jit(solution)/shard_map/ppermute | solution.py:32
  103.9 23.3 %collective-permute-start.17 = (bf16[4,2,128,128]{3,2,1,0:T(8,128)(2,1)S(1)}, bf16[4,2,128,128]{3,2,1,0:T(8,128)(2,1)S(1)}, u32[]{:S(2)}, u32[]{:S(2)}) collective-permute-start(bf16[4,2,128,128]{3,2,1,0:T(8,128)(2,1)S(1)} %get-tuple-element.49.refs_9_), channel_id=1, source_target_pairs={{0,3},{1,0},{2,1},{3,2},{4,7},{5,4},{6,5},{7,6},{8,11},{9,8},{10,9... | collective-permute-start | bytes 786440 | tf_op jit(solution)/shard_map/ppermute | solution.py:32
  106.3 25.3 %collective-permute-start.15 = (bf16[4,2,128,128]{3,2,1,0:T(8,128)(2,1)S(1)}, bf16[4,2,128,128]{3,2,1,0:T(8,128)(2,1)}, u32[]{:S(2)}, u32[]{:S(2)}) collective-permute-start(bf16[4,2,128,128]{3,2,1,0:T(8,128)(2,1)S(1)} %get-tuple-element.49.refs_9_), channel_id=1, source_target_pairs={{0,2},{1,3},{2,0},{3,1},{4,6},{5,7},{6,4},{7,5},{8,10},{9,11},{10,... | collective-permute-start | bytes 786440 | tf_op jit(solution)/shard_map/ppermute | solution.py:32
  113.7 20.4 %collective-permute-start.13 = (bf16[4,2,128,128]{3,2,1,0:T(8,128)(2,1)S(1)}, bf16[4,2,128,128]{3,2,1,0:T(8,128)(2,1)}, u32[]{:S(2)}, u32[]{:S(2)}) collective-permute-start(bf16[4,2,128,128]{3,2,1,0:T(8,128)(2,1)S(1)} %get-tuple-element.49.refs_9_), channel_id=1, source_target_pairs={{0,1},{1,2},{2,3},{3,0},{4,5},{5,6},{6,7},{7,4},{8,9},{9,10},{10,1... | collective-permute-start | bytes 786440 | tf_op jit(solution)/shard_map/ppermute | solution.py:32
  122.7 44.7 %all-to-all-start.2 = ((bf16[8,2,2,96,128]{4,3,2,1,0:T(8,128)(2,1)}), bf16[8,2,2,96,128]{4,3,2,1,0:T(8,128)(2,1)}, u32[]{:S(2)}, u32[]{:S(2)}) async-start(bf16[8,2,2,96,128]{4,3,2,1,0:T(8,128)(2,1)} %get-tuple-element.90), calls=%async_computation.2 | async-start | bytes 1572864 | tf_op jit(solution)/shard_map/all_to_all | solution.py:208
  127.1 16.6 %collective-permute-start.8 = (bf16[8,2,128,128]{3,2,1,0:T(8,128)(2,1)}, bf16[8,2,128,128]{3,2,1,0:T(8,128)(2,1)S(1)}, u32[]{:S(2)}, u32[]{:S(2)}) collective-permute-start(bf16[8,2,128,128]{3,2,1,0:T(8,128)(2,1)} %get-tuple-element.50.refs_0_), channel_id=1, source_target_pairs={{0,8},{1,9},{2,10},{3,11},{4,12},{5,13},{6,14},{7,15},{8,0},{9,1},... | collective-permute-start | bytes 1572872 | tf_op jit(solution)/shard_map/ppermute | solution.py:32
  127.2 27.2 %collective-permute-start.6 = (bf16[8,2,128,128]{3,2,1,0:T(8,128)(2,1)}, bf16[8,2,128,128]{3,2,1,0:T(8,128)(2,1)S(1)}, u32[]{:S(2)}, u32[]{:S(2)}) collective-permute-start(bf16[8,2,128,128]{3,2,1,0:T(8,128)(2,1)} %get-tuple-element.50.refs_0_), channel_id=1, source_target_pairs={{0,4},{1,5},{2,6},{3,7},{4,8},{5,9},{6,10},{7,11},{8,12},{9,13},{1... | collective-permute-start | bytes 1572872 | tf_op jit(solution)/shard_map/ppermute | solution.py:32
  131.6 25.0 %collective-permute-start.16 = (bf16[8,2,128,128]{3,2,1,0:T(8,128)(2,1)S(1)}, bf16[8,2,128,128]{3,2,1,0:T(8,128)(2,1)S(1)}, u32[]{:S(2)}, u32[]{:S(2)}) collective-permute-start(bf16[8,2,128,128]{3,2,1,0:T(8,128)(2,1)S(1)} %get-tuple-element.51.refs_8_), channel_id=1, source_target_pairs={{0,3},{1,0},{2,1},{3,2},{4,7},{5,4},{6,5},{7,6},{8,11},{9,8},{10,9... | collective-permute-start | bytes 1572872 | tf_op jit(solution)/shard_map/ppermute | solution.py:32
  134.1 22.6 %collective-permute-start.14 = (bf16[8,2,128,128]{3,2,1,0:T(8,128)(2,1)S(1)}, bf16[8,2,128,128]{3,2,1,0:T(8,128)(2,1)S(1)}, u32[]{:S(2)}, u32[]{:S(2)}) collective-permute-start(bf16[8,2,128,128]{3,2,1,0:T(8,128)(2,1)S(1)} %get-tuple-element.51.refs_8_), channel_id=1, source_target_pairs={{0,2},{1,3},{2,0},{3,1},{4,6},{5,7},{6,4},{7,5},{8,10},{9,11},{10,... | collective-permute-start | bytes 1572872 | tf_op jit(solution)/shard_map/ppermute | solution.py:32
  136.1 24.2 %collective-permute-start.12 = (bf16[8,2,128,128]{3,2,1,0:T(8,128)(2,1)S(1)}, bf16[8,2,128,128]{3,2,1,0:T(8,128)(2,1)S(1)}, u32[]{:S(2)}, u32[]{:S(2)}) collective-permute-start(bf16[8,2,128,128]{3,2,1,0:T(8,128)(2,1)S(1)} %get-tuple-element.51.refs_8_), channel_id=1, source_target_pairs={{0,1},{1,2},{2,3},{3,0},{4,5},{5,6},{6,7},{7,4},{8,9},{9,10},{10,1... | collective-permute-start | bytes 1572872 | tf_op jit(solution)/shard_map/ppermute | solution.py:32
  167.4 45.0 %all-to-all-start = ((bf16[8,2,2,256,128]{4,3,2,1,0:T(8,128)(2,1)}), bf16[8,2,2,256,128]{4,3,2,1,0:T(8,128)(2,1)}, u32[]{:S(2)}, u32[]{:S(2)}) async-start(bf16[8,2,2,256,128]{4,3,2,1,0:T(8,128)(2,1)} %shard_map.66), calls=%async_computation | async-start | bytes 4194304 | tf_op jit(solution)/shard_map/all_to_all | solution.py:208
  175.5 14.9 %collective-permute-start.33 = (bf16[8,2,128,128]{3,2,1,0:T(8,128)(2,1)S(1)}, bf16[8,2,128,128]{3,2,1,0:T(8,128)(2,1)S(1)}, u32[]{:S(2)}, u32[]{:S(2)}) collective-permute-start(bf16[8,2,128,128]{3,2,1,0:T(8,128)(2,1)S(1)} %get-tuple-element.62.refs_0_), channel_id=1, source_target_pairs={{0,12},{1,13},{2,14},{3,15},{4,0},{5,1},{6,2},{7,3},{8,4},{9,5},{1... | collective-permute-start | bytes 1572872 | tf_op jit(solution)/shard_map/ppermute | solution.py:32
  175.5 16.4 %collective-permute-start.32 = (bf16[8,2,128,128]{3,2,1,0:T(8,128)(2,1)S(1)}, bf16[8,2,128,128]{3,2,1,0:T(8,128)(2,1)S(1)}, u32[]{:S(2)}, u32[]{:S(2)}) collective-permute-start(bf16[8,2,128,128]{3,2,1,0:T(8,128)(2,1)S(1)} %get-tuple-element.62.refs_0_), channel_id=1, source_target_pairs={{0,8},{1,9},{2,10},{3,11},{4,12},{5,13},{6,14},{7,15},{8,0},{9,1},... | collective-permute-start | bytes 1572872 | tf_op jit(solution)/shard_map/ppermute | solution.py:32
  178.0 24.7 %collective-permute-start.31 = (bf16[8,2,128,128]{3,2,1,0:T(8,128)(2,1)S(1)}, bf16[8,2,128,128]{3,2,1,0:T(8,128)(2,1)S(1)}, u32[]{:S(2)}, u32[]{:S(2)}) collective-permute-start(bf16[8,2,128,128]{3,2,1,0:T(8,128)(2,1)S(1)} %get-tuple-element.62.refs_0_), channel_id=1, source_target_pairs={{0,4},{1,5},{2,6},{3,7},{4,8},{5,9},{6,10},{7,11},{8,12},{9,13},{1... | collective-permute-start | bytes 1572872 | tf_op jit(solution)/shard_map/ppermute | solution.py:32
  178.0 24.7 %collective-permute-start.36 = (bf16[8,2,128,128]{3,2,1,0:T(8,128)(2,1)S(1)}, bf16[8,2,128,128]{3,2,1,0:T(8,128)(2,1)S(1)}, u32[]{:S(2)}, u32[]{:S(2)}) collective-permute-start(bf16[8,2,128,128]{3,2,1,0:T(8,128)(2,1)S(1)} %get-tuple-element.63.refs_4_), channel_id=1, source_target_pairs={{0,3},{1,0},{2,1},{3,2},{4,7},{5,4},{6,5},{7,6},{8,11},{9,8},{10,9... | collective-permute-start | bytes 1572872 | tf_op jit(solution)/shard_map/ppermute | solution.py:32
  178.9 23.8 %collective-permute-start.35 = (bf16[8,2,128,128]{3,2,1,0:T(8,128)(2,1)S(1)}, bf16[8,2,128,128]{3,2,1,0:T(8,128)(2,1)S(1)}, u32[]{:S(2)}, u32[]{:S(2)}) collective-permute-start(bf16[8,2,128,128]{3,2,1,0:T(8,128)(2,1)S(1)} %get-tuple-element.63.refs_4_), channel_id=1, source_target_pairs={{0,2},{1,3},{2,0},{3,1},{4,6},{5,7},{6,4},{7,5},{8,10},{9,11},{10,... | collective-permute-start | bytes 1572872 | tf_op jit(solution)/shard_map/ppermute | solution.py:32
  190.3 15.2 %collective-permute-start.34 = (bf16[8,2,128,128]{3,2,1,0:T(8,128)(2,1)S(1)}, bf16[8,2,128,128]{3,2,1,0:T(8,128)(2,1)S(1)}, u32[]{:S(2)}, u32[]{:S(2)}) collective-permute-start(bf16[8,2,128,128]{3,2,1,0:T(8,128)(2,1)S(1)} %get-tuple-element.63.refs_4_), channel_id=1, source_target_pairs={{0,1},{1,2},{2,3},{3,0},{4,5},{5,6},{6,7},{7,4},{8,9},{9,10},{10,1... | collective-permute-start | bytes 1572872 | tf_op jit(solution)/shard_map/ppermute | solution.py:32
  212.3 53.6 %all-to-all-start.1 = ((bf16[8,2,2,256,128]{4,3,2,1,0:T(8,128)(2,1)}), bf16[8,2,2,256,128]{4,3,2,1,0:T(8,128)(2,1)S(1)}, u32[]{:S(2)}, u32[]{:S(2)}) async-start(bf16[8,2,2,256,128]{4,3,2,1,0:T(8,128)(2,1)} %shard_map.70), calls=%async_computation.1 | async-start | bytes 4194304 | tf_op jit(solution)/shard_map/all_to_all | solution.py:208
  223.9 25.8 %collective-permute-start.25 = (bf16[2,2,256,128]{3,2,1,0:T(8,128)(2,1)}, bf16[2,2,256,128]{3,2,1,0:T(8,128)(2,1)S(1)}, u32[]{:S(2)}, u32[]{:S(2)}) collective-permute-start(bf16[2,2,256,128]{3,2,1,0:T(8,128)(2,1)} %get-tuple-element.56), channel_id=1, source_target_pairs={{0,32},{16,48},{32,64},{48,80},{64,96},{80,112},{96,0},{112,16},{1... | collective-permute-start | bytes 786440 | tf_op jit(solution)/shard_map/ppermute | solution.py:217
  225.5 29.0 %collective-permute-start.26 = (bf16[2,2,256,128]{3,2,1,0:T(8,128)(2,1)}, bf16[2,2,256,128]{3,2,1,0:T(8,128)(2,1)S(1)}, u32[]{:S(2)}, u32[]{:S(2)}) collective-permute-start(bf16[2,2,256,128]{3,2,1,0:T(8,128)(2,1)} %get-tuple-element.57), channel_id=1, source_target_pairs={{0,48},{16,32},{32,80},{48,64},{64,112},{80,96},{96,16},{112,0},{1... | collective-permute-start | bytes 786440 | tf_op jit(solution)/shard_map/ppermute | solution.py:217
  226.7 34.7 %collective-permute-start.27 = (bf16[2,2,256,128]{3,2,1,0:T(8,128)(2,1)}, bf16[2,2,256,128]{3,2,1,0:T(8,128)(2,1)S(1)}, u32[]{:S(2)}, u32[]{:S(2)}) collective-permute-start(bf16[2,2,256,128]{3,2,1,0:T(8,128)(2,1)} %get-tuple-element.58), channel_id=1, source_target_pairs={{0,64},{16,80},{32,96},{48,112},{64,0},{80,16},{96,32},{112,48},{1... | collective-permute-start | bytes 786440 | tf_op jit(solution)/shard_map/ppermute | solution.py:217
  228.2 37.7 %collective-permute-start.28 = (bf16[2,2,256,128]{3,2,1,0:T(8,128)(2,1)}, bf16[2,2,256,128]{3,2,1,0:T(8,128)(2,1)S(1)}, u32[]{:S(2)}, u32[]{:S(2)}) collective-permute-start(bf16[2,2,256,128]{3,2,1,0:T(8,128)(2,1)} %get-tuple-element.59), channel_id=1, source_target_pairs={{0,80},{16,64},{32,112},{48,96},{64,16},{80,0},{96,48},{112,32},{1... | collective-permute-start | bytes 786440 | tf_op jit(solution)/shard_map/ppermute | solution.py:217
  230.0 35.9 %collective-permute-start.29 = (bf16[2,2,256,128]{3,2,1,0:T(8,128)(2,1)}, bf16[2,2,256,128]{3,2,1,0:T(8,128)(2,1)}, u32[]{:S(2)}, u32[]{:S(2)}) collective-permute-start(bf16[2,2,256,128]{3,2,1,0:T(8,128)(2,1)} %get-tuple-element.60), channel_id=1, source_target_pairs={{0,96},{16,112},{32,0},{48,16},{64,32},{80,48},{96,64},{112,80},{1... | collective-permute-start | bytes 786440 | tf_op jit(solution)/shard_map/ppermute | solution.py:217
  249.7 16.2 %collective-permute-start.30 = (bf16[2,2,256,128]{3,2,1,0:T(8,128)(2,1)}, bf16[2,2,256,128]{3,2,1,0:T(8,128)(2,1)}, u32[]{:S(2)}, u32[]{:S(2)}) collective-permute-start(bf16[2,2,256,128]{3,2,1,0:T(8,128)(2,1)} %get-tuple-element.61), channel_id=1, source_target_pairs={{0,112},{16,96},{32,16},{48,0},{64,48},{80,32},{96,80},{112,64},{1... | collective-permute-start | bytes 786440 | tf_op jit(solution)/shard_map/ppermute | solution.py:217
  275.3 74.3 %all-to-all-start.3 = ((bf16[16,96,512]{2,1,0:T(8,128)(2,1)}), bf16[16,96,512]{2,1,0:T(8,128)(2,1)S(1)}, u32[]{:S(2)}, u32[]{:S(2)}) async-start(bf16[16,96,512]{2,1,0:T(8,128)(2,1)} %shard_map.74), calls=%async_computation.3 | async-start | bytes 3145728 | tf_op jit(solution)/shard_map/all_to_all | solution.py:496
  281.2 17.6 %collective-permute-start.45 = (bf16[2,2,160,128]{3,2,1,0:T(8,128)(2,1)S(1)}, bf16[2,2,160,128]{3,2,1,0:T(8,128)(2,1)S(1)}, u32[]{:S(2)}, u32[]{:S(2)}) collective-permute-start(bf16[2,2,160,128]{3,2,1,0:T(8,128)(2,1)S(1)} %copy-done.62), channel_id=1, source_target_pairs={{0,48},{16,32},{32,80},{48,64},{64,112},{80,96},{96,16},{112,0},{1... | collective-permute-start | bytes 491528 | tf_op jit(solution)/shard_map/ppermute | solution.py:217
  282.1 16.8 %collective-permute-start.46 = (bf16[2,2,160,128]{3,2,1,0:T(8,128)(2,1)S(1)}, bf16[2,2,160,128]{3,2,1,0:T(8,128)(2,1)S(1)}, u32[]{:S(2)}, u32[]{:S(2)}) collective-permute-start(bf16[2,2,160,128]{3,2,1,0:T(8,128)(2,1)S(1)} %copy-done.61), channel_id=1, source_target_pairs={{0,64},{16,80},{32,96},{48,112},{64,0},{80,16},{96,32},{112,48},{1... | collective-permute-start | bytes 491528 | tf_op jit(solution)/shard_map/ppermute | solution.py:217
  311.4 18.5 %collective-permute-start.51 = (bf16[4,160,256]{2,1,0:T(8,128)(2,1)}, bf16[4,160,256]{2,1,0:T(8,128)(2,1)S(1)}, u32[]{:S(2)}, u32[]{:S(2)}) collective-permute-start(bf16[4,160,256]{2,1,0:T(8,128)(2,1)} %get-tuple-element.76), channel_id=1, source_target_pairs={{0,2},{1,3},{2,0},{3,1},{4,6},{5,7},{6,4},{7,5},{8,10},{9,11},{10,... | collective-permute-start | bytes 983048 | tf_op jit(solution)/shard_map/ppermute | solution.py:32
  314.0 15.8 %collective-permute-start.52 = (bf16[4,160,256]{2,1,0:T(8,128)(2,1)}, bf16[4,160,256]{2,1,0:T(8,128)(2,1)S(1)}, u32[]{:S(2)}, u32[]{:S(2)}) collective-permute-start(bf16[4,160,256]{2,1,0:T(8,128)(2,1)} %get-tuple-element.77), channel_id=1, source_target_pairs={{0,3},{1,0},{2,1},{3,2},{4,7},{5,4},{6,5},{7,6},{8,11},{9,8},{10,9... | collective-permute-start | bytes 983048 | tf_op jit(solution)/shard_map/ppermute | solution.py:32
  315.5 14.3 %collective-permute-start.53 = (bf16[4,160,256]{2,1,0:T(8,128)(2,1)}, bf16[4,160,256]{2,1,0:T(8,128)(2,1)S(1)}, u32[]{:S(2)}, u32[]{:S(2)}) collective-permute-start(bf16[4,160,256]{2,1,0:T(8,128)(2,1)} %get-tuple-element.79), channel_id=1, source_target_pairs={{0,4},{1,5},{2,6},{3,7},{4,8},{5,9},{6,10},{7,11},{8,12},{9,13},{1... | collective-permute-start | bytes 983048 | tf_op jit(solution)/shard_map/ppermute | solution.py:32
  317.0 17.4 %collective-permute-start.54 = (bf16[4,160,256]{2,1,0:T(8,128)(2,1)}, bf16[4,160,256]{2,1,0:T(8,128)(2,1)S(1)}, u32[]{:S(2)}, u32[]{:S(2)}) collective-permute-start(bf16[4,160,256]{2,1,0:T(8,128)(2,1)} %get-tuple-element.80), channel_id=1, source_target_pairs={{0,8},{1,9},{2,10},{3,11},{4,12},{5,13},{6,14},{7,15},{8,0},{9,1},... | collective-permute-start | bytes 983048 | tf_op jit(solution)/shard_map/ppermute | solution.py:32
  (83 other events, 1133.9 us)
